TPU v7x, 32 devices: a whole 2x2x4 slice. The times are simulated.
32 devices in a mesh: seq: 8 (over z, y), fsdp: 4 (over x, core).
Axes of the slice: x: 2, y: 2, z: 4, core: 2. Of those that a mesh axis runs over, the one named last changes fastest.
Arguments:
- hidden_in: bfloat16 [4, 1024, 2048], P('fsdp', 'seq'), may hold values from -18 to 18
- ln1_gain: bfloat16 [2048], P(('seq', 'fsdp')), may hold values from 0.5 to 1.5
- ln1_bias: bfloat16 [2048], P(('seq', 'fsdp')), may hold values from -1.1953125 to 1.1953125
- qkv_weight: bfloat16 [2048, 6144], P(('seq', 'fsdp')), may hold values from -0.125 to 0.125
- qkv_bias: bfloat16 [3, 2048], P(None, ('seq', 'fsdp')), may hold values from -3 to 3
- out_weight: bfloat16 [2048, 2048], P(('seq', 'fsdp')), may hold values from -3 to 3
- ln2_gain: bfloat16 [2048], P(('seq', 'fsdp')), may hold values from 0.5 to 1.5
- ln2_bias: bfloat16 [2048], P(('seq', 'fsdp')), may hold values from -1.1953125 to 1.1953125
- gate_weight: bfloat16 [2048, 5632], P(('seq', 'fsdp')), may hold values from -0.125 to 0.125
- up_weight: bfloat16 [2048, 5632], P(('seq', 'fsdp')), may hold values from -0.125 to 0.125
- down_weight: bfloat16 [5632, 2048], P(('seq', 'fsdp')), may hold values from -0.078125 to 0.078125
- seq_lengths: int32 [4, 3], P('fsdp'), may hold values from 1 to 512, 640 in all within a row
- deal_order: int32 [4, 1024], P('fsdp'), may hold values from 0 to 1023, each once within a row
- out_grad: bfloat16 [4, 1024, 2048], P('fsdp', 'seq'), may hold values from -6 to 6
Outputs:
- layer_out: bfloat16 [4, 1024, 2048], P('fsdp', 'seq')
- input_grad: float32 [4, 1024, 2048], P('fsdp', 'seq')
- ln1_gain_grad: float32 [2048], P(('seq', 'fsdp'))
- ln1_bias_grad: float32 [2048], P(('seq', 'fsdp'))
- qkv_weight_grad: float32 [2048, 6144], P(('seq', 'fsdp'))
- qkv_bias_grad: float32 [3, 2048], P(None, ('seq', 'fsdp'))
- out_weight_grad: float32 [2048, 2048], P(('seq', 'fsdp'))
- ln2_gain_grad: float32 [2048], P(('seq', 'fsdp'))
- ln2_bias_grad: float32 [2048], P(('seq', 'fsdp'))
- gate_weight_grad: float32 [2048, 5632], P(('seq', 'fsdp'))
- up_weight_grad: float32 [2048, 5632], P(('seq', 'fsdp'))
- down_weight_grad: float32 [5632, 2048], P(('seq', 'fsdp'))
- branch_rms: float32 [3], replicated
Inputs may be any that keep to these rules, and one draw needn't show every extreme that they name: `seq_lengths`: each group's lengths sum to 640, and its longest is exactly 512. `deal_order`: each group's row is a permutation of its positions.
All inputs are finite; a program needn't handle non-finite values.
Results may differ from a plain program's by a relative error of at most 0.00705.
The roundings to bfloat16 on the way count: a program that leaves them out, or rounds other values in their place, can miss the bound.
Values may be sent and summed in bfloat16 or wider, within the bound.
A program may use at most 384 MiB of HBM per device.

v0:
```python
import jax
import jax.numpy as jnp
from jax import lax
from jax.sharding import PartitionSpec as P

HEAD_DIM = 64
ROT = 16


EPS = 1e-05


def normalize(values):
    center = values - jnp.mean(values, -1, keepdims=True)
    spread = jnp.mean(center * center, -1, keepdims=True)
    rstd = lax.rsqrt(spread + EPS)
    return (center * rstd, rstd)


def norm_back(grad, normed, rstd, gain):
    scaled = grad * gain
    inner = (
        scaled
        - jnp.mean(scaled, -1, keepdims=True)
        - normed * jnp.mean(scaled * normed, -1, keepdims=True)
    )
    return (rstd * inner, jnp.sum(grad * normed, 0), jnp.sum(grad, 0))


def segment_of(pos, lengths):
    nseg = lengths.shape[0]
    ends = jnp.cumsum(lengths)
    seg = jnp.sum((pos[:, None] >= ends[None, :]).astype(jnp.int32), 1)
    starts = jnp.concatenate([jnp.zeros((1,), jnp.int32), ends[:-1]])
    start = jnp.sum(
        jnp.where(seg[:, None] == jnp.arange(nseg, dtype=jnp.int32)[None, :], starts[None, :], 0), 1
    )
    start = jnp.where(seg < nseg, start, pos)
    return (seg, start)


def rotate(values, rel, sign):
    count = values.shape[0]
    view = values.reshape(count, -1, HEAD_DIM)
    half = ROT // 2
    freq = 10000.0 ** (-2.0 * jnp.arange(half, dtype=jnp.float32) / ROT)
    angle = rel[:, None] * freq[None, :]
    cosine = jnp.cos(angle)[:, None, :]
    sine = jnp.sin(angle)[:, None, :]
    first = view[..., :half]
    second = view[..., half:ROT]
    turned = jnp.concatenate(
        [
            first * cosine - sign * second * sine,
            second * cosine + sign * first * sine,
            view[..., ROT:],
        ],
        -1,
    )
    return turned.reshape(count, -1)


def outer(left, right):
    return lax.dot_general(
        left, right, (((0,), (0,)), ((), ())), preferred_element_type=jnp.float32
    )


def times_transposed(left, right):
    return lax.dot_general(
        left, right, (((1,), (1,)), ((), ())), preferred_element_type=jnp.float32
    )


def mlp_forward(gate, upper):
    sigma = jax.nn.sigmoid(gate)
    return ((gate * sigma * upper).astype(jnp.bfloat16), sigma)


def mlp_backward(hidden_grad, gate, upper, sigma):
    up_act = (hidden_grad * gate * sigma).astype(jnp.bfloat16)
    gate_act = (hidden_grad * upper * sigma * (1.0 + gate * (1.0 - sigma))).astype(jnp.bfloat16)
    return (gate_act, up_act)


def body(
    hidden_in,
    ln1_gain,
    ln1_bias,
    qkv_weight,
    qkv_bias,
    out_weight,
    ln2_gain,
    ln2_bias,
    gate_weight,
    up_weight,
    down_weight,
    seq_lengths,
    deal_order,
    out_grad,
):
    rows = hidden_in.shape[1]
    width = hidden_in.shape[2]
    stream = hidden_in[0].astype(jnp.float32)
    cotangent = out_grad[0].astype(jnp.float32)
    order = deal_order[0]
    lengths = seq_lengths[0]
    nseg = lengths.shape[0]
    group_rows = order.shape[0]
    valid_rows = group_rows * 5 // 8
    longest = valid_rows * 4 // 5
    blk = min(512, group_rows)
    keys = min(group_rows, longest + blk)
    nblocks = group_rows // blk
    scale = HEAD_DIM ** (-0.5)
    local_pos = lax.dynamic_slice_in_dim(order, lax.axis_index("seq") * rows, rows)
    local_seg, local_start = segment_of(local_pos, lengths)
    rel = (local_pos - local_start).astype(jnp.float32)
    valid = (local_pos < valid_rows).astype(jnp.float32)[:, None]
    normed1, rstd1 = normalize(stream)
    inverse = (
        jnp.zeros((group_rows,), jnp.int32).at[order].set(jnp.arange(group_rows, dtype=jnp.int32))
    )
    seg_p, start_p = segment_of(jnp.arange(group_rows, dtype=jnp.int32), lengths)

    def to_pack(values):
        heads_here = values.shape[1] // HEAD_DIM
        return values[inverse].reshape(group_rows, heads_here, HEAD_DIM)

    def window(index, packed):
        query_p, key_p, value_p = packed
        first = index * blk
        key_first = jnp.clip(jnp.minimum(start_p[first], group_rows - keys), 0, group_rows - keys)
        qpos = first + jnp.arange(blk, dtype=jnp.int32)
        kpos = key_first + jnp.arange(keys, dtype=jnp.int32)
        qseg = lax.dynamic_slice_in_dim(seg_p, first, blk)
        kseg = lax.dynamic_slice_in_dim(seg_p, key_first, keys)
        allowed = (qseg[:, None] == kseg[None, :]) & (qseg[:, None] < nseg) & (
            kpos[None, :] <= qpos[:, None]
        ) | (kpos[None, :] == qpos[:, None])
        qblock = lax.dynamic_slice_in_dim(query_p, first, blk)
        kblock = lax.dynamic_slice_in_dim(key_p, key_first, keys)
        vblock = lax.dynamic_slice_in_dim(value_p, key_first, keys)
        scores = (
            jnp.einsum("qhd,khd->hqk", qblock, kblock, preferred_element_type=jnp.float32) * scale
        )
        scores = jnp.where(allowed[None], scores, -1e30)
        return (first, key_first, qblock, kblock, vblock, scores)

    def fetch_full(gain, shift, first_w, middle_w, last_w):
        return (
            lax.all_gather(gain, ("seq", "fsdp"), axis=0, tiled=True),
            lax.all_gather(shift, ("seq", "fsdp"), axis=0, tiled=True),
            lax.all_gather(first_w, ("seq", "fsdp"), axis=0, tiled=True),
            lax.all_gather(middle_w, ("seq", "fsdp"), axis=0, tiled=True),
            lax.all_gather(last_w, ("seq", "fsdp"), axis=0, tiled=True),
        )

    def reduce_full(gain, shift, first_w, middle_w, last_w):
        return (
            lax.psum_scatter(gain, ("seq", "fsdp"), scatter_dimension=0, tiled=True),
            lax.psum_scatter(shift, ("seq", "fsdp"), scatter_dimension=0, tiled=True),
            lax.psum_scatter(first_w, ("seq", "fsdp"), scatter_dimension=0, tiled=True),
            lax.psum_scatter(middle_w, ("seq", "fsdp"), scatter_dimension=0, tiled=True),
            lax.psum_scatter(last_w, ("seq", "fsdp"), scatter_dimension=0, tiled=True),
        )

    gain1, shift1, qkv_w, qkv_b, out_w = fetch_full(
        ln1_gain, ln1_bias, qkv_weight, qkv_bias.T, out_weight
    )
    qkv_shift = qkv_b.T.reshape(-1).astype(jnp.float32)
    first_in = (normed1 * gain1.astype(jnp.float32) + shift1.astype(jnp.float32)).astype(
        jnp.bfloat16
    )
    qkv = jnp.dot(first_in, qkv_w, preferred_element_type=jnp.float32) + qkv_shift
    query = rotate(qkv[:, :width], rel, 1.0).astype(jnp.bfloat16)
    keyset = rotate(qkv[:, width : 2 * width], rel, 1.0).astype(jnp.bfloat16)
    valueset = qkv[:, 2 * width :].astype(jnp.bfloat16)
    query, keyset, valueset = (query, keyset, valueset)
    query_h = lax.all_to_all(query, "seq", split_axis=1, concat_axis=0, tiled=True)
    key_h = lax.all_to_all(keyset, "seq", split_axis=1, concat_axis=0, tiled=True)
    value_h = lax.all_to_all(valueset, "seq", split_axis=1, concat_axis=0, tiled=True)
    packed = (to_pack(query_h), to_pack(key_h), to_pack(value_h))

    def attend_block(index):
        first, key_first, qblock, kblock, vblock, scores = window(index, packed)
        top = jnp.max(scores, -1, keepdims=True)
        expo = jnp.exp(scores - top)
        total = jnp.sum(expo, -1, keepdims=True)
        probs = (expo / total).astype(jnp.bfloat16)
        mixed = jnp.einsum("hqk,khd->qhd", probs, vblock, preferred_element_type=jnp.float32)
        return (mixed, (top + jnp.log(total))[..., 0])

    mixed_all, lse_all = lax.map(attend_block, jnp.arange(nblocks, dtype=jnp.int32))
    mixed_pack = mixed_all.reshape(group_rows, -1)
    heads_out = lax.all_to_all(
        mixed_pack[order].astype(jnp.bfloat16), "seq", split_axis=0, concat_axis=1, tiled=True
    )
    heads_out, packed, lse_all = (heads_out, packed, lse_all)
    attn = jnp.dot(heads_out, out_w, preferred_element_type=jnp.float32)
    resid = stream + attn
    gain2, shift2, gate_w, up_w, down_w = fetch_full(
        ln2_gain, ln2_bias, gate_weight, up_weight, down_weight
    )
    normed2, rstd2 = normalize(resid)
    second_in = (normed2 * gain2.astype(jnp.float32) + shift2.astype(jnp.float32)).astype(
        jnp.bfloat16
    )
    gate = jnp.dot(second_in, gate_w, preferred_element_type=jnp.float32)
    upper = jnp.dot(second_in, up_w, preferred_element_type=jnp.float32)
    hidden, sigma = mlp_forward(gate, upper)
    mlp = jnp.dot(hidden, down_w, preferred_element_type=jnp.float32)
    result = resid + mlp
    sums = lax.psum(
        (
            jnp.sum(valid * result * result),
            jnp.sum(valid * attn * attn),
            jnp.sum(valid * mlp * mlp),
        ),
        ("seq", "fsdp"),
    )
    count = valid_rows * lax.axis_size("fsdp") * width
    rms = jnp.sqrt(jnp.stack(sums) / count)
    gain2, shift2, gate_w, up_w, down_w = fetch_full(
        ln2_gain, ln2_bias, gate_weight, up_weight, down_weight
    )
    mlp_grad = cotangent.astype(jnp.bfloat16)
    down_grad = outer(hidden, mlp_grad)
    hidden_grad = times_transposed(mlp_grad, down_w)
    gate_act, up_act = mlp_backward(hidden_grad, gate, upper, sigma)
    gate_grad = outer(second_in, gate_act)
    up_grad = outer(second_in, up_act)
    second_grad = times_transposed(gate_act, gate_w) + times_transposed(up_act, up_w)
    resid_part, gain2_grad, shift2_grad = norm_back(
        second_grad, normed2, rstd2, gain2.astype(jnp.float32)
    )
    resid_grad = cotangent + resid_part
    mlp_shards = reduce_full(gain2_grad, shift2_grad, gate_grad, up_grad, down_grad)
    gain1, shift1, qkv_w, qkv_b, out_w = fetch_full(
        ln1_gain, ln1_bias, qkv_weight, qkv_bias.T, out_weight
    )
    attn_grad = resid_grad.astype(jnp.bfloat16)
    out_grad_w = outer(heads_out, attn_grad)
    mixed_grad = times_transposed(attn_grad, out_w).astype(jnp.bfloat16)
    mixed_grad_p = to_pack(
        lax.all_to_all(mixed_grad, "seq", split_axis=1, concat_axis=0, tiled=True)
    )

    def back_block(index, carry):
        query_acc, key_acc, value_acc = carry
        first, key_first, qblock, kblock, vblock, scores = window(index, packed)
        probs = jnp.exp(scores - lse_all[index][:, :, None])
        dblock = lax.dynamic_slice_in_dim(mixed_grad_p, first, blk)
        value_part = jnp.einsum(
            "hqk,qhd->khd", probs.astype(jnp.bfloat16), dblock, preferred_element_type=jnp.float32
        )
        prob_grad = jnp.einsum("qhd,khd->hqk", dblock, vblock, preferred_element_type=jnp.float32)
        inner = jnp.sum(probs * prob_grad, -1, keepdims=True)
        score_grad = (probs * (prob_grad - inner)).astype(jnp.bfloat16)
        query_part = (
            jnp.einsum("hqk,khd->qhd", score_grad, kblock, preferred_element_type=jnp.float32)
            * scale
        )
        key_part = (
            jnp.einsum("hqk,qhd->khd", score_grad, qblock, preferred_element_type=jnp.float32)
            * scale
        )
        query_acc = lax.dynamic_update_slice_in_dim(query_acc, query_part, first, 0)
        key_old = lax.dynamic_slice_in_dim(key_acc, key_first, keys)
        key_acc = lax.dynamic_update_slice_in_dim(key_acc, key_old + key_part, key_first, 0)
        value_old = lax.dynamic_slice_in_dim(value_acc, key_first, keys)
        value_acc = lax.dynamic_update_slice_in_dim(value_acc, value_old + value_part, key_first, 0)
        return (query_acc, key_acc, value_acc)

    zeros = jnp.zeros(packed[0].shape, jnp.float32)
    query_acc, key_acc, value_acc = lax.fori_loop(0, nblocks, back_block, (zeros, zeros, zeros))

    def to_dealt(values):
        return values.reshape(group_rows, -1)[order].astype(jnp.bfloat16)

    query_g = lax.all_to_all(to_dealt(query_acc), "seq", split_axis=0, concat_axis=1, tiled=True)
    key_g = lax.all_to_all(to_dealt(key_acc), "seq", split_axis=0, concat_axis=1, tiled=True)
    value_g = lax.all_to_all(to_dealt(value_acc), "seq", split_axis=0, concat_axis=1, tiled=True)
    qkv_act = jnp.concatenate(
        [
            rotate(query_g.astype(jnp.float32), rel, -1.0),
            rotate(key_g.astype(jnp.float32), rel, -1.0),
            value_g.astype(jnp.float32),
        ],
        1,
    ).astype(jnp.bfloat16)
    qkv_bias_grad = jnp.sum(qkv_act.astype(jnp.float32), 0).reshape(3, width).T
    qkv_grad = outer(first_in, qkv_act)
    first_grad = times_transposed(qkv_act, qkv_w)
    input_part, gain1_grad, shift1_grad = norm_back(
        first_grad, normed1, rstd1, gain1.astype(jnp.float32)
    )
    input_grad = resid_grad + input_part
    attn_shards = reduce_full(gain1_grad, shift1_grad, qkv_grad, qkv_bias_grad, out_grad_w)
    return (
        result.astype(jnp.bfloat16)[None],
        input_grad[None],
        attn_shards[0],
        attn_shards[1],
        attn_shards[2],
        attn_shards[3].T,
        attn_shards[4],
        mlp_shards[0],
        mlp_shards[1],
        mlp_shards[2],
        mlp_shards[3],
        mlp_shards[4],
        rms,
    )


def solution(mesh):
    in_specs = (
        P("fsdp", "seq", None),
        P(("seq", "fsdp")),
        P(("seq", "fsdp")),
        P(("seq", "fsdp"), None),
        P(None, ("seq", "fsdp")),
        P(("seq", "fsdp"), None),
        P(("seq", "fsdp")),
        P(("seq", "fsdp")),
        P(("seq", "fsdp"), None),
        P(("seq", "fsdp"), None),
        P(("seq", "fsdp"), None),
        P("fsdp", None),
        P("fsdp", None),
        P("fsdp", "seq", None),
    )
    out_specs = (
        P("fsdp", "seq", None),
        P("fsdp", "seq", None),
        P(("seq", "fsdp")),
        P(("seq", "fsdp")),
        P(("seq", "fsdp"), None),
        P(None, ("seq", "fsdp")),
        P(("seq", "fsdp"), None),
        P(("seq", "fsdp")),
        P(("seq", "fsdp")),
        P(("seq", "fsdp"), None),
        P(("seq", "fsdp"), None),
        P(("seq", "fsdp"), None),
        P(),
    )
    return jax.shard_map(body, mesh=mesh, in_specs=in_specs, out_specs=out_specs, check_vma=False)
```

profile of v0, /device:TPU:0, one launch (start us, length us, event | category | flops | bytes accessed | tf_op | source)
XLA Modules:
  0.0 3146.9 jit_solution(16658378083250577882)
XLA Ops:
  11.4 43.9 %all-gather = bf16[32,64,3]{1,2,0:T(4,128)(2,1)S(1)} all-gather(bf16[1,64,3]{1,2,0:T(4,128)(2,1)} %bitcast.252), channel_id=1, replica_groups=mesh['seq'=8,'fsdp'=4] {'seq','fsdp'}, dimensions={0}, use_global_device_ids=true | all-gather | bytes 12672 | tf_op jit(solution)/shard_map/all_gather | solution.py:155
  58.8 38.6 %all-reduce.9 = (bf16[2048]{0:T(1024)(128)(2,1)S(1)}, bf16[2048]{0:T(1024)(128)(2,1)S(1)}, bf16[2048]{0:T(1024)(128)(2,1)S(1)}, bf16[2048]{0:T(1024)(128)(2,1)S(1)}) all-reduce(bf16[2048]{0:T(1024)(128)(2,1)S(1)} %dynamic-update-slice.1, bf16[2048]{0:T(1024)(128)(2,1)S(1)} %dynamic-update-slice, ...), channel_id=1, replica_groups=mesh['seq'=8,'fsdp'=4] {'seq','fsdp'}, use_global_device_ids=true, to_apply=%add.1 | all-reduce | flops 8192 | bytes 32768
  101.1 69.0 %all-gather.7.cloned.1.call-done = bf16[2048,6144]{1,0:T(8,128)(2,1)} async-done(((bf16[64,6144]{1,0:T(8,128)(2,1)}), bf16[2048,6144]{1,0:T(8,128)(2,1)}) %all-gather.7.cloned.1.call-update) | async-done | bytes 25165840 | tf_op jit(solution)/shard_map/all_gather | solution.py:154
  170.1 10.1 convolution_add_fusion
  187.2 25.5 all_to_all.116
  212.7 3.9 all-to-all-start.1
  218.7 22.3 all-to-all-done.1
  241.0 5.5 all-to-all-start.2
  246.5 4.8 scatter_custom_fusion
  252.4 3.9 gather_fusion
  256.8 3.9 gather_fusion.1
  261.0 3.1 all-to-all-done.2
  264.0 3.9 gather_fusion.2
  268.2 22.6 while.30
  275.7 3.0 fusion.132
  287.0 3.0 fusion.132
  295.2 3.9 gather_fusion.3
  300.1 3.9 all-to-all-start.3
  304.1 29.4 all-to-all-done.3
  334.3 5.9 fusion.73
  340.7 78.7 %all-gather.11.cloned.1.call-done = bf16[2048,5632]{1,0:T(8,128)(2,1)} async-done(((bf16[64,5632]{1,0:T(8,128)(2,1)}), bf16[2048,5632]{1,0:T(8,128)(2,1)}) %all-gather.11.cloned.1.call-update) | async-done | bytes 23068688 | tf_op jit(solution)/shard_map/all_gather | solution.py:154
  419.4 12.5 fusion.76
  431.9 133.0 %all-gather.13.cloned.1.call-done = bf16[2048,5632]{1,0:T(8,128)(2,1)} async-done(((bf16[64,5632]{1,0:T(8,128)(2,1)}), bf16[2048,5632]{1,0:T(8,128)(2,1)}) %all-gather.13.cloned.1.call-update) | async-done | bytes 23068688 | tf_op jit(solution)/shard_map/all_gather | solution.py:155
  564.9 12.3 fusion.77
  577.2 133.2 %all-gather.15.cloned.1.call-done = bf16[5632,2048]{1,0:T(8,128)(2,1)} async-done(((bf16[176,2048]{1,0:T(8,128)(2,1)}), bf16[5632,2048]{1,0:T(8,128)(2,1)}) %all-gather.15.cloned.1.call-update) | async-done | bytes 23068688 | tf_op jit(solution)/shard_map/all_gather | solution.py:156
  710.4 15.6 multiply_convert_fusion.1
  726.0 13.3 fusion.78
  739.3 12.2 convolution_add_fusion.1
  751.6 13.5 fusion.53
  765.7 2.9 convolution_convert_fusion
  769.5 4.2 all-to-all-start.4
  773.7 14.9 all-to-all-done.4
  788.5 5.0 gather_fusion.4
  796.5 44.1 %while.31 = (s32[]{:T(128)}, bf16[1024,4,64]{0,2,1:T(8,128)(2,1)}, f32[1024,4,64]{0,2,1:T(8,128)S(1)}, f32[1024,4,64]{0,2,1:T(8,128)}, s32[1024]{0:T(1024)S(1)},...) while((s32[]{:T(128)}, bf16[1024,4,64]{0,2,1:T(8,128)(2,1)}, ...), condition=%wide.region_18.19_spmd.clone, body=%wide.region_16.18_spmd.clone.sunk | while | flops 1378222080 | bytes 164707824 | solution.py:276
  800.0 3.2 multiply_reduce_fusion.7
  803.2 2.4 multiply_convert_fusion.5
  809.8 3.3 fusion.144
  814.5 3.5 fusion.145
  821.5 3.2 multiply_reduce_fusion.7
  831.3 3.3 fusion.144
  836.0 4.6 fusion.145
  840.8 3.9 gather_fusion.6
  845.7 3.6 all-to-all-start.6
  849.6 3.9 gather_fusion.5
  854.5 9.5 all-to-all-done.6
  864.0 3.8 all-to-all-start.5
  869.3 3.9 gather_fusion.7
  874.3 8.2 all-to-all-done.5
  882.5 3.6 all-to-all-start.7
  886.8 14.0 all-to-all-done.7
  902.9 8.0 fusion.60
  912.0 20.9 fusion.69
  934.4 18.0 fusion.79
  953.7 18.0 fusion.80
  973.2 18.1 fusion.56
  992.6 20.7 fusion.51
  1013.3 44.0 %all-reduce.8 = (f32[2048]{0:T(1024)S(1)}, f32[2048]{0:T(1024)S(1)}, f32[2048]{0:T(1024)S(1)}, f32[2048]{0:T(1024)S(1)}, f32[1]{0:T(128)}, /*index=5*/f32[1]{0:T(128)}, f32[1]{0:T(128)}) all-reduce(f32[2048]{0:T(1024)S(1)} %get-tuple-element.310, ...), channel_id=2, replica_groups=mesh['seq'=8,'fsdp'=4] {'seq','fsdp'}, use_global_device_ids=true, to_apply=%region_22.23.clone | all-reduce | flops 8195 | bytes 65560
  1059.6 2.5 fusion.67
  1062.2 2.6 fusion.50
  1066.2 153.0 %reduce-scatter.11.cloned.1.call-done = f32[64,2048]{1,0:T(8,128)} async-done(((f32[2048,2048]{1,0:T(8,128)}), f32[64,2048]{1,0:T(8,128)}) %reduce-scatter.11.cloned.1.call-update) | async-done | bytes 524304 | tf_op jit(solution)/shard_map/reduce_scatter | solution.py:165
  1219.2 442.0 %reduce-scatter.9.cloned.1.call-done = f32[64,6144]{1,0:T(8,128)} async-done(((f32[2048,6144]{1,0:T(8,128)}), f32[64,6144]{1,0:T(8,128)}) %reduce-scatter.9.cloned.1.call-update) | async-done | bytes 1572880 | tf_op jit(solution)/shard_map/reduce_scatter | solution.py:163
  1661.2 487.0 %reduce-scatter.13.cloned.1.call-done = f32[64,5632]{1,0:T(8,128)} async-done(((f32[2048,5632]{1,0:T(8,128)}), f32[64,5632]{1,0:T(8,128)}) %reduce-scatter.13.cloned.1.call-update) | async-done | bytes 1441808 | tf_op jit(solution)/shard_map/reduce_scatter | solution.py:163
  2148.2 495.9 %reduce-scatter.15.cloned.1.call-done = f32[64,5632]{1,0:T(8,128)} async-done(((f32[2048,5632]{1,0:T(8,128)}), f32[64,5632]{1,0:T(8,128)}) %reduce-scatter.15.cloned.1.call-update) | async-done | bytes 1441808 | tf_op jit(solution)/shard_map/reduce_scatter | solution.py:164
  2644.1 496.0 %reduce-scatter.17.cloned.1.call-done = f32[176,2048]{1,0:T(8,128)} async-done(((f32[5632,2048]{1,0:T(8,128)}), f32[176,2048]{1,0:T(8,128)}) %reduce-scatter.17.cloned.1.call-update) | async-done | bytes 1441808 | tf_op jit(solution)/shard_map/reduce_scatter | solution.py:165
  (274 shorter events, 84.4 us)
Async XLA Ops:
  7.2 92.9 %copy-start.3 = (bf16[1,128,2048]{2,1,0:T(8,128)(2,1)S(1)}, bf16[1,128,2048]{2,1,0:T(8,128)(2,1)}, u32[]{:S(2)}) copy-start(bf16[1,128,2048]{2,1,0:T(8,128)(2,1)} %param.18) | copy-start | bytes 1572868
  7.2 162.9 %all-gather.7.cloned.1.call-start = ((), (), s32[]{:S(2)}) async-start(), calls=%async_computation.14 | async-start | bytes 25952256 | tf_op jit(solution)/shard_map/all_gather | solution.py:154
  7.9 296.1 %all-gather.9.cloned.1.call-start = ((), (), s32[]{:S(2)}) async-start(), calls=%async_computation.15 | async-start | bytes 8650752 | tf_op jit(solution)/shard_map/all_gather | solution.py:156
  8.7 410.7 %all-gather.11.cloned.1.call-start = ((), (), s32[]{:S(2)}) async-start(), calls=%async_computation.16 | async-start | bytes 23789568 | tf_op jit(solution)/shard_map/all_gather | solution.py:154
  9.4 555.5 %all-gather.13.cloned.1.call-start = ((), (), s32[]{:S(2)}) async-start(), calls=%async_computation.17 | async-start | bytes 23789568 | tf_op jit(solution)/shard_map/all_gather | solution.py:155
  10.0 700.4 %all-gather.15.cloned.1.call-start = ((), (), s32[]{:S(2)}) async-start(), calls=%async_computation.18 | async-start | bytes 23789568 | tf_op jit(solution)/shard_map/all_gather | solution.py:156
  97.4 82.8 %copy-start.33 = (f32[2048]{0:T(1024)}, f32[2048]{0:T(1024)S(1)}, u32[]{:S(2)}) copy-start(f32[2048]{0:T(1024)S(1)} %convert_element_type.172) | copy-start | bytes 24580
  97.4 82.8 %copy-start.29 = (f32[2048]{0:T(1024)}, f32[2048]{0:T(1024)S(1)}, u32[]{:S(2)}) copy-start(f32[2048]{0:T(1024)S(1)} %convert_element_type.171) | copy-start | bytes 24580
  100.1 80.2 %copy-start.41 = (f32[128]{0:T(128)}, f32[128]{0:T(128)S(1)}, u32[]{:S(2)}) copy-start(f32[128]{0:T(128)S(1)} %broadcast_multiply_fusion.6) | copy-start | bytes 1540
  100.4 79.9 %copy-start.45 = (f32[128]{0:T(128)}, f32[128]{0:T(128)S(1)}, u32[]{:S(2)}) copy-start(f32[128]{0:T(128)S(1)} %add_rsqrt_fusion.1) | copy-start | bytes 1540
  101.1 84.1 %copy-start.39 = (f32[128,8]{0,1:T(8,128)}, f32[128,8]{0,1:T(8,128)S(1)}, u32[]{:S(2)}) copy-start(f32[128,8]{0,1:T(8,128)S(1)} %get-tuple-element.405) | copy-start | bytes 12292
  180.3 1.8 copy-start.9
  185.2 61.3 %copy-start.48 = (s32[1,1024]{1,0:T(1,128)S(1)}, s32[1,1024]{1,0:T(1,128)}, u32[]{:S(2)}) copy-start(s32[1,1024]{1,0:T(1,128)} %param.30) | copy-start | bytes 12292
  212.7 28.3 all-to-all-start.1
  241.0 23.0 all-to-all-start.2
  252.1 43.0 %copy-start.35 = (s32[1024]{0:T(1024)}, s32[1024]{0:T(1024)S(1)}, u32[]{:S(2)}) copy-start(s32[1024]{0:T(1024)S(1)} %broadcast_clamp_fusion) | copy-start | bytes 12292
  252.2 11.9 copy-start.37
  273.3 2.3 copy-start.31
  284.6 2.3 copy-start.31
  300.1 33.3 %all-to-all-start.3 = ((bf16[8,128,256]{1,2,0:T(8,128)(2,1)}), bf16[8,128,256]{1,2,0:T(8,128)(2,1)S(1)}, u32[]{:S(2)}, u32[]{:S(2)}) async-start(bf16[8,128,256]{1,2,0:T(8,128)(2,1)} %copy.115), calls=%async_computation.3 | async-start | bytes 1048576 | tf_op jit(solution)/shard_map/all_to_all | solution.py:196
  340.7 224.3 %copy-start.7 = (bf16[128,2048]{1,0:T(8,128)(2,1)}, bf16[128,2048]{1,0:T(8,128)(2,1)S(1)}, u32[]{:S(2)}) copy-start(bf16[128,2048]{1,0:T(8,128)(2,1)S(1)} %add_convert_fusion) | copy-start | bytes 1572868
  726.0 13.3 copy-start.11
  739.3 12.2 copy-start.49
  751.5 14.2 slice-start
  751.5 13.5 copy-start.24
  751.5 14.1 slice-start.1
  765.7 2.9 copy-start.5
  765.7 22.8 copy-start.38
  769.5 19.1 all-to-all-start.4
  796.5 44.3 %copy-start.36 = (s32[1024]{0:T(1024)S(1)}, s32[1024]{0:T(1024)}, u32[]{:S(2)}) copy-start(s32[1024]{0:T(1024)} %copy-done.35) | copy-start | bytes 12292
  796.5 3.5 copy-start.16
  797.8 5.4 copy-start
  803.2 4.4 copy-start.26
  805.6 2.0 copy-start.2
  809.8 4.6 copy-start.1
  809.8 4.7 copy-start.17
  818.0 3.5 copy-start.16
  819.3 5.4 copy-start
  824.7 4.4 copy-start.26
  827.1 2.0 copy-start.2
  831.3 4.6 copy-start.1
  831.3 4.7 copy-start.17
  840.6 8.8 copy-start.28
  845.7 18.3 all-to-all-start.6
  864.0 18.5 all-to-all-start.5
  873.3 13.3 copy-start.40
  873.3 13.3 copy-start.47
  882.5 18.3 all-to-all-start.7
  886.1 178.7 %reduce-scatter.19.cloned.1.call-start = ((), (), s32[]{:S(2)}) async-start(), calls=%async_computation.24 | async-start | bytes 1081344
  886.3 16.5 copy-start.6
  886.3 16.5 copy-start.15
  886.7 24.3 copy-start.20
  886.8 24.2 copy-start.22
  900.8 10.2 copy-start.18
  902.8 316.4 %reduce-scatter.11.cloned.1.call-start = ((), (), s32[]{:S(2)}) async-start(), calls=%async_computation.20 | async-start | bytes 17301504 | tf_op jit(solution)/shard_map/reduce_scatter | solution.py:165
  910.9 750.2 %reduce-scatter.9.cloned.1.call-start = ((), (), s32[]{:S(2)}) async-start(), calls=%async_computation.19 | async-start | bytes 51904512 | tf_op jit(solution)/shard_map/reduce_scatter | solution.py:163
  932.8 1.5 copy-start.10
  932.8 1215.3 %reduce-scatter.13.cloned.1.call-start = ((), (), s32[]{:S(2)}) async-start(), calls=%async_computation.21 | async-start | bytes 47579136 | tf_op jit(solution)/shard_map/reduce_scatter | solution.py:163
  952.4 1691.7 %reduce-scatter.15.cloned.1.call-start = ((), (), s32[]{:S(2)}) async-start(), calls=%async_computation.22 | async-start | bytes 47579136 | tf_op jit(solution)/shard_map/reduce_scatter | solution.py:164
  971.7 1.4 copy-start.13
  971.7 1.5 copy-start.25
  971.7 2168.4 %reduce-scatter.17.cloned.1.call-start = ((), (), s32[]{:S(2)}) async-start(), calls=%async_computation.23 | async-start | bytes 47579136 | tf_op jit(solution)/shard_map/reduce_scatter | solution.py:165
  992.6 20.7 copy-start.43
  992.6 20.7 copy-start.44
  (16 other events, 16.6 us)
Sparse Core Ops, SparseCore 0:
  10.9 159.1 all-gather.6
  173.0 90.7 all-gather.8
  266.6 152.7 all-gather.10
  422.1 142.7 all-gather.12
  567.6 142.7 all-gather.14
  902.9 133.6 reduce-scatter.18
  1039.6 179.5 reduce-scatter.10
  1227.3 433.7 reduce-scatter.8
  1664.2 483.9 reduce-scatter.12
  2151.0 493.0 reduce-scatter.14
  2647.1 493.0 reduce-scatter.16
where the time goes:
time: 3160 us; the launch traced here: 3150 us
  waiting for transfers between devices  2590 us (82%)
  matrix products  238 us (8%)
  blocking collectives  152 us (5%)
  local copies, waits for them, and re-layouts  89.1 us (3%)
    reduce_scatter x2, waiting for transfers between devices, reduce_full(): lax.psum_scatter(first_w, ('seq', 'fsdp'), scatter_dimension=0, tiled=True)  929 us
    reduce_scatter x2, waiting for transfers between devices, reduce_full(): lax.psum_scatter(last_w, ('seq', 'fsdp'), scatter_dimension=0, tiled=True)  649 us
    reduce_scatter x1, waiting for transfers between devices, reduce_full(): lax.psum_scatter(middle_w, ('seq', 'fsdp'), scatter_dimension=0, tiled=True)  496 us
    all_gather x2, waiting for transfers between devices, fetch_full(): lax.all_gather(first_w, ('seq', 'fsdp'), axis=0, tiled=True)  148 us
    all_gather x2, waiting for transfers between devices, fetch_full(): lax.all_gather(last_w, ('seq', 'fsdp'), axis=0, tiled=True)  133 us
    all_gather x1, waiting for transfers between devices, fetch_full(): lax.all_gather(middle_w, ('seq', 'fsdp'), axis=0, tiled=True)  133 us
    dot_general x5, matrix products, outer(): lax.dot_general(left, right, (((0,), (0,)), ((), ())), preferred_element_...  83 us
    unnamed x2, blocking collectives  82.5 us
  transfers between devices with their start and end apart: 18, of which 16 were waited for; matrix products, arithmetic and copies ran while one was open for 7% of the time, Pallas kernels for 0%

commit v1 on v0

--- a/solution.py
+++ b/solution.py
@@ -64,6 +64,10 @@
     return lax.dot_general(
         left, right, (((0,), (0,)), ((), ())), preferred_element_type=jnp.float32
     )
+
+
+def times(left, right):
+    return jnp.dot(left, right, preferred_element_type=jnp.float32)
 
 
 def times_transposed(left, right):
@@ -101,6 +105,12 @@
 ):
     rows = hidden_in.shape[1]
     width = hidden_in.shape[2]
+    nseq = lax.axis_size("seq")
+    nfsdp = lax.axis_size("fsdp")
+    local_width = width // nseq
+    part = qkv_weight.shape[0]
+    ff = gate_weight.shape[1]
+    local_ff = ff // nseq
     stream = hidden_in[0].astype(jnp.float32)
     cotangent = out_grad[0].astype(jnp.float32)
     order = deal_order[0]
@@ -114,14 +124,48 @@
     nblocks = group_rows // blk
     scale = HEAD_DIM ** (-0.5)
     local_pos = lax.dynamic_slice_in_dim(order, lax.axis_index("seq") * rows, rows)
-    local_seg, local_start = segment_of(local_pos, lengths)
-    rel = (local_pos - local_start).astype(jnp.float32)
     valid = (local_pos < valid_rows).astype(jnp.float32)[:, None]
-    normed1, rstd1 = normalize(stream)
+    dealt_seg, dealt_start = segment_of(order, lengths)
+    rel = (order - dealt_start).astype(jnp.float32)
     inverse = (
         jnp.zeros((group_rows,), jnp.int32).at[order].set(jnp.arange(group_rows, dtype=jnp.int32))
     )
     seg_p, start_p = segment_of(jnp.arange(group_rows, dtype=jnp.int32), lengths)
+
+    def gather_rows(values):
+        return lax.all_gather(values, "seq", axis=0, tiled=True)
+
+    def scatter_rows(partial):
+        return lax.psum_scatter(
+            partial.astype(jnp.bfloat16), "seq", scatter_dimension=0, tiled=True
+        ).astype(jnp.float32)
+
+    def column_slice(weight, blocks):
+        cols = weight.shape[1] // (blocks * nseq)
+        view = weight.reshape(part, blocks, nseq, cols).transpose(2, 0, 1, 3)
+        mine = lax.all_to_all(
+            view.reshape(nseq * part, blocks * cols), "seq", split_axis=0, concat_axis=0, tiled=True
+        )
+        full = lax.all_gather(mine.reshape(nseq, part, blocks * cols), "fsdp", axis=1)
+        return full.reshape(width, blocks * cols)
+
+    def row_slice(weight):
+        return lax.all_gather(weight, "fsdp", axis=0, tiled=True)
+
+    def column_shard(grad, blocks):
+        cols = grad.shape[1] // blocks
+        view = grad.astype(jnp.bfloat16).reshape(nseq, nfsdp, part, blocks * cols)
+        mine = lax.psum_scatter(view.transpose(1, 0, 2, 3), "fsdp", scatter_dimension=0)
+        got = lax.all_to_all(
+            mine.reshape(nseq * part, blocks * cols), "seq", split_axis=0, concat_axis=0, tiled=True
+        )
+        view = got.reshape(nseq, part, blocks, cols).transpose(1, 2, 0, 3)
+        return view.reshape(part, -1).astype(jnp.float32)
+
+    def row_shard(grad):
+        return lax.psum_scatter(
+            grad.astype(jnp.bfloat16), "fsdp", scatter_dimension=0, tiled=True
+        ).astype(jnp.float32)
 
     def to_pack(values):
         heads_here = values.shape[1] // HEAD_DIM
@@ -147,40 +191,25 @@
         scores = jnp.where(allowed[None], scores, -1e30)
         return (first, key_first, qblock, kblock, vblock, scores)
 
-    def fetch_full(gain, shift, first_w, middle_w, last_w):
-        return (
-            lax.all_gather(gain, ("seq", "fsdp"), axis=0, tiled=True),
-            lax.all_gather(shift, ("seq", "fsdp"), axis=0, tiled=True),
-            lax.all_gather(first_w, ("seq", "fsdp"), axis=0, tiled=True),
-            lax.all_gather(middle_w, ("seq", "fsdp"), axis=0, tiled=True),
-            lax.all_gather(last_w, ("seq", "fsdp"), axis=0, tiled=True),
-        )
-
-    def reduce_full(gain, shift, first_w, middle_w, last_w):
-        return (
-            lax.psum_scatter(gain, ("seq", "fsdp"), scatter_dimension=0, tiled=True),
-            lax.psum_scatter(shift, ("seq", "fsdp"), scatter_dimension=0, tiled=True),
-            lax.psum_scatter(first_w, ("seq", "fsdp"), scatter_dimension=0, tiled=True),
-            lax.psum_scatter(middle_w, ("seq", "fsdp"), scatter_dimension=0, tiled=True),
-            lax.psum_scatter(last_w, ("seq", "fsdp"), scatter_dimension=0, tiled=True),
-        )
-
-    gain1, shift1, qkv_w, qkv_b, out_w = fetch_full(
-        ln1_gain, ln1_bias, qkv_weight, qkv_bias.T, out_weight
-    )
-    qkv_shift = qkv_b.T.reshape(-1).astype(jnp.float32)
-    first_in = (normed1 * gain1.astype(jnp.float32) + shift1.astype(jnp.float32)).astype(
-        jnp.bfloat16
-    )
-    qkv = jnp.dot(first_in, qkv_w, preferred_element_type=jnp.float32) + qkv_shift
-    query = rotate(qkv[:, :width], rel, 1.0).astype(jnp.bfloat16)
-    keyset = rotate(qkv[:, width : 2 * width], rel, 1.0).astype(jnp.bfloat16)
-    valueset = qkv[:, 2 * width :].astype(jnp.bfloat16)
-    query, keyset, valueset = (query, keyset, valueset)
-    query_h = lax.all_to_all(query, "seq", split_axis=1, concat_axis=0, tiled=True)
-    key_h = lax.all_to_all(keyset, "seq", split_axis=1, concat_axis=0, tiled=True)
-    value_h = lax.all_to_all(valueset, "seq", split_axis=1, concat_axis=0, tiled=True)
-    packed = (to_pack(query_h), to_pack(key_h), to_pack(value_h))
+    both = ("seq", "fsdp")
+    norms = lax.all_gather(
+        jnp.stack([ln1_gain, ln1_bias, ln2_gain, ln2_bias, *qkv_bias]), both, axis=1, tiled=True
+    )
+    gain1, shift1, gain2, shift2 = norms[:4].astype(jnp.float32)
+    qkv_shift = lax.dynamic_slice_in_dim(
+        norms[4:], lax.axis_index("seq") * local_width, local_width, 1
+    )
+    qkv_shift = qkv_shift.reshape(-1).astype(jnp.float32)
+
+    normed1, rstd1 = normalize(stream)
+    first_local = (normed1 * gain1 + shift1).astype(jnp.bfloat16)
+    first_in = gather_rows(first_local)
+    qkv_w = column_slice(qkv_weight, 3)
+    qkv = times(first_in, qkv_w) + qkv_shift
+    query = rotate(qkv[:, :local_width], rel, 1.0).astype(jnp.bfloat16)
+    keyset = rotate(qkv[:, local_width : 2 * local_width], rel, 1.0).astype(jnp.bfloat16)
+    valueset = qkv[:, 2 * local_width :].astype(jnp.bfloat16)
+    packed = (to_pack(query), to_pack(keyset), to_pack(valueset))
 
     def attend_block(index):
         first, key_first, qblock, kblock, vblock, scores = window(index, packed)
@@ -189,62 +218,39 @@
         total = jnp.sum(expo, -1, keepdims=True)
         probs = (expo / total).astype(jnp.bfloat16)
         mixed = jnp.einsum("hqk,khd->qhd", probs, vblock, preferred_element_type=jnp.float32)
-        return (mixed, (top + jnp.log(total))[..., 0])
+        return (mixed.astype(jnp.bfloat16), (top + jnp.log(total))[..., 0])
 
     mixed_all, lse_all = lax.map(attend_block, jnp.arange(nblocks, dtype=jnp.int32))
-    mixed_pack = mixed_all.reshape(group_rows, -1)
-    heads_out = lax.all_to_all(
-        mixed_pack[order].astype(jnp.bfloat16), "seq", split_axis=0, concat_axis=1, tiled=True
-    )
-    heads_out, packed, lse_all = (heads_out, packed, lse_all)
-    attn = jnp.dot(heads_out, out_w, preferred_element_type=jnp.float32)
+    mixed = mixed_all.reshape(group_rows, -1)[order]
+    heads_out = lax.all_to_all(mixed, "seq", split_axis=0, concat_axis=1, tiled=True)
+    out_w = lax.all_gather(out_weight, both, axis=0, tiled=True)
+    out_rows = row_slice(out_weight)
+    attn = times(heads_out, out_w)
     resid = stream + attn
-    gain2, shift2, gate_w, up_w, down_w = fetch_full(
-        ln2_gain, ln2_bias, gate_weight, up_weight, down_weight
-    )
     normed2, rstd2 = normalize(resid)
-    second_in = (normed2 * gain2.astype(jnp.float32) + shift2.astype(jnp.float32)).astype(
-        jnp.bfloat16
-    )
-    gate = jnp.dot(second_in, gate_w, preferred_element_type=jnp.float32)
-    upper = jnp.dot(second_in, up_w, preferred_element_type=jnp.float32)
+    second_in = gather_rows((normed2 * gain2 + shift2).astype(jnp.bfloat16))
+    gate_w = column_slice(gate_weight, 1)
+    up_w = column_slice(up_weight, 1)
+    down_w = row_slice(down_weight)
+    gate = times(second_in, gate_w)
+    upper = times(second_in, up_w)
     hidden, sigma = mlp_forward(gate, upper)
-    mlp = jnp.dot(hidden, down_w, preferred_element_type=jnp.float32)
+    mlp = scatter_rows(times(hidden, down_w))
     result = resid + mlp
-    sums = lax.psum(
-        (
-            jnp.sum(valid * result * result),
-            jnp.sum(valid * attn * attn),
-            jnp.sum(valid * mlp * mlp),
-        ),
-        ("seq", "fsdp"),
-    )
-    count = valid_rows * lax.axis_size("fsdp") * width
-    rms = jnp.sqrt(jnp.stack(sums) / count)
-    gain2, shift2, gate_w, up_w, down_w = fetch_full(
-        ln2_gain, ln2_bias, gate_weight, up_weight, down_weight
-    )
-    mlp_grad = cotangent.astype(jnp.bfloat16)
-    down_grad = outer(hidden, mlp_grad)
+
+    mlp_grad = gather_rows(out_grad[0])
     hidden_grad = times_transposed(mlp_grad, down_w)
     gate_act, up_act = mlp_backward(hidden_grad, gate, upper, sigma)
-    gate_grad = outer(second_in, gate_act)
-    up_grad = outer(second_in, up_act)
-    second_grad = times_transposed(gate_act, gate_w) + times_transposed(up_act, up_w)
-    resid_part, gain2_grad, shift2_grad = norm_back(
-        second_grad, normed2, rstd2, gain2.astype(jnp.float32)
-    )
+    second_grad = scatter_rows(times_transposed(gate_act, gate_w) + times_transposed(up_act, up_w))
+    down_grad = row_shard(outer(hidden, mlp_grad))
+    gate_grad = column_shard(outer(second_in, gate_act), 1)
+    up_grad = column_shard(outer(second_in, up_act), 1)
+    resid_part, gain2_grad, shift2_grad = norm_back(second_grad, normed2, rstd2, gain2)
     resid_grad = cotangent + resid_part
-    mlp_shards = reduce_full(gain2_grad, shift2_grad, gate_grad, up_grad, down_grad)
-    gain1, shift1, qkv_w, qkv_b, out_w = fetch_full(
-        ln1_gain, ln1_bias, qkv_weight, qkv_bias.T, out_weight
-    )
-    attn_grad = resid_grad.astype(jnp.bfloat16)
-    out_grad_w = outer(heads_out, attn_grad)
-    mixed_grad = times_transposed(attn_grad, out_w).astype(jnp.bfloat16)
-    mixed_grad_p = to_pack(
-        lax.all_to_all(mixed_grad, "seq", split_axis=1, concat_axis=0, tiled=True)
-    )
+
+    attn_grad = gather_rows(resid_grad.astype(jnp.bfloat16))
+    out_grad_w = row_shard(outer(mixed, attn_grad))
+    mixed_grad_p = to_pack(times_transposed(attn_grad, out_rows).astype(jnp.bfloat16))
 
     def back_block(index, carry):
         query_acc, key_acc, value_acc = carry
@@ -276,40 +282,55 @@
     query_acc, key_acc, value_acc = lax.fori_loop(0, nblocks, back_block, (zeros, zeros, zeros))
 
     def to_dealt(values):
-        return values.reshape(group_rows, -1)[order].astype(jnp.bfloat16)
-
-    query_g = lax.all_to_all(to_dealt(query_acc), "seq", split_axis=0, concat_axis=1, tiled=True)
-    key_g = lax.all_to_all(to_dealt(key_acc), "seq", split_axis=0, concat_axis=1, tiled=True)
-    value_g = lax.all_to_all(to_dealt(value_acc), "seq", split_axis=0, concat_axis=1, tiled=True)
+        return values.astype(jnp.bfloat16).reshape(group_rows, -1)[order]
+
     qkv_act = jnp.concatenate(
         [
-            rotate(query_g.astype(jnp.float32), rel, -1.0),
-            rotate(key_g.astype(jnp.float32), rel, -1.0),
-            value_g.astype(jnp.float32),
+            rotate(to_dealt(query_acc).astype(jnp.float32), rel, -1.0).astype(jnp.bfloat16),
+            rotate(to_dealt(key_acc).astype(jnp.float32), rel, -1.0).astype(jnp.bfloat16),
+            to_dealt(value_acc),
         ],
         1,
-    ).astype(jnp.bfloat16)
-    qkv_bias_grad = jnp.sum(qkv_act.astype(jnp.float32), 0).reshape(3, width).T
-    qkv_grad = outer(first_in, qkv_act)
-    first_grad = times_transposed(qkv_act, qkv_w)
-    input_part, gain1_grad, shift1_grad = norm_back(
-        first_grad, normed1, rstd1, gain1.astype(jnp.float32)
-    )
+    )
+    first_grad = scatter_rows(times_transposed(qkv_act, qkv_w))
+    qkv_grad = column_shard(outer(first_in, qkv_act), 3)
+    qkv_bias_grad = lax.psum_scatter(
+        jnp.sum(qkv_act.astype(jnp.float32), 0).reshape(3, nfsdp, -1),
+        "fsdp",
+        scatter_dimension=1,
+    )
+    input_part, gain1_grad, shift1_grad = norm_back(first_grad, normed1, rstd1, gain1)
     input_grad = resid_grad + input_part
-    attn_shards = reduce_full(gain1_grad, shift1_grad, qkv_grad, qkv_bias_grad, out_grad_w)
+
+    norm_grads = lax.psum(
+        (
+            gain1_grad,
+            shift1_grad,
+            gain2_grad,
+            shift2_grad,
+            jnp.sum(valid * result * result),
+            jnp.sum(valid * attn * attn),
+            jnp.sum(valid * mlp * mlp),
+        ),
+        both,
+    )
+    count = valid_rows * nfsdp * width
+    rms = jnp.sqrt(jnp.stack(norm_grads[4:]) / count)
+    mine = (lax.axis_index("seq") * nfsdp + lax.axis_index("fsdp")) * part
+    norm_shards = [lax.dynamic_slice_in_dim(value, mine, part) for value in norm_grads[:4]]
     return (
         result.astype(jnp.bfloat16)[None],
         input_grad[None],
-        attn_shards[0],
-        attn_shards[1],
-        attn_shards[2],
-        attn_shards[3].T,
-        attn_shards[4],
-        mlp_shards[0],
-        mlp_shards[1],
-        mlp_shards[2],
-        mlp_shards[3],
-        mlp_shards[4],
+        norm_shards[0],
+        norm_shards[1],
+        qkv_grad,
+        qkv_bias_grad,
+        out_grad_w,
+        norm_shards[2],
+        norm_shards[3],
+        gate_grad,
+        up_grad,
+        down_grad,
         rms,
     )
 

time: 3160 us -> 1180 us (0.37)
  waiting for transfers between devices: 2590 us -> 645 us
  matrix products: 238 us -> 123 us
  blocking collectives: 152 us -> 207 us
    reduce_scatter x5 -> x6, waiting for transfers between devices: 2070 us -> 287 us  [the longest x3 252 us: scatter_rows(): lax.psum_scatter(partial.astype(jnp.bfloat16), 'seq', scatter_dimension=0...]
    all_gather x5 -> x10, waiting for transfers between devices: 414 us -> 271 us  [the longest x4 213 us: gather_rows(): return lax.all_gather(values, 'seq', axis=0, tiled=True)]
    all_to_all x1 -> x4, blocking collectives: 25.5 us -> 120 us  [the longest x2 67.6 us: column_slice(): lax.all_to_all(view.reshape(nseq * part, blocks * cols), 'seq', split_axi...]
    unnamed x2 -> x1, blocking collectives: 82.5 us -> 5.83 us
    dot_general x5, matrix products: 83 us -> 32 us  [outer(): lax.dot_general(left, right, (((0,), (0,)), ((), ())), preferred_element_...]
    all_to_all x7 -> x3, waiting for transfers between devices: 101 us -> 53.8 us  [the longest x1 35.7 us: column_slice(): lax.all_to_all(view.reshape(nseq * part, blocks * cols), 'seq', split_axi...]
    psum x0 -> x1, blocking collectives: none -> 41.3 us  [body(): lax.psum((gain1_grad, shift1_grad, gain2_grad, shift2_grad, jnp.sum(valid...]
    dot_general x5, matrix products: 64.7 us -> 32.6 us  [times_transposed(): lax.dot_general(left, right, (((1,), (1,)), ((), ())), preferred_element_...]
  transfers between devices with their start and end apart: 18 -> 20, of which waited for: 16 -> 16; matrix products, arithmetic and copies ran while one was open for 7% -> 22% of each run, Pallas kernels for 0% -> 0%
where the time goes in v1:
time: 1180 us; the launch traced here: 1170 us
  waiting for transfers between devices  645 us (55%)
  blocking collectives  207 us (18%)
  matrix products  123 us (10%)
  local copies, waits for them, and re-layouts  119 us (10%)
  other arithmetic  43.5 us (4%)
  between operations  15.3 us (1%)
  starting transfers between devices  14.3 us (1%)
    reduce_scatter x3, waiting for transfers between devices, scatter_rows(): lax.psum_scatter(partial.astype(jnp.bfloat16), 'seq', scatter_dimension=0...  252 us
    all_gather x4, waiting for transfers between devices, gather_rows(): return lax.all_gather(values, 'seq', axis=0, tiled=True)  213 us
    all_to_all x2, blocking collectives, column_slice(): lax.all_to_all(view.reshape(nseq * part, blocks * cols), 'seq', split_axi...  67.6 us
    all_gather x3, waiting for transfers between devices, column_slice(): lax.all_gather(mine.reshape(nseq, part, blocks * cols), 'fsdp', axis=1)  41.6 us
    psum x1, blocking collectives, body(): lax.psum((gain1_grad, shift1_grad, gain2_grad, shift2_grad, jnp.sum(valid...  41.3 us
    all_gather x1, blocking collectives, body(): lax.all_gather(jnp.stack([ln1_gain, ln1_bias, ln2_gain, ln2_bias, *qkv_bi...  40.1 us
    all_to_all x1, waiting for transfers between devices, column_slice(): lax.all_to_all(view.reshape(nseq * part, blocks * cols), 'seq', split_axi...  35.7 us
    reduce_scatter x2, waiting for transfers between devices, row_shard(): lax.psum_scatter(grad.astype(jnp.bfloat16), 'fsdp', scatter_dimension=0,...  35.3 us
  transfers between devices with their start and end apart: 20, of which 16 were waited for; matrix products, arithmetic and copies ran while one was open for 22% of the time, Pallas kernels for 0%

profile of v1, /device:TPU:0, one launch (start us, length us, event | category | flops | bytes accessed | tf_op | source)
XLA Modules:
  0.0 1171.6 jit_solution(12868852306584055459)
XLA Ops:
  10.0 27.5 %all_to_all.73 = bf16[8,64,768]{2,1,0:T(8,128)(2,1)} all-to-all(bf16[8,64,768]{2,1,0:T(8,128)(2,1)S(1)} %all_to_all.50), channel_id=1, replica_groups=mesh['seq'=8,'fsdp'=4] {'seq'}, dimensions={0} | all-to-all | bytes 1572864 | tf_op jit(solution)/shard_map/all_to_all | solution.py:146
  37.6 40.1 %all-gather.4 = bf16[32,64,7]{1,2,0:T(8,128)(2,1)S(1)} all-gather(bf16[1,64,7]{1,2,0:T(8,128)(2,1)S(1)} %bitcast.317), channel_id=1, replica_groups=mesh['seq'=8,'fsdp'=4] {'seq','fsdp'}, dimensions={0}, use_global_device_ids=true | all-gather | bytes 29568 | tf_op jit(solution)/shard_map/all_gather | solution.py:195
  81.8 40.1 %all_to_all.74 = bf16[8,64,704]{2,1,0:T(8,128)(2,1)S(1)} all-to-all(bf16[8,64,704]{2,1,0:T(8,128)(2,1)S(1)} %copy.172), channel_id=1, replica_groups=mesh['seq'=8,'fsdp'=4] {'seq'}, dimensions={0} | all-to-all | bytes 1441792 | tf_op jit(solution)/shard_map/all_to_all | solution.py:146
  125.0 3.6 all-to-all-start.3
  129.0 4.3 scatter_custom_fusion
  135.0 35.7 %all-to-all-done.3 = bf16[8,64,704]{2,1,0:T(8,128)(2,1)S(1)} async-done(((bf16[8,64,704]{2,1,0:T(8,128)(2,1)}), bf16[8,64,704]{2,1,0:T(8,128)(2,1)S(1)}, u32[]{:S(2)}, u32[]{:S(2)}) %all-to-all-start.3) | async-done | bytes 720928 | tf_op jit(solution)/shard_map/all_to_all | solution.py:146
  172.3 7.7 all-gather.16.cloned.1.call-done
  180.0 6.2 convolution_add_fusion
  188.5 5.0 gather_fusion.2
  196.6 4.6 gather_fusion.1
  201.7 4.6 gather_fusion
  206.5 22.4 %while.30 = (s32[]{:T(128)}, bf16[2,512,4,64]{1,3,2,0:T(8,128)(2,1)S(1)}, f32[2,4,512]{2,1,0:T(4,128)S(1)}, s32[2]{0:T(128)S(1)}, s32[1024]{0:T(1024)S(1)}, /*in...) while((s32[]{:T(128)}, ...), condition=%wide.region_11.12_spmd, body=%wide.region_8.11_spmd.sunk | while | flops 565313536 | bytes 28925200 | solution.py:223
  214.6 3.0 fusion.145
  225.8 3.0 fusion.145
  232.4 3.9 gather_fusion.3
  236.6 28.5 %all_to_all.75 = bf16[8,128,256]{1,2,0:T(8,128)(2,1)} all-to-all(bf16[8,128,256]{1,2,0:T(8,128)(2,1)S(1)} %copy.171), channel_id=1, replica_groups=mesh['seq'=8,'fsdp'=4] {'seq'}, dimensions={0} | all-to-all | bytes 1048576 | tf_op jit(solution)/shard_map/all_to_all | solution.py:225
  267.6 5.8 fusion.83
  276.3 20.8 %all-gather.30.cloned.1.call-done = bf16[8,256,704]{2,0,1:T(8,128)(2,1)} async-done(((bf16[8,64,704]{2,0,1:T(8,128)(2,1)}), bf16[8,256,704]{2,0,1:T(8,128)(2,1)}) %all-gather.30.cloned.1.call-update) | async-done | bytes 2883600 | tf_op jit(solution)/shard_map/all_gather | solution.py:149
  297.1 5.4 copy.174
  302.4 4.4 copy.202
  306.8 20.8 %all-gather.32.cloned.1.call-done = bf16[8,256,704]{2,0,1:T(8,128)(2,1)} async-done(((bf16[8,64,704]{2,0,1:T(8,128)(2,1)}), bf16[8,256,704]{2,0,1:T(8,128)(2,1)}) %all-gather.32.cloned.1.call-update) | async-done | bytes 2883600 | tf_op jit(solution)/shard_map/all_gather | solution.py:149
  327.6 5.8 copy.177
  333.4 4.4 copy.203
  337.8 65.8 %all-gather.20.cloned.1.call-done = bf16[1024,2048]{1,0:T(8,128)(2,1)} async-done(((bf16[128,2048]{1,0:T(8,128)(2,1)}), bf16[1024,2048]{1,0:T(8,128)(2,1)}) %all-gather.20.cloned.1.call-update) | async-done | bytes 4194320 | tf_op jit(solution)/shard_map/all_gather | solution.py:136
  403.6 8.0 fusion.88
  411.7 4.7 fusion.87
  416.4 14.1 %all-gather.22.cloned.1.call-done = bf16[704,2048]{1,0:T(8,128)(2,1)} async-done(((bf16[176,2048]{1,0:T(8,128)(2,1)}), bf16[704,2048]{1,0:T(8,128)(2,1)}) %all-gather.22.cloned.1.call-update) | async-done | bytes 2883600 | tf_op jit(solution)/shard_map/all_gather | solution.py:153
  430.5 75.6 %all-gather.34.cloned.1.call-done = bf16[1,1024,2048]{2,1,0:T(8,128)(2,1)} async-done(((bf16[1,128,2048]{2,1,0:T(8,128)(2,1)}), bf16[1,1024,2048]{2,1,0:T(8,128)(2,1)}) %all-gather.34.cloned.1.call-update) | async-done | bytes 4194320 | tf_op jit(solution)/shard_map/all_gather | solution.py:136
  506.1 10.6 multiply_convert_fusion.1
  517.8 5.1 convolution_convert_fusion
  523.2 5.9 fusion.89
  529.2 5.4 add_convert_fusion
  536.0 73.4 %reduce-scatter.10.cloned.1.call-done = bf16[128,2048]{1,0:T(8,128)(2,1)} async-done(((bf16[1024,2048]{1,0:T(8,128)(2,1)}), bf16[128,2048]{1,0:T(8,128)(2,1)}) %reduce-scatter.10.cloned.1.call-update) | async-done | bytes 524304 | tf_op jit(solution)/shard_map/reduce_scatter | solution.py:139
  609.4 91.6 %reduce-scatter.12.cloned.1.call-done = bf16[128,2048]{1,0:T(8,128)(2,1)} async-done(((bf16[1024,2048]{1,0:T(8,128)(2,1)}), bf16[128,2048]{1,0:T(8,128)(2,1)}) %reduce-scatter.12.cloned.1.call-update) | async-done | bytes 524304 | tf_op jit(solution)/shard_map/reduce_scatter | solution.py:139
  701.0 3.8 fusion.71
  706.7 7.5 convolution_convert_fusion.4
  714.2 4.6 copy.188
  718.8 7.4 convolution_convert_fusion.3
  726.2 4.7 copy.190
  731.2 63.9 %all-gather.24.cloned.1.call-done = bf16[1024,2048]{1,0:T(8,128)(2,1)} async-done(((bf16[128,2048]{1,0:T(8,128)(2,1)}), bf16[1024,2048]{1,0:T(8,128)(2,1)}) %all-gather.24.cloned.1.call-update) | async-done | bytes 4194320 | tf_op jit(solution)/shard_map/all_gather | solution.py:136
  795.1 3.8 convolution_convert_fusion.6
  798.9 5.0 gather_fusion.4
  806.0 29.5 %while.31 = (s32[]{:T(128)}, bf16[1024,4,64]{0,2,1:T(8,128)(2,1)}, f32[1024,4,64]{0,2,1:T(8,128)S(1)}, f32[1024,4,64]{0,2,1:T(8,128)}, s32[1024]{0:T(1024)S(1)},...) while((s32[]{:T(128)}, bf16[1024,4,64]{0,2,1:T(8,128)(2,1)}, ...), condition=%wide.region_20.21_spmd.clone, body=%wide.region_18.20_spmd.clone.sunk | while | flops 1378222080 | bytes 85015968 | solution.py:282
  812.7 3.2 multiply_reduce_fusion.3
  824.9 2.6 fusion.158
  827.5 3.2 multiply_reduce_fusion.3
  836.7 3.9 gather_fusion.5
  842.3 4.3 gather_fusion.6
  848.6 3.9 gather_fusion.7
  856.0 5.9 convolution_convert_fusion.2
  865.5 6.7 fusion.41
  872.3 4.4 convolution_convert_fusion.5
  876.8 6.9 convolution_convert_fusion.1
  885.0 30.6 %all-reduce.7.cloned.1.call-done = (bf16[4,8,64,704]{3,2,0,1:T(8,128)(2,1)}, bf16[4,8,64,704]{3,2,0,1:T(8,128)(2,1)}) async-done(((bf16[4,8,64,704]{3,2,0,1:T(8,128)(2,1)}, bf16[4,8,64,704]{3,2,0,1:T(8,128)(2,1)}), (bf16[4,8,64,704]{3,2,0,1:T(8,128)(2,1)}, bf16[4,8,64,704]{3,2,0,1:T(8,128)(2,1)})) %all-reduce.7.cloned.1.call-update) | async-done | bytes 5767184
  915.6 2.7 dynamic-slice_bitcast_fusion.2
  918.3 5.5 all-to-all-start.5
  925.7 18.1 %all-to-all-done.5 = bf16[8,64,704]{2,1,0:T(8,128)(2,1)S(1)} async-done(((bf16[8,64,704]{2,1,0:T(8,128)(2,1)}), bf16[8,64,704]{2,1,0:T(8,128)(2,1)S(1)}, u32[]{:S(2)}, u32[]{:S(2)}) %all-to-all-start.5) | async-done | bytes 720928 | tf_op jit(solution)/shard_map/all_to_all | solution.py:159
  943.8 23.6 %all_to_all.76 = bf16[8,64,704]{2,1,0:T(8,128)(2,1)S(1)} all-to-all(bf16[8,64,704]{2,1,0:T(8,128)(2,1)S(1)} %dynamic-slice_bitcast_fusion.1), channel_id=1, replica_groups=mesh['seq'=8,'fsdp'=4] {'seq'}, dimensions={0} | all-to-all | bytes 1441792 | tf_op jit(solution)/shard_map/all_to_all | solution.py:159
  967.4 3.8 all-to-all-start.4
  976.7 18.3 %reduce-scatter.20.cloned.1.call-done = bf16[176,2048]{1,0:T(8,128)(2,1)} async-done(((bf16[704,2048]{1,0:T(8,128)(2,1)}), bf16[176,2048]{1,0:T(8,128)(2,1)}) %reduce-scatter.20.cloned.1.call-update) | async-done | bytes 720912 | tf_op jit(solution)/shard_map/reduce_scatter | solution.py:166
  998.8 5.8 all-reduce
  1005.9 17.0 %reduce-scatter.18.cloned.1.call-done = bf16[64,2048]{1,0:T(8,128)(2,1)} async-done(((bf16[256,2048]{1,0:T(8,128)(2,1)}), bf16[64,2048]{1,0:T(8,128)(2,1)}) %reduce-scatter.18.cloned.1.call-update) | async-done | bytes 262160 | tf_op jit(solution)/shard_map/reduce_scatter | solution.py:166
  1028.2 86.6 %reduce-scatter.14.cloned.1.call-done = bf16[128,2048]{1,0:T(8,128)(2,1)} async-done(((bf16[1024,2048]{1,0:T(8,128)(2,1)}), bf16[128,2048]{1,0:T(8,128)(2,1)}) %reduce-scatter.14.cloned.1.call-update) | async-done | bytes 524304 | tf_op jit(solution)/shard_map/reduce_scatter | solution.py:139
  1116.3 41.3 %all-reduce.3 = (f32[2048]{0:T(1024)S(1)}, f32[2048]{0:T(1024)S(1)}, f32[2048]{0:T(1024)S(1)}, f32[2048]{0:T(1024)S(1)}, f32[1]{0:T(128)}, /*index=5*/f32[1]{0:T(128)}, f32[1]{0:T(128)}) all-reduce(f32[2048]{0:T(1024)S(1)} %get-tuple-element.310, f32[2048]{0:T(1024)S(1)} %get-tuple-element.316, ...), channel_id=1, replica_groups=mesh['seq'=8,'fsdp'=4] {'seq','fsdp'}, use_global_device_ids=true, to_apply=%region_25.26 | all-reduce | flops 8195 | bytes 65560 | tf_op jit(solution)/shard_map/psum | solution.py:305
  (298 shorter events, 107.4 us)
Async XLA Ops:
  7.2 165.1 %all-gather.28.cloned.1.call-start = ((), (), s32[]{:S(2)}) async-start(), calls=%async_computation.25 | async-start | bytes 3932160 | tf_op jit(solution)/shard_map/all_gather | solution.py:149
  8.5 29.0 %copy-start.40 = (bf16[3,64]{1,0:T(4,128)(2,1)S(1)}, bf16[3,64]{1,0:T(4,128)(2,1)}, u32[]{:S(2)}) copy-start(bf16[3,64]{1,0:T(4,128)(2,1)} %param.22) | copy-start | bytes 1156
  8.5 29.0 %copy-start.41 = (bf16[64]{0:T(256)(128)(2,1)S(1)}, bf16[64]{0:T(256)(128)(2,1)}, u32[]{:S(2)}) copy-start(bf16[64]{0:T(256)(128)(2,1)} %param.19) | copy-start | bytes 388
  8.5 29.0 %copy-start.42 = (bf16[64]{0:T(256)(128)(2,1)S(1)}, bf16[64]{0:T(256)(128)(2,1)}, u32[]{:S(2)}) copy-start(bf16[64]{0:T(256)(128)(2,1)} %param.20) | copy-start | bytes 388
  8.6 29.0 %copy-start.43 = (bf16[64]{0:T(256)(128)(2,1)S(1)}, bf16[64]{0:T(256)(128)(2,1)}, u32[]{:S(2)}) copy-start(bf16[64]{0:T(256)(128)(2,1)} %param.24) | copy-start | bytes 388
  8.6 29.0 %copy-start.44 = (bf16[64]{0:T(256)(128)(2,1)S(1)}, bf16[64]{0:T(256)(128)(2,1)}, u32[]{:S(2)}) copy-start(bf16[64]{0:T(256)(128)(2,1)} %param.25) | copy-start | bytes 388
  8.6 69.2 %copy-start = (bf16[1,128,2048]{2,1,0:T(8,128)(2,1)S(1)}, bf16[1,128,2048]{2,1,0:T(8,128)(2,1)}, u32[]{:S(2)}) copy-start(bf16[1,128,2048]{2,1,0:T(8,128)(2,1)} %param.18) | copy-start | bytes 1572868
  10.0 71.0 %copy-start.18 = (bf16[64,5632]{1,0:T(8,128)(2,1)S(1)}, bf16[64,5632]{1,0:T(8,128)(2,1)}, u32[]{:S(2)}) copy-start(bf16[64,5632]{1,0:T(8,128)(2,1)} %param.26) | copy-start | bytes 2162692
  37.5 142.5 %all-gather.16.cloned.1.call-start = ((), (), s32[]{:S(2)}) async-start(), calls=%async_computation.13 | async-start | bytes 4718592 | tf_op jit(solution)/shard_map/all_gather | solution.py:136
  78.0 43.9 %copy-start.36 = (f32[128]{0:T(128)}, f32[128]{0:T(128)S(1)}, u32[]{:S(2)}) copy-start(f32[128]{0:T(128)S(1)} %broadcast_multiply_fusion.6) | copy-start | bytes 1540
  78.3 43.6 %copy-start.38 = (f32[128]{0:T(128)}, f32[128]{0:T(128)S(1)}, u32[]{:S(2)}) copy-start(f32[128]{0:T(128)S(1)} %add_rsqrt_fusion.1) | copy-start | bytes 1540
  78.9 43.0 %copy-start.24 = (f32[1,2048]{1,0:T(1,128)}, f32[1,2048]{1,0:T(1,128)S(1)}, u32[]{:S(2)}) copy-start(f32[1,2048]{1,0:T(1,128)S(1)} %get-tuple-element.411) | copy-start | bytes 24580
  80.2 187.4 %all-gather.18.cloned.1.call-start = ((), (), s32[]{:S(2)}) async-start(), calls=%async_computation.14 | async-start | bytes 8650752 | tf_op jit(solution)/shard_map/all_gather | solution.py:226
  80.9 42.4 %copy-start.19 = (bf16[64,5632]{1,0:T(8,128)(2,1)S(1)}, bf16[64,5632]{1,0:T(8,128)(2,1)}, u32[]{:S(2)}) copy-start(bf16[64,5632]{1,0:T(8,128)(2,1)} %param.27) | copy-start | bytes 2162692
  80.9 216.2 %all-gather.30.cloned.1.call-start = ((), (), s32[]{:S(2)}) async-start(), calls=%async_computation.26 | async-start | bytes 3932160 | tf_op jit(solution)/shard_map/all_gather | solution.py:149
  121.9 6.8 copy-start.47
  123.3 5.6 copy-start.32
  125.0 45.7 %all-to-all-start.3 = ((bf16[8,64,704]{2,1,0:T(8,128)(2,1)}), bf16[8,64,704]{2,1,0:T(8,128)(2,1)S(1)}, u32[]{:S(2)}, u32[]{:S(2)}) async-start(bf16[8,64,704]{2,1,0:T(8,128)(2,1)} %copy.175), calls=%async_computation.3 | async-start | bytes 1572864 | tf_op jit(solution)/shard_map/all_to_all | solution.py:146
  128.6 199.0 %all-gather.32.cloned.1.call-start = ((), (), s32[]{:S(2)}) async-start(), calls=%async_computation.27 | async-start | bytes 3932160 | tf_op jit(solution)/shard_map/all_gather | solution.py:149
  133.6 98.8 %copy-start.28 = (s32[1024]{0:T(1024)}, s32[1024]{0:T(1024)S(1)}, u32[]{:S(2)}) copy-start(s32[1024]{0:T(1024)S(1)} %broadcast_clamp_fusion) | copy-start | bytes 12292
  133.6 54.9 %copy-start.30 = (s32[1024]{0:T(1024)}, s32[1024]{0:T(1024)S(1)}, u32[]{:S(2)}) copy-start(s32[1024]{0:T(1024)S(1)} %fusion.76) | copy-start | bytes 12292
  172.0 231.6 %all-gather.20.cloned.1.call-start = ((), (), s32[]{:S(2)}) async-start(), calls=%async_computation.15 | async-start | bytes 4718592 | tf_op jit(solution)/shard_map/all_gather | solution.py:136
  196.6 4.8 copy-start.22
  196.6 4.8 copy-start.23
  201.6 4.8 copy-start.20
  201.7 4.8 copy-start.27
  236.3 31.2 %copy-start.14 = (bf16[1024,256]{1,0:T(8,128)(2,1)}, bf16[1024,256]{1,0:T(8,128)(2,1)S(1)}, u32[]{:S(2)}) copy-start(bf16[1024,256]{1,0:T(8,128)(2,1)S(1)} %gather_fusion.3) | copy-start | bytes 1572868
  267.6 6.1 copy-start.35
  274.7 155.8 %all-gather.22.cloned.1.call-start = ((), (), s32[]{:S(2)}) async-start(), calls=%async_computation.16 | async-start | bytes 3604480 | tf_op jit(solution)/shard_map/all_gather | solution.py:153
  275.5 230.6 %all-gather.34.cloned.1.call-start = ((), (), s32[]{:S(2)}) async-start(), calls=%async_computation.28 | async-start | bytes 4718592 | tf_op jit(solution)/shard_map/all_gather | solution.py:136
  276.2 333.2 %reduce-scatter.10.cloned.1.call-start = ((), (), s32[]{:S(2)}) async-start(), calls=%async_computation.17 | async-start | bytes 4718592 | tf_op jit(solution)/shard_map/reduce_scatter | solution.py:139
  403.6 8.0 copy-start.3
  403.6 8.0 copy-start.45
  506.1 11.7 %copy-start.46 = (bf16[704,2048]{1,0:T(8,128)(2,1)S(1)}, bf16[704,2048]{1,0:T(8,128)(2,1)}, u32[]{:S(2)}) copy-start(bf16[704,2048]{1,0:T(8,128)(2,1)} %all-gather.22.cloned.1.call-done) | copy-start | bytes 8650756
  523.0 178.1 %reduce-scatter.12.cloned.1.call-start = ((), (), s32[]{:S(2)}) async-start(), calls=%async_computation.18 | async-start | bytes 4718592 | tf_op jit(solution)/shard_map/reduce_scatter | solution.py:139
  523.2 6.0 copy-start.4
  523.2 6.0 copy-start.49
  534.5 170.3 %copy-start.5 = (bf16[1,128,2048]{2,1,0:T(8,128)(2,1)S(1)}, bf16[1,128,2048]{2,1,0:T(8,128)(2,1)}, u32[]{:S(2)}) copy-start(bf16[1,128,2048]{2,1,0:T(8,128)(2,1)} %param.31) | copy-start | bytes 1572868
  534.6 196.7 %all-gather.26.cloned.1.call-start = ((), (), s32[]{:S(2)}) async-start(), calls=%async_computation.20 | async-start | bytes 1310720 | tf_op jit(solution)/shard_map/all_gather | solution.py:153
  535.3 259.8 %all-gather.24.cloned.1.call-start = ((), (), s32[]{:S(2)}) async-start(), calls=%async_computation.19 | async-start | bytes 4718592 | tf_op jit(solution)/shard_map/all_gather | solution.py:136
  706.6 209.0 %all-reduce.7.cloned.1.call-start = ((), (), s32[]{:S(2)}) async-start(), calls=%async_computation.29 | async-start | bytes 12582912
  730.9 68.0 %copy-start.31 = (s32[1024]{0:T(1024)S(1)}, s32[1024]{0:T(1024)}, u32[]{:S(2)}) copy-start(s32[1024]{0:T(1024)} %copy-done.30) | copy-start | bytes 12292
  730.9 236.4 %reduce-scatter.16.cloned.1.call-start = ((), (), s32[]{:S(2)}) async-start(), calls=%async_computation.22 | async-start | bytes 3932160 | tf_op jit(solution)/shard_map/reduce_scatter | solution.py:158
  806.0 30.8 %copy-start.29 = (s32[1024]{0:T(1024)S(1)}, s32[1024]{0:T(1024)}, u32[]{:S(2)}) copy-start(s32[1024]{0:T(1024)} %copy-done.28) | copy-start | bytes 12292
  848.3 4.2 copy-start.21
  848.3 4.2 copy-start.26
  852.5 24.3 %copy-start.13 = (bf16[1024,256]{1,0:T(8,128)(2,1)}, bf16[1024,256]{1,0:T(8,128)(2,1)S(1)}, u32[]{:S(2)}) copy-start(bf16[1024,256]{1,0:T(8,128)(2,1)S(1)} %gather_fusion.7) | copy-start | bytes 1572868
  854.7 22.1 %copy-start.6 = (bf16[1024,256]{1,0:T(8,128)(2,1)}, bf16[1024,256]{1,0:T(8,128)(2,1)S(1)}, u32[]{:S(2)}) copy-start(bf16[1024,256]{1,0:T(8,128)(2,1)S(1)} %copy.184) | copy-start | bytes 1572868
  856.0 20.9 %copy-start.8 = (bf16[1024,256]{1,0:T(8,128)(2,1)}, bf16[1024,256]{1,0:T(8,128)(2,1)S(1)}, u32[]{:S(2)}) copy-start(bf16[1024,256]{1,0:T(8,128)(2,1)S(1)} %copy.185) | copy-start | bytes 1572868
  863.9 8.3 copy-start.15
  863.9 131.1 %reduce-scatter.20.cloned.1.call-start = ((), (), s32[]{:S(2)}) async-start(), calls=%async_computation.24 | async-start | bytes 3604480 | tf_op jit(solution)/shard_map/reduce_scatter | solution.py:166
  872.2 150.7 %reduce-scatter.18.cloned.1.call-start = ((), (), s32[]{:S(2)}) async-start(), calls=%async_computation.23 | async-start | bytes 1310720 | tf_op jit(solution)/shard_map/reduce_scatter | solution.py:166
  876.7 238.0 %reduce-scatter.14.cloned.1.call-start = ((), (), s32[]{:S(2)}) async-start(), calls=%async_computation.21 | async-start | bytes 4718592 | tf_op jit(solution)/shard_map/reduce_scatter | solution.py:139
  918.3 25.5 %all-to-all-start.5 = ((bf16[8,64,704]{2,1,0:T(8,128)(2,1)}), bf16[8,64,704]{2,1,0:T(8,128)(2,1)S(1)}, u32[]{:S(2)}, u32[]{:S(2)}) async-start(bf16[8,64,704]{2,1,0:T(8,128)(2,1)} %dynamic-slice_bitcast_fusion.2), calls=%async_computation.10 | async-start | bytes 1572864 | tf_op jit(solution)/shard_map/all_to_all | solution.py:159
  967.4 57.3 %all-to-all-start.4 = ((bf16[8,64,768]{2,1,0:T(8,128)(2,1)}), bf16[8,64,768]{2,1,0:T(8,128)(2,1)S(1)}, u32[]{:S(2)}, u32[]{:S(2)}) async-start(bf16[8,64,768]{2,1,0:T(8,128)(2,1)} %bitcast.302), calls=%async_computation.8 | async-start | bytes 1572864 | tf_op jit(solution)/shard_map/all_to_all | solution.py:159
  975.0 22.4 %copy-start.7 = (bf16[1024,256]{1,0:T(8,128)(2,1)S(1)}, bf16[1024,256]{1,0:T(8,128)(2,1)}, u32[]{:S(2)}) copy-start(bf16[1024,256]{1,0:T(8,128)(2,1)} %copy-done.6) | copy-start | bytes 1572868
  975.0 22.4 %copy-start.9 = (bf16[1024,256]{1,0:T(8,128)(2,1)S(1)}, bf16[1024,256]{1,0:T(8,128)(2,1)}, u32[]{:S(2)}) copy-start(bf16[1024,256]{1,0:T(8,128)(2,1)} %copy-done.8) | copy-start | bytes 1572868
  1025.6 89.2 %copy-start.1 = (bf16[1,128,2048]{2,1,0:T(8,128)(2,1)S(1)}, bf16[1,128,2048]{2,1,0:T(8,128)(2,1)}, u32[]{:S(2)}) copy-start(bf16[1,128,2048]{2,1,0:T(8,128)(2,1)} %param.18) | copy-start | bytes 1572868
  1025.6 89.2 %copy-start.25 = (f32[1,2048]{1,0:T(1,128)S(1)}, f32[1,2048]{1,0:T(1,128)}, u32[]{:S(2)}) copy-start(f32[1,2048]{1,0:T(1,128)} %copy-done.24) | copy-start | bytes 24580
  1025.6 89.2 %copy-start.37 = (f32[128]{0:T(128)S(1)}, f32[128]{0:T(128)}, u32[]{:S(2)}) copy-start(f32[128]{0:T(128)} %copy-done.36) | copy-start | bytes 1540
  1025.6 89.1 %copy-start.39 = (f32[128]{0:T(128)S(1)}, f32[128]{0:T(128)}, u32[]{:S(2)}) copy-start(f32[128]{0:T(128)} %copy-done.38) | copy-start | bytes 1540
  1025.6 90.7 %copy-start.33 = (f32[2048]{0:T(1024)S(1)}, f32[2048]{0:T(1024)}, u32[]{:S(2)}) copy-start(f32[2048]{0:T(1024)} %get-tuple-element.399) | copy-start | bytes 24580
  1025.6 90.7 %copy-start.34 = (f32[2048]{0:T(1024)S(1)}, f32[2048]{0:T(1024)}, u32[]{:S(2)}) copy-start(f32[2048]{0:T(1024)} %get-tuple-element.403) | copy-start | bytes 24580
  1026.6 135.8 %copy-start.2 = (f32[128,2048]{1,0:T(8,128)S(1)}, f32[128,2048]{1,0:T(8,128)}, u32[]{:S(2)}) copy-start(f32[128,2048]{1,0:T(8,128)} %get-tuple-element.377) | copy-start | bytes 3145732
  (12 other events, 22.9 us)
Sparse Core Ops, SparseCore 0:
  37.6 27.8 all-gather.27
  80.3 99.6 all-gather.15
  182.8 84.6 all-gather.17
  269.5 27.5 all-gather.29
  299.1 28.5 all-gather.31
  330.2 73.3 all-gather.19
  405.2 25.2 all-gather.21
  432.6 73.3 all-gather.33
  523.1 86.3 reduce-scatter.9
  613.4 87.6 reduce-scatter.11
  702.6 16.4 all-gather.25
  721.7 73.3 all-gather.23
  797.5 118.0 all-reduce.6
  918.0 38.1 reduce-scatter.15
  958.7 36.3 reduce-scatter.19
  998.0 24.8 reduce-scatter.17
  1026.8 87.8 reduce-scatter.13

commit v2 on v1

--- a/solution.py
+++ b/solution.py
@@ -1,6 +1,10 @@
+import functools
+
 import jax
 import jax.numpy as jnp
 from jax import lax
+from jax.experimental import pallas as pl
+from jax.experimental.pallas import tpu as pltpu
 from jax.sharding import PartitionSpec as P
 
 HEAD_DIM = 64
@@ -335,6 +339,676 @@
     )
 
 
+MESH = pl.DeviceIdType.MESH
+
+def where_am_i():
+    s = lax.axis_index("seq"); f = lax.axis_index("fsdp")
+    return s, f, s // 2, s % 2
+
+def remote(src, dst, ssem, rsem, dev):
+    return pltpu.make_async_remote_copy(src, dst, ssem, rsem, device_id=dev, device_id_type=MESH)
+
+def greet_line(s, f, z, y):
+    bar = pltpu.get_barrier_semaphore()
+    pl.semaphore_signal(bar, inc=1, device_id=(s + 1 - 2 * y, f), device_id_type=MESH)
+    @pl.when(z > 0)
+    def _(): pl.semaphore_signal(bar, inc=1, device_id=(s - 2, f), device_id_type=MESH)
+    @pl.when(z < 3)
+    def _(): pl.semaphore_signal(bar, inc=1, device_id=(s + 2, f), device_id_type=MESH)
+    edge = jnp.where((z == 0) | (z == 3), 1, 0)
+    pl.semaphore_wait(bar, 3 - edge)
+
+def ag_kernel(x_ref, o_ref, own_sem, recv, sy, su, sd):
+    s, f, z, y = where_am_i()
+    greet_line(s, f, z, y)
+    other = s + 1 - 2 * y
+    own = pltpu.make_async_copy(x_ref, o_ref.at[s], own_sem)
+    own.start()
+    def ysend(zb, src): return remote(src, o_ref.at[2 * zb + y], sy.at[zb], recv.at[2 * zb + y], (other, f))
+    def usend(zb, src): return remote(src, o_ref.at[2 * zb + y], su.at[zb], recv.at[2 * zb + y], (s + 2, f))
+    def dsend(zb, src): return remote(src, o_ref.at[2 * zb + y], sd.at[zb], recv.at[2 * zb + y], (s - 2, f))
+    def arrived(blk): return remote(o_ref.at[blk], o_ref.at[blk], sy.at[0], recv.at[blk], (other, f))
+    @pl.when(z < 3)
+    def _(): usend(z, x_ref).start()
+    @pl.when(z > 0)
+    def _(): dsend(z, x_ref).start()
+    ysend(z, x_ref).start()
+    for t in range(1, 4):
+        @pl.when(z >= t)
+        def _():
+            zb = z - t
+            arrived(2 * zb + y).wait_recv()
+            @pl.when(z < 3)
+            def _(): usend(zb, o_ref.at[2 * zb + y]).start()
+            ysend(zb, o_ref.at[2 * zb + y]).start()
+        @pl.when(z + t <= 3)
+        def _():
+            zb = z + t
+            arrived(2 * zb + y).wait_recv()
+            @pl.when(z > 0)
+            def _(): dsend(zb, o_ref.at[2 * zb + y]).start()
+            ysend(zb, o_ref.at[2 * zb + y]).start()
+    for zb in range(4):
+        arrived(2 * zb + 1 - y).wait_recv()
+    own.wait()
+    for zb in range(4):
+        ysend(zb, x_ref).wait_send()
+        @pl.when((z < 3) & (zb <= z))
+        def _(): usend(zb, x_ref).wait_send()
+        @pl.when((z > 0) & (zb >= z))
+        def _(): dsend(zb, x_ref).wait_send()
+
+def all_gather_rows(x, cid, vmem_in=True):
+    return pl.pallas_call(ag_kernel, out_shape=jax.ShapeDtypeStruct((8,) + x.shape, x.dtype),
+        in_specs=[pl.BlockSpec(memory_space=pltpu.VMEM)], out_specs=pl.BlockSpec(memory_space=pl.ANY),
+        scratch_shapes=[pltpu.SemaphoreType.DMA, pltpu.SemaphoreType.DMA((8,)), pltpu.SemaphoreType.DMA((4,)), pltpu.SemaphoreType.DMA((4,)), pltpu.SemaphoreType.DMA((4,))],
+        compiler_params=pltpu.CompilerParams(collective_id=cid, has_side_effects=True))(x)
+
+CH = 2
+def rs_kernel(p_ref, o_ref, mine, ybuf, up, down, send_up, send_down, load_sem, ry, ru, rd, sy, su, sd):
+    s, f, z, y = where_am_i()
+    rows = p_ref.shape[1]
+    ch = rows // CH
+    greet_line(s, f, z, y)
+    other = s + 1 - 2 * y
+    def order(k):
+        a = [3, 2, 1, 0]; b = [3, 0, 2, 1]; c = [0, 3, 1, 2]; d = [0, 1, 2, 3]
+        return jnp.where(z == 0, a[k], jnp.where(z == 1, b[k], jnp.where(z == 2, c[k], d[k])))
+    def part(c): return pl.ds(c * ch, ch)
+    def ysend(zb, c): return remote(p_ref.at[2 * zb + 1 - y, part(c)], ybuf.at[zb, part(c)], sy.at[zb, c], ry.at[zb, c], (other, f))
+    def load(zb): return pltpu.make_async_copy(p_ref.at[2 * zb + y], mine.at[zb], load_sem.at[zb])
+    def usend(zb, c): return remote(send_up.at[zb, part(c)], up.at[zb, part(c)], su.at[zb, c], ru.at[zb, c], (s + 2, f))
+    def dsend(zb, c): return remote(send_down.at[zb, part(c)], down.at[zb, part(c)], sd.at[zb, c], rd.at[zb, c], (s - 2, f))
+    for k in range(4):
+        zb = order(k)
+        for c in range(CH): ysend(zb, c).start()
+        load(zb).start()
+    STEP = 16
+    def add2(dst, a, b):
+        @pl.loop(0, ch // STEP)
+        def _(i):
+            r = pl.ds(pl.multiple_of(i * STEP, STEP), STEP)
+            dst[r] = (a[r].astype(jnp.float32) + b[r].astype(jnp.float32)).astype(dst.dtype)
+    def add3(dst, a, b, d):
+        @pl.loop(0, ch // STEP)
+        def _(i):
+            r = pl.ds(pl.multiple_of(i * STEP, STEP), STEP)
+            dst[r] = (a[r].astype(jnp.float32) + b[r].astype(jnp.float32) + d[r].astype(jnp.float32)).astype(dst.dtype)
+    for k in range(4):
+        zb = order(k)
+        load(zb).wait()
+        for c in range(CH):
+            ysend(zb, c).wait_recv()
+            a = mine.at[zb, part(c)]; b = ybuf.at[zb, part(c)]
+            @pl.when(zb > z)
+            def _():
+                @pl.when(z == 0)
+                def _(): add2(send_up.at[zb, part(c)], a, b)
+                @pl.when(z > 0)
+                def _():
+                    usend(zb, c).wait_recv()
+                    add3(send_up.at[zb, part(c)], a, b, up.at[zb, part(c)])
+                usend(zb, c).start()
+            @pl.when(zb < z)
+            def _():
+                @pl.when(z == 3)
+                def _(): add2(send_down.at[zb, part(c)], a, b)
+                @pl.when(z < 3)
+                def _():
+                    dsend(zb, c).wait_recv()
+                    add3(send_down.at[zb, part(c)], a, b, down.at[zb, part(c)])
+                dsend(zb, c).start()
+            @pl.when(zb == z)
+            def _():
+                @pl.when(z > 0)
+                def _(): usend(zb, c).wait_recv()
+                @pl.when(z < 3)
+                def _(): dsend(zb, c).wait_recv()
+                o = o_ref.at[part(c)]
+                @pl.when(z == 0)
+                def _(): add3(o, a, b, down.at[zb, part(c)])
+                @pl.when(z == 3)
+                def _(): add3(o, a, b, up.at[zb, part(c)])
+                @pl.when((z > 0) & (z < 3))
+                def _():
+                    @pl.loop(0, ch // STEP)
+                    def _(i):
+                        r = pl.ds(pl.multiple_of(i * STEP, STEP), STEP)
+                        o[r] = (a[r].astype(jnp.float32) + b[r].astype(jnp.float32)) + (up[zb, part(c)][r] if False else up.at[zb, part(c)][r].astype(jnp.float32) + down.at[zb, part(c)][r].astype(jnp.float32))
+    for zb in range(4):
+        for c in range(CH):
+            ysend(zb, c).wait_send()
+            @pl.when(zb > z)
+            def _(): usend(zb, c).wait_send()
+            @pl.when(zb < z)
+            def _(): dsend(zb, c).wait_send()
+
+def reduce_scatter_rows(p, cid):
+    _, rows, w = p.shape
+    big = lambda: pltpu.VMEM((4, rows, w), p.dtype)
+    sems = lambda: pltpu.SemaphoreType.DMA((4, CH))
+    return pl.pallas_call(rs_kernel, out_shape=jax.ShapeDtypeStruct((rows, w), jnp.float32),
+        in_specs=[pl.BlockSpec(memory_space=pl.ANY)], out_specs=pl.BlockSpec(memory_space=pltpu.VMEM),
+        scratch_shapes=[big() for _ in range(6)] + [pltpu.SemaphoreType.DMA((4,))] + [sems() for _ in range(6)],
+        compiler_params=pltpu.CompilerParams(collective_id=cid, has_side_effects=True, vmem_limit_bytes=40<<20))(p)
+
+def flip(v, bit):
+    return v + bit * (1 - 2 * ((v // bit) % 2))
+
+def peer(s, k):
+    for bit in (1, 2, 4):
+        if k & bit:
+            s = flip(s, bit)
+    return s
+
+def greet_columns(s, f):
+    bar = pltpu.get_barrier_semaphore()
+    for k in range(1, 8):
+        pl.semaphore_signal(bar, inc=1, device_id=(peer(s, k), f), device_id_type=MESH)
+    pl.semaphore_signal(bar, inc=1, device_id=(s, flip(f, 1)), device_id_type=MESH)
+    pl.semaphore_signal(bar, inc=1, device_id=(s, flip(f, 2)), device_id_type=MESH)
+    pl.semaphore_wait(bar, 9)
+
+class ColGather:
+    @staticmethod
+    def sems():
+        D = pltpu.SemaphoreType.DMA
+        return [D, D((8, 4)), D((8,)), D((8, 2)), D((8,))]
+    def __init__(self, x, o, own, recv, direct, core, xs, s, f):
+        self.__dict__.update(locals())
+        self.fc = flip(f, 1); self.fx = flip(f, 2); self.fd = flip(flip(f, 1), 2)
+        self.mine = pltpu.make_async_copy(x.at[s], o.at[s, f], own)
+    def send_direct(self, k):
+        s, f = self.s, self.f; t = peer(s, k)
+        return remote(self.x.at[t], self.o.at[s, f], self.direct.at[k], self.recv.at[s, f], (t, f))
+    def send_core(self, k, which, src):
+        t = peer(self.s, k); ff = self.f if which == 0 else self.fx
+        return remote(src, self.o.at[t, ff], self.core.at[k, which], self.recv.at[t, ff], (self.s, self.fc))
+    def send_x(self, k, src):
+        t = peer(self.s, k)
+        return remote(src, self.o.at[t, self.f], self.xs.at[k], self.recv.at[t, self.f], (self.s, self.fx))
+    def arrived(self, k, ff):
+        t = peer(self.s, k)
+        return remote(self.o.at[t, ff], self.o.at[t, ff], self.own, self.recv.at[t, ff], (self.s, self.fc))
+    def start(self):
+        self.mine.start()
+        for k in range(1, 8): self.send_direct(k).start()
+        self.send_x(0, self.x.at[self.s]).start()
+        self.send_core(0, 0, self.x.at[self.s]).start()
+    def step(self, k):
+        t = peer(self.s, k)
+        self.arrived(k, self.f).wait_recv()
+        self.send_x(k, self.o.at[t, self.f]).start()
+        self.send_core(k, 0, self.o.at[t, self.f]).start()
+    def xstep(self, k):
+        t = peer(self.s, k)
+        self.arrived(k, self.fx).wait_recv()
+        self.send_core(k, 1, self.o.at[t, self.fx]).start()
+    def finish(self):
+        self.mine.wait()
+        for k in range(8):
+            self.arrived(k, self.fc).wait_recv()
+            self.arrived(k, self.fd).wait_recv()
+        for k in range(8):
+            if k: self.send_direct(k).wait_send()
+            self.send_x(k, self.x.at[0]).wait_send()
+            self.send_core(k, 0, self.x.at[0]).wait_send()
+            self.send_core(k, 1, self.x.at[0]).wait_send()
+
+def cg_kernel(x_ref, o_ref, *sems):
+    s, f, z, y = where_am_i()
+    greet_columns(s, f)
+    g = ColGather(x_ref, o_ref, *sems, s, f)
+    g.start()
+    for k in range(1, 8):
+        g.step(k)
+    for k in range(8):
+        g.xstep(k)
+    g.finish()
+
+def column_gather(x, cid):
+    return pl.pallas_call(cg_kernel, out_shape=jax.ShapeDtypeStruct((8, 4) + x.shape[1:], x.dtype),
+        in_specs=[pl.BlockSpec(memory_space=pltpu.VMEM)], out_specs=pl.BlockSpec(memory_space=pl.ANY),
+        scratch_shapes=ColGather.sems(),
+        compiler_params=pltpu.CompilerParams(collective_id=cid, has_side_effects=True))(x)
+
+def adder(dst, srcs, step=16):
+    rows = dst.shape[0]
+    @pl.loop(0, rows // step)
+    def _(i):
+        r = pl.ds(pl.multiple_of(i * step, step), step)
+        tot = srcs[0][r].astype(jnp.float32)
+        for v in srcs[1:]:
+            tot = tot + v[r].astype(jnp.float32)
+        dst[r] = tot.astype(dst.dtype)
+
+class ColReduce:
+    @staticmethod
+    def scratch(n, r, c, exchange):
+        V = lambda *lead: pltpu.VMEM(lead + (n, r, c), jnp.bfloat16)
+        D = pltpu.SemaphoreType.DMA
+        return [V(2), V(2), V(), V(), V() if exchange else pltpu.VMEM((8, 128), jnp.bfloat16),
+                D((2, n)), D((2, n)), D((2, n)), D((n,)), D((n,)), D((n,)), D((n,))]
+    def __init__(self, g, o, ld, cb, hx, xb, ob, ldsem, cs, cr, xs, xr, es, er, s, f, exchange):
+        self.__dict__.update(locals())
+        self.fc = flip(f, 1); self.fx = flip(f, 2); self.fd = flip(flip(f, 1), 2)
+        self.n = g.shape[0]
+    def idx(self, k): return peer(self.s, k) if self.exchange else k
+    def core(self, w, k):
+        i = self.idx(k)
+        return remote(self.g.at[i, self.fd if w == 0 else self.fc], self.cb.at[w, i], self.cs.at[w, k], self.cr.at[w, k], (self.s, self.fc))
+    def load(self, w, k):
+        i = self.idx(k)
+        return pltpu.make_async_copy(self.g.at[i, self.fx if w == 0 else self.f], self.ld.at[w, i], self.ldsem.at[w, k])
+    def xsend(self, k):
+        i = self.idx(k)
+        return remote(self.hx.at[i], self.xb.at[i], self.xs.at[k], self.xr.at[k], (self.s, self.fx))
+    def esend(self, k):
+        t = peer(self.s, k)
+        return remote(self.ob.at[t], self.o.at[self.s], self.es.at[k], self.er.at[k], (t, self.f))
+    def start(self):
+        for w in range(2):
+            for k in reversed(range(self.n)):
+                self.core(w, k).start(); self.load(w, k).start()
+    def step(self, k):
+        i = self.idx(k)
+        self.core(0, k).wait_recv(); self.load(0, k).wait()
+        adder(self.hx.at[i], [self.ld.at[0, i], self.cb.at[0, i]])
+        self.xsend(k).start()
+    def own(self, k):
+        i = self.idx(k)
+        self.core(1, k).wait_recv(); self.load(1, k).wait(); self.xsend(k).wait_recv()
+        if self.exchange and k:
+            adder(self.ob.at[i], [self.ld.at[1, i], self.cb.at[1, i], self.xb.at[i]])
+            self.esend(k).start()
+        else:
+            adder(self.o.at[i], [self.ld.at[1, i], self.cb.at[1, i], self.xb.at[i]])
+    def finish(self):
+        for k in range(self.n):
+            self.core(0, k).wait_send(); self.core(1, k).wait_send(); self.xsend(k).wait_send()
+            if self.exchange and k:
+                self.esend(k).wait_recv(); self.esend(k).wait_send()
+
+def cr_kernel(exchange, g_ref, o_ref, *scr):
+    s, f, z, y = where_am_i()
+    greet_columns(s, f)
+    g = ColReduce(g_ref, o_ref, *scr, s, f, exchange)
+    g.start()
+    for k in reversed(range(g.n)): g.step(k)
+    for k in reversed(range(g.n)): g.own(k)
+    g.finish()
+
+def column_reduce(g, cid, exchange=True):
+    n, _, r, c = g.shape
+    return pl.pallas_call(functools.partial(cr_kernel, exchange), out_shape=jax.ShapeDtypeStruct((n, r, c), jnp.bfloat16 if exchange else jnp.float32),
+        in_specs=[pl.BlockSpec(memory_space=pl.ANY)], out_specs=pl.BlockSpec(memory_space=pltpu.VMEM),
+        scratch_shapes=ColReduce.scratch(n, r, c, exchange),
+        compiler_params=pltpu.CompilerParams(collective_id=cid, has_side_effects=True, vmem_limit_bytes=40<<20))(g)
+QB = 128
+NEG = -1e30
+
+def dot(a, b, ca=1, cb=0):
+    return lax.dot_general(a, b, (((ca,), (cb,)), ((), ())), preferred_element_type=jnp.float32)
+
+def starts_of(pos, lengths_ref, nseg):
+    start = jnp.zeros_like(pos); end = 0
+    for i in range(nseg - 1):
+        end = end + lengths_ref[0, i]
+        start = jnp.where(pos >= end, end, start)
+    return start
+
+def head_lanes(h):
+    lane = lax.broadcasted_iota(jnp.int32, (1, 128), 1)
+    return (lane // HEAD_DIM) == h
+
+def turn(x, c, s1, s2, sign):
+    return x * c + (pltpu.roll(x, 128 - ROT // 2, 1) * s1 + pltpu.roll(x, ROT // 2, 1) * s2) * sign
+
+def block_mask(qb, lengths_ref, nseg):
+    keys = (qb + 1) * QB
+    row = qb * QB + lax.broadcasted_iota(jnp.int32, (QB, 1), 0)
+    col = lax.broadcasted_iota(jnp.int32, (1, keys), 1)
+    return (col >= starts_of(row, lengths_ref, nseg)) & (col <= row)
+
+def attn_fwd_kernel(valid, qkv_ref, c_ref, s1_ref, s2_ref, orow_ref, ocol_ref, len_ref, o_ref, pk_ref, lse_ref, rot, opk):
+    rows, w3 = qkv_ref.shape
+    w = w3 // 3
+    nseg = len_ref.shape[1]
+    scale = HEAD_DIM ** -0.5
+    @pl.loop(0, rows // QB)
+    def _(i):
+        r = pl.ds(pl.multiple_of(i * QB, QB), QB)
+        c, s1, s2 = c_ref[r], s1_ref[r], s2_ref[r]
+        for t in range(w3 // 128):
+            cols = slice(t * 128, t * 128 + 128)
+            x = qkv_ref[r, cols]
+            if t < 2 * w // 128: x = turn(x, c, s1, s2, 1.0)
+            rot[r, cols] = x.astype(jnp.bfloat16)
+    @pl.loop(0, valid // QB)
+    def _(i):
+        r = pl.ds(pl.multiple_of(i * QB, QB), QB)
+        p = (lax.broadcasted_iota(jnp.int32, (QB, 1), 0) + i * QB == orow_ref[...])
+        pk_ref[r] = dot(jnp.where(p, 1.0, 0.0).astype(jnp.bfloat16), rot[...]).astype(jnp.bfloat16)
+    nq = valid // QB
+    for qb in range(nq):
+        keys = (qb + 1) * QB
+        rows_q = slice(qb * QB, qb * QB + QB)
+        mask = block_mask(qb, len_ref, nseg)
+        for t in range(w // 128):
+            q = pk_ref[rows_q, t * 128:t * 128 + 128]
+            k = pk_ref[0:keys, w + t * 128:w + t * 128 + 128]
+            v = pk_ref[0:keys, 2 * w + t * 128:2 * w + t * 128 + 128]
+            tot = None
+            for h in range(2):
+                qh = jnp.where(head_lanes(h), q, jnp.zeros_like(q))
+                s = dot(qh, k, 1, 1) * scale
+                s = jnp.where(mask, s, NEG)
+                top = jnp.max(s, -1, keepdims=True)
+                e = jnp.exp(s - top)
+                total = jnp.sum(e, -1, keepdims=True)
+                p = (e / total).astype(jnp.bfloat16)
+                lse_ref[2 * t + h, rows_q] = top + jnp.log(total)
+                oh = dot(p, v)
+                tot = oh if h == 0 else jnp.where(head_lanes(1), oh, tot)
+            opk[rows_q, t * 128:t * 128 + 128] = tot.astype(jnp.bfloat16)
+    @pl.loop(0, rows // QB)
+    def _(i):
+        r = pl.ds(pl.multiple_of(i * QB, QB), QB)
+        oc = ocol_ref[r]
+        pt = jnp.where(oc == lax.broadcasted_iota(jnp.int32, (1, valid), 1), 1.0, 0.0).astype(jnp.bfloat16)
+        back = dot(pt, opk[...])
+        o_ref[r] = jnp.where(oc >= valid, rot[r, 2 * w:].astype(jnp.float32), back).astype(jnp.bfloat16)
+
+VM = lambda: pl.BlockSpec(memory_space=pltpu.VMEM)
+SM = lambda: pl.BlockSpec(memory_space=pltpu.SMEM)
+
+def attn_fwd(qkv, tables, orow, ocol, lengths, valid):
+    rows, w3 = qkv.shape
+    heads = w3 // 3 // HEAD_DIM
+    return pl.pallas_call(functools.partial(attn_fwd_kernel, valid),
+        out_shape=(jax.ShapeDtypeStruct((rows, w3 // 3), jnp.bfloat16), jax.ShapeDtypeStruct((valid, w3), jnp.bfloat16), jax.ShapeDtypeStruct((heads, valid, 1), jnp.float32)),
+        in_specs=[VM()] * 6 + [SM()], out_specs=(VM(), VM(), VM()),
+        scratch_shapes=[pltpu.VMEM((rows, w3), jnp.bfloat16), pltpu.VMEM((valid, w3 // 3), jnp.bfloat16)],
+        compiler_params=pltpu.CompilerParams(vmem_limit_bytes=40 << 20))(qkv, *tables, orow, ocol, lengths)
+
+def attn_bwd_kernel(valid, pk_ref, do_ref, lse_ref, c_ref, s1_ref, s2_ref, orow_ref, ocol_ref, len_ref, g_ref, b_ref, dpk, dq, dk, dv, gpk):
+    rows, w = do_ref.shape
+    nseg = len_ref.shape[1]
+    scale = HEAD_DIM ** -0.5
+    @pl.loop(0, valid // QB)
+    def _(i):
+        r = pl.ds(pl.multiple_of(i * QB, QB), QB)
+        p = (lax.broadcasted_iota(jnp.int32, (QB, 1), 0) + i * QB == orow_ref[...])
+        dpk[r] = dot(jnp.where(p, 1.0, 0.0).astype(jnp.bfloat16), do_ref[...]).astype(jnp.bfloat16)
+        dk[r] = jnp.zeros((QB, w), jnp.float32)
+        dv[r] = jnp.zeros((QB, w), jnp.float32)
+    for qb in range(valid // QB):
+        keys = (qb + 1) * QB
+        rows_q = slice(qb * QB, qb * QB + QB)
+        mask = block_mask(qb, len_ref, nseg)
+        for t in range(w // 128):
+            ct = slice(t * 128, t * 128 + 128)
+            q = pk_ref[rows_q, ct]
+            k = pk_ref[0:keys, w + t * 128:w + t * 128 + 128]
+            v = pk_ref[0:keys, 2 * w + t * 128:2 * w + t * 128 + 128]
+            d = dpk[rows_q, ct]
+            tq = None
+            for h in range(2):
+                hl = head_lanes(h)
+                qh = jnp.where(hl, q, jnp.zeros_like(q))
+                dh = jnp.where(hl, d, jnp.zeros_like(d))
+                s = dot(qh, k, 1, 1) * scale
+                s = jnp.where(mask, s, NEG)
+                p = jnp.exp(s - lse_ref[2 * t + h, rows_q])
+                dp = dot(dh, v, 1, 1)
+                inner = jnp.sum(p * dp, -1, keepdims=True)
+                ds = (p * (dp - inner)).astype(jnp.bfloat16)
+                dv[0:keys, ct] += dot(p.astype(jnp.bfloat16), dh, 0, 0)
+                dk[0:keys, ct] += dot(ds, qh, 0, 0)
+                qp = dot(ds, k)
+                tq = qp if h == 0 else jnp.where(head_lanes(1), qp, tq)
+            dq[rows_q, ct] = tq
+    @pl.loop(0, valid // QB)
+    def _(i):
+        r = pl.ds(pl.multiple_of(i * QB, QB), QB)
+        c, s1, s2 = c_ref[r], s1_ref[r], s2_ref[r]
+        for t in range(w // 128):
+            ct = slice(t * 128, t * 128 + 128)
+            for j, src in ((0, dq), (1, dk)):
+                x = (src[r, ct] * scale).astype(jnp.bfloat16).astype(jnp.float32)
+                gpk[r, j * w + t * 128:j * w + t * 128 + 128] = turn(x, c, s1, s2, -1.0).astype(jnp.bfloat16)
+            gpk[r, 2 * w + t * 128:2 * w + t * 128 + 128] = dv[r, ct].astype(jnp.bfloat16)
+    b_ref[...] = jnp.zeros_like(b_ref)
+    @pl.loop(0, rows // QB)
+    def _(i):
+        r = pl.ds(pl.multiple_of(i * QB, QB), QB)
+        oc = ocol_ref[r]
+        pt = jnp.where(oc == lax.broadcasted_iota(jnp.int32, (1, valid), 1), 1.0, 0.0).astype(jnp.bfloat16)
+        back = dot(pt, gpk[...])
+        pad = jnp.where(oc >= valid, do_ref[r].astype(jnp.float32), 0.0)
+        back = jnp.concatenate([back[:, :2 * w], back[:, 2 * w:] + pad], 1)
+        g_ref[r] = back.astype(jnp.bfloat16)
+        b_ref[...] += jnp.sum(back, 0, keepdims=True)
+
+def attn_bwd(pk, do, lse, tables, orow, ocol, lengths):
+    rows, w = do.shape
+    valid = pk.shape[0]
+    F = lambda c: pltpu.VMEM((valid, c), jnp.float32)
+    return pl.pallas_call(functools.partial(attn_bwd_kernel, valid),
+        out_shape=(jax.ShapeDtypeStruct((rows, 3 * w), jnp.bfloat16), jax.ShapeDtypeStruct((1, 3 * w), jnp.float32)),
+        in_specs=[VM()] * 8 + [SM()], out_specs=(VM(), VM()),
+        scratch_shapes=[pltpu.VMEM((valid, w), jnp.bfloat16), F(w), F(w), F(w), pltpu.VMEM((valid, 3 * w), jnp.bfloat16)],
+        compiler_params=pltpu.CompilerParams(vmem_limit_bytes=48 << 20))(pk, do, lse, *tables, orow, ocol, lengths)
+
+def rotary_tables(rel):
+    half = ROT // 2
+    d = jnp.arange(128, dtype=jnp.int32) % HEAD_DIM
+    freq = 10000.0 ** (-2.0 * (d % half).astype(jnp.float32) / ROT)
+    angle = rel[:, None] * freq[None, :]
+    c, s = jnp.cos(angle), jnp.sin(angle)
+    return (jnp.where(d < ROT, c, 1.0), jnp.where(d < half, -s, 0.0), jnp.where((d >= half) & (d < ROT), s, 0.0))
+
+def a2a_kernel(x_ref, o_ref, own, send, recv):
+    s, f, z, y = where_am_i()
+    bar = pltpu.get_barrier_semaphore()
+    for k in range(1, 8):
+        pl.semaphore_signal(bar, inc=1, device_id=(peer(s, k), f), device_id_type=MESH)
+    pl.semaphore_wait(bar, 7)
+    mine = pltpu.make_async_copy(x_ref.at[s], o_ref.at[s], own)
+    mine.start()
+    def piece(k):
+        t = peer(s, k)
+        return remote(x_ref.at[t], o_ref.at[s], send.at[k], recv.at[k], (t, f))
+    for k in reversed(range(1, 8)): piece(k).start()
+    mine.wait()
+    for k in reversed(range(1, 8)):
+        piece(k).wait_recv()
+        piece(k).wait_send()
+
+def exchange_rows(x, cid):
+    D = pltpu.SemaphoreType.DMA
+    return pl.pallas_call(a2a_kernel, out_shape=jax.ShapeDtypeStruct(x.shape, x.dtype), in_specs=[VM()], out_specs=VM(),
+        scratch_shapes=[D, D((8,)), D((8,))],
+        compiler_params=pltpu.CompilerParams(collective_id=cid, has_side_effects=True))(x)
+
+def sum_kernel(x_ref, o_ref, got, send, recv):
+    s, f, z, y = where_am_i()
+    me = s * 4 + f
+    bar = pltpu.get_barrier_semaphore()
+    def dev(i): return (i // 4, i % 4)
+    @pl.loop(1, 32)
+    def _(k):
+        pl.semaphore_signal(bar, inc=1, device_id=dev((me + k) % 32), device_id_type=MESH)
+    pl.semaphore_wait(bar, 31)
+    def piece(k):
+        i = (me + k) % 32
+        return remote(x_ref.at[i], got.at[k], send.at[k], recv.at[k], dev(i))
+    @pl.loop(1, 32)
+    def _(k): piece(k).start()
+    @pl.loop(1, 32)
+    def _(k):
+        piece(k).wait_recv()
+        piece(k).wait_send()
+    o_ref[...] = x_ref[me]
+    @pl.loop(1, 32)
+    def _(k): o_ref[...] += got[k]
+
+def sum_parts(x, cid):
+    D = pltpu.SemaphoreType.DMA
+    return pl.pallas_call(sum_kernel, out_shape=jax.ShapeDtypeStruct(x.shape[1:], x.dtype), in_specs=[VM()], out_specs=VM(),
+        scratch_shapes=[pltpu.VMEM(x.shape, x.dtype), D((32,)), D((32,))],
+        compiler_params=pltpu.CompilerParams(collective_id=cid, has_side_effects=True))(x)
+
+
+def line_body(
+    hidden_in,
+    ln1_gain,
+    ln1_bias,
+    qkv_weight,
+    qkv_bias,
+    out_weight,
+    ln2_gain,
+    ln2_bias,
+    gate_weight,
+    up_weight,
+    down_weight,
+    seq_lengths,
+    deal_order,
+    out_grad,
+):
+    rows = hidden_in.shape[1]
+    width = hidden_in.shape[2]
+    nseq = lax.axis_size("seq")
+    nfsdp = lax.axis_size("fsdp")
+    lw = width // nseq
+    part = qkv_weight.shape[0]
+    ff = gate_weight.shape[1]
+    lf = ff // nseq
+    both = ("seq", "fsdp")
+    seq_at, fsdp_at = lax.axis_index("seq"), lax.axis_index("fsdp")
+    stream = hidden_in[0].astype(jnp.float32)
+    cotangent = out_grad[0].astype(jnp.float32)
+    order = deal_order[0]
+    lengths = seq_lengths[0]
+    group_rows = order.shape[0]
+    valid_rows = group_rows * 5 // 8
+    orow, ocol = order[None, :], order[:, None]
+    local_pos = lax.dynamic_slice_in_dim(order, seq_at * rows, rows)
+    valid = (local_pos < valid_rows).astype(jnp.float32)[:, None]
+    dealt_seg, dealt_start = segment_of(order, lengths)
+    dealt_tables = rotary_tables((order - dealt_start).astype(jnp.float32))
+    packed_pos = jnp.arange(valid_rows, dtype=jnp.int32)
+    packed_seg, packed_start = segment_of(packed_pos, lengths)
+    packed_tables = rotary_tables((packed_pos - packed_start).astype(jnp.float32))
+
+    def column_parts(weights):
+        views = [w.reshape(part, nseq, -1) for w in weights]
+        return jnp.concatenate(views, 2).transpose(1, 0, 2)
+
+    def full_columns(weights, cid):
+        return column_gather(column_parts(weights), cid).reshape(width, -1)
+
+    norms = lax.all_gather(
+        jnp.stack([ln1_gain, ln1_bias, ln2_gain, ln2_bias, *qkv_bias]), both, axis=1, tiled=True
+    )
+    gain1, shift1, gain2, shift2 = norms[:4].astype(jnp.float32)
+    qkv_shift = lax.dynamic_slice_in_dim(norms[4:], seq_at * lw, lw, 1)
+    qkv_shift = qkv_shift.reshape(-1).astype(jnp.float32)
+
+    stream_full = all_gather_rows(hidden_in[0], 1).reshape(group_rows, width)
+    qkv_parts = qkv_weight.reshape(part, 3, nseq, lw).transpose(2, 0, 1, 3).reshape(nseq, part, -1)
+    qkv_w = column_gather(qkv_parts, 2).reshape(width, 3 * lw)
+    normed_full, _ = normalize(stream_full.astype(jnp.float32))
+    first_in = (normed_full * gain1 + shift1).astype(jnp.bfloat16)
+    normed1, rstd1 = normalize(stream)
+    qkv = times(first_in, qkv_w) + qkv_shift
+    mixed, packed, lse = attn_fwd(qkv, dealt_tables, orow, ocol, seq_lengths, valid_rows)
+    heads_out = exchange_rows(mixed.reshape(nseq, rows, lw), 3)
+    heads_out = heads_out.transpose(1, 0, 2).reshape(rows, width)
+    out_w = lax.all_gather(out_weight, both, axis=0, tiled=True)
+    out_rows = lax.all_gather(out_weight, "fsdp", axis=0, tiled=True)
+    down_w = lax.all_gather(down_weight, "fsdp", axis=0, tiled=True)
+    wide_w = full_columns([gate_weight, up_weight], 4)
+    attn = times(heads_out, out_w)
+    resid = stream + attn
+    normed2, rstd2 = normalize(resid)
+    second_local = (normed2 * gain2 + shift2).astype(jnp.bfloat16)
+    second_in = all_gather_rows(second_local, 5).reshape(group_rows, width)
+    mlp_grad = all_gather_rows(out_grad[0], 6).reshape(group_rows, width)
+    wide = times(second_in, wide_w)
+    gate, upper = wide[:, :lf], wide[:, lf:]
+    hidden, sigma = mlp_forward(gate, upper)
+    mlp_part = times(hidden, down_w).astype(jnp.bfloat16).reshape(nseq, rows, width)
+    hidden_grad = times_transposed(mlp_grad, down_w)
+    wide_act = jnp.concatenate(mlp_backward(hidden_grad, gate, upper, sigma), 1)
+    second_part = times_transposed(wide_act, wide_w).astype(jnp.bfloat16)
+    second_grad = reduce_scatter_rows(second_part.reshape(nseq, rows, width), 7)
+    resid_part, gain2_grad, shift2_grad = norm_back(second_grad, normed2, rstd2, gain2)
+    resid_grad = cotangent + resid_part
+    attn_grad = all_gather_rows(resid_grad.astype(jnp.bfloat16), 8).reshape(group_rows, width)
+    mixed_grad = times_transposed(attn_grad, out_rows).astype(jnp.bfloat16)
+    qkv_act, bias_sums = attn_bwd(packed, mixed_grad, lse, packed_tables, orow, ocol, seq_lengths)
+    first_part = times_transposed(qkv_act, qkv_w).astype(jnp.bfloat16)
+    first_grad = reduce_scatter_rows(first_part.reshape(nseq, rows, width), 9)
+    input_part, gain1_grad, shift1_grad = norm_back(first_grad, normed1, rstd1, gain1)
+    input_grad = resid_grad + input_part
+
+    mlp = reduce_scatter_rows(mlp_part, 10)
+    result = resid + mlp
+
+    def column_shard(left, right, cid):
+        grad = outer(left, right).astype(jnp.bfloat16).reshape(nseq, nfsdp, part, -1)
+        return column_reduce(grad, cid).astype(jnp.float32)
+
+    def row_shard(left, right, cid):
+        grad = outer(left, right).astype(jnp.bfloat16).reshape(1, nfsdp, -1, width)
+        return column_reduce(grad, cid, False)[0]
+
+    down_grad = row_shard(hidden, mlp_grad, 11)
+    wide_grad = column_shard(second_in, wide_act, 12)
+    gate_grad = wide_grad[:, :, :lf].transpose(1, 0, 2).reshape(part, ff)
+    up_grad = wide_grad[:, :, lf:].transpose(1, 0, 2).reshape(part, ff)
+    out_grad_w = row_shard(mixed, attn_grad, 13)
+    qkv_grad = column_shard(first_in, qkv_act, 14)
+    qkv_grad = qkv_grad.reshape(nseq, part, 3, lw).transpose(1, 2, 0, 3).reshape(part, 3 * width)
+
+    vectors = jnp.stack([gain1_grad, shift1_grad, gain2_grad, shift2_grad])
+    vectors = vectors.reshape(4, nseq * nfsdp, part).transpose(1, 0, 2).reshape(-1, 2, 128)
+    sums = jnp.stack(
+        [
+            jnp.sum(valid * result * result),
+            jnp.sum(valid * attn * attn),
+            jnp.sum(valid * mlp * mlp),
+        ]
+    )
+    sums = jnp.broadcast_to(jnp.pad(sums, (0, 125)), (nseq * nfsdp, 1, 128))
+    bias = bias_sums.reshape(3, nfsdp, part).transpose(1, 0, 2).reshape(nfsdp, 3 * part)
+    bias = jnp.pad(bias, ((0, 0), (0, 64))).reshape(1, nfsdp, 2, 128)
+    here = (jnp.arange(nseq) == seq_at)[:, None, None, None]
+    bias = jnp.where(here, bias, 0.0).reshape(-1, 2, 128)
+    message = jnp.concatenate([vectors, sums, bias, jnp.zeros_like(vectors), sums], 1)
+    total = sum_parts(message, 15)
+    count = valid_rows * nfsdp * width
+    rms = jnp.sqrt(total[2, :3] / count)
+    shards = total[:2].reshape(4, part)
+    qkv_bias_grad = total[3:5].reshape(4, part)[:3]
+    return (
+        result.astype(jnp.bfloat16)[None],
+        input_grad[None],
+        shards[0],
+        shards[1],
+        qkv_grad,
+        qkv_bias_grad,
+        out_grad_w,
+        shards[2],
+        shards[3],
+        gate_grad,
+        up_grad,
+        down_grad,
+        rms,
+    )
+
+
 def solution(mesh):
     in_specs = (
         P("fsdp", "seq", None),
@@ -367,4 +1041,11 @@
         P(("seq", "fsdp"), None),
         P(),
     )
-    return jax.shard_map(body, mesh=mesh, in_specs=in_specs, out_specs=out_specs, check_vma=False)
+    line = dict(mesh.shape) == {"seq": 8, "fsdp": 4}
+    return jax.shard_map(
+        line_body if line else body,
+        mesh=mesh,
+        in_specs=in_specs,
+        out_specs=out_specs,
+        check_vma=False,
+    )

time: 1180 us -> 805 us (0.68)
  waiting for transfers between devices: 645 us -> 2.06 us
  Pallas kernels: 0 us -> 591 us
  blocking collectives: 207 us -> 44 us
  local copies, waits for them, and re-layouts: 119 us -> 40.2 us
  matrix products: 123 us -> 78.6 us
  starting transfers between devices: 14.3 us -> 0.11 us
  other arithmetic: 43.5 us -> 29.7 us
    pallas_call x0 -> x17, Pallas kernels: none -> 591 us  [the longest x4 217 us: all_gather_rows(): pl.pallas_call(ag_kernel, out_shape=jax.ShapeDtypeStruct((8,) + x.shape,...]
    reduce_scatter x6 -> x0, waiting for transfers between devices: 287 us -> none  [the longest x3 252 us: scatter_rows(): lax.psum_scatter(partial.astype(jnp.bfloat16), 'seq', scatter_dimension=0...]
    all_gather x10 -> x3, waiting for transfers between devices: 271 us -> 0.01 us  [the longest x1 0.01 us: line_body(): out_w = lax.all_gather(out_weight, both, axis=0, tiled=True)]
    all_to_all x4 -> x0, blocking collectives: 120 us -> none  [the longest x2 67.6 us: column_slice(): lax.all_to_all(view.reshape(nseq * part, blocks * cols), 'seq', split_axi...]
    all_to_all x3 -> x0, waiting for transfers between devices: 53.8 us -> none  [the longest x1 35.7 us: column_slice(): lax.all_to_all(view.reshape(nseq * part, blocks * cols), 'seq', split_axi...]
    psum x1 -> x0, blocking collectives: 41.3 us -> none  [body(): lax.psum((gain1_grad, shift1_grad, gain2_grad, shift2_grad, jnp.sum(valid...]
    gather x14 -> x0, local copies, waits for them, and re-layouts: 38.6 us -> none  [the longest x8 22 us: to_pack(): return values[inverse].reshape(group_rows, heads_here, HEAD_DIM)]
    unnamed x18 -> x3, waiting for transfers between devices: 33.6 us -> 2.06 us
  transfers between devices with their start and end apart: 20 -> 3, of which waited for: 16 -> 0; matrix products, arithmetic and copies ran while one was open for 22% -> 11% of each run, Pallas kernels for 0% -> 52%
where the time goes in v2:
time: 805 us; the launch traced here: 801 us
  Pallas kernels  591 us (73%)
  matrix products  78.6 us (10%)
  blocking collectives  44 us (5%)
  local copies, waits for them, and re-layouts  40.2 us (5%)
  other arithmetic  29.7 us (4%)
  between operations  14.7 us (2%)
    pallas_call x4, Pallas kernels, all_gather_rows(): pl.pallas_call(ag_kernel, out_shape=jax.ShapeDtypeStruct((8,) + x.shape,...  217 us
    pallas_call x3, Pallas kernels, reduce_scatter_rows(): pl.pallas_call(rs_kernel, out_shape=jax.ShapeDtypeStruct((rows, w), jnp.f...  136 us
    pallas_call x4, Pallas kernels, column_reduce(): pl.pallas_call(functools.partial(cr_kernel, exchange), out_shape=jax.Shap...  106 us
    pallas_call x2, Pallas kernels, column_gather(): pl.pallas_call(cg_kernel, out_shape=jax.ShapeDtypeStruct((8, 4) + x.shape...  77.6 us
    all_gather x1, blocking collectives, line_body(): lax.all_gather(jnp.stack([ln1_gain, ln1_bias, ln2_gain, ln2_bias, *qkv_bi...  44 us
    dot_general x4, matrix products, outer(): lax.dot_general(left, right, (((0,), (0,)), ((), ())), preferred_element_...  28.5 us
    dot_general x4, matrix products, times_transposed(): lax.dot_general(left, right, (((1,), (1,)), ((), ())), preferred_element_...  25.5 us
    dot_general x4, matrix products, times(): return jnp.dot(left, right, preferred_element_type=jnp.float32)  24.6 us
  transfers between devices with their start and end apart: 3, of which 0 were waited for; matrix products, arithmetic and copies ran while one was open for 11% of the time, Pallas kernels for 52%

profile of v2, /device:TPU:0, one launch (start us, length us, event | category | flops | bytes accessed | tf_op | source)
XLA Modules:
  0.0 800.9 jit_solution(4400421294865751005)
XLA Ops:
  9.4 0.8 stack.47
  10.2 44.0 %all-gather = bf16[32,64,7]{1,2,0:T(8,128)(2,1)S(1)} all-gather(bf16[1,64,7]{1,2,0:T(8,128)(2,1)S(1)} %bitcast.176), channel_id=1, replica_groups=mesh['seq'=8,'fsdp'=4] {'seq','fsdp'}, dimensions={0}, use_global_device_ids=true | all-gather | bytes 29568 | tf_op jit(solution)/shard_map/all_gather | solution.py:911
  54.4 1.2 convert_reduce_fusion.1
  55.6 72.1 %shard_map.237 = bf16[8,128,2048]{2,1,0:T(8,128)(2,1)} custom-call(bf16[128,2048]{1,0:T(8,128)(2,1)} %bitcast.142), custom_call_target="tpu_custom_call" | custom-call | tf_op jit(solution)/shard_map/pallas_call | solution.py:402
  127.7 3.0 convert_reduce_fusion
  131.2 1.2 multiply_reduce_fusion
  133.1 2.2 reshape.310.x_ref
  135.3 31.4 %shard_map.238 = bf16[8,4,64,768]{3,2,1,0:T(8,128)(2,1)} custom-call(bf16[8,64,768]{2,1,0:T(8,128)(2,1)} %reshape.310.x_ref), custom_call_target="tpu_custom_call" | custom-call | tf_op jit(solution)/shard_map/pallas_call | solution.py:570
  167.5 3.5 add_convert_fusion
  171.0 3.4 convolution_add_fusion.qkv_ref
  174.4 2.0 fusion.19
  176.4 12.8 %shard_map.239 = (bf16[1024,256]{1,0:T(8,128)(2,1)S(1)}, bf16[640,768]{1,0:T(8,128)(2,1)S(1)}, f32[4,640,1]{2,1,0:T(8,128)S(1)}) custom-call(f32[1024,768]{1,0:T(8,128)S(1)} %convolution_add_fusion.qkv_ref, f32[1024,128]{1,0:T(8,128)S(1)} %get-tuple-element.57.c_ref, f32[1024,128]{1,0:T(8,128)S(1)} %get-tuple-element.56.s1_ref, ...), custom_call_target="tpu_custom_call" | custom-call | tf_op jit(solution)/shard_map/pallas_call | solution.py:728
  189.2 0.9 copy-done.3
  190.2 0.8 copy-done.5
  190.9 17.7 %shard_map.240 = bf16[8,128,256]{2,1,0:T(8,128)(2,1)} custom-call(bf16[8,128,256]{2,1,0:T(8,128)(2,1)} %bitcast.137), custom_call_target="tpu_custom_call" | custom-call | tf_op jit(solution)/shard_map/pallas_call | solution.py:830
  208.7 2.0 copy.72
  211.5 2.0 reshape.317
  213.7 1.6 maximum_bitcast_fusion.x_ref
  215.3 46.2 %shard_map.242 = bf16[8,4,64,1408]{3,2,1,0:T(8,128)(2,1)} custom-call(bf16[8,64,1408]{2,1,0:T(8,128)(2,1)} %maximum_bitcast_fusion.x_ref), custom_call_target="tpu_custom_call" | custom-call | tf_op jit(solution)/shard_map/pallas_call | solution.py:570
  261.5 53.1 %shard_map.244 = bf16[8,128,2048]{2,1,0:T(8,128)(2,1)} custom-call(bf16[128,2048]{1,0:T(8,128)(2,1)} %bitcast.160), custom_call_target="tpu_custom_call" | custom-call | tf_op jit(solution)/shard_map/pallas_call | solution.py:402
  314.7 1.2 fusion.23
  316.2 4.7 fusion.3
  320.9 5.9 fusion.38
  327.7 1.0 add_convert_fusion.1.x_ref
  328.7 46.6 %shard_map.241 = bf16[8,128,2048]{2,1,0:T(8,128)(2,1)} custom-call(bf16[128,2048]{1,0:T(8,128)(2,1)} %add_convert_fusion.1.x_ref), custom_call_target="tpu_custom_call" | custom-call | tf_op jit(solution)/shard_map/pallas_call | solution.py:402
  375.4 11.7 %fusion.41 = f32[1024,1408]{1,0:T(8,128)} fusion(bf16[1024,2048]{1,0:T(8,128)(2,1)} %bitcast.151, bf16[2048,1408]{1,0:T(8,128)(2,1)} %bitcast.145), kind=kOutput, calls=%fused_computation.125 | convolution fusion | flops 5905580032 | bytes 15728640 | tf_op jit(solution)/shard_map/dot_general | solution.py:74
  387.1 9.0 %multiply_convert_fusion.1 = (bf16[1024,704]{1,0:T(8,128)(2,1)S(1)}, bf16[1024,704]{1,0:T(8,128)(2,1)S(1)}, bf16[1024,704]{1,0:T(8,128)(2,1)S(1)}) fusion(f32[1024,1408]{1,0:T(8,128)} %fusion.41, bf16[1024,2048]{1,0:T(8,128)(2,1)} %bitcast.149, bf16[704,2048]{1,0:T(8,128)(2,1)} %all-gather.7.cloned.1.call-done), kind=kOutput, calls=%fused_computation.15 | convolution fusion | flops 2964324352 | bytes 17170432 | tf_op jit(solution)/shard_map/dot_general | solution.py:78
  396.2 1.1 copy-done.25
  397.8 8.7 %convolution_convert_fusion.1 = bf16[1024,2048]{1,0:T(8,128)(2,1)S(1)} fusion(bf16[2048,1408]{1,0:T(8,128)(2,1)} %bitcast.146, bf16[1024,704]{1,0:T(8,128)(2,1)S(1)} %get-tuple-element.42, bf16[1024,704]{1,0:T(8,128)(2,1)S(1)} %get-tuple-element.41), kind=kOutput, calls=%fused_computation.9 | convolution fusion | flops 5913444352 | bytes 12845056 | tf_op jit(solution)/shard_map/dot_general | solution.py:78
  406.6 45.5 %shard_map.245 = f32[128,2048]{1,0:T(8,128)S(1)} custom-call(bf16[8,128,2048]{2,1,0:T(8,128)(2,1)S(1)} %bitcast.130), custom_call_target="tpu_custom_call" | custom-call | tf_op jit(solution)/shard_map/pallas_call | solution.py:490
  452.1 3.6 convolution_convert_fusion.2
  455.8 44.6 %shard_map.243 = f32[128,2048]{1,0:T(8,128)S(1)} custom-call(bf16[8,128,2048]{2,1,0:T(8,128)(2,1)S(1)} %bitcast.131), custom_call_target="tpu_custom_call" | custom-call | tf_op jit(solution)/shard_map/pallas_call | solution.py:490
  500.4 2.2 fusion.16
  502.6 1.7 fusion.37
  504.2 45.5 %shard_map.246 = bf16[8,128,2048]{2,1,0:T(8,128)(2,1)} custom-call(bf16[128,2048]{1,0:T(8,128)(2,1)} %get-tuple-element.37.x_ref), custom_call_target="tpu_custom_call" | custom-call | tf_op jit(solution)/shard_map/pallas_call | solution.py:402
  549.8 4.6 convolution_convert_fusion.6
  554.4 10.2 %convolution_convert_fusion = bf16[2048,1408]{1,0:T(8,128)(2,1)} fusion(bf16[1024,2048]{1,0:T(8,128)(2,1)S(1)} %bitcast.152, bf16[1024,704]{1,0:T(8,128)(2,1)} %copy-done.27, bf16[1024,704]{1,0:T(8,128)(2,1)S(1)} %copy-done.26), kind=kOutput, calls=%fused_computation.8 | convolution fusion | flops 5914230784 | bytes 12845056 | tf_op jit(solution)/shard_map/dot_general | solution.py:68
  564.7 3.9 convolution_convert_fusion.7.do_ref
  568.6 13.5 %shard_map.247 = (bf16[1024,768]{1,0:T(8,128)(2,1)S(1)}, f32[1,768]{1,0:T(1,128)S(1)}) custom-call(bf16[640,768]{1,0:T(8,128)(2,1)S(1)} %copy-done.4, bf16[1024,256]{1,0:T(8,128)(2,1)S(1)} %convolution_convert_fusion.7.do_ref, f32[4,640,1]{2,1,0:T(8,128)S(1)} %get-tuple-element.20.lse_ref, f32[640,128]{1,0:T(8,128)S(1)} %get-tuple-element.54.c_ref, ...), custom_call_target="tpu_custom_call" | custom-call | tf_op jit(solution)/shard_map/pallas_call | solution.py:797
  582.1 3.9 convolution_convert_fusion.3
  586.0 46.1 %shard_map.248 = f32[128,2048]{1,0:T(8,128)S(1)} custom-call(bf16[8,128,2048]{2,1,0:T(8,128)(2,1)S(1)} %bitcast.132), custom_call_target="tpu_custom_call" | custom-call | tf_op jit(solution)/shard_map/pallas_call | solution.py:490
  633.5 2.0 select_maximum_fusion
  635.5 0.8 concatenate.17.x_ref
  636.3 10.2 %shard_map.249 = f32[8,128]{1,0:T(8,128)} custom-call(f32[32,8,128]{2,1,0:T(8,128)} %concatenate.17.x_ref), custom_call_target="tpu_custom_call" | custom-call | tf_op jit(solution)/shard_map/pallas_call | solution.py:858
  647.3 1.2 sqrt_bitcast_fusion
  648.5 7.4 convolution_convert_fusion.5
  655.9 2.6 copy-done
  658.5 45.3 %shard_map.252 = bf16[8,64,1408]{2,1,0:T(8,128)(2,1)S(1)} custom-call(bf16[8,4,64,1408]{3,2,1,0:T(8,128)(2,1)S(1)} %bitcast.128), custom_call_target="tpu_custom_call" | custom-call | tf_op jit(solution)/shard_map/pallas_call | solution.py:643
  704.1 1.7 slice_bitcast_fusion
  705.8 0.9 copy.80
  706.8 1.7 reshape.335
  708.4 3.6 copy.81
  712.0 2.8 reshape.336
  714.8 10.9 %shard_map.251 = f32[1,64,2048]{2,1,0:T(8,128)S(1)} custom-call(bf16[1,4,64,2048]{3,2,1,0:T(8,128)(2,1)S(1)} %bitcast.136), custom_call_target="tpu_custom_call" | custom-call | tf_op jit(solution)/shard_map/pallas_call | solution.py:643
  725.7 6.2 convolution_convert_fusion.4
  731.9 28.0 %shard_map.250 = bf16[8,64,768]{2,1,0:T(8,128)(2,1)S(1)} custom-call(bf16[8,4,64,768]{3,2,1,0:T(8,128)(2,1)S(1)} %bitcast.133), custom_call_target="tpu_custom_call" | custom-call | tf_op jit(solution)/shard_map/pallas_call | solution.py:643
  759.9 1.9 reshape.345
  761.8 2.5 copy.79
  764.3 1.6 copy.84
  767.2 1.8 copy-done.1
  769.0 21.7 %shard_map.253 = f32[1,176,2048]{2,1,0:T(8,128)S(1)} custom-call(bf16[1,4,176,2048]{3,2,1,0:T(8,128)(2,1)S(1)} %bitcast.134), custom_call_target="tpu_custom_call" | custom-call | tf_op jit(solution)/shard_map/pallas_call | solution.py:643
  790.8 1.4 fusion.13
  792.2 0.8 copy.91
  793.0 1.1 copy.92
  (121 shorter events, 10.5 us)
Async XLA Ops:
  7.2 313.7 %all-gather.5.cloned.1.call-start = ((), (), s32[]{:S(2)}) async-start(), calls=%async_computation | async-start | bytes 8650752 | tf_op jit(solution)/shard_map/all_gather | solution.py:928
  7.9 379.2 %all-gather.7.cloned.1.call-start = ((), (), s32[]{:S(2)}) async-start(), calls=%async_computation.1 | async-start | bytes 3604480 | tf_op jit(solution)/shard_map/all_gather | solution.py:930
  8.7 556.0 %all-gather.9.cloned.1.call-start = ((), (), s32[]{:S(2)}) async-start(), calls=%async_computation.2 | async-start | bytes 1310720 | tf_op jit(solution)/shard_map/all_gather | solution.py:929
  127.7 3.5 copy-start.10
  130.7 1.8 copy-start.21
  133.1 33.6 %copy-start.8 = (s32[1,3]{1,0:T(1,128)S(1)}, s32[1,3]{1,0:T(1,128)}, u32[]{:S(2)}) copy-start(s32[1,3]{1,0:T(1,128)} %len_ref.3) | copy-start | bytes 40
  133.1 33.9 %copy-start.7 = (s32[1,1024]{1,0:T(1,128)S(1)}, s32[1,1024]{1,0:T(1,128)}, u32[]{:S(2)}) copy-start(s32[1,1024]{1,0:T(1,128)} %orow_ref.3) | copy-start | bytes 12292
  167.5 3.5 copy-start.18
  176.4 34.3 %copy-start.22 = (bf16[64,5632]{1,0:T(8,128)(2,1)S(1)}, bf16[64,5632]{1,0:T(8,128)(2,1)}, u32[]{:S(2)}) copy-start(bf16[64,5632]{1,0:T(8,128)(2,1)} %param.22) | copy-start | bytes 2162692
  189.2 0.9 copy-start.3
  190.1 0.8 copy-start.5
  316.2 4.7 copy-start.13
  326.7 1.0 copy-start.11
  396.2 1.2 copy-start.25
  396.2 1.7 copy-start.27
  396.2 55.9 %copy-start.24 = (bf16[1024,704]{1,0:T(8,128)(2,1)}, bf16[1024,704]{1,0:T(8,128)(2,1)S(1)}, u32[]{:S(2)}) copy-start(bf16[1024,704]{1,0:T(8,128)(2,1)S(1)} %get-tuple-element.43) | copy-start | bytes 4325380
  406.6 45.5 %copy-start.23 = (bf16[704,2048]{1,0:T(8,128)(2,1)S(1)}, bf16[704,2048]{1,0:T(8,128)(2,1)}, u32[]{:S(2)}) copy-start(bf16[704,2048]{1,0:T(8,128)(2,1)} %all-gather.7.cloned.1.call-done) | copy-start | bytes 8650756
  455.7 44.6 %copy-start.12 = (f32[128,2048]{1,0:T(8,128)S(1)}, f32[128,2048]{1,0:T(8,128)}, u32[]{:S(2)}) copy-start(f32[128,2048]{1,0:T(8,128)} %copy-done.11) | copy-start | bytes 3145732
  455.7 44.6 %copy-start.17 = (f32[128,2048]{1,0:T(8,128)S(1)}, f32[128,2048]{1,0:T(8,128)}, u32[]{:S(2)}) copy-start(f32[128,2048]{1,0:T(8,128)} %get-tuple-element.68) | copy-start | bytes 3145732
  500.4 2.2 copy-start.20
  504.2 45.6 %copy-start.6 = (bf16[1024,256]{1,0:T(8,128)(2,1)S(1)}, bf16[1024,256]{1,0:T(8,128)(2,1)}, u32[]{:S(2)}) copy-start(bf16[1024,256]{1,0:T(8,128)(2,1)} %copy-done.5) | copy-start | bytes 1572868
  549.8 4.6 copy-start.15
  549.8 4.6 copy-start.26
  564.7 3.9 copy-start.4
  568.5 13.6 %copy-start.19 = (bf16[8,4,64,768]{3,2,1,0:T(8,128)(2,1)S(1)}, bf16[8,4,64,768]{3,2,1,0:T(8,128)(2,1)}, u32[]{:S(2)}) copy-start(bf16[8,4,64,768]{3,2,1,0:T(8,128)(2,1)} %shard_map.238) | copy-start | bytes 9437188
  582.1 3.9 copy-start.9
  586.0 46.2 %copy-start.14 = (bf16[1,128,2048]{2,1,0:T(8,128)(2,1)S(1)}, bf16[1,128,2048]{2,1,0:T(8,128)(2,1)}, u32[]{:S(2)}) copy-start(bf16[1,128,2048]{2,1,0:T(8,128)(2,1)} %param.14) | copy-start | bytes 1572868
  655.9 2.6 copy-start
  708.4 6.4 copy-start.2
  764.3 26.5 %copy-start.16 = (f32[128,2048]{1,0:T(8,128)S(1)}, f32[128,2048]{1,0:T(8,128)}, u32[]{:S(2)}) copy-start(f32[128,2048]{1,0:T(8,128)} %get-tuple-element.38) | copy-start | bytes 3145732
  767.2 1.8 copy-start.1
Sparse Core Ops, SparseCore 0:
  10.9 95.8 all-gather.4
  108.3 31.1 all-gather.6
  141.1 22.3 all-gather.8

commit v3 on v1

--- a/solution.py
+++ b/solution.py
@@ -1,6 +1,10 @@
+import functools
+
 import jax
 import jax.numpy as jnp
 from jax import lax
+from jax.experimental import pallas as pl
+from jax.experimental.pallas import tpu as pltpu
 from jax.sharding import PartitionSpec as P
 
 HEAD_DIM = 64
@@ -335,6 +339,1438 @@
     )
 
 
+MESH = pl.DeviceIdType.MESH
+QB = 128
+NEG = -1e30
+CH = 2
+VMEM_SPEC = pl.BlockSpec(memory_space=pltpu.VMEM)
+SMEM_SPEC = pl.BlockSpec(memory_space=pltpu.SMEM)
+ANY_SPEC = pl.BlockSpec(memory_space=pl.ANY)
+DMA = pltpu.SemaphoreType.DMA
+
+
+def comm_params(collective, limit=48):
+    return pltpu.CompilerParams(
+        collective_id=collective, has_side_effects=True, vmem_limit_bytes=limit << 20
+    )
+
+
+def where_am_i():
+    s = lax.axis_index("seq")
+    f = lax.axis_index("fsdp")
+    return s, f, s // 2, s % 2
+
+
+def remote(src, dst, send, recv, device):
+    return pltpu.make_async_remote_copy(
+        src, dst, send, recv, device_id=device, device_id_type=MESH
+    )
+
+
+def flip(v, bit):
+    return v + bit * (1 - 2 * ((v // bit) % 2))
+
+
+def peer(s, k):
+    for bit in (1, 2, 4):
+        if k & bit:
+            s = flip(s, bit)
+    return s
+
+
+def dealer(i):
+    return (i // 4, i % 4)
+
+
+def greet_all(s, f):
+    bar = pltpu.get_barrier_semaphore()
+    me = s * 4 + f
+
+    @pl.loop(1, 32)
+    def _(k):
+        pl.semaphore_signal(bar, inc=1, device_id=dealer((me + k) % 32), device_id_type=MESH)
+
+    pl.semaphore_wait(bar, 31)
+
+
+def greet_line(s, f, z, y):
+    bar = pltpu.get_barrier_semaphore()
+    pl.semaphore_signal(bar, inc=1, device_id=(flip(s, 1), f), device_id_type=MESH)
+
+    @pl.when(z > 0)
+    def _():
+        pl.semaphore_signal(bar, inc=1, device_id=(s - 2, f), device_id_type=MESH)
+
+    @pl.when(z < 3)
+    def _():
+        pl.semaphore_signal(bar, inc=1, device_id=(s + 2, f), device_id_type=MESH)
+
+    edge = jnp.where((z == 0) | (z == 3), 1, 0)
+    pl.semaphore_wait(bar, 3 - edge)
+
+
+def greet_columns(s, f):
+    bar = pltpu.get_barrier_semaphore()
+    for k in range(1, 8):
+        pl.semaphore_signal(bar, inc=1, device_id=(peer(s, k), f), device_id_type=MESH)
+    pl.semaphore_signal(bar, inc=1, device_id=(s, flip(f, 1)), device_id_type=MESH)
+    pl.semaphore_signal(bar, inc=1, device_id=(s, flip(f, 2)), device_id_type=MESH)
+    pl.semaphore_wait(bar, 9)
+
+
+def adder(dst, srcs, step=16):
+    @pl.loop(0, dst.shape[0] // step)
+    def _(i):
+        r = pl.ds(pl.multiple_of(i * step, step), step)
+        total = srcs[0][r].astype(jnp.float32)
+        for v in srcs[1:]:
+            total = total + v[r].astype(jnp.float32)
+        dst[r] = total.astype(dst.dtype)
+
+
+class SeqGather:
+    @staticmethod
+    def scratch():
+        return [DMA, DMA((8,)), DMA((4,)), DMA((4,)), DMA((4,))]
+
+    def __init__(self, x, o, own, recv, sy, su, sd):
+        self.x, self.o, self.recv, self.sy, self.su, self.sd = x, o, recv, sy, su, sd
+        self.s, self.f, self.z, self.y = where_am_i()
+        self.other = flip(self.s, 1)
+        self.own = pltpu.make_async_copy(x, o.at[self.s], own)
+
+    def at(self, zb):
+        return 2 * zb + self.y
+
+    def ysend(self, zb, src):
+        b = self.at(zb)
+        return remote(src, self.o.at[b], self.sy.at[zb], self.recv.at[b], (self.other, self.f))
+
+    def usend(self, zb, src):
+        b = self.at(zb)
+        return remote(src, self.o.at[b], self.su.at[zb], self.recv.at[b], (self.s + 2, self.f))
+
+    def dsend(self, zb, src):
+        b = self.at(zb)
+        return remote(src, self.o.at[b], self.sd.at[zb], self.recv.at[b], (self.s - 2, self.f))
+
+    def arrived(self, b):
+        o = self.o.at[b]
+        return remote(o, o, self.sy.at[0], self.recv.at[b], (self.other, self.f))
+
+    def start(self):
+        @pl.when(self.z < 3)
+        def _():
+            self.usend(self.z, self.x).start()
+
+        @pl.when(self.z > 0)
+        def _():
+            self.dsend(self.z, self.x).start()
+
+        self.ysend(self.z, self.x).start()
+        self.own.start()
+
+    def below(self, t, use=None):
+        @pl.when(self.z >= t)
+        def _():
+            zb = self.z - t
+            b = self.at(zb)
+            self.arrived(b).wait_recv()
+
+            @pl.when(self.z < 3)
+            def _():
+                self.usend(zb, self.o.at[b]).start()
+
+            self.ysend(zb, self.o.at[b]).start()
+            if use is not None:
+                use(b)
+
+    def above(self, t, use=None):
+        @pl.when(self.z + t <= 3)
+        def _():
+            zb = self.z + t
+            b = self.at(zb)
+            self.arrived(b).wait_recv()
+
+            @pl.when(self.z > 0)
+            def _():
+                self.dsend(zb, self.o.at[b]).start()
+
+            self.ysend(zb, self.o.at[b]).start()
+            if use is not None:
+                use(b)
+
+    def across(self, t, use=None):
+        for sign in (0,) if t == 0 else (-1, 1):
+            zb = self.z + sign * t
+
+            @pl.when((zb >= 0) & (zb <= 3))
+            def _():
+                b = 2 * zb + 1 - self.y
+                self.arrived(b).wait_recv()
+                if use is not None:
+                    use(b)
+
+    def steps(self):
+        out = []
+        for t in (1, 2, 3):
+            out.append(functools.partial(self.below, t))
+            out.append(functools.partial(self.above, t))
+        return out
+
+    def finish(self):
+        self.own.wait()
+        for zb in range(4):
+            self.ysend(zb, self.x).wait_send()
+
+            @pl.when((self.z < 3) & (zb <= self.z))
+            def _():
+                self.usend(zb, self.x).wait_send()
+
+            @pl.when((self.z > 0) & (zb >= self.z))
+            def _():
+                self.dsend(zb, self.x).wait_send()
+
+
+class SeqReduce:
+    @staticmethod
+    def scratch(rows, w):
+        big = [pltpu.VMEM((4, rows, w), jnp.bfloat16) for _ in range(6)]
+        return big + [DMA((4,))] + [DMA((4, CH)) for _ in range(6)]
+
+    def __init__(self, p, o, mine, ybuf, up, down, send_up, send_down, load, ry, ru, rd, sy, su, sd):
+        self.p, self.o, self.mine, self.ybuf, self.up, self.down = p, o, mine, ybuf, up, down
+        self.send_up, self.send_down, self.load_sem = send_up, send_down, load
+        self.ry, self.ru, self.rd, self.sy, self.su, self.sd = ry, ru, rd, sy, su, sd
+        self.s, self.f, self.z, self.y = where_am_i()
+        self.other = flip(self.s, 1)
+        self.ch = p.shape[1] // CH
+
+    def order(self, k):
+        a, b, c, d = [3, 2, 1, 0][k], [3, 0, 2, 1][k], [0, 3, 1, 2][k], [0, 1, 2, 3][k]
+        z = self.z
+        return jnp.where(z == 0, a, jnp.where(z == 1, b, jnp.where(z == 2, c, d)))
+
+    def rows(self, c):
+        return pl.ds(c * self.ch, self.ch)
+
+    def ysend(self, zb, c):
+        r = self.rows(c)
+        src = self.p.at[2 * zb + 1 - self.y, r]
+        dst = self.ybuf.at[zb, r]
+        return remote(src, dst, self.sy.at[zb, c], self.ry.at[zb, c], (self.other, self.f))
+
+    def load(self, zb):
+        src = self.p.at[2 * zb + self.y]
+        return pltpu.make_async_copy(src, self.mine.at[zb], self.load_sem.at[zb])
+
+    def usend(self, zb, c):
+        r = self.rows(c)
+        src, dst = self.send_up.at[zb, r], self.up.at[zb, r]
+        return remote(src, dst, self.su.at[zb, c], self.ru.at[zb, c], (self.s + 2, self.f))
+
+    def dsend(self, zb, c):
+        r = self.rows(c)
+        src, dst = self.send_down.at[zb, r], self.down.at[zb, r]
+        return remote(src, dst, self.sd.at[zb, c], self.rd.at[zb, c], (self.s - 2, self.f))
+
+    def start(self):
+        for k in range(4):
+            zb = self.order(k)
+            for c in range(CH):
+                self.ysend(zb, c).start()
+            self.load(zb).start()
+
+    def step(self, k, c):
+        z, zb, r = self.z, self.order(k), self.rows(c)
+        if c == 0:
+            self.load(zb).wait()
+        self.ysend(zb, c).wait_recv()
+        a, b = self.mine.at[zb, r], self.ybuf.at[zb, r]
+        u, d = self.up.at[zb, r], self.down.at[zb, r]
+
+        @pl.when(zb > z)
+        def _():
+            @pl.when(z == 0)
+            def _():
+                adder(self.send_up.at[zb, r], [a, b])
+
+            @pl.when(z > 0)
+            def _():
+                self.usend(zb, c).wait_recv()
+                adder(self.send_up.at[zb, r], [a, b, u])
+
+            self.usend(zb, c).start()
+
+        @pl.when(zb < z)
+        def _():
+            @pl.when(z == 3)
+            def _():
+                adder(self.send_down.at[zb, r], [a, b])
+
+            @pl.when(z < 3)
+            def _():
+                self.dsend(zb, c).wait_recv()
+                adder(self.send_down.at[zb, r], [a, b, d])
+
+            self.dsend(zb, c).start()
+
+        @pl.when(zb == z)
+        def _():
+            @pl.when(z > 0)
+            def _():
+                self.usend(zb, c).wait_recv()
+
+            @pl.when(z < 3)
+            def _():
+                self.dsend(zb, c).wait_recv()
+
+            o = self.o.at[r]
+
+            @pl.when(z == 0)
+            def _():
+                adder(o, [a, b, d])
+
+            @pl.when(z == 3)
+            def _():
+                adder(o, [a, b, u])
+
+            @pl.when((z > 0) & (z < 3))
+            def _():
+                adder(o, [a, b, u, d])
+
+    def steps(self):
+        return [functools.partial(self.step, k, c) for k in range(4) for c in range(CH)]
+
+    def finish(self):
+        for zb in range(4):
+            for c in range(CH):
+                self.ysend(zb, c).wait_send()
+
+                @pl.when(zb > self.z)
+                def _():
+                    self.usend(zb, c).wait_send()
+
+                @pl.when(zb < self.z)
+                def _():
+                    self.dsend(zb, c).wait_send()
+
+
+class ColGather:
+    @staticmethod
+    def scratch():
+        return [DMA, DMA((8, 4)), DMA((8,)), DMA((8, 2)), DMA((8,))]
+
+    def __init__(self, x, o, own, recv, direct, core, xs):
+        self.x, self.o, self.own, self.recv = x, o, own, recv
+        self.direct, self.core, self.xs = direct, core, xs
+        self.s, self.f, _, _ = where_am_i()
+        self.fc, self.fx = flip(self.f, 1), flip(self.f, 2)
+        self.fd = flip(self.fc, 2)
+        self.mine = pltpu.make_async_copy(x.at[self.s], o.at[self.s, self.f], own)
+
+    def send_direct(self, k):
+        s, f, t = self.s, self.f, peer(self.s, k)
+        return remote(self.x.at[t], self.o.at[s, f], self.direct.at[k], self.recv.at[s, f], (t, f))
+
+    def send_core(self, k, which, src):
+        t, ff = peer(self.s, k), self.f if which == 0 else self.fx
+        dst = self.o.at[t, ff]
+        return remote(src, dst, self.core.at[k, which], self.recv.at[t, ff], (self.s, self.fc))
+
+    def send_x(self, k, src):
+        t = peer(self.s, k)
+        dst = self.o.at[t, self.f]
+        return remote(src, dst, self.xs.at[k], self.recv.at[t, self.f], (self.s, self.fx))
+
+    def arrived(self, k, ff):
+        t = peer(self.s, k)
+        o = self.o.at[t, ff]
+        return remote(o, o, self.own, self.recv.at[t, ff], (self.s, self.fc))
+
+    def start(self):
+        for k in reversed(range(1, 8)):
+            self.send_direct(k).start()
+        self.send_x(0, self.x.at[self.s]).start()
+        self.send_core(0, 0, self.x.at[self.s]).start()
+        self.mine.start()
+
+    def step(self, k):
+        t = peer(self.s, k)
+        self.arrived(k, self.f).wait_recv()
+        self.send_x(k, self.o.at[t, self.f]).start()
+        self.send_core(k, 0, self.o.at[t, self.f]).start()
+
+    def xstep(self, k):
+        t = peer(self.s, k)
+        self.arrived(k, self.fx).wait_recv()
+        self.send_core(k, 1, self.o.at[t, self.fx]).start()
+
+    def steps(self):
+        first = [functools.partial(self.step, k) for k in reversed(range(1, 8))]
+        then = [functools.partial(self.xstep, k) for k in (0, 7, 6, 5, 4, 3, 2, 1)]
+        return first + then
+
+    def finish(self):
+        self.mine.wait()
+        for k in range(8):
+            self.arrived(k, self.fc).wait_recv()
+            self.arrived(k, self.fd).wait_recv()
+        for k in range(8):
+            if k:
+                self.send_direct(k).wait_send()
+            self.send_x(k, self.x.at[0]).wait_send()
+            self.send_core(k, 0, self.x.at[0]).wait_send()
+            self.send_core(k, 1, self.x.at[0]).wait_send()
+
+
+class ColReduce:
+    @staticmethod
+    def scratch(r, c):
+        def v(*lead):
+            return pltpu.VMEM(lead + (8, r, c), jnp.bfloat16)
+
+        return [v(2), v(2), v(), v(), v()] + [DMA((2, 8)) for _ in range(3)] + [DMA((8,)) for _ in range(4)]
+
+    def __init__(self, g, o, ld, cb, hx, xb, ob, ldsem, cs, cr, xs, xr, es, er):
+        self.g, self.o, self.ld, self.cb, self.hx, self.xb, self.ob = g, o, ld, cb, hx, xb, ob
+        self.ldsem, self.cs, self.cr, self.xs, self.xr, self.es, self.er = ldsem, cs, cr, xs, xr, es, er
+        self.s, self.f, _, _ = where_am_i()
+        self.fc, self.fx = flip(self.f, 1), flip(self.f, 2)
+        self.fd = flip(self.fc, 2)
+
+    def core(self, w, k):
+        i = peer(self.s, k)
+        src = self.g.at[i, self.fd if w == 0 else self.fc]
+        dst = self.cb.at[w, i]
+        return remote(src, dst, self.cs.at[w, k], self.cr.at[w, k], (self.s, self.fc))
+
+    def load(self, w, k):
+        i = peer(self.s, k)
+        src = self.g.at[i, self.fx if w == 0 else self.f]
+        return pltpu.make_async_copy(src, self.ld.at[w, i], self.ldsem.at[w, k])
+
+    def xsend(self, k):
+        i = peer(self.s, k)
+        return remote(self.hx.at[i], self.xb.at[i], self.xs.at[k], self.xr.at[k], (self.s, self.fx))
+
+    def esend(self, k):
+        t = peer(self.s, k)
+        dst = self.o.at[self.s]
+        return remote(self.ob.at[t], dst, self.es.at[k], self.er.at[k], (t, self.f))
+
+    def start(self):
+        for w in range(2):
+            for k in reversed(range(8)):
+                self.core(w, k).start()
+                self.load(w, k).start()
+
+    def step(self, k):
+        i = peer(self.s, k)
+        self.core(0, k).wait_recv()
+        self.load(0, k).wait()
+        adder(self.hx.at[i], [self.ld.at[0, i], self.cb.at[0, i]])
+        self.xsend(k).start()
+
+    def total(self, k):
+        i = peer(self.s, k)
+        self.core(1, k).wait_recv()
+        self.load(1, k).wait()
+        self.xsend(k).wait_recv()
+        dst = self.ob if k else self.o
+        adder(dst.at[i], [self.ld.at[1, i], self.cb.at[1, i], self.xb.at[i]])
+        if k:
+            self.esend(k).start()
+
+    def steps(self):
+        first = [functools.partial(self.step, k) for k in reversed(range(8))]
+        then = [functools.partial(self.total, k) for k in reversed(range(8))]
+        return first + then
+
+    def finish(self):
+        for k in range(8):
+            self.core(0, k).wait_send()
+            self.core(1, k).wait_send()
+            self.xsend(k).wait_send()
+            if k:
+                self.esend(k).wait_recv()
+                self.esend(k).wait_send()
+
+
+class FsdpGather:
+    @staticmethod
+    def scratch():
+        return [DMA, DMA((4,)), DMA((3,))]
+
+    def __init__(self, x, o, own, recv, send):
+        self.x, self.o, self.own, self.recv, self.send = x, o, own, recv, send
+        self.s, self.f, _, _ = where_am_i()
+        self.fc, self.fx = flip(self.f, 1), flip(self.f, 2)
+        self.fd = flip(self.fc, 2)
+        self.mine = pltpu.make_async_copy(x, o.at[self.f], own)
+
+    def pass_on(self, n, src, ff, to):
+        return remote(src, self.o.at[ff], self.send.at[n], self.recv.at[ff], (self.s, to))
+
+    def arrived(self, ff):
+        o = self.o.at[ff]
+        return remote(o, o, self.own, self.recv.at[ff], (self.s, self.fc))
+
+    def start(self):
+        self.pass_on(0, self.x, self.f, self.fx).start()
+        self.pass_on(1, self.x, self.f, self.fc).start()
+        self.mine.start()
+
+    def step(self):
+        self.arrived(self.fx).wait_recv()
+        self.pass_on(2, self.o.at[self.fx], self.fx, self.fc).start()
+
+    def finish(self):
+        self.mine.wait()
+        self.arrived(self.fc).wait_recv()
+        self.arrived(self.fd).wait_recv()
+        for n in range(3):
+            self.pass_on(n, self.x, self.f, self.fc).wait_send()
+
+
+class WholeGather:
+    @staticmethod
+    def scratch():
+        return [DMA, DMA((32,)), DMA((4,)), DMA((4,)), DMA((4,)), DMA((4, 2)), DMA((4, 2, 2))]
+
+    def __init__(self, x, o, own, recv, su, sd, sy, sx, sc):
+        self.x, self.o, self.own, self.recv = x, o, own, recv
+        self.su, self.sd, self.sy, self.sx, self.sc = su, sd, sy, sx, sc
+        self.s, self.f, self.z, self.y = where_am_i()
+        self.fc, self.fx = flip(self.f, 1), flip(self.f, 2)
+        self.fd = flip(self.fc, 2)
+        self.me = self.s * 4 + self.f
+        self.mine = pltpu.make_async_copy(x, o.at[self.me], own)
+
+    def at(self, zb, yy, ff):
+        return (2 * zb + (self.y if yy == 0 else 1 - self.y)) * 4 + ff
+
+    def src(self, b, first):
+        return self.x if first else self.o.at[b]
+
+    def up(self, zb, first=False):
+        b = self.at(zb, 0, self.f)
+        to = (self.s + 2, self.f)
+        return remote(self.src(b, first), self.o.at[b], self.su.at[zb], self.recv.at[b], to)
+
+    def down(self, zb, first=False):
+        b = self.at(zb, 0, self.f)
+        to = (self.s - 2, self.f)
+        return remote(self.src(b, first), self.o.at[b], self.sd.at[zb], self.recv.at[b], to)
+
+    def over_y(self, zb, first=False):
+        b = self.at(zb, 0, self.f)
+        to = (flip(self.s, 1), self.f)
+        return remote(self.src(b, first), self.o.at[b], self.sy.at[zb], self.recv.at[b], to)
+
+    def over_x(self, zb, yy, first=False):
+        b = self.at(zb, yy, self.f)
+        to = (self.s, self.fx)
+        return remote(self.src(b, first), self.o.at[b], self.sx.at[zb, yy], self.recv.at[b], to)
+
+    def over_core(self, zb, yy, xx, first=False):
+        b = self.at(zb, yy, self.f if xx == 0 else self.fx)
+        to = (self.s, self.fc)
+        return remote(self.src(b, first), self.o.at[b], self.sc.at[zb, yy, xx], self.recv.at[b], to)
+
+    def arrived(self, b):
+        o = self.o.at[b]
+        return remote(o, o, self.own, self.recv.at[b], (self.s, self.fc))
+
+    def start(self):
+        z = self.z
+
+        @pl.when(z < 3)
+        def _():
+            self.up(z, True).start()
+
+        @pl.when(z > 0)
+        def _():
+            self.down(z, True).start()
+
+        self.over_y(z, True).start()
+        self.over_x(z, 0, True).start()
+        self.over_core(z, 0, 0, True).start()
+        self.mine.start()
+
+    def line(self, sign, t):
+        zb = self.z + sign * t
+
+        @pl.when((zb >= 0) & (zb <= 3))
+        def _():
+            self.arrived(self.at(zb, 0, self.f)).wait_recv()
+            if sign < 0:
+
+                @pl.when(self.z < 3)
+                def _():
+                    self.up(zb).start()
+
+            else:
+
+                @pl.when(self.z > 0)
+                def _():
+                    self.down(zb).start()
+
+            self.over_y(zb).start()
+            self.over_x(zb, 0).start()
+            self.over_core(zb, 0, 0).start()
+
+    def column(self, sign, t):
+        zb = self.z + sign * t
+
+        @pl.when((zb >= 0) & (zb <= 3))
+        def _():
+            self.arrived(self.at(zb, 1, self.f)).wait_recv()
+            self.over_x(zb, 1).start()
+            self.over_core(zb, 1, 0).start()
+
+    def side(self, sign, t, yy):
+        zb = self.z + sign * t
+
+        @pl.when((zb >= 0) & (zb <= 3))
+        def _():
+            self.arrived(self.at(zb, yy, self.fx)).wait_recv()
+            self.over_core(zb, yy, 1).start()
+
+    def steps(self):
+        p = functools.partial
+        out = []
+        for t in range(4):
+            for sign in (-1, 1) if t else (1,):
+                if t:
+                    out.append(p(self.line, sign, t))
+        for t in range(4):
+            for sign in (-1, 1) if t else (1,):
+                out.append(p(self.column, sign, t))
+                out.append(p(self.side, sign, t, 0))
+        for t in range(4):
+            for sign in (-1, 1) if t else (1,):
+                out.append(p(self.side, sign, t, 1))
+        return out
+
+    def finish(self):
+        self.mine.wait()
+        for zb in range(4):
+            for yy in range(2):
+                self.arrived(self.at(zb, yy, self.fc)).wait_recv()
+                self.arrived(self.at(zb, yy, self.fd)).wait_recv()
+        for zb in range(4):
+            self.over_y(zb).wait_send()
+
+            @pl.when((self.z < 3) & (zb <= self.z))
+            def _():
+                self.up(zb).wait_send()
+
+            @pl.when((self.z > 0) & (zb >= self.z))
+            def _():
+                self.down(zb).wait_send()
+
+            for yy in range(2):
+                self.over_x(zb, yy).wait_send()
+                for xx in range(2):
+                    self.over_core(zb, yy, xx).wait_send()
+
+
+class RowExchange:
+    @staticmethod
+    def scratch():
+        return [DMA, DMA((8,)), DMA((8,))]
+
+    def __init__(self, x, o, own, send, recv):
+        self.x, self.o, self.send, self.recv = x, o, send, recv
+        self.s, self.f, _, _ = where_am_i()
+        self.mine = pltpu.make_async_copy(x.at[self.s], o.at[self.s], own)
+
+    def piece(self, k):
+        t = peer(self.s, k)
+        dst = self.o.at[self.s]
+        return remote(self.x.at[t], dst, self.send.at[k], self.recv.at[k], (t, self.f))
+
+    def start(self):
+        for k in reversed(range(1, 8)):
+            self.piece(k).start()
+        self.mine.start()
+
+    def finish(self):
+        self.mine.wait()
+        for k in reversed(range(1, 8)):
+            self.piece(k).wait_recv()
+            self.piece(k).wait_send()
+
+
+def merged(*lists):
+    keyed = []
+    for n, items in enumerate(lists):
+        keyed += [((i + 0.5) / len(items), n, item) for i, item in enumerate(items)]
+    return [item for _, _, item in sorted(keyed, key=lambda v: v[:2])]
+
+
+def entry_kernel(
+    x_ref, p_ref, w_ref, ow_ref, a_ref, wo_ref, g_ref, oo_ref, xs, got, psend, precv, *sems
+):
+    s, f, z, y = where_am_i()
+    me = s * 4 + f
+    greet_all(s, f)
+    gather = SeqGather(x_ref, xs, *sems[:5])
+    slices = ColGather(w_ref, wo_ref, *sems[5:10])
+    whole = WholeGather(ow_ref, oo_ref, *sems[10:])
+
+    def param(k):
+        i = (me + k) % 32
+        return remote(p_ref, got.at[me], psend.at[k], precv.at[k], dealer(i))
+
+    @pl.loop(1, 32)
+    def _(k):
+        param(k).start()
+
+    gather.start()
+    slices.start()
+    whole.start()
+    got[me] = p_ref[...]
+
+    @pl.loop(1, 32)
+    def _(k):
+        param(k).wait_recv()
+
+    for i in range(16):
+        g_ref[:, i * 128 : i * 128 + 128] = got[2 * i] + got[2 * i + 1]
+    step = 16
+
+    def norm(b):
+        gain, shift = g_ref[0:1], g_ref[1:2]
+
+        @pl.loop(0, x_ref.shape[0] // step)
+        def _(i):
+            r = pl.ds(pl.multiple_of(i * step, step), step)
+            normed, _ = normalize(xs[b, r].astype(jnp.float32))
+            a_ref[b, r] = (normed * gain + shift).astype(jnp.bfloat16)
+
+    gather.own.wait()
+    norm(s)
+    todo = slices.steps()
+    lines = whole.steps()
+    for t in (1, 2, 3):
+        gather.below(t)
+        gather.above(t)
+        for item in todo[:3] + lines[:2]:
+            item()
+        todo, lines = todo[3:], lines[2:]
+        gather.across(t - 1, norm)
+        for zb in (z - t, z + t):
+
+            @pl.when((zb >= 0) & (zb <= 3))
+            def _():
+                norm(2 * zb + y)
+
+    for item in todo[:2]:
+        item()
+    gather.across(3, norm)
+    for item in merged(todo[2:], lines):
+        item()
+    slices.finish()
+    whole.finish()
+
+    @pl.loop(1, 32)
+    def _(k):
+        param(k).wait_send()
+
+    for zb in range(4):
+        gather.ysend(zb, x_ref).wait_send()
+
+        @pl.when((z < 3) & (zb <= z))
+        def _():
+            gather.usend(zb, x_ref).wait_send()
+
+        @pl.when((z > 0) & (zb >= z))
+        def _():
+            gather.dsend(zb, x_ref).wait_send()
+
+
+def entry(x, params, weight, rows_weight, collective):
+    rows, width = x.shape
+    return pl.pallas_call(
+        entry_kernel,
+        out_shape=(
+            jax.ShapeDtypeStruct((8, rows, width), jnp.bfloat16),
+            jax.ShapeDtypeStruct((8, 4) + weight.shape[1:], weight.dtype),
+            jax.ShapeDtypeStruct((8, width), jnp.float32),
+            jax.ShapeDtypeStruct((32,) + rows_weight.shape, rows_weight.dtype),
+        ),
+        in_specs=[VMEM_SPEC] * 4,
+        out_specs=(VMEM_SPEC, ANY_SPEC, VMEM_SPEC, ANY_SPEC),
+        scratch_shapes=[
+            pltpu.VMEM((8, rows, width), x.dtype),
+            pltpu.VMEM((32, 8, 128), jnp.float32),
+            DMA((32,)),
+            DMA((32,)),
+        ]
+        + SeqGather.scratch()
+        + ColGather.scratch()
+        + WholeGather.scratch(),
+        compiler_params=comm_params(collective),
+    )(x, params, weight, rows_weight)
+
+
+def gather_kernel(x_ref, o_ref, *sems):
+    s, f, z, y = where_am_i()
+    greet_line(s, f, z, y)
+    task = SeqGather(x_ref, o_ref, *sems)
+    task.start()
+    for item in task.steps():
+        item()
+    for t in range(4):
+        task.across(t)
+    task.finish()
+
+
+def gather_rows_line(x, collective):
+    return pl.pallas_call(
+        gather_kernel,
+        out_shape=jax.ShapeDtypeStruct((8,) + x.shape, x.dtype),
+        in_specs=[VMEM_SPEC],
+        out_specs=ANY_SPEC,
+        scratch_shapes=SeqGather.scratch(),
+        compiler_params=comm_params(collective),
+    )(x)
+
+
+def reduce_kernel(p_ref, o_ref, *scratch):
+    s, f, z, y = where_am_i()
+    greet_line(s, f, z, y)
+    task = SeqReduce(p_ref, o_ref, *scratch)
+    task.start()
+    for item in task.steps():
+        item()
+    task.finish()
+
+
+def reduce_rows_line(p, collective):
+    _, rows, width = p.shape
+    return pl.pallas_call(
+        reduce_kernel,
+        out_shape=jax.ShapeDtypeStruct((rows, width), jnp.float32),
+        in_specs=[ANY_SPEC],
+        out_specs=VMEM_SPEC,
+        scratch_shapes=SeqReduce.scratch(rows, width),
+        compiler_params=comm_params(collective),
+    )(p)
+
+
+def dot(a, b, ca=1, cb=0):
+    return lax.dot_general(a, b, (((ca,), (cb,)), ((), ())), preferred_element_type=jnp.float32)
+
+
+def starts_of(pos, lengths_ref, nseg):
+    start = jnp.zeros_like(pos)
+    end = 0
+    for i in range(nseg - 1):
+        end = end + lengths_ref[0, i]
+        start = jnp.where(pos >= end, end, start)
+    return start
+
+
+def head_lanes(h):
+    lane = lax.broadcasted_iota(jnp.int32, (1, 128), 1)
+    return (lane // HEAD_DIM) == h
+
+
+def turn(x, c, s1, s2, sign):
+    half = ROT // 2
+    return x * c + (pltpu.roll(x, 128 - half, 1) * s1 + pltpu.roll(x, half, 1) * s2) * sign
+
+
+def block_mask(qb, lengths_ref):
+    keys = (qb + 1) * QB
+    row = qb * QB + lax.broadcasted_iota(jnp.int32, (QB, 1), 0)
+    col = lax.broadcasted_iota(jnp.int32, (1, keys), 1)
+    return (col >= starts_of(row, lengths_ref, lengths_ref.shape[1])) & (col <= row)
+
+
+def row_at(i, step=QB):
+    return pl.ds(pl.multiple_of(i * step, step), step)
+
+
+def picks(orow_ref, i):
+    p = lax.broadcasted_iota(jnp.int32, (QB, 1), 0) + i * QB == orow_ref[...]
+    return jnp.where(p, 1.0, 0.0).astype(jnp.bfloat16)
+
+
+def puts(oc, valid):
+    p = oc == lax.broadcasted_iota(jnp.int32, (1, valid), 1)
+    return jnp.where(p, 1.0, 0.0).astype(jnp.bfloat16)
+
+
+def attend(
+    a_ref, w_ref, shift_ref, tables, orow_ref, ocol_ref, len_ref, o_ref, pk_ref, lse_ref, rot, opk
+):
+    rows, w3 = rot.shape
+    w = w3 // 3
+    valid = pk_ref.shape[0]
+    scale = HEAD_DIM**-0.5
+    c_ref, s1_ref, s2_ref = tables
+
+    def project():
+        @pl.loop(0, rows // 256)
+        def _(i):
+            r = row_at(i, 256)
+            c, s1, s2 = c_ref[r], s1_ref[r], s2_ref[r]
+            qkv = dot(a_ref[r], w_ref[...]) + shift_ref[...]
+            for t in range(w3 // 128):
+                cols = slice(t * 128, t * 128 + 128)
+                x = qkv[:, cols]
+                if t < 2 * w // 128:
+                    x = turn(x, c, s1, s2, 1.0)
+                rot[r, cols] = x.astype(jnp.bfloat16)
+
+    def pack():
+        @pl.loop(0, valid // QB)
+        def _(i):
+            pk_ref[row_at(i)] = dot(picks(orow_ref, i), rot[...]).astype(jnp.bfloat16)
+
+    def block(qb, t):
+        keys = (qb + 1) * QB
+        rq = slice(qb * QB, qb * QB + QB)
+        ct = slice(t * 128, t * 128 + 128)
+        mask = block_mask(qb, len_ref)
+        q = pk_ref[rq, ct]
+        k = pk_ref[0:keys, w + t * 128 : w + t * 128 + 128]
+        v = pk_ref[0:keys, 2 * w + t * 128 : 2 * w + t * 128 + 128]
+        total = None
+        for h in range(2):
+            qh = jnp.where(head_lanes(h), q, jnp.zeros_like(q))
+            scores = jnp.where(mask, dot(qh, k, 1, 1) * scale, NEG)
+            top = jnp.max(scores, -1, keepdims=True)
+            expo = jnp.exp(scores - top)
+            norm = jnp.sum(expo, -1, keepdims=True)
+            probs = (expo / norm).astype(jnp.bfloat16)
+            lse_ref[2 * t + h, rq] = top + jnp.log(norm)
+            out = dot(probs, v)
+            total = out if h == 0 else jnp.where(head_lanes(1), out, total)
+        opk[rq, ct] = total.astype(jnp.bfloat16)
+
+    def unpack():
+        per = o_ref.shape[1]
+
+        @pl.loop(0, rows // per)
+        def _(i):
+            r = row_at(i, per)
+            oc = ocol_ref[r]
+            back = dot(puts(oc, valid), opk[...])
+            pad = rot[r, 2 * w :].astype(jnp.float32)
+            o_ref[i] = jnp.where(oc >= valid, pad, back).astype(jnp.bfloat16)
+
+    blocks = [
+        functools.partial(block, qb, t) for qb in range(valid // QB) for t in range(w // 128)
+    ]
+    return [project, pack] + blocks + [unpack]
+
+
+def attend_back(
+    pk_ref, do_ref, lse_ref, tables, orow_ref, ocol_ref, len_ref, g_ref, b_ref, dpk, dq, dk, dv, gpk
+):
+    rows, w = do_ref.shape
+    valid = pk_ref.shape[0]
+    scale = HEAD_DIM**-0.5
+    c_ref, s1_ref, s2_ref = tables
+
+    def pack():
+        @pl.loop(0, valid // QB)
+        def _(i):
+            r = row_at(i)
+            dpk[r] = dot(picks(orow_ref, i), do_ref[...]).astype(jnp.bfloat16)
+            dk[r] = jnp.zeros((QB, w), jnp.float32)
+            dv[r] = jnp.zeros((QB, w), jnp.float32)
+
+    def block(qb, t):
+        keys = (qb + 1) * QB
+        rq = slice(qb * QB, qb * QB + QB)
+        ct = slice(t * 128, t * 128 + 128)
+        mask = block_mask(qb, len_ref)
+        q, d = pk_ref[rq, ct], dpk[rq, ct]
+        k = pk_ref[0:keys, w + t * 128 : w + t * 128 + 128]
+        v = pk_ref[0:keys, 2 * w + t * 128 : 2 * w + t * 128 + 128]
+        total = None
+        for h in range(2):
+            hl = head_lanes(h)
+            qh = jnp.where(hl, q, jnp.zeros_like(q))
+            dh = jnp.where(hl, d, jnp.zeros_like(d))
+            scores = jnp.where(mask, dot(qh, k, 1, 1) * scale, NEG)
+            p = jnp.exp(scores - lse_ref[2 * t + h, rq])
+            dp = dot(dh, v, 1, 1)
+            inner = jnp.sum(p * dp, -1, keepdims=True)
+            ds = (p * (dp - inner)).astype(jnp.bfloat16)
+            dv[0:keys, ct] += dot(p.astype(jnp.bfloat16), dh, 0, 0)
+            dk[0:keys, ct] += dot(ds, qh, 0, 0)
+            part = dot(ds, k)
+            total = part if h == 0 else jnp.where(head_lanes(1), part, total)
+        dq[rq, ct] = total
+
+    def rotary():
+        @pl.loop(0, valid // QB)
+        def _(i):
+            r = row_at(i)
+            c, s1, s2 = c_ref[r], s1_ref[r], s2_ref[r]
+            for t in range(w // 128):
+                ct = slice(t * 128, t * 128 + 128)
+                for j, src in ((0, dq), (1, dk)):
+                    x = (src[r, ct] * scale).astype(jnp.bfloat16).astype(jnp.float32)
+                    at = j * w + t * 128
+                    gpk[r, at : at + 128] = turn(x, c, s1, s2, -1.0).astype(jnp.bfloat16)
+                at = 2 * w + t * 128
+                gpk[r, at : at + 128] = dv[r, ct].astype(jnp.bfloat16)
+
+    def unpack():
+        b_ref[...] = jnp.zeros_like(b_ref)
+
+        @pl.loop(0, rows // QB)
+        def _(i):
+            r = row_at(i)
+            oc = ocol_ref[r]
+            back = dot(puts(oc, valid), gpk[...])
+            pad = jnp.where(oc >= valid, do_ref[r].astype(jnp.float32), 0.0)
+            back = jnp.concatenate([back[:, : 2 * w], back[:, 2 * w :] + pad], 1)
+            g_ref[r] = back.astype(jnp.bfloat16)
+            b_ref[...] += jnp.sum(back, 0, keepdims=True)
+
+    blocks = [
+        functools.partial(block, qb, t) for qb in range(valid // QB) for t in range(w // 128)
+    ]
+    return [pack] + blocks + [rotary, unpack]
+
+
+def forward_kernel(
+    a_ref,
+    qw_ref,
+    shift_ref,
+    c_ref,
+    s1_ref,
+    s2_ref,
+    orow_ref,
+    ocol_ref,
+    len_ref,
+    dm_ref,
+    w_ref,
+    dw_ref,
+    ho_ref,
+    pk_ref,
+    lse_ref,
+    dmo_ref,
+    wo_ref,
+    dwo_ref,
+    mix_ref,
+    rot,
+    opk,
+    *sems,
+):
+    s, f, z, y = where_am_i()
+    greet_columns(s, f)
+    gather = SeqGather(dm_ref, dmo_ref, *sems[:5])
+    slices = ColGather(w_ref, wo_ref, *sems[5:10])
+    side = FsdpGather(dw_ref, dwo_ref, *sems[10:13])
+    swap = RowExchange(mix_ref, ho_ref, *sems[13:])
+    work = attend(
+        a_ref,
+        qw_ref,
+        shift_ref,
+        (c_ref, s1_ref, s2_ref),
+        orow_ref,
+        ocol_ref,
+        len_ref,
+        mix_ref,
+        pk_ref,
+        lse_ref,
+        rot,
+        opk,
+    )
+    gather.start()
+    slices.start()
+    side.start()
+    for item in work[:-6]:
+        item()
+    gather.below(1)
+    gather.above(1)
+    todo = slices.steps()
+    for item in merged(work[-6:], todo[:3]):
+        item()
+    swap.start()
+    todo = todo[3:] + [side.step]
+    for t in (2, 3):
+        gather.below(t)
+        gather.above(t)
+        for item in todo[:4]:
+            item()
+        todo = todo[4:]
+    for item in todo:
+        item()
+    for t in range(4):
+        gather.across(t)
+    swap.finish()
+    slices.finish()
+    side.finish()
+    gather.finish()
+
+
+def attention_forward(
+    a, w_qkv, shift, tables, orow, ocol, lengths, valid, dm, weight, rows_weight, collective
+):
+    rows, w3 = a.shape[0], w_qkv.shape[1]
+    w = w3 // 3
+    heads = w // HEAD_DIM
+    mixed = jax.ShapeDtypeStruct((8, rows // 8, w), jnp.bfloat16)
+    return pl.pallas_call(
+        forward_kernel,
+        out_shape=(
+            mixed,
+            jax.ShapeDtypeStruct((valid, w3), jnp.bfloat16),
+            jax.ShapeDtypeStruct((heads, valid, 1), jnp.float32),
+            jax.ShapeDtypeStruct((8,) + dm.shape, dm.dtype),
+            jax.ShapeDtypeStruct((8, 4) + weight.shape[1:], weight.dtype),
+            jax.ShapeDtypeStruct((4,) + rows_weight.shape, rows_weight.dtype),
+            mixed,
+        ),
+        in_specs=[VMEM_SPEC] * 8 + [SMEM_SPEC] + [VMEM_SPEC] * 3,
+        out_specs=(VMEM_SPEC,) * 3 + (ANY_SPEC,) * 3 + (VMEM_SPEC,),
+        scratch_shapes=[
+            pltpu.VMEM((rows, w3), jnp.bfloat16),
+            pltpu.VMEM((valid, w), jnp.bfloat16),
+        ]
+        + SeqGather.scratch()
+        + ColGather.scratch()
+        + FsdpGather.scratch()
+        + RowExchange.scratch(),
+        compiler_params=comm_params(collective),
+    )(a, w_qkv, shift, *tables, orow, ocol, lengths, dm, weight, rows_weight)
+
+
+def backward_kernel(
+    pk_ref,
+    do_ref,
+    lse_ref,
+    c_ref,
+    s1_ref,
+    s2_ref,
+    orow_ref,
+    ocol_ref,
+    len_ref,
+    p_ref,
+    wg_ref,
+    g_ref,
+    b_ref,
+    o_ref,
+    wo_ref,
+    dpk,
+    dq,
+    dk,
+    dv,
+    gpk,
+    *scratch,
+):
+    s, f, z, y = where_am_i()
+    greet_columns(s, f)
+    reduce = SeqReduce(p_ref, o_ref, *scratch[:13])
+    slices = ColReduce(wg_ref, wo_ref, *scratch[13:])
+    work = attend_back(
+        pk_ref,
+        do_ref,
+        lse_ref,
+        (c_ref, s1_ref, s2_ref),
+        orow_ref,
+        ocol_ref,
+        len_ref,
+        g_ref,
+        b_ref,
+        dpk,
+        dq,
+        dk,
+        dv,
+        gpk,
+    )
+    reduce.start()
+    slices.start()
+    for item in merged(work, slices.steps()[:8]):
+        item()
+    for item in merged(reduce.steps(), slices.steps()[8:]):
+        item()
+    reduce.finish()
+    slices.finish()
+
+
+def attention_backward(pk, do, lse, tables, orow, ocol, lengths, partial, wide_grad, collective):
+    rows, w = do.shape
+    valid = pk.shape[0]
+    width = partial.shape[2]
+
+    def acc(c):
+        return pltpu.VMEM((valid, c), jnp.float32)
+
+    return pl.pallas_call(
+        backward_kernel,
+        out_shape=(
+            jax.ShapeDtypeStruct((rows, 3 * w), jnp.bfloat16),
+            jax.ShapeDtypeStruct((1, 3 * w), jnp.float32),
+            jax.ShapeDtypeStruct((rows // 8, width), jnp.float32),
+            jax.ShapeDtypeStruct((8,) + wide_grad.shape[2:], jnp.bfloat16),
+        ),
+        in_specs=[VMEM_SPEC] * 8 + [SMEM_SPEC] + [ANY_SPEC] * 2,
+        out_specs=(VMEM_SPEC,) * 4,
+        scratch_shapes=[
+            pltpu.VMEM((valid, w), jnp.bfloat16),
+            acc(w),
+            acc(w),
+            acc(w),
+            pltpu.VMEM((valid, 3 * w), jnp.bfloat16),
+        ]
+        + SeqReduce.scratch(rows // 8, width)
+        + ColReduce.scratch(*wide_grad.shape[2:]),
+        compiler_params=comm_params(collective, 56),
+    )(pk, do, lse, *tables, orow, ocol, lengths, partial, wide_grad)
+
+
+def last_kernel(p_ref, wg_ref, o_ref, wo_ref, *scratch):
+    s, f, z, y = where_am_i()
+    greet_columns(s, f)
+    reduce = SeqReduce(p_ref, o_ref, *scratch[:13])
+    slices = ColReduce(wg_ref, wo_ref, *scratch[13:])
+    reduce.start()
+    slices.start()
+    for item in slices.steps()[:8]:
+        item()
+    for item in merged(reduce.steps(), slices.steps()[8:]):
+        item()
+    reduce.finish()
+    slices.finish()
+
+
+def last_reduce(partial, grad, collective):
+    _, rows, width = partial.shape
+    return pl.pallas_call(
+        last_kernel,
+        out_shape=(
+            jax.ShapeDtypeStruct((rows, width), jnp.float32),
+            jax.ShapeDtypeStruct((8,) + grad.shape[2:], jnp.bfloat16),
+        ),
+        in_specs=[ANY_SPEC] * 2,
+        out_specs=(VMEM_SPEC,) * 2,
+        scratch_shapes=SeqReduce.scratch(rows, width) + ColReduce.scratch(*grad.shape[2:]),
+        compiler_params=comm_params(collective),
+    )(partial, grad)
+
+
+def sum_kernel(x_ref, o_ref, got, send, recv):
+    s, f, z, y = where_am_i()
+    me = s * 4 + f
+    greet_all(s, f)
+
+    def piece(k):
+        i = (me + k) % 32
+        return remote(x_ref.at[i], got.at[k], send.at[k], recv.at[k], dealer(i))
+
+    @pl.loop(1, 32)
+    def _(k):
+        piece(k).start()
+
+    @pl.loop(1, 32)
+    def _(k):
+        piece(k).wait_recv()
+        piece(k).wait_send()
+
+    o_ref[...] = x_ref[me]
+
+    @pl.loop(1, 32)
+    def _(k):
+        o_ref[...] += got[k]
+
+
+def sum_parts(x, collective):
+    return pl.pallas_call(
+        sum_kernel,
+        out_shape=jax.ShapeDtypeStruct(x.shape[1:], x.dtype),
+        in_specs=[VMEM_SPEC],
+        out_specs=VMEM_SPEC,
+        scratch_shapes=[pltpu.VMEM(x.shape, x.dtype), DMA((32,)), DMA((32,))],
+        compiler_params=comm_params(collective),
+    )(x)
+
+
+def rotary_tables(rel):
+    half = ROT // 2
+    d = jnp.arange(128, dtype=jnp.int32) % HEAD_DIM
+    freq = 10000.0 ** (-2.0 * (d % half).astype(jnp.float32) / ROT)
+    angle = rel[:, None] * freq[None, :]
+    c, s = jnp.cos(angle), jnp.sin(angle)
+    second = (d >= half) & (d < ROT)
+    return (jnp.where(d < ROT, c, 1.0), jnp.where(d < half, -s, 0.0), jnp.where(second, s, 0.0))
+
+
+def line_body(
+    hidden_in,
+    ln1_gain,
+    ln1_bias,
+    qkv_weight,
+    qkv_bias,
+    out_weight,
+    ln2_gain,
+    ln2_bias,
+    gate_weight,
+    up_weight,
+    down_weight,
+    seq_lengths,
+    deal_order,
+    out_grad,
+):
+    rows = hidden_in.shape[1]
+    width = hidden_in.shape[2]
+    nseq = lax.axis_size("seq")
+    nfsdp = lax.axis_size("fsdp")
+    lw = width // nseq
+    part = qkv_weight.shape[0]
+    ff = gate_weight.shape[1]
+    lf = ff // nseq
+    seq_at, fsdp_at = lax.axis_index("seq"), lax.axis_index("fsdp")
+    stream = hidden_in[0].astype(jnp.float32)
+    cotangent = out_grad[0].astype(jnp.float32)
+    order = deal_order[0]
+    lengths = seq_lengths[0]
+    group_rows = order.shape[0]
+    valid_rows = group_rows * 5 // 8
+    orow, ocol = order[None, :], order[:, None]
+    local_pos = lax.dynamic_slice_in_dim(order, seq_at * rows, rows)
+    valid = (local_pos < valid_rows).astype(jnp.float32)[:, None]
+    dealt_seg, dealt_start = segment_of(order, lengths)
+    dealt_tables = rotary_tables((order - dealt_start).astype(jnp.float32))
+    packed_pos = jnp.arange(valid_rows, dtype=jnp.int32)
+    packed_seg, packed_start = segment_of(packed_pos, lengths)
+    packed_tables = rotary_tables((packed_pos - packed_start).astype(jnp.float32))
+
+    def column_parts(weights):
+        views = [w.reshape(part, nseq, -1) for w in weights]
+        return jnp.concatenate(views, 2).transpose(1, 0, 2)
+
+    params = jnp.stack([ln1_gain, ln1_bias, ln2_gain, ln2_bias, *qkv_bias])
+    params = jnp.pad(params.astype(jnp.float32), ((0, 1), (0, 64)))
+    params = jnp.where(fsdp_at % 2 == 0, params, jnp.roll(params, part, 1))
+    qkv_parts = qkv_weight.reshape(part, 3, nseq, lw).transpose(2, 0, 1, 3).reshape(nseq, part, -1)
+    first_in, qkv_w, norms, out_w = entry(hidden_in[0], params, qkv_parts, out_weight, 1)
+    first_in = first_in.reshape(group_rows, width)
+    qkv_w = qkv_w.reshape(width, 3 * lw)
+    gain1, shift1, gain2, shift2 = norms[:4]
+    qkv_shift = lax.dynamic_slice_in_dim(norms[4:7], seq_at * lw, lw, 1).reshape(1, -1)
+    normed1, rstd1 = normalize(stream)
+    heads_out, packed, lse, mlp_grad, wide_w, down_w, mixed = attention_forward(
+        first_in,
+        qkv_w,
+        qkv_shift,
+        dealt_tables,
+        orow,
+        ocol,
+        seq_lengths,
+        valid_rows,
+        out_grad[0],
+        column_parts([gate_weight, up_weight]),
+        down_weight,
+        2,
+    )
+    mixed = mixed.reshape(group_rows, lw)
+    heads_out = heads_out.transpose(1, 0, 2).reshape(rows, width)
+    wide_w = wide_w.reshape(width, 2 * lf)
+    mlp_grad = mlp_grad.reshape(group_rows, width)
+    out_rows = lax.dynamic_slice_in_dim(out_w, seq_at * nfsdp, nfsdp).reshape(lw, width)
+    out_w = out_w.reshape(width, width)
+    down_w = down_w.reshape(lf, width)
+    attn = times(heads_out, out_w)
+    resid = stream + attn
+    normed2, rstd2 = normalize(resid)
+    second_local = (normed2 * gain2 + shift2).astype(jnp.bfloat16)
+    second_in = gather_rows_line(second_local, 3).reshape(group_rows, width)
+    wide = times(second_in, wide_w)
+    gate, upper = wide[:, :lf], wide[:, lf:]
+    hidden, sigma = mlp_forward(gate, upper)
+    hidden_grad = times_transposed(mlp_grad, down_w)
+    wide_act = jnp.concatenate(mlp_backward(hidden_grad, gate, upper, sigma), 1)
+    second_part = times_transposed(wide_act, wide_w).astype(jnp.bfloat16)
+    second_grad = reduce_rows_line(second_part.reshape(nseq, rows, width), 4)
+    resid_part, gain2_grad, shift2_grad = norm_back(second_grad, normed2, rstd2, gain2)
+    resid_grad = cotangent + resid_part
+    attn_grad = gather_rows_line(resid_grad.astype(jnp.bfloat16), 5).reshape(group_rows, width)
+    mixed_grad = times_transposed(attn_grad, out_rows).astype(jnp.bfloat16)
+
+    def row_shard(left, right):
+        grad = outer(left, right).astype(jnp.bfloat16)
+        return lax.psum_scatter(grad, "fsdp", scatter_dimension=0, tiled=True).astype(jnp.float32)
+
+    def column_parts_grad(left, right):
+        return outer(left, right).astype(jnp.bfloat16).reshape(nseq, nfsdp, part, -1)
+
+    down_grad = row_shard(hidden, mlp_grad)
+    mlp_part = times(hidden, down_w).astype(jnp.bfloat16).reshape(nseq, rows, width)
+    qkv_act, bias_sums, mlp, wide_grad = attention_backward(
+        packed,
+        mixed_grad,
+        lse,
+        packed_tables,
+        orow,
+        ocol,
+        seq_lengths,
+        mlp_part,
+        column_parts_grad(second_in, wide_act),
+        6,
+    )
+    result = resid + mlp
+    out_grad_w = row_shard(mixed, attn_grad)
+    first_part = times_transposed(qkv_act, qkv_w).astype(jnp.bfloat16)
+    first_grad, qkv_grad = last_reduce(
+        first_part.reshape(nseq, rows, width), column_parts_grad(first_in, qkv_act), 7
+    )
+    input_part, gain1_grad, shift1_grad = norm_back(first_grad, normed1, rstd1, gain1)
+    input_grad = resid_grad + input_part
+    wide_grad = wide_grad.astype(jnp.float32)
+    gate_grad = wide_grad[:, :, :lf].transpose(1, 0, 2).reshape(part, ff)
+    up_grad = wide_grad[:, :, lf:].transpose(1, 0, 2).reshape(part, ff)
+    qkv_grad = qkv_grad.astype(jnp.float32).reshape(nseq, part, 3, lw)
+    qkv_grad = qkv_grad.transpose(1, 2, 0, 3).reshape(part, 3 * width)
+
+    vectors = jnp.stack([gain1_grad, shift1_grad, gain2_grad, shift2_grad])
+    vectors = vectors.reshape(4, nseq * nfsdp, part).transpose(1, 0, 2).reshape(-1, 2, 128)
+    sums = jnp.stack(
+        [
+            jnp.sum(valid * result * result),
+            jnp.sum(valid * attn * attn),
+            jnp.sum(valid * mlp * mlp),
+        ]
+    )
+    sums = jnp.broadcast_to(jnp.pad(sums, (0, 125)), (nseq * nfsdp, 1, 128))
+    bias = bias_sums.reshape(3, nfsdp, part).transpose(1, 0, 2).reshape(nfsdp, 3 * part)
+    bias = jnp.pad(bias, ((0, 0), (0, 64))).reshape(1, nfsdp, 2, 128)
+    here = (jnp.arange(nseq) == seq_at)[:, None, None, None]
+    bias = jnp.where(here, bias, 0.0).reshape(-1, 2, 128)
+    message = jnp.concatenate([vectors, sums, bias, jnp.zeros_like(vectors), sums], 1)
+    total = sum_parts(message, 8)
+    count = valid_rows * nfsdp * width
+    rms = jnp.sqrt(total[2, :3] / count)
+    shards = total[:2].reshape(4, part)
+    qkv_bias_grad = total[3:5].reshape(4, part)[:3]
+    return (
+        result.astype(jnp.bfloat16)[None],
+        input_grad[None],
+        shards[0],
+        shards[1],
+        qkv_grad,
+        qkv_bias_grad,
+        out_grad_w,
+        shards[2],
+        shards[3],
+        gate_grad,
+        up_grad,
+        down_grad,
+        rms,
+    )
+
+
 def solution(mesh):
     in_specs = (
         P("fsdp", "seq", None),
@@ -367,4 +1803,11 @@
         P(("seq", "fsdp"), None),
         P(),
     )
-    return jax.shard_map(body, mesh=mesh, in_specs=in_specs, out_specs=out_specs, check_vma=False)
+    line = dict(mesh.shape) == {"seq": 8, "fsdp": 4}
+    return jax.shard_map(
+        line_body if line else body,
+        mesh=mesh,
+        in_specs=in_specs,
+        out_specs=out_specs,
+        check_vma=False,
+    )

time: 1180 us -> 653 us (0.55)
  waiting for transfers between devices: 645 us -> 0.04 us
  Pallas kernels: 0 us -> 501 us
  blocking collectives: 207 us -> 0 us
  local copies, waits for them, and re-layouts: 119 us -> 38.7 us
  matrix products: 123 us -> 68.8 us
  other arithmetic: 43.5 us -> 26.3 us
  starting transfers between devices: 14.3 us -> 0.08 us
    pallas_call x0 -> x8, Pallas kernels: none -> 501 us  [the longest x1 113 us: entry(): pl.pallas_call(entry_kernel, out_shape=(jax.ShapeDtypeStruct((8, rows, wi...]
    reduce_scatter x6 -> x2, waiting for transfers between devices: 287 us -> 0.01 us  [row_shard(): lax.psum_scatter(grad, 'fsdp', scatter_dimension=0, tiled=True)]
    all_gather x10 -> x0, waiting for transfers between devices: 271 us -> none  [the longest x4 213 us: gather_rows(): return lax.all_gather(values, 'seq', axis=0, tiled=True)]
    all_to_all x4 -> x0, blocking collectives: 120 us -> none  [the longest x2 67.6 us: column_slice(): lax.all_to_all(view.reshape(nseq * part, blocks * cols), 'seq', split_axi...]
    all_to_all x3 -> x0, waiting for transfers between devices: 53.8 us -> none  [the longest x1 35.7 us: column_slice(): lax.all_to_all(view.reshape(nseq * part, blocks * cols), 'seq', split_axi...]
    psum x1 -> x0, blocking collectives: 41.3 us -> none  [body(): lax.psum((gain1_grad, shift1_grad, gain2_grad, shift2_grad, jnp.sum(valid...]
    all_gather x1 -> x0, blocking collectives: 40.1 us -> none  [body(): lax.all_gather(jnp.stack([ln1_gain, ln1_bias, ln2_gain, ln2_bias, *qkv_bi...]
    gather x14 -> x0, local copies, waits for them, and re-layouts: 38.6 us -> none  [the longest x8 22 us: to_pack(): return values[inverse].reshape(group_rows, heads_here, HEAD_DIM)]
  transfers between devices with their start and end apart: 20 -> 2, of which waited for: 16 -> 0; matrix products, arithmetic and copies ran while one was open for 22% -> 12% of each run, Pallas kernels for 0% -> 24%
where the time goes in v3:
time: 653 us; the launch traced here: 649 us
  Pallas kernels  501 us (77%)
  matrix products  68.8 us (11%)
  local copies, waits for them, and re-layouts  38.7 us (6%)
  other arithmetic  26.3 us (4%)
  between operations  14.8 us (2%)
    pallas_call x1, Pallas kernels, entry(): pl.pallas_call(entry_kernel, out_shape=(jax.ShapeDtypeStruct((8, rows, wi...  113 us
    pallas_call x1, Pallas kernels, attention_forward(): pl.pallas_call(forward_kernel, out_shape=(mixed, jax.ShapeDtypeStruct((va...  98.5 us
    pallas_call x2, Pallas kernels, gather_rows_line(): pl.pallas_call(gather_kernel, out_shape=jax.ShapeDtypeStruct((8,) + x.sha...  90.7 us
    pallas_call x1, Pallas kernels, attention_backward(): pl.pallas_call(backward_kernel, out_shape=(jax.ShapeDtypeStruct((rows, 3...  81.9 us
    pallas_call x1, Pallas kernels, last_reduce(): pl.pallas_call(last_kernel, out_shape=(jax.ShapeDtypeStruct((rows, width)...  61.9 us
    pallas_call x1, Pallas kernels, reduce_rows_line(): pl.pallas_call(reduce_kernel, out_shape=jax.ShapeDtypeStruct((rows, width...  46.2 us
    dot_general x4, matrix products, times_transposed(): lax.dot_general(left, right, (((1,), (1,)), ((), ())), preferred_element_...  26.4 us
    dot_general x4, matrix products, outer(): lax.dot_general(left, right, (((0,), (0,)), ((), ())), preferred_element_...  21.9 us
  transfers between devices with their start and end apart: 2, of which 0 were waited for; matrix products, arithmetic and copies ran while one was open for 12% of the time, Pallas kernels for 24%

profile of v3, /device:TPU:0, one launch (start us, length us, event | category | flops | bytes accessed | tf_op | source)
XLA Modules:
  0.0 649.5 jit_solution(10619355836079148872)
XLA Ops:
  7.3 1.3 convert_reduce_fusion
  8.6 0.8 stack.47
  9.4 1.3 copy.72
  10.7 0.4 copy.77
  11.1 0.9 reshape.253.w_ref
  12.1 112.6 %shard_map.237 = (bf16[8,128,2048]{2,1,0:T(8,128)(2,1)}, bf16[8,4,64,768]{3,2,1,0:T(8,128)(2,1)S(1)}, f32[8,2048]{1,0:T(8,128)S(1)}, bf16[32,64,2048]{2,1,0:T(8,128)(2,1)}) custom-call(bf16[128,2048]{1,0:T(8,128)(2,1)S(1)} %bitcast.113, f32[8,128]{1,0:T(8,128)S(1)} %pad_select_fusion.p_ref, bf16[8,64,768]{2,1,0:T(8,128)(2,1)S(1)} %reshape.253.w_ref, ...), custom_call_target="tpu_custom_call" | custom-call | tf_op jit(solution)/shard_map/pallas_call | solution.py:1096
  124.7 1.7 copy-done.5
  126.9 0.2 copy.60.ocol_ref
  127.2 0.7 reshape.258
  127.8 1.0 copy.58
  128.9 1.5 reshape.259
  130.4 2.2 copy.59
  132.7 2.9 maximum_bitcast_fusion.w_ref
  135.6 2.0 fusion.16
  137.6 98.5 %shard_map.238 = (bf16[8,128,256]{2,1,0:T(8,128)(2,1)S(1)}, bf16[640,768]{1,0:T(8,128)(2,1)S(1)}, f32[4,640,1]{2,1,0:T(8,128)}, bf16[8,128,2048]{2,1,0:T(8,128)(...) custom-call(bf16[1024,2048]{1,0:T(8,128)(2,1)} %bitcast.131, ...), custom_call_target="tpu_custom_call" | custom-call | tf_op jit(solution)/shard_map/pallas_call | solution.py:1425
  236.1 0.9 copy-done.7
  237.0 0.3 copy.61
  237.3 5.7 fusion.33
  243.0 0.3 multiply_reduce_fusion.2
  243.3 0.2 add_convert_fusion.x_ref
  243.5 46.0 %shard_map.239 = bf16[8,128,2048]{2,1,0:T(8,128)(2,1)S(1)} custom-call(bf16[128,2048]{1,0:T(8,128)(2,1)S(1)} %add_convert_fusion.x_ref), custom_call_target="tpu_custom_call" | custom-call | tf_op jit(solution)/shard_map/pallas_call | solution.py:1132
  289.5 8.0 %fusion.36 = f32[1024,1408]{0,1:T(8,128)} fusion(bf16[1024,2048]{1,0:T(8,128)(2,1)S(1)} %bitcast.115, bf16[2048,1408]{1,0:T(8,128)(2,1)S(1)} %bitcast.156), kind=kOutput, calls=%fused_computation.116 | convolution fusion | flops 5905580032 | bytes 15728640 | tf_op jit(solution)/shard_map/dot_general | solution.py:74
  297.6 7.0 %multiply_convert_fusion.2 = (bf16[1024,704]{0,1:T(8,128)(2,1)S(1)}, bf16[1024,704]{0,1:T(8,128)(2,1)S(1)}, bf16[1024,704]{0,1:T(8,128)(2,1)}) fusion(f32[1024,1408]{0,1:T(8,128)} %fusion.36, bf16[1024,2048]{1,0:T(8,128)(2,1)S(1)} %bitcast.159, bf16[704,2048]{1,0:T(8,128)(2,1)S(1)} %bitcast.161), kind=kOutput, calls=%fused_computation.9 | convolution fusion | flops 2964324352 | bytes 17170432 | tf_op jit(solution)/shard_map/dot_general | solution.py:78
  304.6 6.9 %convolution_convert_fusion.2 = bf16[1024,2048]{1,0:T(8,128)(2,1)S(1)} fusion(bf16[2048,1408]{1,0:T(8,128)(2,1)S(1)} %bitcast.157, bf16[1024,704]{0,1:T(8,128)(2,1)S(1)} %get-tuple-element.63, bf16[1024,704]{0,1:T(8,128)(2,1)S(1)} %get-tuple-element.62), kind=kOutput, calls=%fused_computation.2 | convolution fusion | flops 5913444352 | bytes 12845056 | tf_op jit(solution)/shard_map/dot_general | solution.py:78
  311.6 46.2 %shard_map.240 = f32[128,2048]{1,0:T(8,128)S(1)} custom-call(bf16[8,128,2048]{2,1,0:T(8,128)(2,1)S(1)} %bitcast.114), custom_call_target="tpu_custom_call" | custom-call | tf_op jit(solution)/shard_map/pallas_call | solution.py:1154
  357.7 0.4 multiply_reduce_fusion
  358.2 1.5 fusion.32
  359.7 44.8 %shard_map.241 = bf16[8,128,2048]{2,1,0:T(8,128)(2,1)S(1)} custom-call(bf16[128,2048]{1,0:T(8,128)(2,1)S(1)} %get-tuple-element.58.x_ref), custom_call_target="tpu_custom_call" | custom-call | tf_op jit(solution)/shard_map/pallas_call | solution.py:1132
  404.5 2.1 copy-done
  406.5 2.2 fusion
  408.9 7.3 %convolution_convert_fusion.5 = bf16[704,2048]{1,0:T(8,128)(2,1)} fusion(bf16[1024,704]{0,1:T(8,128)(2,1)} %get-tuple-element.64, bf16[1024,2048]{1,0:T(8,128)(2,1)} %bitcast.158), kind=kOutput, calls=%fused_computation.5 | convolution fusion | flops 2954231808 | bytes 8519680 | tf_op jit(solution)/shard_map/dot_general | solution.py:68
  416.3 1.2 copy-done.25
  417.6 6.8 %convolution_convert_fusion.1 = bf16[1024,2048]{1,0:T(8,128)(2,1)} fusion(bf16[1024,704]{0,1:T(8,128)(2,1)S(1)} %copy-done.25, bf16[704,2048]{1,0:T(8,128)(2,1)} %bitcast.160), kind=kOutput, calls=%fused_computation.1 | convolution fusion | flops 2954887168 | bytes 8519680 | tf_op jit(solution)/shard_map/dot_general | solution.py:74
  424.5 0.6 broadcast_in_dim.139
  425.2 2.2 fusion.20
  427.3 1.3 constant_dynamic-slice_fusion.1
  428.8 4.4 convolution_convert_fusion.6.do_ref
  433.3 8.6 %convolution_convert_fusion = bf16[2048,1408]{1,0:T(8,128)(2,1)} fusion(bf16[1024,2048]{1,0:T(8,128)(2,1)S(1)} %bitcast.116, bf16[1024,704]{0,1:T(8,128)(2,1)S(1)} %copy-done.29, bf16[1024,704]{0,1:T(8,128)(2,1)S(1)} %copy-done.27), kind=kOutput, calls=%fused_computation | convolution fusion | flops 5914230784 | bytes 12845056 | tf_op jit(solution)/shard_map/dot_general | solution.py:68
  441.9 81.9 %shard_map.242 = (bf16[1024,768]{1,0:T(8,128)(2,1)}, f32[1,768]{1,0:T(1,128)}, f32[128,2048]{1,0:T(8,128)}, bf16[8,64,1408]{2,1,0:T(8,128)(2,1)}) custom-call(bf16[640,768]{1,0:T(8,128)(2,1)} %copy-done.7, bf16[1024,256]{1,0:T(8,128)(2,1)} %convolution_convert_fusion.6.do_ref, f32[4,640,1]{2,1,0:T(8,128)} %get-tuple-element.39.lse_ref, ...), custom_call_target="tpu_custom_call" | custom-call | tf_op jit(solution)/shard_map/pallas_call | solution.py:1511
  523.8 0.7 reduce
  524.7 8.0 %convolution_convert_fusion.3 = bf16[1024,2048]{1,0:T(8,128)(2,1)} fusion(bf16[1024,768]{1,0:T(8,128)(2,1)} %get-tuple-element.41, bf16[2048,768]{1,0:T(8,128)(2,1)} %bitcast.119), kind=kOutput, calls=%fused_computation.3 | convolution fusion | flops 3223322624 | bytes 8912896 | tf_op jit(solution)/shard_map/dot_general | solution.py:78
  532.7 3.7 convolution_convert_fusion.4
  536.5 61.9 %shard_map.243 = (f32[128,2048]{1,0:T(8,128)S(1)}, bf16[8,64,768]{2,1,0:T(8,128)(2,1)S(1)}) custom-call(bf16[8,128,2048]{2,1,0:T(8,128)(2,1)} %bitcast.134, bf16[8,4,64,768]{3,2,1,0:T(8,128)(2,1)S(1)} %bitcast.117), custom_call_target="tpu_custom_call" | custom-call | tf_op jit(solution)/shard_map/pallas_call | solution.py:1551
  598.4 1.0 fusion.11
  599.7 0.8 bitcast_select_fusion
  600.5 0.7 fusion.28
  601.1 3.3 fusion.13
  604.5 2.0 select_maximum_fusion
  606.7 8.9 %shard_map.244 = f32[8,128]{1,0:T(8,128)S(1)} custom-call(f32[32,8,128]{2,1,0:T(8,128)S(1)} %concatenate.22.x_ref), custom_call_target="tpu_custom_call" | custom-call | tf_op jit(solution)/shard_map/pallas_call | solution.py:1590
  615.6 0.7 reshape.280
  616.4 1.8 reshape.288
  618.2 2.6 copy.66
  620.8 1.6 copy.74
  622.4 0.2 convert_element_type.128
  622.7 1.7 slice_bitcast_fusion
  624.4 2.2 copy.69
  626.5 2.8 reshape.282
  629.3 3.7 copy.68
  633.0 2.8 reshape.281
  635.8 0.5 slice_bitcast_fusion.2
  636.3 0.5 sqrt_bitcast_fusion
  636.9 1.4 fusion.10
  638.3 1.8 convert_element_type.127
  640.1 2.4 convert_element_type.130
  (106 shorter events, 2.0 us)
Async XLA Ops:
  7.2 631.1 %reduce-scatter.3.cloned.1.call-start = ((), (), s32[]{:S(2)}) async-start(), calls=%async_computation.2 | async-start | bytes 1310720 | tf_op jit(solution)/shard_map/reduce_scatter | solution.py:1704
  7.3 4.8 copy-start.1
  7.3 4.8 copy-start.9
  10.6 115.8 %copy-start.11 = (s32[1,3]{1,0:T(1,128)S(1)}, s32[1,3]{1,0:T(1,128)}, u32[]{:S(2)}) copy-start(s32[1,3]{1,0:T(1,128)} %len_ref.3) | copy-start | bytes 40
  10.7 116.1 %copy-start.10 = (s32[1,1024]{1,0:T(1,128)S(1)}, s32[1,1024]{1,0:T(1,128)}, u32[]{:S(2)}) copy-start(s32[1,1024]{1,0:T(1,128)} %orow_ref.3) | copy-start | bytes 12292
  10.7 116.5 %copy-start.15 = (bf16[64,5632]{1,0:T(8,128)(2,1)S(1)}, bf16[64,5632]{1,0:T(8,128)(2,1)}, u32[]{:S(2)}) copy-start(bf16[64,5632]{1,0:T(8,128)(2,1)} %param.22) | copy-start | bytes 2162692
  12.0 116.8 %copy-start.16 = (bf16[64,5632]{1,0:T(8,128)(2,1)S(1)}, bf16[64,5632]{1,0:T(8,128)(2,1)}, u32[]{:S(2)}) copy-start(bf16[64,5632]{1,0:T(8,128)(2,1)} %param.23) | copy-start | bytes 2162692
  124.7 1.7 copy-start.5
  127.2 10.4 %copy-start.2 = (s32[1024,1]{1,0:T(8,128)}, s32[1024,1]{1,0:T(8,128)S(1)}, u32[]{:S(2)}) copy-start(s32[1024,1]{1,0:T(8,128)S(1)} %copy.60.ocol_ref) | copy-start | bytes 12292
  130.4 7.2 %copy-start.6 = (bf16[1,128,2048]{2,1,0:T(8,128)(2,1)S(1)}, bf16[1,128,2048]{2,1,0:T(8,128)(2,1)}, u32[]{:S(2)}) copy-start(bf16[1,128,2048]{2,1,0:T(8,128)(2,1)} %param.27) | copy-start | bytes 1572868
  130.4 7.2 %copy-start.8 = (bf16[176,2048]{1,0:T(8,128)(2,1)S(1)}, bf16[176,2048]{1,0:T(8,128)(2,1)}, u32[]{:S(2)}) copy-start(bf16[176,2048]{1,0:T(8,128)(2,1)} %dw_ref.1) | copy-start | bytes 2162692
  236.1 0.9 copy-start.7
  243.3 46.2 %copy-start.21 = (bf16[8,4,64,1408]{3,2,1,0:T(8,128)(2,1)S(1)}, bf16[8,4,64,1408]{3,2,1,0:T(8,128)(2,1)}, u32[]{:S(2)}) copy-start(bf16[8,4,64,1408]{3,2,1,0:T(8,128)(2,1)} %get-tuple-element.38) | copy-start | bytes 17301508
  289.5 8.1 %copy-start.3 = (bf16[8,128,2048]{2,1,0:T(8,128)(2,1)}, bf16[8,128,2048]{2,1,0:T(8,128)(2,1)S(1)}, u32[]{:S(2)}) copy-start(bf16[8,128,2048]{2,1,0:T(8,128)(2,1)S(1)} %shard_map.239) | copy-start | bytes 12582916
  289.5 8.1 %copy-start.22 = (bf16[8,128,2048]{2,1,0:T(8,128)(2,1)S(1)}, bf16[8,128,2048]{2,1,0:T(8,128)(2,1)}, u32[]{:S(2)}) copy-start(bf16[8,128,2048]{2,1,0:T(8,128)(2,1)} %get-tuple-element.36) | copy-start | bytes 12582916
  289.5 8.1 %copy-start.23 = (bf16[4,176,2048]{2,1,0:T(8,128)(2,1)S(1)}, bf16[4,176,2048]{2,1,0:T(8,128)(2,1)}, u32[]{:S(2)}) copy-start(bf16[4,176,2048]{2,1,0:T(8,128)(2,1)} %get-tuple-element.37) | copy-start | bytes 8650756
  304.6 6.9 %copy-start.26 = (bf16[1024,704]{0,1:T(8,128)(2,1)}, bf16[1024,704]{0,1:T(8,128)(2,1)S(1)}, u32[]{:S(2)}) copy-start(bf16[1024,704]{0,1:T(8,128)(2,1)S(1)} %get-tuple-element.62) | copy-start | bytes 4325380
  304.6 6.9 %copy-start.28 = (bf16[1024,704]{0,1:T(8,128)(2,1)}, bf16[1024,704]{0,1:T(8,128)(2,1)S(1)}, u32[]{:S(2)}) copy-start(bf16[1024,704]{0,1:T(8,128)(2,1)S(1)} %get-tuple-element.63) | copy-start | bytes 4325380
  404.5 2.1 copy-start
  408.8 231.3 %reduce-scatter.5.cloned.1.call-start = ((), (), s32[]{:S(2)}) async-start(), calls=%async_computation.3 | async-start | bytes 3604480 | tf_op jit(solution)/shard_map/reduce_scatter | solution.py:1704
  416.2 1.4 copy-start.25
  428.8 4.5 copy-start.4
  428.8 4.5 copy-start.27
  428.8 4.5 copy-start.29
  524.7 8.0 %copy-start.12 = (bf16[8,128,2048]{2,1,0:T(8,128)(2,1)S(1)}, bf16[8,128,2048]{2,1,0:T(8,128)(2,1)}, u32[]{:S(2)}) copy-start(bf16[8,128,2048]{2,1,0:T(8,128)(2,1)} %get-tuple-element.30) | copy-start | bytes 12582916
  524.7 8.0 %copy-start.24 = (bf16[1024,768]{1,0:T(8,128)(2,1)S(1)}, bf16[1024,768]{1,0:T(8,128)(2,1)}, u32[]{:S(2)}) copy-start(bf16[1024,768]{1,0:T(8,128)(2,1)} %get-tuple-element.41) | copy-start | bytes 4718596
  598.3 1.1 copy-start.17
  618.2 4.2 copy-start.14
  629.3 6.5 copy-start.20
  629.3 6.5 copy-start.19
  629.3 7.5 %copy-start.13 = (f32[128,2048]{1,0:T(8,128)S(1)}, f32[128,2048]{1,0:T(8,128)}, u32[]{:S(2)}) copy-start(f32[128,2048]{1,0:T(8,128)} %get-tuple-element.59) | copy-start | bytes 3145732
  629.3 7.5 %copy-start.18 = (f32[128]{0:T(128)S(1)}, f32[128]{0:T(128)}, u32[]{:S(2)}) copy-start(f32[128]{0:T(128)} %copy-done.17) | copy-start | bytes 1540
Sparse Core Ops, SparseCore 0:
  408.9 23.0 reduce-scatter.2
  434.7 52.5 reduce-scatter.4

commit v4 on v3

--- a/solution.py
+++ b/solution.py
@@ -470,56 +470,57 @@
         self.ysend(self.z, self.x).start()
         self.own.start()
 
-    def below(self, t, use=None):
-        @pl.when(self.z >= t)
+    def near(self, i):
+        low = jnp.where(self.z < 2, self.z, 3 - self.z)
+        base = jnp.where(low == 0, i, jnp.where(i < 2, 1 - i, i))
+        return jnp.where(self.z < 2, base, 3 - base)
+
+    def arrive(self, i):
+        zb = self.near(i)
+        b = self.at(zb)
+        self.arrived(b).wait_recv()
+
+        @pl.when((zb < self.z) & (self.z < 3))
         def _():
-            zb = self.z - t
-            b = self.at(zb)
-            self.arrived(b).wait_recv()
-
-            @pl.when(self.z < 3)
+            self.usend(zb, self.o.at[b]).start()
+
+        @pl.when((zb > self.z) & (self.z > 0))
+        def _():
+            self.dsend(zb, self.o.at[b]).start()
+
+        self.ysend(zb, self.o.at[b]).start()
+        return b
+
+    def cross(self, i):
+        b = 2 * self.near(i) + 1 - self.y
+        self.arrived(b).wait_recv()
+        return b
+
+    def steps(self):
+        return [functools.partial(self.arrive, i) for i in (1, 2, 3)]
+
+    def each(self, use):
+        @pl.loop(0, 8)
+        def _(j):
+            i = (j + 1) // 2
+            column = (j == 0) | ((j % 2 == 1) & (j < 7))
+
+            @pl.when(column & (j > 0))
             def _():
-                self.usend(zb, self.o.at[b]).start()
-
-            self.ysend(zb, self.o.at[b]).start()
-            if use is not None:
-                use(b)
-
-    def above(self, t, use=None):
-        @pl.when(self.z + t <= 3)
-        def _():
-            zb = self.z + t
-            b = self.at(zb)
-            self.arrived(b).wait_recv()
-
-            @pl.when(self.z > 0)
+                self.arrive(i)
+
+            other = jnp.where(j == 7, 3, j // 2 - 1)
+
+            @pl.when(jnp.logical_not(column))
             def _():
-                self.dsend(zb, self.o.at[b]).start()
-
-            self.ysend(zb, self.o.at[b]).start()
-            if use is not None:
-                use(b)
-
-    def across(self, t, use=None):
-        for sign in (0,) if t == 0 else (-1, 1):
-            zb = self.z + sign * t
-
-            @pl.when((zb >= 0) & (zb <= 3))
-            def _():
-                b = 2 * zb + 1 - self.y
-                self.arrived(b).wait_recv()
-                if use is not None:
-                    use(b)
-
-    def steps(self):
-        out = []
-        for t in (1, 2, 3):
-            out.append(functools.partial(self.below, t))
-            out.append(functools.partial(self.above, t))
-        return out
-
-    def finish(self):
-        self.own.wait()
+                self.cross(other)
+
+            zb = self.near(jnp.where(column, i, other))
+            use(2 * zb + jnp.where(column, self.y, 1 - self.y))
+
+    def finish(self, own=True):
+        if own:
+            self.own.wait()
         for zb in range(4):
             self.ysend(zb, self.x).wait_send()
 
@@ -535,13 +536,12 @@
 class SeqReduce:
     @staticmethod
     def scratch(rows, w):
-        big = [pltpu.VMEM((4, rows, w), jnp.bfloat16) for _ in range(6)]
-        return big + [DMA((4,))] + [DMA((4, CH)) for _ in range(6)]
-
-    def __init__(self, p, o, mine, ybuf, up, down, send_up, send_down, load, ry, ru, rd, sy, su, sd):
-        self.p, self.o, self.mine, self.ybuf, self.up, self.down = p, o, mine, ybuf, up, down
-        self.send_up, self.send_down, self.load_sem = send_up, send_down, load
-        self.ry, self.ru, self.rd, self.sy, self.su, self.sd = ry, ru, rd, sy, su, sd
+        big = [pltpu.VMEM((n, rows, w), jnp.bfloat16) for n in (4, 5)]
+        return big + [DMA((4, CH)), DMA((5, CH)), DMA((4, CH)), DMA((4, CH))]
+
+    def __init__(self, p, o, ybuf, got, ry, rl, sy, sl):
+        self.p, self.o, self.ybuf, self.got = p, o, ybuf, got
+        self.ry, self.rl, self.sy, self.sl = ry, rl, sy, sl
         self.s, self.f, self.z, self.y = where_am_i()
         self.other = flip(self.s, 1)
         self.ch = p.shape[1] // CH
@@ -560,83 +560,71 @@
         dst = self.ybuf.at[zb, r]
         return remote(src, dst, self.sy.at[zb, c], self.ry.at[zb, c], (self.other, self.f))
 
-    def load(self, zb):
-        src = self.p.at[2 * zb + self.y]
-        return pltpu.make_async_copy(src, self.mine.at[zb], self.load_sem.at[zb])
-
     def usend(self, zb, c):
         r = self.rows(c)
-        src, dst = self.send_up.at[zb, r], self.up.at[zb, r]
-        return remote(src, dst, self.su.at[zb, c], self.ru.at[zb, c], (self.s + 2, self.f))
+        src, dst = self.ybuf.at[zb, r], self.got.at[zb, r]
+        return remote(src, dst, self.sl.at[zb, c], self.rl.at[zb, c], (self.s + 2, self.f))
 
     def dsend(self, zb, c):
         r = self.rows(c)
-        src, dst = self.send_down.at[zb, r], self.down.at[zb, r]
-        return remote(src, dst, self.sd.at[zb, c], self.rd.at[zb, c], (self.s - 2, self.f))
+        slot = jnp.where(zb == self.z - 1, 4, zb)
+        src, dst = self.ybuf.at[zb, r], self.got.at[slot, r]
+        return remote(src, dst, self.sl.at[zb, c], self.rl.at[slot, c], (self.s - 2, self.f))
+
+    def landed(self, slot, c):
+        v = self.got.at[slot, self.rows(c)]
+        return remote(v, v, self.sl.at[0, c], self.rl.at[slot, c], (self.other, self.f))
+
+    def send(self, k):
+        for c in range(CH):
+            self.ysend(self.order(k), c).start()
 
     def start(self):
         for k in range(4):
-            zb = self.order(k)
-            for c in range(CH):
-                self.ysend(zb, c).start()
-            self.load(zb).start()
+            self.send(k)
 
     def step(self, k, c):
         z, zb, r = self.z, self.order(k), self.rows(c)
-        if c == 0:
-            self.load(zb).wait()
         self.ysend(zb, c).wait_recv()
-        a, b = self.mine.at[zb, r], self.ybuf.at[zb, r]
-        u, d = self.up.at[zb, r], self.down.at[zb, r]
+        a, b = self.p.at[2 * zb + self.y, r], self.ybuf.at[zb, r]
+        u, d = self.got.at[zb, r], self.got.at[4, r]
+        alone = ((zb > z) & (z == 0)) | ((zb < z) & (z == 3))
+
+        @pl.when(alone)
+        def _():
+            adder(b, [a, b])
+
+        @pl.when((zb != z) & jnp.logical_not(alone))
+        def _():
+            self.landed(zb, c).wait_recv()
+            adder(b, [a, b, u])
 
         @pl.when(zb > z)
         def _():
+            self.usend(zb, c).start()
+
+        @pl.when(zb < z)
+        def _():
+            self.dsend(zb, c).start()
+
+        @pl.when(zb == z)
+        def _():
+            o = self.o.at[r]
+
             @pl.when(z == 0)
             def _():
-                adder(self.send_up.at[zb, r], [a, b])
-
-            @pl.when(z > 0)
-            def _():
-                self.usend(zb, c).wait_recv()
-                adder(self.send_up.at[zb, r], [a, b, u])
-
-            self.usend(zb, c).start()
-
-        @pl.when(zb < z)
-        def _():
+                self.landed(4, c).wait_recv()
+                adder(o, [a, b, d])
+
             @pl.when(z == 3)
             def _():
-                adder(self.send_down.at[zb, r], [a, b])
-
-            @pl.when(z < 3)
-            def _():
-                self.dsend(zb, c).wait_recv()
-                adder(self.send_down.at[zb, r], [a, b, d])
-
-            self.dsend(zb, c).start()
-
-        @pl.when(zb == z)
-        def _():
-            @pl.when(z > 0)
-            def _():
-                self.usend(zb, c).wait_recv()
-
-            @pl.when(z < 3)
-            def _():
-                self.dsend(zb, c).wait_recv()
-
-            o = self.o.at[r]
-
-            @pl.when(z == 0)
-            def _():
-                adder(o, [a, b, d])
-
-            @pl.when(z == 3)
-            def _():
+                self.landed(zb, c).wait_recv()
                 adder(o, [a, b, u])
 
             @pl.when((z > 0) & (z < 3))
             def _():
+                self.landed(zb, c).wait_recv()
+                self.landed(4, c).wait_recv()
                 adder(o, [a, b, u, d])
 
     def steps(self):
@@ -647,13 +635,9 @@
             for c in range(CH):
                 self.ysend(zb, c).wait_send()
 
-                @pl.when(zb > self.z)
+                @pl.when(zb != self.z)
                 def _():
                     self.usend(zb, c).wait_send()
-
-                @pl.when(zb < self.z)
-                def _():
-                    self.dsend(zb, c).wait_send()
 
 
 class ColGather:
@@ -667,25 +651,29 @@
         self.s, self.f, _, _ = where_am_i()
         self.fc, self.fx = flip(self.f, 1), flip(self.f, 2)
         self.fd = flip(self.fc, 2)
-        self.mine = pltpu.make_async_copy(x.at[self.s], o.at[self.s, self.f], own)
+        self.mine = pltpu.make_async_copy(x.at[self.s], self.piece(self.s, self.f), own)
+
+    def piece(self, t, ff):
+        r = self.x.shape[1]
+        return self.o.at[pl.ds(pl.multiple_of((t * 4 + ff) * r, r), r)]
 
     def send_direct(self, k):
         s, f, t = self.s, self.f, peer(self.s, k)
-        return remote(self.x.at[t], self.o.at[s, f], self.direct.at[k], self.recv.at[s, f], (t, f))
+        return remote(self.x.at[t], self.piece(s, f), self.direct.at[k], self.recv.at[s, f], (t, f))
 
     def send_core(self, k, which, src):
         t, ff = peer(self.s, k), self.f if which == 0 else self.fx
-        dst = self.o.at[t, ff]
+        dst = self.piece(t, ff)
         return remote(src, dst, self.core.at[k, which], self.recv.at[t, ff], (self.s, self.fc))
 
     def send_x(self, k, src):
         t = peer(self.s, k)
-        dst = self.o.at[t, self.f]
+        dst = self.piece(t, self.f)
         return remote(src, dst, self.xs.at[k], self.recv.at[t, self.f], (self.s, self.fx))
 
     def arrived(self, k, ff):
         t = peer(self.s, k)
-        o = self.o.at[t, ff]
+        o = self.piece(t, ff)
         return remote(o, o, self.own, self.recv.at[t, ff], (self.s, self.fc))
 
     def start(self):
@@ -698,13 +686,13 @@
     def step(self, k):
         t = peer(self.s, k)
         self.arrived(k, self.f).wait_recv()
-        self.send_x(k, self.o.at[t, self.f]).start()
-        self.send_core(k, 0, self.o.at[t, self.f]).start()
+        self.send_x(k, self.piece(t, self.f)).start()
+        self.send_core(k, 0, self.piece(t, self.f)).start()
 
     def xstep(self, k):
         t = peer(self.s, k)
         self.arrived(k, self.fx).wait_recv()
-        self.send_core(k, 1, self.o.at[t, self.fx]).start()
+        self.send_core(k, 1, self.piece(t, self.fx)).start()
 
     def steps(self):
         first = [functools.partial(self.step, k) for k in reversed(range(1, 8))]
@@ -724,77 +712,90 @@
             self.send_core(k, 1, self.x.at[0]).wait_send()
 
 
-class ColReduce:
+class ColSum:
     @staticmethod
     def scratch(r, c):
         def v(*lead):
             return pltpu.VMEM(lead + (8, r, c), jnp.bfloat16)
 
-        return [v(2), v(2), v(), v(), v()] + [DMA((2, 8)) for _ in range(3)] + [DMA((8,)) for _ in range(4)]
-
-    def __init__(self, g, o, ld, cb, hx, xb, ob, ldsem, cs, cr, xs, xr, es, er):
-        self.g, self.o, self.ld, self.cb, self.hx, self.xb, self.ob = g, o, ld, cb, hx, xb, ob
-        self.ldsem, self.cs, self.cr, self.xs, self.xr, self.es, self.er = ldsem, cs, cr, xs, xr, es, er
+        return [v(2), v(), DMA((2, 8)), DMA((2, 8)), DMA((8,)), DMA((8,))]
+
+    def __init__(self, g, h, cb, xb, cs, cr, xs, xr):
+        self.g, self.h, self.cb, self.xb = g, h, cb, xb
+        self.cs, self.cr, self.xs, self.xr = cs, cr, xs, xr
         self.s, self.f, _, _ = where_am_i()
         self.fc, self.fx = flip(self.f, 1), flip(self.f, 2)
         self.fd = flip(self.fc, 2)
-
-    def core(self, w, k):
-        i = peer(self.s, k)
-        src = self.g.at[i, self.fd if w == 0 else self.fc]
+        self.r, self.c = h.shape[1:]
+
+    def piece(self, i, ff):
+        at = pl.multiple_of((i * 4 + ff) * self.r, self.r)
+        return self.g.at[pl.ds(at, self.r), pl.ds(0, self.c)]
+
+    def core(self, w, i):
+        src = self.piece(i, self.fd if w == 0 else self.fc)
         dst = self.cb.at[w, i]
-        return remote(src, dst, self.cs.at[w, k], self.cr.at[w, k], (self.s, self.fc))
-
-    def load(self, w, k):
-        i = peer(self.s, k)
-        src = self.g.at[i, self.fx if w == 0 else self.f]
-        return pltpu.make_async_copy(src, self.ld.at[w, i], self.ldsem.at[w, k])
-
-    def xsend(self, k):
-        i = peer(self.s, k)
-        return remote(self.hx.at[i], self.xb.at[i], self.xs.at[k], self.xr.at[k], (self.s, self.fx))
-
-    def esend(self, k):
-        t = peer(self.s, k)
-        dst = self.o.at[self.s]
-        return remote(self.ob.at[t], dst, self.es.at[k], self.er.at[k], (t, self.f))
+        return remote(src, dst, self.cs.at[w, i], self.cr.at[w, i], (self.s, self.fc))
+
+    def xsend(self, i):
+        src, dst = self.cb.at[0, i], self.xb.at[i]
+        return remote(src, dst, self.xs.at[i], self.xr.at[i], (self.s, self.fx))
+
+    def send(self, i):
+        self.core(0, i).start()
+        self.core(1, i).start()
+
+    def step(self, i):
+        self.core(0, i).wait_recv()
+        adder(self.cb.at[0, i], [self.piece(i, self.fx), self.cb.at[0, i]])
+        self.xsend(i).start()
+
+    def total(self, i):
+        self.core(1, i).wait_recv()
+        self.xsend(i).wait_recv()
+        adder(self.h.at[i], [self.piece(i, self.f), self.cb.at[1, i], self.xb.at[i]])
+
+    def finish(self):
+        for i in range(8):
+            self.core(0, i).wait_send()
+            self.core(1, i).wait_send()
+            self.xsend(i).wait_send()
+
+
+class FsdpReduce:
+    @staticmethod
+    def scratch(r, c):
+        return [pltpu.VMEM((2, r, c), jnp.bfloat16), pltpu.VMEM((r, c), jnp.bfloat16), DMA((3,)), DMA((3,))]
+
+    def __init__(self, g, o, cb, xb, send, recv):
+        self.g, self.o, self.cb, self.xb = g, o, cb, xb
+        self.s, self.f, _, _ = where_am_i()
+        f = self.f
+        self.fx = flip(f, 2)
+        fc = flip(f, 1)
+        core = (self.s, fc)
+        self.far = remote(g.at[flip(fc, 2)], cb.at[0], send.at[0], recv.at[0], core)
+        self.near = remote(g.at[fc], cb.at[1], send.at[1], recv.at[1], core)
+        self.over = remote(cb.at[0], xb, send.at[2], recv.at[2], (self.s, self.fx))
 
     def start(self):
-        for w in range(2):
-            for k in reversed(range(8)):
-                self.core(w, k).start()
-                self.load(w, k).start()
-
-    def step(self, k):
-        i = peer(self.s, k)
-        self.core(0, k).wait_recv()
-        self.load(0, k).wait()
-        adder(self.hx.at[i], [self.ld.at[0, i], self.cb.at[0, i]])
-        self.xsend(k).start()
-
-    def total(self, k):
-        i = peer(self.s, k)
-        self.core(1, k).wait_recv()
-        self.load(1, k).wait()
-        self.xsend(k).wait_recv()
-        dst = self.ob if k else self.o
-        adder(dst.at[i], [self.ld.at[1, i], self.cb.at[1, i], self.xb.at[i]])
-        if k:
-            self.esend(k).start()
-
-    def steps(self):
-        first = [functools.partial(self.step, k) for k in reversed(range(8))]
-        then = [functools.partial(self.total, k) for k in reversed(range(8))]
-        return first + then
+        self.far.start()
+        self.near.start()
+
+    def step(self):
+        self.far.wait_recv()
+        adder(self.cb.at[0], [self.g.at[self.fx], self.cb.at[0]])
+        self.over.start()
+
+    def total(self):
+        self.near.wait_recv()
+        self.over.wait_recv()
+        adder(self.o, [self.g.at[self.f], self.cb.at[1], self.xb])
 
     def finish(self):
-        for k in range(8):
-            self.core(0, k).wait_send()
-            self.core(1, k).wait_send()
-            self.xsend(k).wait_send()
-            if k:
-                self.esend(k).wait_recv()
-                self.esend(k).wait_send()
+        self.far.wait_send()
+        self.near.wait_send()
+        self.over.wait_send()
 
 
 class FsdpGather:
@@ -1010,157 +1011,6 @@
     return [item for _, _, item in sorted(keyed, key=lambda v: v[:2])]
 
 
-def entry_kernel(
-    x_ref, p_ref, w_ref, ow_ref, a_ref, wo_ref, g_ref, oo_ref, xs, got, psend, precv, *sems
-):
-    s, f, z, y = where_am_i()
-    me = s * 4 + f
-    greet_all(s, f)
-    gather = SeqGather(x_ref, xs, *sems[:5])
-    slices = ColGather(w_ref, wo_ref, *sems[5:10])
-    whole = WholeGather(ow_ref, oo_ref, *sems[10:])
-
-    def param(k):
-        i = (me + k) % 32
-        return remote(p_ref, got.at[me], psend.at[k], precv.at[k], dealer(i))
-
-    @pl.loop(1, 32)
-    def _(k):
-        param(k).start()
-
-    gather.start()
-    slices.start()
-    whole.start()
-    got[me] = p_ref[...]
-
-    @pl.loop(1, 32)
-    def _(k):
-        param(k).wait_recv()
-
-    for i in range(16):
-        g_ref[:, i * 128 : i * 128 + 128] = got[2 * i] + got[2 * i + 1]
-    step = 16
-
-    def norm(b):
-        gain, shift = g_ref[0:1], g_ref[1:2]
-
-        @pl.loop(0, x_ref.shape[0] // step)
-        def _(i):
-            r = pl.ds(pl.multiple_of(i * step, step), step)
-            normed, _ = normalize(xs[b, r].astype(jnp.float32))
-            a_ref[b, r] = (normed * gain + shift).astype(jnp.bfloat16)
-
-    gather.own.wait()
-    norm(s)
-    todo = slices.steps()
-    lines = whole.steps()
-    for t in (1, 2, 3):
-        gather.below(t)
-        gather.above(t)
-        for item in todo[:3] + lines[:2]:
-            item()
-        todo, lines = todo[3:], lines[2:]
-        gather.across(t - 1, norm)
-        for zb in (z - t, z + t):
-
-            @pl.when((zb >= 0) & (zb <= 3))
-            def _():
-                norm(2 * zb + y)
-
-    for item in todo[:2]:
-        item()
-    gather.across(3, norm)
-    for item in merged(todo[2:], lines):
-        item()
-    slices.finish()
-    whole.finish()
-
-    @pl.loop(1, 32)
-    def _(k):
-        param(k).wait_send()
-
-    for zb in range(4):
-        gather.ysend(zb, x_ref).wait_send()
-
-        @pl.when((z < 3) & (zb <= z))
-        def _():
-            gather.usend(zb, x_ref).wait_send()
-
-        @pl.when((z > 0) & (zb >= z))
-        def _():
-            gather.dsend(zb, x_ref).wait_send()
-
-
-def entry(x, params, weight, rows_weight, collective):
-    rows, width = x.shape
-    return pl.pallas_call(
-        entry_kernel,
-        out_shape=(
-            jax.ShapeDtypeStruct((8, rows, width), jnp.bfloat16),
-            jax.ShapeDtypeStruct((8, 4) + weight.shape[1:], weight.dtype),
-            jax.ShapeDtypeStruct((8, width), jnp.float32),
-            jax.ShapeDtypeStruct((32,) + rows_weight.shape, rows_weight.dtype),
-        ),
-        in_specs=[VMEM_SPEC] * 4,
-        out_specs=(VMEM_SPEC, ANY_SPEC, VMEM_SPEC, ANY_SPEC),
-        scratch_shapes=[
-            pltpu.VMEM((8, rows, width), x.dtype),
-            pltpu.VMEM((32, 8, 128), jnp.float32),
-            DMA((32,)),
-            DMA((32,)),
-        ]
-        + SeqGather.scratch()
-        + ColGather.scratch()
-        + WholeGather.scratch(),
-        compiler_params=comm_params(collective),
-    )(x, params, weight, rows_weight)
-
-
-def gather_kernel(x_ref, o_ref, *sems):
-    s, f, z, y = where_am_i()
-    greet_line(s, f, z, y)
-    task = SeqGather(x_ref, o_ref, *sems)
-    task.start()
-    for item in task.steps():
-        item()
-    for t in range(4):
-        task.across(t)
-    task.finish()
-
-
-def gather_rows_line(x, collective):
-    return pl.pallas_call(
-        gather_kernel,
-        out_shape=jax.ShapeDtypeStruct((8,) + x.shape, x.dtype),
-        in_specs=[VMEM_SPEC],
-        out_specs=ANY_SPEC,
-        scratch_shapes=SeqGather.scratch(),
-        compiler_params=comm_params(collective),
-    )(x)
-
-
-def reduce_kernel(p_ref, o_ref, *scratch):
-    s, f, z, y = where_am_i()
-    greet_line(s, f, z, y)
-    task = SeqReduce(p_ref, o_ref, *scratch)
-    task.start()
-    for item in task.steps():
-        item()
-    task.finish()
-
-
-def reduce_rows_line(p, collective):
-    _, rows, width = p.shape
-    return pl.pallas_call(
-        reduce_kernel,
-        out_shape=jax.ShapeDtypeStruct((rows, width), jnp.float32),
-        in_specs=[ANY_SPEC],
-        out_specs=VMEM_SPEC,
-        scratch_shapes=SeqReduce.scratch(rows, width),
-        compiler_params=comm_params(collective),
-    )(p)
-
-
 def dot(a, b, ca=1, cb=0):
     return lax.dot_general(a, b, (((ca,), (cb,)), ((), ())), preferred_element_type=jnp.float32)
 
@@ -1206,7 +1056,7 @@
 
 
 def attend(
-    a_ref, w_ref, shift_ref, tables, orow_ref, ocol_ref, len_ref, o_ref, pk_ref, lse_ref, rot, opk
+    a_ref, w_ref, shift_of, tables, orow_ref, ocol_ref, len_ref, o_ref, pk_ref, lse_ref, rot, opk
 ):
     rows, w3 = rot.shape
     w = w3 // 3
@@ -1215,11 +1065,14 @@
     c_ref, s1_ref, s2_ref = tables
 
     def project():
+        shift = shift_of()
+
         @pl.loop(0, rows // 256)
         def _(i):
             r = row_at(i, 256)
             c, s1, s2 = c_ref[r], s1_ref[r], s2_ref[r]
-            qkv = dot(a_ref[r], w_ref[...]) + shift_ref[...]
+            left = jnp.concatenate([a_ref[2 * i], a_ref[2 * i + 1]], 0)
+            qkv = dot(left, w_ref[...]) + shift
             for t in range(w3 // 128):
                 cols = slice(t * 128, t * 128 + 128)
                 x = qkv[:, cols]
@@ -1344,39 +1197,93 @@
 
 
 def forward_kernel(
-    a_ref,
-    qw_ref,
-    shift_ref,
+    x_ref,
+    p_ref,
+    qp_ref,
+    op_ref,
+    dm_ref,
+    wp_ref,
+    dp_ref,
     c_ref,
     s1_ref,
     s2_ref,
     orow_ref,
     ocol_ref,
     len_ref,
-    dm_ref,
-    w_ref,
-    dw_ref,
+    a_ref,
+    qw_ref,
+    n_ref,
+    ow_ref,
     ho_ref,
     pk_ref,
     lse_ref,
     dmo_ref,
-    wo_ref,
-    dwo_ref,
+    ww_ref,
+    dw_ref,
     mix_ref,
+    xs,
+    got,
     rot,
     opk,
+    psend,
+    precv,
     *sems,
 ):
     s, f, z, y = where_am_i()
-    greet_columns(s, f)
-    gather = SeqGather(dm_ref, dmo_ref, *sems[:5])
-    slices = ColGather(w_ref, wo_ref, *sems[5:10])
-    side = FsdpGather(dw_ref, dwo_ref, *sems[10:13])
-    swap = RowExchange(mix_ref, ho_ref, *sems[13:])
+    me = s * 4 + f
+    greet_all(s, f)
+    gather = SeqGather(x_ref, xs, *sems[:5])
+    slices = ColGather(qp_ref, qw_ref, *sems[5:10])
+    whole = WholeGather(op_ref, ow_ref, *sems[10:17])
+    grads = SeqGather(dm_ref, dmo_ref, *sems[17:22])
+    wide = ColGather(wp_ref, ww_ref, *sems[22:27])
+    down = FsdpGather(dp_ref, dw_ref, *sems[27:30])
+    swap = RowExchange(mix_ref, ho_ref, *sems[30:])
+
+    def param(k):
+        i = (me + k) % 32
+        return remote(p_ref, got.at[me], psend.at[k], precv.at[k], dealer(i))
+
+    @pl.loop(1, 32)
+    def _(k):
+        param(k).start()
+
+    gather.start()
+    slices.start()
+    got[me] = p_ref[...]
+
+    @pl.loop(1, 32)
+    def _(k):
+        param(k).wait_recv()
+
+    for i in range(16):
+        n_ref[:, i * 128 : i * 128 + 128] = got[2 * i] + got[2 * i + 1]
+    step = 16
+
+    def norm(b):
+        gain, shift = n_ref[0:1], n_ref[1:2]
+
+        @pl.loop(0, x_ref.shape[0] // step)
+        def _(i):
+            r = row_at(i, step)
+            normed, _ = normalize(xs[b, r].astype(jnp.float32))
+            a_ref[b, r] = (normed * gain + shift).astype(jnp.bfloat16)
+
+    def shift_of():
+        w = rot.shape[1] // 3
+        parts = []
+        for n in range(3):
+            part = jnp.zeros((1, w), jnp.float32)
+            for i in range(8):
+                piece = n_ref[4 + n : 5 + n, i * w : i * w + w]
+                part = part + jnp.where(s == i, piece, jnp.zeros_like(piece))
+            parts.append(part)
+        return jnp.concatenate(parts, 1)
+
     work = attend(
         a_ref,
         qw_ref,
-        shift_ref,
+        shift_of,
         (c_ref, s1_ref, s2_ref),
         orow_ref,
         ocol_ref,
@@ -1387,69 +1294,274 @@
         rot,
         opk,
     )
-    gather.start()
-    slices.start()
-    side.start()
-    for item in work[:-6]:
+    p = functools.partial
+
+    def own():
+        gather.own.wait()
+        norm(s)
+
+    first = [own]
+    for i in range(3):
+        first.append(p(gather.arrive, i + 1))
+        first.append(lambda i=i: norm(gather.cross(i)))
+        first.append(lambda i=i: norm(2 * gather.near(i + 1) + y))
+    first.append(lambda: norm(gather.cross(3)))
+    lead, rest = slices.steps(), wide.steps()
+    for item in merged(first[:7], lead[:6]):
         item()
-    gather.below(1)
-    gather.above(1)
-    todo = slices.steps()
-    for item in merged(work[-6:], todo[:3]):
+    grads.start()
+    wide.start()
+    for item in merged(first[7:], lead[6:]):
+        item()
+    whole.start()
+    down.start()
+    slices.finish()
+    lines = whole.steps()
+    side = [p(grads.arrive, 1)] + rest[:3] + [p(grads.arrive, 2)] + rest[3:7] + [p(grads.arrive, 3)]
+    for item in merged(work, side, lines[:6]):
         item()
     swap.start()
-    todo = todo[3:] + [side.step]
-    for t in (2, 3):
-        gather.below(t)
-        gather.above(t)
-        for item in todo[:4]:
-            item()
-        todo = todo[4:]
-    for item in todo:
+    for item in merged(rest[7:], lines[6:]):
         item()
-    for t in range(4):
-        gather.across(t)
+    down.step()
+    for i in range(4):
+        grads.cross(i)
     swap.finish()
-    slices.finish()
-    side.finish()
-    gather.finish()
-
-
-def attention_forward(
-    a, w_qkv, shift, tables, orow, ocol, lengths, valid, dm, weight, rows_weight, collective
+    wide.finish()
+    whole.finish()
+    down.finish()
+    grads.finish()
+    gather.finish(False)
+
+    @pl.loop(1, 32)
+    def _(k):
+        param(k).wait_send()
+
+
+def forward(
+    x, params, qkv_p, out_p, dm, wide_p, down_p, tables, orow, ocol, lengths, valid, collective
 ):
-    rows, w3 = a.shape[0], w_qkv.shape[1]
+    rows, width = x.shape
+    w3 = qkv_p.shape[2]
     w = w3 // 3
+    group = 8 * rows
     heads = w // HEAD_DIM
-    mixed = jax.ShapeDtypeStruct((8, rows // 8, w), jnp.bfloat16)
+
+    def out(shape, dtype=jnp.bfloat16):
+        return jax.ShapeDtypeStruct(shape, dtype)
+
     return pl.pallas_call(
         forward_kernel,
         out_shape=(
-            mixed,
-            jax.ShapeDtypeStruct((valid, w3), jnp.bfloat16),
-            jax.ShapeDtypeStruct((heads, valid, 1), jnp.float32),
-            jax.ShapeDtypeStruct((8,) + dm.shape, dm.dtype),
-            jax.ShapeDtypeStruct((8, 4) + weight.shape[1:], weight.dtype),
-            jax.ShapeDtypeStruct((4,) + rows_weight.shape, rows_weight.dtype),
-            mixed,
+            out((8, rows, width)),
+            out((width, w3)),
+            out((8, width), jnp.float32),
+            out((32,) + out_p.shape),
+            out((8, rows, w)),
+            out((valid, w3)),
+            out((heads, valid, 1), jnp.float32),
+            out((8, rows, width)),
+            out((width, wide_p.shape[2])),
+            out((4,) + down_p.shape),
+            out((8, rows, w)),
         ),
-        in_specs=[VMEM_SPEC] * 8 + [SMEM_SPEC] + [VMEM_SPEC] * 3,
-        out_specs=(VMEM_SPEC,) * 3 + (ANY_SPEC,) * 3 + (VMEM_SPEC,),
+        in_specs=[VMEM_SPEC] * 12 + [SMEM_SPEC],
+        out_specs=(VMEM_SPEC,) * 3
+        + (ANY_SPEC,)
+        + (VMEM_SPEC,) * 3
+        + (ANY_SPEC,) * 3
+        + (VMEM_SPEC,),
         scratch_shapes=[
-            pltpu.VMEM((rows, w3), jnp.bfloat16),
+            pltpu.VMEM((8, rows, width), jnp.bfloat16),
+            pltpu.VMEM((32, 8, 128), jnp.float32),
+            pltpu.VMEM((group, w3), jnp.bfloat16),
             pltpu.VMEM((valid, w), jnp.bfloat16),
+            DMA((32,)),
+            DMA((32,)),
         ]
+        + SeqGather.scratch()
+        + ColGather.scratch()
+        + WholeGather.scratch()
         + SeqGather.scratch()
         + ColGather.scratch()
         + FsdpGather.scratch()
         + RowExchange.scratch(),
         compiler_params=comm_params(collective),
-    )(a, w_qkv, shift, *tables, orow, ocol, lengths, dm, weight, rows_weight)
+    )(x, params, qkv_p, out_p, dm, wide_p, down_p, *tables, orow, ocol, lengths)
+
+
+def tall(rows, step=16):
+    def wrap(fn):
+        @pl.loop(0, rows // step)
+        def _(i):
+            fn(row_at(i, step))
+
+    return wrap
+
+
+def middle_kernel(
+    ho_ref,
+    ow_ref,
+    x_ref,
+    n_ref,
+    ww_ref,
+    dw_ref,
+    dm_ref,
+    attn_ref,
+    res_ref,
+    rg_ref,
+    vec_ref,
+    mp_ref,
+    dg_ref,
+    h_ref,
+    big,
+    cloc,
+    c_ref,
+    hid,
+    act,
+    part,
+    second,
+    load,
+    *scratch,
+):
+    s, f, z, y = where_am_i()
+    rows, width = x_ref.shape
+    lf = dw_ref.shape[0]
+    lw = ho_ref.shape[2]
+    fetch = pltpu.make_async_copy(ow_ref, big, load)
+    fetch.start()
+    greet_columns(s, f)
+    gather = SeqGather(cloc, c_ref, *scratch[:5])
+    reduce = SeqReduce(part, second, *scratch[5:11])
+    sums = ColSum(big, h_ref, *scratch[11:])
+    gain, shift = n_ref[2:3], n_ref[3:4]
+    fetch.wait()
+
+    @pl.loop(0, width // 512)
+    def _(j):
+        cols = pl.ds(pl.multiple_of(j * 512, 512), 512)
+        total = dot(ho_ref[0], big[0:lw, cols])
+        for k in range(1, 8):
+            total = total + dot(ho_ref[k], big[k * lw : k * lw + lw, cols])
+        attn_ref[:, cols] = total
+        res_ref[:, cols] = x_ref[:, cols].astype(jnp.float32) + total
+
+    @tall(rows)
+    def _(r):
+        normed, _ = normalize(res_ref[r])
+        cloc[r] = (normed * gain + shift).astype(jnp.bfloat16)
+
+    gather.start()
+    gather.own.wait()
+
+    def block(b):
+        at = pl.ds(pl.multiple_of(b * rows, rows), rows)
+        wide = dot(c_ref[b], ww_ref[...])
+        gate, upper = wide[:, :lf], wide[:, lf:]
+        hidden, sigma = mlp_forward(gate, upper)
+        hid[at] = hidden
+        grad = dot(dm_ref[b], dw_ref[...], 1, 1)
+        gate_act, up_act = mlp_backward(grad, gate, upper, sigma)
+        act[at] = jnp.concatenate([gate_act, up_act], 1)
+        part[b] = dot(act[at], ww_ref[...], 1, 1).astype(jnp.bfloat16)
+
+    gather.each(block)
+    reduce.start()
+
+    def wide_grad(i):
+        left = [c_ref[b, :, i * 256 : i * 256 + 256] for b in range(8)]
+        left = jnp.concatenate(left, 0)
+        big[i * 256 : i * 256 + 256, 0 : 2 * lf] = dot(left, act[...], 0, 0).astype(jnp.bfloat16)
+        sums.send(i)
+
+    def mlp_part(i):
+        @pl.loop(2 * i, 2 * i + 2)
+        def _(b):
+            at = pl.ds(pl.multiple_of(b * rows, rows), rows)
+            mp_ref[b] = dot(hid[at], dw_ref[...]).astype(jnp.bfloat16)
+
+    def down_grad(i):
+        cols = slice(i * 256, i * 256 + 256)
+        right = jnp.concatenate([dm_ref[b, :, cols] for b in range(8)], 0)
+        dg_ref[:, cols] = dot(hid[...], right, 0, 0).astype(jnp.bfloat16)
+
+    p = functools.partial
+    work = []
+    for i in range(8):
+        work.append(p(wide_grad, i))
+        if i:
+            work.append(p(sums.step, i - 1))
+    work += [p(mlp_part, 0), p(sums.step, 7)] + [p(mlp_part, i) for i in (1, 2, 3)]
+    work += [p(down_grad, i) for i in range(8)]
+    later = reduce.steps()
+    for item in merged(work, later[:6]):
+        item()
+    for item in merged([p(sums.total, i) for i in range(8)], later[6:]):
+        item()
+    vec_ref[...] = jnp.zeros_like(vec_ref)
+
+    @tall(rows)
+    def _(r):
+        grad = second[r]
+        normed, rstd = normalize(res_ref[r])
+        inner, gain_part, shift_part = norm_back(grad, normed, rstd, gain)
+        rg_ref[r] = dm_ref[s, r].astype(jnp.float32) + inner
+        vec_ref[0:1] += gain_part[None]
+        vec_ref[1:2] += shift_part[None]
+
+    gather.finish(False)
+    reduce.finish()
+    sums.finish()
+
+
+def middle(heads_out, out_w, x, norms, wide_w, down_w, dm, collective):
+    rows, width = x.shape
+    lf = down_w.shape[0]
+    group = 8 * rows
+    part = width // 32
+
+    def out(shape, dtype=jnp.bfloat16):
+        return jax.ShapeDtypeStruct(shape, dtype)
+
+    def vm(shape, dtype=jnp.bfloat16):
+        return pltpu.VMEM(shape, dtype)
+
+    wide = (rows, width)
+    return pl.pallas_call(
+        middle_kernel,
+        out_shape=(
+            out(wide, jnp.float32),
+            out(wide, jnp.float32),
+            out(wide, jnp.float32),
+            out((8, width), jnp.float32),
+            out((8,) + wide),
+            out((lf, width)),
+            out((8, part, 2 * lf)),
+        ),
+        in_specs=[VMEM_SPEC, ANY_SPEC] + [VMEM_SPEC] * 5,
+        out_specs=(VMEM_SPEC,) * 7,
+        scratch_shapes=[
+            vm((width, width)),
+            vm(wide),
+            vm((8,) + wide),
+            vm((group, lf)),
+            vm((group, 2 * lf)),
+            vm((8,) + wide),
+            vm(wide, jnp.float32),
+            DMA,
+        ]
+        + SeqGather.scratch()
+        + SeqReduce.scratch(rows, width)
+        + ColSum.scratch(part, 2 * lf),
+        compiler_params=comm_params(collective, 63),
+    )(heads_out, out_w, x, norms, wide_w, down_w, dm)
 
 
 def backward_kernel(
+    rg_ref,
+    or_ref,
+    mix_ref,
     pk_ref,
-    do_ref,
     lse_ref,
     c_ref,
     s1_ref,
@@ -1457,12 +1569,26 @@
     orow_ref,
     ocol_ref,
     len_ref,
-    p_ref,
-    wg_ref,
+    attn_ref,
+    res_ref,
+    valid_ref,
+    mp_ref,
+    dg_ref,
+    h_ref,
     g_ref,
     b_ref,
-    o_ref,
-    wo_ref,
+    lo_ref,
+    sum_ref,
+    gate_ref,
+    up_ref,
+    down_ref,
+    out_ref,
+    da,
+    full,
+    do_ref,
+    og,
+    mlp,
+    got,
     dpk,
     dq,
     dk,
@@ -1471,9 +1597,41 @@
     *scratch,
 ):
     s, f, z, y = where_am_i()
+    rows, width = rg_ref.shape
+    part, ff = gate_ref.shape
+    lf = ff // 8
     greet_columns(s, f)
-    reduce = SeqReduce(p_ref, o_ref, *scratch[:13])
-    slices = ColReduce(wg_ref, wo_ref, *scratch[13:])
+    gather = SeqGather(da, full, *scratch[:5])
+    reduce = SeqReduce(mp_ref, mlp, *scratch[5:11])
+    swap = RowExchange(h_ref, got, *scratch[11:14])
+    down = FsdpReduce(dg_ref, down_ref, *scratch[14:18])
+    outer_sum = FsdpReduce(og, out_ref, *scratch[18:])
+
+    @tall(rows)
+    def _(r):
+        da[r] = rg_ref[r].astype(jnp.bfloat16)
+
+    gather.start()
+    down.start()
+    gather.own.wait()
+    down.step()
+
+    def block(b):
+        at = pl.ds(pl.multiple_of(b * rows, rows), rows)
+        do_ref[at] = dot(full[b], or_ref[...], 1, 1).astype(jnp.bfloat16)
+
+    gather.each(block)
+    reduce.start()
+    swap.start()
+
+    def out_grad(i):
+        cols = slice(i * 256, i * 256 + 256)
+        right = jnp.concatenate([full[b, :, cols] for b in range(8)], 0)
+        value = dot(mix_ref[...], right, 0, 0).astype(jnp.bfloat16)
+        for k in range(4):
+            og[k, :, cols] = value[k * part : k * part + part]
+
+    p = functools.partial
     work = attend_back(
         pk_ref,
         do_ref,
@@ -1490,111 +1648,242 @@
         dv,
         gpk,
     )
-    reduce.start()
-    slices.start()
-    for item in merged(work, slices.steps()[:8]):
+    work += [p(out_grad, i) for i in range(8)] + [outer_sum.start, outer_sum.step, down.total]
+    later = reduce.steps()
+    for item in merged(work, later[:4]):
         item()
-    for item in merged(reduce.steps(), slices.steps()[8:]):
+    for item in later[4:]:
         item()
+    outer_sum.total()
+    sum_ref[...] = jnp.zeros_like(sum_ref)
+
+    @tall(rows)
+    def _(r):
+        m = mlp[r]
+        result = res_ref[r] + m
+        lo_ref[r] = result.astype(jnp.bfloat16)
+        keep = valid_ref[r]
+        for n, v in enumerate((result, attn_ref[r], m)):
+            total = jnp.sum(jnp.sum(v * v, -1, keepdims=True) * keep, 0, keepdims=True)
+            sum_ref[n : n + 1] += jnp.broadcast_to(total, (1, 128))
+
+    swap.finish()
+    for n, ref in enumerate((gate_ref, up_ref)):
+        for i in range(8):
+            ref[:, i * lf : i * lf + lf] = got[i, :, n * lf : n * lf + lf].astype(jnp.float32)
+    gather.finish(False)
     reduce.finish()
-    slices.finish()
-
-
-def attention_backward(pk, do, lse, tables, orow, ocol, lengths, partial, wide_grad, collective):
-    rows, w = do.shape
+    down.finish()
+    outer_sum.finish()
+
+
+def backward(
+    rg, out_rows, mixed, pk, lse, tables, orow, ocol, lengths, attn, res, keep, mp, dg, h, collective
+):
+    rows, width = rg.shape
+    group, w = mixed.shape
     valid = pk.shape[0]
-    width = partial.shape[2]
-
-    def acc(c):
-        return pltpu.VMEM((valid, c), jnp.float32)
+    part = h.shape[1]
+    ff = h.shape[2] * 4
+
+    def out(shape, dtype=jnp.float32):
+        return jax.ShapeDtypeStruct(shape, dtype)
+
+    def vm(shape, dtype=jnp.bfloat16):
+        return pltpu.VMEM(shape, dtype)
 
     return pl.pallas_call(
         backward_kernel,
         out_shape=(
-            jax.ShapeDtypeStruct((rows, 3 * w), jnp.bfloat16),
-            jax.ShapeDtypeStruct((1, 3 * w), jnp.float32),
-            jax.ShapeDtypeStruct((rows // 8, width), jnp.float32),
-            jax.ShapeDtypeStruct((8,) + wide_grad.shape[2:], jnp.bfloat16),
+            out((group, 3 * w), jnp.bfloat16),
+            out((1, 3 * w)),
+            out((rows, width), jnp.bfloat16),
+            out((8, 128)),
+            out((part, ff)),
+            out((part, ff)),
+            out(dg.shape[1:]),
+            out((part, width)),
         ),
-        in_specs=[VMEM_SPEC] * 8 + [SMEM_SPEC] + [ANY_SPEC] * 2,
-        out_specs=(VMEM_SPEC,) * 4,
+        in_specs=[VMEM_SPEC] * 10 + [SMEM_SPEC] + [VMEM_SPEC] * 6,
+        out_specs=(VMEM_SPEC,) * 8,
         scratch_shapes=[
-            pltpu.VMEM((valid, w), jnp.bfloat16),
-            acc(w),
-            acc(w),
-            acc(w),
-            pltpu.VMEM((valid, 3 * w), jnp.bfloat16),
+            vm((rows, width)),
+            vm((8, rows, width)),
+            vm((group, w)),
+            vm((4, part, width)),
+            vm((rows, width), jnp.float32),
+            vm(h.shape),
+            vm((valid, w)),
+            vm((valid, w), jnp.float32),
+            vm((valid, w), jnp.float32),
+            vm((valid, w), jnp.float32),
+            vm((valid, 3 * w)),
         ]
-        + SeqReduce.scratch(rows // 8, width)
-        + ColReduce.scratch(*wide_grad.shape[2:]),
-        compiler_params=comm_params(collective, 56),
-    )(pk, do, lse, *tables, orow, ocol, lengths, partial, wide_grad)
-
-
-def last_kernel(p_ref, wg_ref, o_ref, wo_ref, *scratch):
+        + SeqGather.scratch()
+        + SeqReduce.scratch(rows, width)
+        + RowExchange.scratch()
+        + FsdpReduce.scratch(*dg.shape[1:])
+        + FsdpReduce.scratch(part, width),
+        compiler_params=comm_params(collective, 60),
+    )(rg, out_rows, mixed, pk, lse, *tables, orow, ocol, lengths, attn, res, keep, mp, dg, h)
+
+
+def last_kernel(
+    g_ref,
+    b_ref,
+    qw_ref,
+    a_ref,
+    x_ref,
+    rg_ref,
+    n_ref,
+    vec_ref,
+    sum_ref,
+    ig_ref,
+    qg_ref,
+    total_ref,
+    part,
+    first,
+    grad,
+    h,
+    got,
+    msg,
+    inbox,
+    vec,
+    msend,
+    mrecv,
+    *scratch,
+):
     s, f, z, y = where_am_i()
-    greet_columns(s, f)
-    reduce = SeqReduce(p_ref, o_ref, *scratch[:13])
-    slices = ColReduce(wg_ref, wo_ref, *scratch[13:])
-    reduce.start()
-    slices.start()
-    for item in slices.steps()[:8]:
+    me = s * 4 + f
+    rows, width = x_ref.shape
+    w3 = g_ref.shape[1]
+    w = w3 // 3
+    pr = qg_ref.shape[0]
+    greet_all(s, f)
+    reduce = SeqReduce(part, first, *scratch[:6])
+    sums = ColSum(grad, h, *scratch[6:12])
+    swap = RowExchange(h, got, *scratch[12:])
+
+    def block(b):
+        at = pl.ds(pl.multiple_of(b * rows, rows), rows)
+        part[b] = dot(g_ref[at], qw_ref[...], 1, 1).astype(jnp.bfloat16)
+
+    for k in range(4):
+        block(2 * reduce.order(k) + 1 - y)
+        reduce.send(k)
+
+    def own_block(k):
+        block(2 * reduce.order(k) + y)
+
+    def qkv_grad(i):
+        left = [a_ref[b, :, i * 256 : i * 256 + 256] for b in range(8)]
+        left = jnp.concatenate(left, 0)
+        grad[i * 256 : i * 256 + 256] = dot(left, g_ref[...], 0, 0).astype(jnp.bfloat16)
+        sums.send(i)
+
+    p = functools.partial
+    for k in range(4):
+        own_block(k)
+    work = []
+    for i in range(8):
+        work.append(p(qkv_grad, i))
+        if i:
+            work.append(p(sums.step, i - 1))
+    work.append(p(sums.step, 7))
+
+    def hand_over(k):
+        sums.total(peer(s, k))
+        if k:
+            swap.piece(k).start()
+        else:
+            swap.mine.start()
+
+    work += [p(hand_over, k) for k in reversed(range(8))]
+    for item in merged(work, reduce.steps()):
         item()
-    for item in merged(reduce.steps(), slices.steps()[8:]):
-        item()
+    vec[0:2] = jnp.zeros((2, width), jnp.float32)
+    vec[2:4] = vec_ref[0:2]
+    gain = n_ref[0:1]
+
+    @tall(rows)
+    def _(r):
+        normed, rstd = normalize(x_ref[r].astype(jnp.float32))
+        inner, gain_part, shift_part = norm_back(first[r], normed, rstd, gain)
+        ig_ref[r] = rg_ref[r] + inner
+        vec[0:1] += gain_part[None]
+        vec[1:2] += shift_part[None]
+
+    lane = lax.broadcasted_iota(jnp.int32, (1, 128), 1)
+    scalars = jnp.where(lane == 0, sum_ref[0:1], jnp.where(lane == 1, sum_ref[1:2], sum_ref[2:3]))
+    for i in range(16):
+        cols = slice(i * 128, i * 128 + 128)
+        msg[i, 0:4] = vec[0:4, cols]
+        msg[i, 4:5] = scalars
+        at = (i % 2) * 128
+        for n in range(3):
+            piece = b_ref[0:1, n * w + at : n * w + at + 128]
+            msg[i, 5 + n : 6 + n] = jnp.where(s == i // 2, piece, jnp.zeros_like(piece))
+
+    def message(k):
+        i = (me + k) % 32
+        return remote(msg.at[i // 2], inbox.at[k], msend.at[k], mrecv.at[k], dealer(i))
+
+    @pl.loop(1, 32)
+    def _(k):
+        message(k).start()
+
+    swap.finish()
+    for i in range(8):
+        for n in range(3):
+            at = n * width + i * w
+            qg_ref[:, at : at + w] = got[i, :, n * w : n * w + w].astype(jnp.float32)
     reduce.finish()
-    slices.finish()
-
-
-def last_reduce(partial, grad, collective):
-    _, rows, width = partial.shape
+    sums.finish()
+    total_ref[...] = msg[me // 2]
+
+    @pl.loop(1, 32)
+    def _(k):
+        message(k).wait_recv()
+        total_ref[...] += inbox[k]
+
+    @pl.loop(1, 32)
+    def _(k):
+        message(k).wait_send()
+
+
+def last(g, b, qkv_w, a, x, rg, norms, vec, sums, collective):
+    rows, width = x.shape
+    w3 = g.shape[1]
+    pr = width // 32
+
+    def out(shape, dtype=jnp.float32):
+        return jax.ShapeDtypeStruct(shape, dtype)
+
+    def vm(shape, dtype=jnp.bfloat16):
+        return pltpu.VMEM(shape, dtype)
+
     return pl.pallas_call(
         last_kernel,
-        out_shape=(
-            jax.ShapeDtypeStruct((rows, width), jnp.float32),
-            jax.ShapeDtypeStruct((8,) + grad.shape[2:], jnp.bfloat16),
-        ),
-        in_specs=[ANY_SPEC] * 2,
-        out_specs=(VMEM_SPEC,) * 2,
-        scratch_shapes=SeqReduce.scratch(rows, width) + ColReduce.scratch(*grad.shape[2:]),
-        compiler_params=comm_params(collective),
-    )(partial, grad)
-
-
-def sum_kernel(x_ref, o_ref, got, send, recv):
-    s, f, z, y = where_am_i()
-    me = s * 4 + f
-    greet_all(s, f)
-
-    def piece(k):
-        i = (me + k) % 32
-        return remote(x_ref.at[i], got.at[k], send.at[k], recv.at[k], dealer(i))
-
-    @pl.loop(1, 32)
-    def _(k):
-        piece(k).start()
-
-    @pl.loop(1, 32)
-    def _(k):
-        piece(k).wait_recv()
-        piece(k).wait_send()
-
-    o_ref[...] = x_ref[me]
-
-    @pl.loop(1, 32)
-    def _(k):
-        o_ref[...] += got[k]
-
-
-def sum_parts(x, collective):
-    return pl.pallas_call(
-        sum_kernel,
-        out_shape=jax.ShapeDtypeStruct(x.shape[1:], x.dtype),
-        in_specs=[VMEM_SPEC],
-        out_specs=VMEM_SPEC,
-        scratch_shapes=[pltpu.VMEM(x.shape, x.dtype), DMA((32,)), DMA((32,))],
-        compiler_params=comm_params(collective),
-    )(x)
+        out_shape=(out((rows, width)), out((pr, 3 * width)), out((8, 128))),
+        in_specs=[VMEM_SPEC] * 9,
+        out_specs=(VMEM_SPEC,) * 3,
+        scratch_shapes=[
+            vm((8, rows, width)),
+            vm((rows, width), jnp.float32),
+            vm((width, w3)),
+            vm((8, pr, w3)),
+            vm((8, pr, w3)),
+            vm((16, 8, 128), jnp.float32),
+            vm((32, 8, 128), jnp.float32),
+            vm((4, width), jnp.float32),
+            DMA((32,)),
+            DMA((32,)),
+        ]
+        + SeqReduce.scratch(rows, width)
+        + ColSum.scratch(pr, w3)
+        + RowExchange.scratch(),
+        compiler_params=comm_params(collective, 56),
+    )(g, b, qkv_w, a, x, rg, norms, vec, sums)
 
 
 def rotary_tables(rel):
@@ -1632,8 +1921,6 @@
     ff = gate_weight.shape[1]
     lf = ff // nseq
     seq_at, fsdp_at = lax.axis_index("seq"), lax.axis_index("fsdp")
-    stream = hidden_in[0].astype(jnp.float32)
-    cotangent = out_grad[0].astype(jnp.float32)
     order = deal_order[0]
     lengths = seq_lengths[0]
     group_rows = order.shape[0]
@@ -1655,107 +1942,60 @@
     params = jnp.pad(params.astype(jnp.float32), ((0, 1), (0, 64)))
     params = jnp.where(fsdp_at % 2 == 0, params, jnp.roll(params, part, 1))
     qkv_parts = qkv_weight.reshape(part, 3, nseq, lw).transpose(2, 0, 1, 3).reshape(nseq, part, -1)
-    first_in, qkv_w, norms, out_w = entry(hidden_in[0], params, qkv_parts, out_weight, 1)
-    first_in = first_in.reshape(group_rows, width)
-    qkv_w = qkv_w.reshape(width, 3 * lw)
-    gain1, shift1, gain2, shift2 = norms[:4]
-    qkv_shift = lax.dynamic_slice_in_dim(norms[4:7], seq_at * lw, lw, 1).reshape(1, -1)
-    normed1, rstd1 = normalize(stream)
-    heads_out, packed, lse, mlp_grad, wide_w, down_w, mixed = attention_forward(
-        first_in,
-        qkv_w,
-        qkv_shift,
+    first_in, qkv_w, norms, out_w, heads_out, packed, lse, mlp_grad, wide_w, down_w, mixed = forward(
+        hidden_in[0],
+        params,
+        qkv_parts,
+        out_weight,
+        out_grad[0],
+        column_parts([gate_weight, up_weight]),
+        down_weight,
         dealt_tables,
         orow,
         ocol,
         seq_lengths,
         valid_rows,
-        out_grad[0],
-        column_parts([gate_weight, up_weight]),
-        down_weight,
-        2,
-    )
-    mixed = mixed.reshape(group_rows, lw)
-    heads_out = heads_out.transpose(1, 0, 2).reshape(rows, width)
-    wide_w = wide_w.reshape(width, 2 * lf)
-    mlp_grad = mlp_grad.reshape(group_rows, width)
+        1,
+    )
     out_rows = lax.dynamic_slice_in_dim(out_w, seq_at * nfsdp, nfsdp).reshape(lw, width)
-    out_w = out_w.reshape(width, width)
-    down_w = down_w.reshape(lf, width)
-    attn = times(heads_out, out_w)
-    resid = stream + attn
-    normed2, rstd2 = normalize(resid)
-    second_local = (normed2 * gain2 + shift2).astype(jnp.bfloat16)
-    second_in = gather_rows_line(second_local, 3).reshape(group_rows, width)
-    wide = times(second_in, wide_w)
-    gate, upper = wide[:, :lf], wide[:, lf:]
-    hidden, sigma = mlp_forward(gate, upper)
-    hidden_grad = times_transposed(mlp_grad, down_w)
-    wide_act = jnp.concatenate(mlp_backward(hidden_grad, gate, upper, sigma), 1)
-    second_part = times_transposed(wide_act, wide_w).astype(jnp.bfloat16)
-    second_grad = reduce_rows_line(second_part.reshape(nseq, rows, width), 4)
-    resid_part, gain2_grad, shift2_grad = norm_back(second_grad, normed2, rstd2, gain2)
-    resid_grad = cotangent + resid_part
-    attn_grad = gather_rows_line(resid_grad.astype(jnp.bfloat16), 5).reshape(group_rows, width)
-    mixed_grad = times_transposed(attn_grad, out_rows).astype(jnp.bfloat16)
-
-    def row_shard(left, right):
-        grad = outer(left, right).astype(jnp.bfloat16)
-        return lax.psum_scatter(grad, "fsdp", scatter_dimension=0, tiled=True).astype(jnp.float32)
-
-    def column_parts_grad(left, right):
-        return outer(left, right).astype(jnp.bfloat16).reshape(nseq, nfsdp, part, -1)
-
-    down_grad = row_shard(hidden, mlp_grad)
-    mlp_part = times(hidden, down_w).astype(jnp.bfloat16).reshape(nseq, rows, width)
-    qkv_act, bias_sums, mlp, wide_grad = attention_backward(
+    attn, resid, resid_grad, norm2_grads, mlp_part, down_part, wide_sum = middle(
+        heads_out,
+        out_w.reshape(width, width),
+        hidden_in[0],
+        norms,
+        wide_w,
+        down_w.reshape(lf, width),
+        mlp_grad,
+        3,
+    )
+    qkv_act, bias_sums, result, sums, gate_grad, up_grad, down_grad, out_grad_w = backward(
+        resid_grad,
+        out_rows,
+        mixed.reshape(group_rows, lw),
         packed,
-        mixed_grad,
         lse,
         packed_tables,
         orow,
         ocol,
         seq_lengths,
+        attn,
+        resid,
+        valid,
         mlp_part,
-        column_parts_grad(second_in, wide_act),
-        6,
-    )
-    result = resid + mlp
-    out_grad_w = row_shard(mixed, attn_grad)
-    first_part = times_transposed(qkv_act, qkv_w).astype(jnp.bfloat16)
-    first_grad, qkv_grad = last_reduce(
-        first_part.reshape(nseq, rows, width), column_parts_grad(first_in, qkv_act), 7
-    )
-    input_part, gain1_grad, shift1_grad = norm_back(first_grad, normed1, rstd1, gain1)
-    input_grad = resid_grad + input_part
-    wide_grad = wide_grad.astype(jnp.float32)
-    gate_grad = wide_grad[:, :, :lf].transpose(1, 0, 2).reshape(part, ff)
-    up_grad = wide_grad[:, :, lf:].transpose(1, 0, 2).reshape(part, ff)
-    qkv_grad = qkv_grad.astype(jnp.float32).reshape(nseq, part, 3, lw)
-    qkv_grad = qkv_grad.transpose(1, 2, 0, 3).reshape(part, 3 * width)
-
-    vectors = jnp.stack([gain1_grad, shift1_grad, gain2_grad, shift2_grad])
-    vectors = vectors.reshape(4, nseq * nfsdp, part).transpose(1, 0, 2).reshape(-1, 2, 128)
-    sums = jnp.stack(
-        [
-            jnp.sum(valid * result * result),
-            jnp.sum(valid * attn * attn),
-            jnp.sum(valid * mlp * mlp),
-        ]
-    )
-    sums = jnp.broadcast_to(jnp.pad(sums, (0, 125)), (nseq * nfsdp, 1, 128))
-    bias = bias_sums.reshape(3, nfsdp, part).transpose(1, 0, 2).reshape(nfsdp, 3 * part)
-    bias = jnp.pad(bias, ((0, 0), (0, 64))).reshape(1, nfsdp, 2, 128)
-    here = (jnp.arange(nseq) == seq_at)[:, None, None, None]
-    bias = jnp.where(here, bias, 0.0).reshape(-1, 2, 128)
-    message = jnp.concatenate([vectors, sums, bias, jnp.zeros_like(vectors), sums], 1)
-    total = sum_parts(message, 8)
+        down_part.reshape(nfsdp, -1, width),
+        wide_sum,
+        4,
+    )
+    input_grad, qkv_grad, total = last(
+        qkv_act, bias_sums, qkv_w, first_in, hidden_in[0], resid_grad, norms, norm2_grads, sums, 5
+    )
     count = valid_rows * nfsdp * width
-    rms = jnp.sqrt(total[2, :3] / count)
-    shards = total[:2].reshape(4, part)
-    qkv_bias_grad = total[3:5].reshape(4, part)[:3]
+    rms = jnp.sqrt(total[4, :3] / count)
+    halves = lax.dynamic_slice_in_dim(total, (fsdp_at % 2) * part, part, 1)
+    shards = halves[:4]
+    qkv_bias_grad = halves[5:8]
     return (
-        result.astype(jnp.bfloat16)[None],
+        result[None],
         input_grad[None],
         shards[0],
         shards[1],

time: 653 us -> 588 us (0.900)
  matrix products: 68.8 us -> 0 us
  Pallas kernels: 501 us -> 540 us
  other arithmetic: 26.3 us -> 10.7 us
  between operations: 14.8 us -> 1.39 us
  local copies, waits for them, and re-layouts: 38.7 us -> 27.2 us
    dot_general x11 -> x0, matrix products: 68.8 us -> none  [the longest x4 26.4 us: times_transposed(): lax.dot_general(left, right, (((1,), (1,)), ((), ())), preferred_element_...]
    pallas_call x8 -> x4, Pallas kernels: 501 us -> 540 us  [the longest x1 206 us: forward(): pl.pallas_call(forward_kernel, out_shape=(out((8, rows, width)), out((wid...]
    reshape x10 -> x0, local copies, waits for them, and re-layouts: 11 us -> none  [the longest x2 4.44 us: line_body(): qkv_grad = qkv_grad.transpose(1, 2, 0, 3).reshape(part, 3 * width)]
    transpose x4 -> x0, local copies, waits for them, and re-layouts: 7.79 us -> none  [the longest x2 3.86 us: line_body(): up_grad = wide_grad[:, :, lf:].transpose(1, 0, 2).reshape(part, ff)]
    unnamed x64 -> x48, local copies, waits for them, and re-layouts: 8.97 us -> 14.4 us
  transfers between devices with their start and end apart: 2 -> 0, of which waited for: 0 -> 0; matrix products, arithmetic and copies ran while one was open for 12% -> 0% of each run, Pallas kernels for 24% -> 0%
where the time goes in v4:
time: 588 us; the launch traced here: 579 us
  Pallas kernels  540 us (92%)
  local copies, waits for them, and re-layouts  27.2 us (5%)
  other arithmetic  10.7 us (2%)
    pallas_call x1, Pallas kernels, forward(): pl.pallas_call(forward_kernel, out_shape=(out((8, rows, width)), out((wid...  206 us
    pallas_call x1, Pallas kernels, middle(): pl.pallas_call(middle_kernel, out_shape=(out(wide, jnp.float32), out(wide...  128 us
    pallas_call x1, Pallas kernels, backward(): pl.pallas_call(backward_kernel, out_shape=(out((group, 3 * w), jnp.bfloat...  118 us
    pallas_call x1, Pallas kernels, last(): pl.pallas_call(last_kernel, out_shape=(out((rows, width)), out((pr, 3 * w...  87.1 us
    unnamed x48, local copies, waits for them, and re-layouts  14.4 us

profile of v4, /device:TPU:0, one launch (start us, length us, event | category | flops | bytes accessed | tf_op | source)
XLA Modules:
  0.0 578.9 jit_solution(6530206160229937090)
XLA Ops:
  0.6 0.0 copy-start.9
  0.7 0.0 copy-start.17
  0.7 0.8 stack.20
  1.5 0.1 pad_select_fusion.p_ref
  1.6 0.8 reduce-window.4
  2.4 0.8 convert_reduce_fusion
  3.2 0.1 pad_add_fusion
  3.3 0.1 select_reduce_fusion
  3.4 0.7 fusion.8
  4.1 3.0 fusion
  7.1 0.0 copy-done.9
  7.1 0.2 copy.38.ocol_ref
  7.3 0.0 copy-done.17
  7.4 0.0 copy-start.1
  7.4 0.7 reshape.138
  8.0 0.1 copy.36
  8.2 1.9 reshape.139
  10.1 0.1 copy.37
  10.2 0.0 copy-start.16
  10.2 1.6 maximum_bitcast_fusion.wp_ref
  11.8 0.0 copy-done.16
  11.8 0.2 copy.41
  11.9 0.0 copy-start
  11.9 0.0 copy-start.8
  12.0 0.0 copy-start.10
  12.0 1.4 copy.43
  13.3 2.6 reshape.137.qp_ref
  15.9 0.0 copy-done.1
  15.9 0.0 copy-done
  16.0 0.0 copy-done.8
  16.0 0.0 copy-done.10
  16.0 0.0 copy-start.2
  16.0 1.0 copy-done.2
  17.0 1.1 copy-done.3
  18.1 1.0 copy-done.4
  19.2 206.5 %shard_map.237 = (bf16[8,128,2048]{2,1,0:T(8,128)(2,1)}, bf16[2048,768]{1,0:T(8,128)(2,1)}, f32[8,2048]{1,0:T(8,128)S(1)}, bf16[32,64,2048]{2,1,0:T(8,128)(2,1)}...) custom-call(bf16[128,2048]{1,0:T(8,128)(2,1)S(1)} %bitcast.42, ...), custom_call_target="tpu_custom_call" | custom-call | tf_op jit(solution)/shard_map/pallas_call | solution.py:1353
  225.6 0.0 copy-start.5
  225.7 0.8 copy-done.5
  226.4 0.8 copy-done.6
  227.2 0.6 copy-done.7
  227.9 128.4 %shard_map.238 = (f32[128,2048]{1,0:T(8,128)}, f32[128,2048]{1,0:T(8,128)}, f32[128,2048]{1,0:T(8,128)}, f32[8,2048]{1,0:T(8,128)}, bf16[8,128,2048]{2,1,0:T(8,1...) custom-call(bf16[8,128,256]{2,1,0:T(8,128)(2,1)} %copy-done.6, bf16[2048,2048]{1,0:T(8,128)(2,1)} %bitcast.49, ...), custom_call_target="tpu_custom_call" | custom-call | tf_op jit(solution)/shard_map/pallas_call | solution.py:1530
  356.3 2.3 constant_dynamic-slice_fusion.2
  358.6 0.1 convert_reduce_fusion.1
  358.7 0.1 select_reduce_fusion.1
  358.8 2.2 fusion.4
  360.9 0.7 copy.40.valid_ref
  361.7 117.7 %shard_map.239 = (bf16[1024,768]{1,0:T(8,128)(2,1)}, f32[1,768]{1,0:T(1,128)}, bf16[128,2048]{1,0:T(8,128)(2,1)}, f32[8,128]{1,0:T(8,128)}, f32[64,5632]{1,0:T(8...) custom-call(f32[128,2048]{1,0:T(8,128)} %get-tuple-element.48.rg_ref, ...), custom_call_target="tpu_custom_call" | custom-call | tf_op jit(solution)/shard_map/pallas_call | solution.py:1695
  479.4 0.0 copy-start.19
  479.4 87.1 %shard_map.240 = (f32[128,2048]{1,0:T(8,128)}, f32[64,6144]{1,0:T(8,128)}, f32[8,128]{1,0:T(8,128)}) custom-call(bf16[1024,768]{1,0:T(8,128)(2,1)} %get-tuple-element.58.g_ref, f32[1,768]{1,0:T(1,128)} %get-tuple-element.59.b_ref, bf16[2048,768]{1,0:T(8,128)(2,1)} %get-tuple-element.60.qw_ref, bf16[8,128,2048]{2,1,0:T(8,128)(2,1)} %get-tuple-element.61.a_ref, ...), custom_call_target="tpu_custom_call" | custom-call | tf_op jit(solution)/shard_map/pallas_call | solution.py:1865
  566.5 0.0 copy-start.15
  566.5 0.8 constant_dynamic-slice_fusion
  567.3 0.5 slice_bitcast_fusion
  567.9 0.6 slice.42
  568.4 1.2 sqrt_bitcast_fusion
  569.7 0.8 copy.51
  570.5 1.0 copy.52
  571.4 1.1 copy.53
  572.6 0.2 copy-done.18
  572.8 0.8 copy.54
  573.6 1.1 copy.55
  574.7 0.8 copy-done.13
  575.5 1.1 copy.56
  576.6 0.8 copy-done.12
  577.4 1.1 copy.57
  (20 shorter events, 0.1 us)
Async XLA Ops:
  0.6 6.5 %copy-start.9 = (s32[1,1024]{1,0:T(1,128)S(1)}, s32[1,1024]{1,0:T(1,128)}, u32[]{:S(2)}) copy-start(s32[1,1024]{1,0:T(1,128)} %orow_ref.3) | copy-start | bytes 12292
  0.7 6.7 %copy-start.17 = (bf16[64,5632]{1,0:T(8,128)(2,1)S(1)}, bf16[64,5632]{1,0:T(8,128)(2,1)}, u32[]{:S(2)}) copy-start(bf16[64,5632]{1,0:T(8,128)(2,1)} %param.22) | copy-start | bytes 2162692
  7.4 8.6 %copy-start.1 = (s32[1024,1]{1,0:T(8,128)}, s32[1024,1]{1,0:T(8,128)S(1)}, u32[]{:S(2)}) copy-start(s32[1024,1]{1,0:T(8,128)S(1)} %copy.38.ocol_ref) | copy-start | bytes 12292
  10.2 1.6 copy-start.16
  11.9 4.0 copy-start
  11.9 4.0 copy-start.8
  12.0 4.0 copy-start.10
  16.0 1.0 copy-start.2
  17.0 1.1 copy-start.3
  18.1 1.0 copy-start.4
  225.6 0.8 copy-start.5
  226.4 0.8 copy-start.6
  227.2 0.6 copy-start.7
  479.4 90.3 %copy-start.19 = (bf16[128,2048]{1,0:T(8,128)(2,1)S(1)}, bf16[128,2048]{1,0:T(8,128)(2,1)}, u32[]{:S(2)}) copy-start(bf16[128,2048]{1,0:T(8,128)(2,1)} %get-tuple-element.57) | copy-start | bytes 1572868
  566.5 4.0 copy-start.15
  569.7 1.8 copy-start.11
  571.4 1.4 copy-start.18
  571.4 2.2 copy-start.14
  573.6 1.9 copy-start.13
  575.5 1.9 copy-start.12

commit v5 on v4

--- a/solution.py
+++ b/solution.py
@@ -491,6 +491,10 @@
         self.ysend(zb, self.o.at[b]).start()
         return b
 
+    def column(self, i):
+        b = self.at(self.near(i))
+        return b
+
     def cross(self, i):
         b = 2 * self.near(i) + 1 - self.y
         self.arrived(b).wait_recv()
@@ -505,9 +509,14 @@
             i = (j + 1) // 2
             column = (j == 0) | ((j % 2 == 1) & (j < 7))
 
-            @pl.when(column & (j > 0))
+            @pl.when(j == 1)
             def _():
-                self.arrive(i)
+                self.arrive(1)
+                self.arrive(2)
+
+            @pl.when(j == 4)
+            def _():
+                self.arrive(3)
 
             other = jnp.where(j == 7, 3, j // 2 - 1)
 
@@ -699,11 +708,13 @@
         then = [functools.partial(self.xstep, k) for k in (0, 7, 6, 5, 4, 3, 2, 1)]
         return first + then
 
-    def finish(self):
+    def complete(self):
         self.mine.wait()
         for k in range(8):
             self.arrived(k, self.fc).wait_recv()
             self.arrived(k, self.fd).wait_recv()
+
+    def finish(self):
         for k in range(8):
             if k:
                 self.send_direct(k).wait_send()
@@ -1004,6 +1015,26 @@
             self.piece(k).wait_send()
 
 
+def idle():
+    pass
+
+
+def perform(plan, queues):
+    left = {name: list(items) for name, items in queues.items()}
+    for name in "".join(plan):
+        left[name].pop(0)()
+    assert not any(left.values())
+
+
+FORWARD_PLAN = (
+    "nFngnWggssswwVnsnswwssvswsvsnsnssvsvwsnvDwwwcwcc",
+    "wcfvccvwvdvdcwwcwwvcwcwcccvcccwdwvwwwcwwcXvvvww",
+)
+MIDDLE_PLAN = ("raaarmrmleeetaaateraeamllteletelhhthlthhhllhmthtz",)
+BACKWARD_PLAN = ("FbrggXbfbbgbrZbbttborcqctcocotccrooctoooOtccpcccctPtz",)
+LAST_PLAN = ("daddeawdahtaeeaaahatewwttheteetehhhwhttzhZ",)
+
+
 def merged(*lists):
     keyed = []
     for n, items in enumerate(lists):
@@ -1064,10 +1095,10 @@
     scale = HEAD_DIM**-0.5
     c_ref, s1_ref, s2_ref = tables
 
-    def project():
+    def project(lo, hi):
         shift = shift_of()
 
-        @pl.loop(0, rows // 256)
+        @pl.loop(lo, hi)
         def _(i):
             r = row_at(i, 256)
             c, s1, s2 = c_ref[r], s1_ref[r], s2_ref[r]
@@ -1080,8 +1111,8 @@
                     x = turn(x, c, s1, s2, 1.0)
                 rot[r, cols] = x.astype(jnp.bfloat16)
 
-    def pack():
-        @pl.loop(0, valid // QB)
+    def pack(lo, hi):
+        @pl.loop(lo, hi)
         def _(i):
             pk_ref[row_at(i)] = dot(picks(orow_ref, i), rot[...]).astype(jnp.bfloat16)
 
@@ -1106,10 +1137,10 @@
             total = out if h == 0 else jnp.where(head_lanes(1), out, total)
         opk[rq, ct] = total.astype(jnp.bfloat16)
 
-    def unpack():
+    def unpack(lo, hi):
         per = o_ref.shape[1]
 
-        @pl.loop(0, rows // per)
+        @pl.loop(lo, hi)
         def _(i):
             r = row_at(i, per)
             oc = ocol_ref[r]
@@ -1120,7 +1151,11 @@
     blocks = [
         functools.partial(block, qb, t) for qb in range(valid // QB) for t in range(w // 128)
     ]
-    return [project, pack] + blocks + [unpack]
+    p = functools.partial
+    steps, half, blks = rows // 256, valid // QB // 2, rows // o_ref.shape[1]
+    head = [p(project, 0, steps // 2), p(project, steps // 2, steps)]
+    head += [p(pack, 0, half), p(pack, half, valid // QB)]
+    return head + blocks + [p(unpack, 0, blks // 2), p(unpack, blks // 2, blks)]
 
 
 def attend_back(
@@ -1300,37 +1335,35 @@
         gather.own.wait()
         norm(s)
 
-    first = [own]
-    for i in range(3):
-        first.append(p(gather.arrive, i + 1))
-        first.append(lambda i=i: norm(gather.cross(i)))
-        first.append(lambda i=i: norm(2 * gather.near(i + 1) + y))
-    first.append(lambda: norm(gather.cross(3)))
-    lead, rest = slices.steps(), wide.steps()
-    for item in merged(first[:7], lead[:6]):
-        item()
-    grads.start()
-    wide.start()
-    for item in merged(first[7:], lead[6:]):
-        item()
-    whole.start()
-    down.start()
-    slices.finish()
-    lines = whole.steps()
-    side = [p(grads.arrive, 1)] + rest[:3] + [p(grads.arrive, 2)] + rest[3:7] + [p(grads.arrive, 3)]
-    for item in merged(work, side, lines[:6]):
-        item()
-    swap.start()
-    for item in merged(rest[7:], lines[6:]):
-        item()
-    down.step()
+    norms = [own]
+    for i in range(4):
+        norms.append(lambda i=i: norm(gather.cross(i)))
+        if i < 3:
+            norms.append(lambda i=i: norm(2 * gather.near(i + 1) + y))
+    work = [slices.complete, work[0], idle, work[1], idle] + work[2:]
+    queues = dict(
+        g=gather.steps(),
+        n=norms,
+        s=slices.steps(),
+        d=grads.steps(),
+        v=wide.steps(),
+        w=whole.steps(),
+        f=[down.step],
+        c=work,
+        D=[grads.start],
+        V=[wide.start],
+        W=[whole.start],
+        F=[down.start],
+        X=[swap.start],
+    )
+    work[0:2] = [lambda first=work[0], then=work[1]: (first(), then())]
+    perform(FORWARD_PLAN, queues)
     for i in range(4):
         grads.cross(i)
     swap.finish()
-    wide.finish()
-    whole.finish()
-    down.finish()
-    grads.finish()
+    wide.complete()
+    for task in (slices, wide, whole, down, grads):
+        task.finish()
     gather.finish(False)
 
     @pl.loop(1, 32)
@@ -1466,7 +1499,6 @@
         part[b] = dot(act[at], ww_ref[...], 1, 1).astype(jnp.bfloat16)
 
     gather.each(block)
-    reduce.start()
 
     def wide_grad(i):
         left = [c_ref[b, :, i * 256 : i * 256 + 256] for b in range(8)]
@@ -1485,30 +1517,31 @@
         right = jnp.concatenate([dm_ref[b, :, cols] for b in range(8)], 0)
         dg_ref[:, cols] = dot(hid[...], right, 0, 0).astype(jnp.bfloat16)
 
+    def norm_backward():
+        vec_ref[...] = jnp.zeros_like(vec_ref)
+
+        @tall(rows)
+        def _(r):
+            grad = second[r]
+            normed, rstd = normalize(res_ref[r])
+            inner, gain_part, shift_part = norm_back(grad, normed, rstd, gain)
+            rg_ref[r] = dm_ref[s, r].astype(jnp.float32) + inner
+            vec_ref[0:1] += gain_part[None]
+            vec_ref[1:2] += shift_part[None]
+
     p = functools.partial
-    work = []
-    for i in range(8):
-        work.append(p(wide_grad, i))
-        if i:
-            work.append(p(sums.step, i - 1))
-    work += [p(mlp_part, 0), p(sums.step, 7)] + [p(mlp_part, i) for i in (1, 2, 3)]
-    work += [p(down_grad, i) for i in range(8)]
-    later = reduce.steps()
-    for item in merged(work, later[:6]):
-        item()
-    for item in merged([p(sums.total, i) for i in range(8)], later[6:]):
-        item()
-    vec_ref[...] = jnp.zeros_like(vec_ref)
-
-    @tall(rows)
-    def _(r):
-        grad = second[r]
-        normed, rstd = normalize(res_ref[r])
-        inner, gain_part, shift_part = norm_back(grad, normed, rstd, gain)
-        rg_ref[r] = dm_ref[s, r].astype(jnp.float32) + inner
-        vec_ref[0:1] += gain_part[None]
-        vec_ref[1:2] += shift_part[None]
-
+    each = range(8)
+    queues = dict(
+        r=[p(reduce.send, k) for k in range(4)],
+        t=reduce.steps(),
+        a=[p(wide_grad, i) for i in each],
+        e=[p(sums.step, i) for i in each],
+        h=[p(sums.total, i) for i in each],
+        m=[p(mlp_part, i) for i in range(4)],
+        l=[p(down_grad, i) for i in each],
+        z=[norm_backward],
+    )
+    perform(MIDDLE_PLAN, queues)
     gather.finish(False)
     reduce.finish()
     sums.finish()
@@ -1612,17 +1645,20 @@
         da[r] = rg_ref[r].astype(jnp.bfloat16)
 
     gather.start()
-    down.start()
-    gather.own.wait()
-    down.step()
 
     def block(b):
         at = pl.ds(pl.multiple_of(b * rows, rows), rows)
         do_ref[at] = dot(full[b], or_ref[...], 1, 1).astype(jnp.bfloat16)
 
-    gather.each(block)
-    reduce.start()
-    swap.start()
+    def own_block():
+        gather.own.wait()
+        block(s)
+
+    blocks = [own_block]
+    for i in range(4):
+        if i < 3:
+            blocks.append(lambda i=i: block(gather.column(i + 1)))
+        blocks.append(lambda i=i: block(gather.cross(i)))
 
     def out_grad(i):
         cols = slice(i * 256, i * 256 + 256)
@@ -1648,29 +1684,44 @@
         dv,
         gpk,
     )
-    work += [p(out_grad, i) for i in range(8)] + [outer_sum.start, outer_sum.step, down.total]
-    later = reduce.steps()
-    for item in merged(work, later[:4]):
-        item()
-    for item in later[4:]:
-        item()
-    outer_sum.total()
-    sum_ref[...] = jnp.zeros_like(sum_ref)
-
-    @tall(rows)
-    def _(r):
-        m = mlp[r]
-        result = res_ref[r] + m
-        lo_ref[r] = result.astype(jnp.bfloat16)
-        keep = valid_ref[r]
-        for n, v in enumerate((result, attn_ref[r], m)):
-            total = jnp.sum(jnp.sum(v * v, -1, keepdims=True) * keep, 0, keepdims=True)
-            sum_ref[n : n + 1] += jnp.broadcast_to(total, (1, 128))
-
-    swap.finish()
-    for n, ref in enumerate((gate_ref, up_ref)):
-        for i in range(8):
-            ref[:, i * lf : i * lf + lf] = got[i, :, n * lf : n * lf + lf].astype(jnp.float32)
+    def results():
+        sum_ref[...] = jnp.zeros_like(sum_ref)
+
+        @tall(rows)
+        def _(r):
+            m = mlp[r]
+            result = res_ref[r] + m
+            lo_ref[r] = result.astype(jnp.bfloat16)
+            keep = valid_ref[r]
+            for n, v in enumerate((result, attn_ref[r], m)):
+                total = jnp.sum(jnp.sum(v * v, -1, keepdims=True) * keep, 0, keepdims=True)
+                sum_ref[n : n + 1] += jnp.broadcast_to(total, (1, 128))
+
+    def spread():
+        swap.finish()
+        for n, ref in enumerate((gate_ref, up_ref)):
+            for i in range(8):
+                value = got[i, :, n * lf : n * lf + lf]
+                ref[:, i * lf : i * lf + lf] = value.astype(jnp.float32)
+
+    queues = dict(
+        F=[down.start],
+        f=[down.step],
+        q=[down.total],
+        b=blocks,
+        g=gather.steps(),
+        r=[p(reduce.send, k) for k in range(4)],
+        t=reduce.steps(),
+        X=[swap.start],
+        Z=[spread],
+        c=work,
+        o=[p(out_grad, i) for i in range(8)],
+        O=[outer_sum.start],
+        p=[outer_sum.step],
+        P=[outer_sum.total],
+        z=[results],
+    )
+    perform(BACKWARD_PLAN, queues)
     gather.finish(False)
     reduce.finish()
     down.finish()
@@ -1768,28 +1819,19 @@
         at = pl.ds(pl.multiple_of(b * rows, rows), rows)
         part[b] = dot(g_ref[at], qw_ref[...], 1, 1).astype(jnp.bfloat16)
 
-    for k in range(4):
+    def far_block(k):
         block(2 * reduce.order(k) + 1 - y)
         reduce.send(k)
 
     def own_block(k):
         block(2 * reduce.order(k) + y)
 
-    def qkv_grad(i):
-        left = [a_ref[b, :, i * 256 : i * 256 + 256] for b in range(8)]
-        left = jnp.concatenate(left, 0)
-        grad[i * 256 : i * 256 + 256] = dot(left, g_ref[...], 0, 0).astype(jnp.bfloat16)
+    def qkv_grad(k):
+        i = peer(s, k)
+        at = pl.ds(pl.multiple_of(i * 256, 256), 256)
+        left = jnp.concatenate([a_ref[b, :, at] for b in range(8)], 0)
+        grad[at] = dot(left, g_ref[...], 0, 0).astype(jnp.bfloat16)
         sums.send(i)
-
-    p = functools.partial
-    for k in range(4):
-        own_block(k)
-    work = []
-    for i in range(8):
-        work.append(p(qkv_grad, i))
-        if i:
-            work.append(p(sums.step, i - 1))
-    work.append(p(sums.step, 7))
 
     def hand_over(k):
         sums.total(peer(s, k))
@@ -1798,45 +1840,58 @@
         else:
             swap.mine.start()
 
-    work += [p(hand_over, k) for k in reversed(range(8))]
-    for item in merged(work, reduce.steps()):
-        item()
-    vec[0:2] = jnp.zeros((2, width), jnp.float32)
-    vec[2:4] = vec_ref[0:2]
-    gain = n_ref[0:1]
-
-    @tall(rows)
-    def _(r):
-        normed, rstd = normalize(x_ref[r].astype(jnp.float32))
-        inner, gain_part, shift_part = norm_back(first[r], normed, rstd, gain)
-        ig_ref[r] = rg_ref[r] + inner
-        vec[0:1] += gain_part[None]
-        vec[1:2] += shift_part[None]
-
-    lane = lax.broadcasted_iota(jnp.int32, (1, 128), 1)
-    scalars = jnp.where(lane == 0, sum_ref[0:1], jnp.where(lane == 1, sum_ref[1:2], sum_ref[2:3]))
-    for i in range(16):
-        cols = slice(i * 128, i * 128 + 128)
-        msg[i, 0:4] = vec[0:4, cols]
-        msg[i, 4:5] = scalars
-        at = (i % 2) * 128
-        for n in range(3):
-            piece = b_ref[0:1, n * w + at : n * w + at + 128]
-            msg[i, 5 + n : 6 + n] = jnp.where(s == i // 2, piece, jnp.zeros_like(piece))
-
     def message(k):
         i = (me + k) % 32
         return remote(msg.at[i // 2], inbox.at[k], msend.at[k], mrecv.at[k], dealer(i))
 
-    @pl.loop(1, 32)
-    def _(k):
-        message(k).start()
-
-    swap.finish()
-    for i in range(8):
-        for n in range(3):
-            at = n * width + i * w
-            qg_ref[:, at : at + w] = got[i, :, n * w : n * w + w].astype(jnp.float32)
+    def norm_backward():
+        vec[0:2] = jnp.zeros((2, width), jnp.float32)
+        vec[2:4] = vec_ref[0:2]
+        gain = n_ref[0:1]
+
+        @tall(rows)
+        def _(r):
+            normed, rstd = normalize(x_ref[r].astype(jnp.float32))
+            inner, gain_part, shift_part = norm_back(first[r], normed, rstd, gain)
+            ig_ref[r] = rg_ref[r] + inner
+            vec[0:1] += gain_part[None]
+            vec[1:2] += shift_part[None]
+
+        lane = lax.broadcasted_iota(jnp.int32, (1, 128), 1)
+        scalars = jnp.where(lane == 0, sum_ref[0:1], jnp.where(lane == 1, sum_ref[1:2], sum_ref[2:3]))
+        for i in range(16):
+            cols = slice(i * 128, i * 128 + 128)
+            msg[i, 0:4] = vec[0:4, cols]
+            msg[i, 4:5] = scalars
+            at = (i % 2) * 128
+            for n in range(3):
+                piece = b_ref[0:1, n * w + at : n * w + at + 128]
+                msg[i, 5 + n : 6 + n] = jnp.where(s == i // 2, piece, jnp.zeros_like(piece))
+
+        @pl.loop(1, 32)
+        def _(k):
+            message(k).start()
+
+    def spread():
+        swap.finish()
+        for i in range(8):
+            for n in range(3):
+                at = n * width + i * w
+                qg_ref[:, at : at + w] = got[i, :, n * w : n * w + w].astype(jnp.float32)
+
+    p = functools.partial
+    ks = [7, 6, 5, 4, 3, 2, 1, 0]
+    queues = dict(
+        d=[p(far_block, k) for k in range(4)],
+        w=[p(own_block, k) for k in range(4)],
+        t=reduce.steps(),
+        a=[p(qkv_grad, k) for k in ks],
+        e=[lambda k=k: sums.step(peer(s, k)) for k in ks],
+        h=[p(hand_over, k) for k in ks],
+        z=[norm_backward],
+        Z=[spread],
+    )
+    perform(LAST_PLAN, queues)
     reduce.finish()
     sums.finish()
     total_ref[...] = msg[me // 2]

time: 588 us -> 528 us (0.90)
  Pallas kernels: 540 us -> 479 us
    pallas_call x1, Pallas kernels: 206 us -> 167 us  [forward(): pl.pallas_call(forward_kernel, out_shape=(out((8, rows, width)), out((wid...]
    pallas_call x1, Pallas kernels: 87.1 us -> 73.3 us  [last(): pl.pallas_call(last_kernel, out_shape=(out((rows, width)), out((pr, 3 * w...]
    pallas_call x1, Pallas kernels: 128 us -> 118 us  [middle(): pl.pallas_call(middle_kernel, out_shape=(out(wide, jnp.float32), out(wide...]
where the time goes in v5:
time: 528 us; the launch traced here: 519 us
  Pallas kernels  479 us (91%)
  local copies, waits for them, and re-layouts  27.2 us (5%)
  other arithmetic  10.7 us (2%)
    pallas_call x1, Pallas kernels, forward(): pl.pallas_call(forward_kernel, out_shape=(out((8, rows, width)), out((wid...  167 us
    pallas_call x1, Pallas kernels, backward(): pl.pallas_call(backward_kernel, out_shape=(out((group, 3 * w), jnp.bfloat...  121 us
    pallas_call x1, Pallas kernels, middle(): pl.pallas_call(middle_kernel, out_shape=(out(wide, jnp.float32), out(wide...  118 us
    pallas_call x1, Pallas kernels, last(): pl.pallas_call(last_kernel, out_shape=(out((rows, width)), out((pr, 3 * w...  73.3 us
    unnamed x48, local copies, waits for them, and re-layouts  14.4 us

profile of v5, /device:TPU:0, one launch (start us, length us, event | category | flops | bytes accessed | tf_op | source)
XLA Modules:
  0.0 518.7 jit_solution(9952385689468185068)
XLA Ops:
  0.6 0.0 copy-start.9
  0.7 0.0 copy-start.17
  0.7 0.8 stack.20
  1.5 0.1 pad_select_fusion.p_ref
  1.6 0.8 reduce-window.4
  2.4 0.8 convert_reduce_fusion
  3.2 0.1 pad_add_fusion
  3.3 0.1 select_reduce_fusion
  3.4 0.7 fusion.8
  4.1 3.0 fusion
  7.1 0.0 copy-done.9
  7.1 0.2 copy.38.ocol_ref
  7.3 0.0 copy-done.17
  7.4 0.0 copy-start.1
  7.4 0.7 reshape.138
  8.0 0.1 copy.36
  8.2 1.9 reshape.139
  10.1 0.1 copy.37
  10.2 0.0 copy-start.16
  10.2 1.6 maximum_bitcast_fusion.wp_ref
  11.8 0.0 copy-done.16
  11.8 0.2 copy.41
  11.9 0.0 copy-start
  11.9 0.0 copy-start.8
  12.0 0.0 copy-start.10
  12.0 1.4 copy.43
  13.3 2.6 reshape.137.qp_ref
  15.9 0.0 copy-done.1
  15.9 0.0 copy-done
  16.0 0.0 copy-done.8
  16.0 0.0 copy-done.10
  16.0 0.0 copy-start.2
  16.0 1.0 copy-done.2
  17.0 1.1 copy-done.3
  18.1 1.0 copy-done.4
  19.2 167.3 %shard_map.237 = (bf16[8,128,2048]{2,1,0:T(8,128)(2,1)}, bf16[2048,768]{1,0:T(8,128)(2,1)}, f32[8,2048]{1,0:T(8,128)S(1)}, bf16[32,64,2048]{2,1,0:T(8,128)(2,1)}...) custom-call(bf16[128,2048]{1,0:T(8,128)(2,1)S(1)} %bitcast.42, ...), custom_call_target="tpu_custom_call" | custom-call | tf_op jit(solution)/shard_map/pallas_call | solution.py:1386
  186.5 0.0 copy-start.5
  186.5 0.8 copy-done.5
  187.3 0.8 copy-done.6
  188.0 0.6 copy-done.7
  188.7 118.4 %shard_map.238 = (f32[128,2048]{1,0:T(8,128)}, f32[128,2048]{1,0:T(8,128)}, f32[128,2048]{1,0:T(8,128)}, f32[8,2048]{1,0:T(8,128)}, bf16[8,128,2048]{2,1,0:T(8,1...) custom-call(bf16[8,128,256]{2,1,0:T(8,128)(2,1)} %copy-done.6, bf16[2048,2048]{1,0:T(8,128)(2,1)} %bitcast.49, ...), custom_call_target="tpu_custom_call" | custom-call | tf_op jit(solution)/shard_map/pallas_call | solution.py:1563
  307.1 2.3 constant_dynamic-slice_fusion.2
  309.4 0.1 convert_reduce_fusion.1
  309.4 0.1 select_reduce_fusion.1
  309.5 2.2 fusion.4
  311.7 0.7 copy.40.valid_ref
  312.4 120.5 %shard_map.239 = (bf16[1024,768]{1,0:T(8,128)(2,1)}, f32[1,768]{1,0:T(1,128)}, bf16[128,2048]{1,0:T(8,128)(2,1)}, f32[8,128]{1,0:T(8,128)}, f32[64,5632]{1,0:T(8...) custom-call(f32[128,2048]{1,0:T(8,128)} %get-tuple-element.48.rg_ref, ...), custom_call_target="tpu_custom_call" | custom-call | tf_op jit(solution)/shard_map/pallas_call | solution.py:1746
  433.0 0.0 copy-start.19
  433.0 73.3 %shard_map.240 = (f32[128,2048]{1,0:T(8,128)}, f32[64,6144]{1,0:T(8,128)}, f32[8,128]{1,0:T(8,128)}) custom-call(bf16[1024,768]{1,0:T(8,128)(2,1)} %get-tuple-element.58.g_ref, f32[1,768]{1,0:T(1,128)} %get-tuple-element.59.b_ref, bf16[2048,768]{1,0:T(8,128)(2,1)} %get-tuple-element.60.qw_ref, bf16[8,128,2048]{2,1,0:T(8,128)(2,1)} %get-tuple-element.61.a_ref, ...), custom_call_target="tpu_custom_call" | custom-call | tf_op jit(solution)/shard_map/pallas_call | solution.py:1920
  506.3 0.8 constant_dynamic-slice_fusion
  507.1 0.5 slice_bitcast_fusion
  507.6 0.6 slice.42
  508.2 1.2 sqrt_bitcast_fusion
  509.4 0.8 copy.51
  510.2 0.0 copy-done.15
  510.2 1.0 copy.52
  511.2 1.1 copy.53
  512.3 0.2 copy-done.18
  512.6 0.8 copy.54
  513.4 1.1 copy.55
  514.5 0.8 copy-done.13
  515.3 1.1 copy.56
  516.4 0.8 copy-done.12
  517.1 1.1 copy.57
  (20 shorter events, 0.1 us)
Async XLA Ops:
  0.6 6.5 %copy-start.9 = (s32[1,1024]{1,0:T(1,128)S(1)}, s32[1,1024]{1,0:T(1,128)}, u32[]{:S(2)}) copy-start(s32[1,1024]{1,0:T(1,128)} %orow_ref.3) | copy-start | bytes 12292
  0.7 6.7 %copy-start.17 = (bf16[64,5632]{1,0:T(8,128)(2,1)S(1)}, bf16[64,5632]{1,0:T(8,128)(2,1)}, u32[]{:S(2)}) copy-start(bf16[64,5632]{1,0:T(8,128)(2,1)} %param.22) | copy-start | bytes 2162692
  7.4 8.6 %copy-start.1 = (s32[1024,1]{1,0:T(8,128)}, s32[1024,1]{1,0:T(8,128)S(1)}, u32[]{:S(2)}) copy-start(s32[1024,1]{1,0:T(8,128)S(1)} %copy.38.ocol_ref) | copy-start | bytes 12292
  10.2 1.6 copy-start.16
  11.9 4.0 copy-start
  11.9 4.0 copy-start.8
  12.0 4.0 copy-start.10
  16.0 1.0 copy-start.2
  17.0 1.1 copy-start.3
  18.1 1.0 copy-start.4
  186.5 0.8 copy-start.5
  187.2 0.8 copy-start.6
  188.0 0.6 copy-start.7
  433.0 76.5 %copy-start.19 = (bf16[128,2048]{1,0:T(8,128)(2,1)S(1)}, bf16[128,2048]{1,0:T(8,128)(2,1)}, u32[]{:S(2)}) copy-start(bf16[128,2048]{1,0:T(8,128)(2,1)} %get-tuple-element.57) | copy-start | bytes 1572868
  506.2 4.0 copy-start.15
  509.4 1.8 copy-start.11
  511.2 1.4 copy-start.18
  511.2 2.2 copy-start.14
  513.4 1.9 copy-start.13
  515.2 1.9 copy-start.12

commit v6 on v5

--- a/solution.py
+++ b/solution.py
@@ -346,10 +346,11 @@
 VMEM_SPEC = pl.BlockSpec(memory_space=pltpu.VMEM)
 SMEM_SPEC = pl.BlockSpec(memory_space=pltpu.SMEM)
 ANY_SPEC = pl.BlockSpec(memory_space=pl.ANY)
+HBM_SPEC = pl.BlockSpec(memory_space=pltpu.HBM)
 DMA = pltpu.SemaphoreType.DMA
 
 
-def comm_params(collective, limit=48):
+def comm_params(collective, limit=63):
     return pltpu.CompilerParams(
         collective_id=collective, has_side_effects=True, vmem_limit_bytes=limit << 20
     )
@@ -430,44 +431,53 @@
 
 class SeqGather:
     @staticmethod
-    def scratch():
-        return [DMA, DMA((8,)), DMA((4,)), DMA((4,)), DMA((4,))]
+    def scratch(parts=1):
+        return [DMA, DMA((8, parts)), DMA((4, parts)), DMA((4, parts)), DMA((4, parts))]
 
     def __init__(self, x, o, own, recv, sy, su, sd):
         self.x, self.o, self.recv, self.sy, self.su, self.sd = x, o, recv, sy, su, sd
         self.s, self.f, self.z, self.y = where_am_i()
+        self.parts = recv.shape[1]
         self.other = flip(self.s, 1)
         self.own = pltpu.make_async_copy(x, o.at[self.s], own)
 
+    def rows(self, c):
+        n = self.x.shape[0] // self.parts
+        return pl.ds(c * n, n)
+
     def at(self, zb):
         return 2 * zb + self.y
 
-    def ysend(self, zb, src):
-        b = self.at(zb)
-        return remote(src, self.o.at[b], self.sy.at[zb], self.recv.at[b], (self.other, self.f))
-
-    def usend(self, zb, src):
-        b = self.at(zb)
-        return remote(src, self.o.at[b], self.su.at[zb], self.recv.at[b], (self.s + 2, self.f))
-
-    def dsend(self, zb, src):
-        b = self.at(zb)
-        return remote(src, self.o.at[b], self.sd.at[zb], self.recv.at[b], (self.s - 2, self.f))
-
-    def arrived(self, b):
-        o = self.o.at[b]
-        return remote(o, o, self.sy.at[0], self.recv.at[b], (self.other, self.f))
+    def copy(self, zb, c, own, sems, to):
+        b, r = self.at(zb), self.rows(c)
+        src = self.x.at[r] if own else self.o.at[b, r]
+        return remote(src, self.o.at[b, r], sems.at[zb, c], self.recv.at[b, c], (to, self.f))
+
+    def ysend(self, zb, c, own=False):
+        return self.copy(zb, c, own, self.sy, self.other)
+
+    def usend(self, zb, c, own=False):
+        return self.copy(zb, c, own, self.su, self.s + 2)
+
+    def dsend(self, zb, c, own=False):
+        return self.copy(zb, c, own, self.sd, self.s - 2)
+
+    def arrived(self, b, c):
+        o = self.o.at[b, self.rows(c)]
+        return remote(o, o, self.sy.at[0, c], self.recv.at[b, c], (self.other, self.f))
 
     def start(self):
-        @pl.when(self.z < 3)
-        def _():
-            self.usend(self.z, self.x).start()
-
-        @pl.when(self.z > 0)
-        def _():
-            self.dsend(self.z, self.x).start()
-
-        self.ysend(self.z, self.x).start()
+        for c in range(self.parts):
+
+            @pl.when(self.z < 3)
+            def _():
+                self.usend(self.z, c, True).start()
+
+            @pl.when(self.z > 0)
+            def _():
+                self.dsend(self.z, c, True).start()
+
+            self.ysend(self.z, c, True).start()
         self.own.start()
 
     def near(self, i):
@@ -475,48 +485,47 @@
         base = jnp.where(low == 0, i, jnp.where(i < 2, 1 - i, i))
         return jnp.where(self.z < 2, base, 3 - base)
 
-    def arrive(self, i):
+    def arrive(self, i, c=0):
         zb = self.near(i)
-        b = self.at(zb)
-        self.arrived(b).wait_recv()
+        self.arrived(self.at(zb), c).wait_recv()
 
         @pl.when((zb < self.z) & (self.z < 3))
         def _():
-            self.usend(zb, self.o.at[b]).start()
+            self.usend(zb, c).start()
 
         @pl.when((zb > self.z) & (self.z > 0))
         def _():
-            self.dsend(zb, self.o.at[b]).start()
-
-        self.ysend(zb, self.o.at[b]).start()
-        return b
+            self.dsend(zb, c).start()
+
+        self.ysend(zb, c).start()
 
     def column(self, i):
-        b = self.at(self.near(i))
-        return b
+        return self.at(self.near(i))
 
     def cross(self, i):
         b = 2 * self.near(i) + 1 - self.y
-        self.arrived(b).wait_recv()
+        for c in range(self.parts):
+            self.arrived(b, c).wait_recv()
         return b
 
     def steps(self):
-        return [functools.partial(self.arrive, i) for i in (1, 2, 3)]
-
-    def each(self, use):
+        return [functools.partial(self.arrive, i, c) for i in (1, 2, 3) for c in range(self.parts)]
+
+    def each(self, use, counts):
+        left = self.steps()
+
         @pl.loop(0, 8)
         def _(j):
             i = (j + 1) // 2
             column = (j == 0) | ((j % 2 == 1) & (j < 7))
-
-            @pl.when(j == 1)
-            def _():
-                self.arrive(1)
-                self.arrive(2)
-
-            @pl.when(j == 4)
-            def _():
-                self.arrive(3)
+            for n, count in enumerate(counts):
+                now = [left.pop(0) for _ in range(count)]
+                if now:
+
+                    @pl.when(j == n)
+                    def _():
+                        for item in now:
+                            item()
 
             other = jnp.where(j == 7, 3, j // 2 - 1)
 
@@ -530,16 +539,17 @@
     def finish(self, own=True):
         if own:
             self.own.wait()
-        for zb in range(4):
-            self.ysend(zb, self.x).wait_send()
-
-            @pl.when((self.z < 3) & (zb <= self.z))
-            def _():
-                self.usend(zb, self.x).wait_send()
-
-            @pl.when((self.z > 0) & (zb >= self.z))
-            def _():
-                self.dsend(zb, self.x).wait_send()
+        for c in range(self.parts):
+            for zb in range(4):
+                self.ysend(zb, c).wait_send()
+
+                @pl.when((self.z < 3) & (zb <= self.z))
+                def _():
+                    self.usend(zb, c).wait_send()
+
+                @pl.when((self.z > 0) & (zb >= self.z))
+                def _():
+                    self.dsend(zb, c).wait_send()
 
 
 class SeqReduce:
@@ -1019,6 +1029,23 @@
     pass
 
 
+def fetch(refs, sems):
+    copies = [pltpu.make_async_copy(a, b, sems.at[i]) for i, (a, b) in enumerate(refs)]
+    for copy in copies:
+        copy.start()
+    return copies
+
+
+def rotary_rows(pos, lengths_ref, freq):
+    half = ROT // 2
+    d = lax.broadcasted_iota(jnp.int32, (1, 128), 1) % HEAD_DIM
+    rel = pos - starts_of(pos, lengths_ref, lengths_ref.shape[1])
+    angle = rel.astype(jnp.float32) * freq
+    c, s = jnp.cos(angle), jnp.sin(angle)
+    second = (d >= half) & (d < ROT)
+    return jnp.where(d < ROT, c, 1.0), jnp.where(d < half, -s, 0.0), jnp.where(second, s, 0.0)
+
+
 def perform(plan, queues):
     left = {name: list(items) for name, items in queues.items()}
     for name in "".join(plan):
@@ -1030,8 +1057,9 @@
     "nFngnWggssswwVnsnswwssvswsvsnsnssvsvwsnvDwwwcwcc",
     "wcfvccvwvdvdcwwcwwvcwcwcccvcccwdwvwwwcwwcXvvvww",
 )
-MIDDLE_PLAN = ("raaarmrmleeetaaateraeamllteletelhhthlthhhllhmthtz",)
-BACKWARD_PLAN = ("FbrggXbfbbgbrZbbttborcqctcocotccrooctoooOtccpcccctPtz",)
+MIDDLE_ARRIVALS = (1, 2, 0, 1, 1, 1)
+MIDDLE_PLAN = ("ramaarteeraatelalmmetalteretlemmalltlehhthllhhhhtzhh",)
+BACKWARD_PLAN = ("bFggrgbbXgbgbgrbfbrtZtbcrotccoocotocootocqOcccptccccPttz",)
 LAST_PLAN = ("daddeawdahtaeeaaahatewwttheteetehhhwhttzhZ",)
 
 
@@ -1093,7 +1121,7 @@
     w = w3 // 3
     valid = pk_ref.shape[0]
     scale = HEAD_DIM**-0.5
-    c_ref, s1_ref, s2_ref = tables
+    freq_ref = tables
 
     def project(lo, hi):
         shift = shift_of()
@@ -1101,7 +1129,7 @@
         @pl.loop(lo, hi)
         def _(i):
             r = row_at(i, 256)
-            c, s1, s2 = c_ref[r], s1_ref[r], s2_ref[r]
+            c, s1, s2 = rotary_rows(ocol_ref[r], len_ref, freq_ref[...])
             left = jnp.concatenate([a_ref[2 * i], a_ref[2 * i + 1]], 0)
             qkv = dot(left, w_ref[...]) + shift
             for t in range(w3 // 128):
@@ -1164,7 +1192,7 @@
     rows, w = do_ref.shape
     valid = pk_ref.shape[0]
     scale = HEAD_DIM**-0.5
-    c_ref, s1_ref, s2_ref = tables
+    freq_ref = tables
 
     def pack():
         @pl.loop(0, valid // QB)
@@ -1202,7 +1230,8 @@
         @pl.loop(0, valid // QB)
         def _(i):
             r = row_at(i)
-            c, s1, s2 = c_ref[r], s1_ref[r], s2_ref[r]
+            pos = lax.broadcasted_iota(jnp.int32, (QB, 1), 0) + i * QB
+            c, s1, s2 = rotary_rows(pos, len_ref, freq_ref[...])
             for t in range(w // 128):
                 ct = slice(t * 128, t * 128 + 128)
                 for j, src in ((0, dq), (1, dk)):
@@ -1232,16 +1261,15 @@
 
 
 def forward_kernel(
-    x_ref,
+    x_hbm,
     p_ref,
-    qp_ref,
-    op_ref,
-    dm_ref,
-    wp_ref,
-    dp_ref,
-    c_ref,
-    s1_ref,
-    s2_ref,
+    qkv_ref,
+    op_hbm,
+    dm_hbm,
+    gate_hbm,
+    up_hbm,
+    dp_hbm,
+    freq_ref,
     orow_ref,
     ocol_ref,
     len_ref,
@@ -1256,16 +1284,37 @@
     ww_ref,
     dw_ref,
     mix_ref,
+    x_ref,
+    op_ref,
+    dm_ref,
+    gate_ref,
+    up_ref,
+    dp_ref,
     xs,
     got,
     rot,
     opk,
+    qp_ref,
+    wp_ref,
+    load,
     psend,
     precv,
     *sems,
 ):
     s, f, z, y = where_am_i()
     me = s * 4 + f
+    w = rot.shape[1] // 3
+    lf = wp_ref.shape[2] // 2
+
+    def piece_of(i):
+        t, n = i // 3, i % 3
+        at = n * x_ref.shape[1] + t * w
+        return qkv_ref.at[:, at : at + w], qp_ref.at[t, :, n * w : n * w + w]
+
+    operands = [(x_hbm, x_ref)] + [piece_of(i) for i in range(24)]
+    operands += [(op_hbm, op_ref), (dm_hbm, dm_ref), (dp_hbm, dp_ref)]
+    operands += [(gate_hbm, gate_ref), (up_hbm, up_ref)]
+    loads = fetch(operands, load)
     greet_all(s, f)
     gather = SeqGather(x_ref, xs, *sems[:5])
     slices = ColGather(qp_ref, qw_ref, *sems[5:10])
@@ -1283,7 +1332,10 @@
     def _(k):
         param(k).start()
 
+    loads[0].wait()
     gather.start()
+    for copy in loads[1:]:
+        copy.wait()
     slices.start()
     got[me] = p_ref[...]
 
@@ -1305,7 +1357,6 @@
             a_ref[b, r] = (normed * gain + shift).astype(jnp.bfloat16)
 
     def shift_of():
-        w = rot.shape[1] // 3
         parts = []
         for n in range(3):
             part = jnp.zeros((1, w), jnp.float32)
@@ -1319,7 +1370,7 @@
         a_ref,
         qw_ref,
         shift_of,
-        (c_ref, s1_ref, s2_ref),
+        freq_ref,
         orow_ref,
         ocol_ref,
         len_ref,
@@ -1334,6 +1385,13 @@
     def own():
         gather.own.wait()
         norm(s)
+
+    def wide_start():
+        for i in range(8):
+            at = slice(i * lf, i * lf + lf)
+            wp_ref[i, :, 0:lf] = gate_ref[:, at]
+            wp_ref[i, :, lf : 2 * lf] = up_ref[:, at]
+        wide.start()
 
     norms = [own]
     for i in range(4):
@@ -1351,7 +1409,7 @@
         f=[down.step],
         c=work,
         D=[grads.start],
-        V=[wide.start],
+        V=[wide_start],
         W=[whole.start],
         F=[down.start],
         X=[swap.start],
@@ -1372,10 +1430,11 @@
 
 
 def forward(
-    x, params, qkv_p, out_p, dm, wide_p, down_p, tables, orow, ocol, lengths, valid, collective
+    x, params, qkv, out_p, dm, gate, up, down_p, freq, orow, ocol, lengths, valid, collective
 ):
     rows, width = x.shape
-    w3 = qkv_p.shape[2]
+    w3 = qkv.shape[1] // 8
+    part, wide = gate.shape[0], gate.shape[1] // 4
     w = w3 // 3
     group = 8 * rows
     heads = w // HEAD_DIM
@@ -1394,21 +1453,25 @@
             out((valid, w3)),
             out((heads, valid, 1), jnp.float32),
             out((8, rows, width)),
-            out((width, wide_p.shape[2])),
+            out((width, wide)),
             out((4,) + down_p.shape),
             out((8, rows, w)),
         ),
-        in_specs=[VMEM_SPEC] * 12 + [SMEM_SPEC],
+        in_specs=[HBM_SPEC, VMEM_SPEC] + [HBM_SPEC] * 6 + [VMEM_SPEC] * 3 + [SMEM_SPEC],
         out_specs=(VMEM_SPEC,) * 3
         + (ANY_SPEC,)
         + (VMEM_SPEC,) * 3
         + (ANY_SPEC,) * 3
         + (VMEM_SPEC,),
-        scratch_shapes=[
+        scratch_shapes=[pltpu.VMEM(v.shape, v.dtype) for v in (x, out_p, dm, gate, up, down_p)]
+        + [
             pltpu.VMEM((8, rows, width), jnp.bfloat16),
             pltpu.VMEM((32, 8, 128), jnp.float32),
             pltpu.VMEM((group, w3), jnp.bfloat16),
             pltpu.VMEM((valid, w), jnp.bfloat16),
+            pltpu.VMEM((8, part, w3), jnp.bfloat16),
+            pltpu.VMEM((8, part, wide), jnp.bfloat16),
+            DMA((30,)),
             DMA((32,)),
             DMA((32,)),
         ]
@@ -1420,7 +1483,7 @@
         + FsdpGather.scratch()
         + RowExchange.scratch(),
         compiler_params=comm_params(collective),
-    )(x, params, qkv_p, out_p, dm, wide_p, down_p, *tables, orow, ocol, lengths)
+    )(x, params, qkv, out_p, dm, gate, up, down_p, freq, orow, ocol, lengths)
 
 
 def tall(rows, step=16):
@@ -1433,17 +1496,27 @@
 
 
 def middle_kernel(
+    ho_hbm,
+    ow_ref,
+    x_hbm,
+    n_ref,
+    ww_hbm,
+    dw_hbm,
+    dm_hbm,
+    attn_hbm,
+    res_hbm,
+    rg_ref,
+    vec_ref,
+    mp_hbm,
+    dg_hbm,
+    h_hbm,
     ho_ref,
-    ow_ref,
     x_ref,
-    n_ref,
     ww_ref,
     dw_ref,
     dm_ref,
     attn_ref,
     res_ref,
-    rg_ref,
-    vec_ref,
     mp_ref,
     dg_ref,
     h_ref,
@@ -1455,20 +1528,22 @@
     part,
     second,
     load,
+    store,
     *scratch,
 ):
     s, f, z, y = where_am_i()
     rows, width = x_ref.shape
     lf = dw_ref.shape[0]
     lw = ho_ref.shape[2]
-    fetch = pltpu.make_async_copy(ow_ref, big, load)
-    fetch.start()
+    first = [(ho_hbm, ho_ref), (x_hbm, x_ref), (ow_ref, big)]
+    loads = fetch(first + [(ww_hbm, ww_ref), (dw_hbm, dw_ref), (dm_hbm, dm_ref)], load)
     greet_columns(s, f)
     gather = SeqGather(cloc, c_ref, *scratch[:5])
     reduce = SeqReduce(part, second, *scratch[5:11])
     sums = ColSum(big, h_ref, *scratch[11:])
     gain, shift = n_ref[2:3], n_ref[3:4]
-    fetch.wait()
+    for copy in loads[:3]:
+        copy.wait()
 
     @pl.loop(0, width // 512)
     def _(j):
@@ -1485,7 +1560,10 @@
         cloc[r] = (normed * gain + shift).astype(jnp.bfloat16)
 
     gather.start()
+    stores = fetch([(attn_ref, attn_hbm), (res_ref, res_hbm)], store)
     gather.own.wait()
+    for copy in loads[3:]:
+        copy.wait()
 
     def block(b):
         at = pl.ds(pl.multiple_of(b * rows, rows), rows)
@@ -1498,7 +1576,7 @@
         act[at] = jnp.concatenate([gate_act, up_act], 1)
         part[b] = dot(act[at], ww_ref[...], 1, 1).astype(jnp.bfloat16)
 
-    gather.each(block)
+    gather.each(block, MIDDLE_ARRIVALS)
 
     def wide_grad(i):
         left = [c_ref[b, :, i * 256 : i * 256 + 256] for b in range(8)]
@@ -1541,7 +1619,16 @@
         l=[p(down_grad, i) for i in each],
         z=[norm_backward],
     )
+    out_copies = [
+        pltpu.make_async_copy(mp_ref, mp_hbm, store.at[2]),
+        pltpu.make_async_copy(dg_ref, dg_hbm, store.at[3]),
+        pltpu.make_async_copy(h_ref, h_hbm, store.at[4]),
+    ]
+    for name, copy in zip("mlh", out_copies):
+        queues[name].append(copy.start)
     perform(MIDDLE_PLAN, queues)
+    for copy in stores + out_copies:
+        copy.wait()
     gather.finish(False)
     reduce.finish()
     sums.finish()
@@ -1571,9 +1658,19 @@
             out((lf, width)),
             out((8, part, 2 * lf)),
         ),
-        in_specs=[VMEM_SPEC, ANY_SPEC] + [VMEM_SPEC] * 5,
-        out_specs=(VMEM_SPEC,) * 7,
+        in_specs=[HBM_SPEC] * 3 + [VMEM_SPEC] + [HBM_SPEC] * 3,
+        out_specs=(ANY_SPEC,) * 2 + (VMEM_SPEC,) * 2 + (ANY_SPEC,) * 3,
         scratch_shapes=[
+            vm(heads_out.shape),
+            vm(wide),
+            vm(wide_w.shape),
+            vm(down_w.shape),
+            vm(dm.shape),
+            vm(wide, jnp.float32),
+            vm(wide, jnp.float32),
+            vm((8,) + wide),
+            vm((lf, width)),
+            vm((8, part, 2 * lf)),
             vm((width, width)),
             vm(wide),
             vm((8,) + wide),
@@ -1581,58 +1678,80 @@
             vm((group, 2 * lf)),
             vm((8,) + wide),
             vm(wide, jnp.float32),
-            DMA,
+            DMA((6,)),
+            DMA((5,)),
         ]
-        + SeqGather.scratch()
+        + SeqGather.scratch(2)
         + SeqReduce.scratch(rows, width)
         + ColSum.scratch(part, 2 * lf),
-        compiler_params=comm_params(collective, 63),
+        compiler_params=comm_params(collective),
     )(heads_out, out_w, x, norms, wide_w, down_w, dm)
 
 
 def backward_kernel(
     rg_ref,
+    freq_ref,
+    orow_ref,
+    ocol_ref,
+    len_ref,
+    ow_hbm,
+    mix_hbm,
+    pk_hbm,
+    lse_hbm,
+    attn_hbm,
+    res_hbm,
+    mp_hbm,
+    dg_hbm,
+    h_hbm,
+    g_ref,
+    b_ref,
+    lo_ref,
+    sum_ref,
+    got,
+    down_hbm,
+    out_ref,
     or_ref,
     mix_ref,
     pk_ref,
     lse_ref,
-    c_ref,
-    s1_ref,
-    s2_ref,
-    orow_ref,
-    ocol_ref,
-    len_ref,
     attn_ref,
     res_ref,
-    valid_ref,
     mp_ref,
     dg_ref,
     h_ref,
-    g_ref,
-    b_ref,
-    lo_ref,
-    sum_ref,
-    gate_ref,
-    up_ref,
     down_ref,
-    out_ref,
     da,
     full,
     do_ref,
     og,
     mlp,
-    got,
     dpk,
     dq,
     dk,
     dv,
     gpk,
+    load,
+    store,
     *scratch,
 ):
     s, f, z, y = where_am_i()
     rows, width = rg_ref.shape
-    part, ff = gate_ref.shape
-    lf = ff // 8
+    part = out_ref.shape[0]
+    valid = pk_ref.shape[0]
+    loads = fetch(
+        [
+            (ow_hbm.at[pl.ds(pl.multiple_of(s * 4, 4), 4)], or_ref),
+            (dg_hbm, dg_ref),
+            (mp_hbm, mp_ref),
+            (h_hbm, h_ref),
+            (pk_hbm, pk_ref),
+            (lse_hbm, lse_ref),
+            (mix_hbm, mix_ref),
+            (attn_hbm, attn_ref),
+            (res_hbm, res_ref),
+        ],
+        load,
+    )
     greet_columns(s, f)
     gather = SeqGather(da, full, *scratch[:5])
     reduce = SeqReduce(mp_ref, mlp, *scratch[5:11])
@@ -1648,11 +1767,27 @@
 
     def block(b):
         at = pl.ds(pl.multiple_of(b * rows, rows), rows)
-        do_ref[at] = dot(full[b], or_ref[...], 1, 1).astype(jnp.bfloat16)
+        out_rows = jnp.concatenate([or_ref[k] for k in range(4)], 0)
+        do_ref[at] = dot(full[b], out_rows, 1, 1).astype(jnp.bfloat16)
 
     def own_block():
         gather.own.wait()
+        loads[0].wait()
         block(s)
+
+    def before(copies, then):
+        def run():
+            for copy in copies:
+                copy.wait()
+            then()
+
+        return run
+
+    out_copies = [pltpu.make_async_copy(down_ref, down_hbm, store)]
+
+    def down_total():
+        down.total()
+        out_copies[0].start()
 
     blocks = [own_block]
     for i in range(4):
@@ -1672,7 +1807,7 @@
         pk_ref,
         do_ref,
         lse_ref,
-        (c_ref, s1_ref, s2_ref),
+        freq_ref,
         orow_ref,
         ocol_ref,
         len_ref,
@@ -1687,55 +1822,55 @@
     def results():
         sum_ref[...] = jnp.zeros_like(sum_ref)
 
-        @tall(rows)
-        def _(r):
+        step = 16
+
+        @pl.loop(0, rows // step)
+        def _(i):
+            r = row_at(i, step)
             m = mlp[r]
             result = res_ref[r] + m
             lo_ref[r] = result.astype(jnp.bfloat16)
-            keep = valid_ref[r]
+            pos = ocol_ref[pl.ds(pl.multiple_of(s * rows + i * step, step), step)]
+            keep = jnp.where(pos < valid, 1.0, 0.0)
             for n, v in enumerate((result, attn_ref[r], m)):
                 total = jnp.sum(jnp.sum(v * v, -1, keepdims=True) * keep, 0, keepdims=True)
                 sum_ref[n : n + 1] += jnp.broadcast_to(total, (1, 128))
 
-    def spread():
-        swap.finish()
-        for n, ref in enumerate((gate_ref, up_ref)):
-            for i in range(8):
-                value = got[i, :, n * lf : n * lf + lf]
-                ref[:, i * lf : i * lf + lf] = value.astype(jnp.float32)
-
+    sends = [p(reduce.send, k) for k in range(4)]
+    outs = [p(out_grad, i) for i in range(8)]
     queues = dict(
-        F=[down.start],
+        F=[before(loads[1:2], down.start)],
         f=[down.step],
-        q=[down.total],
+        q=[down_total],
         b=blocks,
         g=gather.steps(),
-        r=[p(reduce.send, k) for k in range(4)],
+        r=[before(loads[2:3], sends[0])] + sends[1:],
         t=reduce.steps(),
-        X=[swap.start],
-        Z=[spread],
-        c=work,
-        o=[p(out_grad, i) for i in range(8)],
+        X=[before(loads[3:4], swap.start)],
+        Z=[swap.finish],
+        c=[before(loads[4:6], work[0])] + work[1:],
+        o=[before(loads[6:7], outs[0])] + outs[1:],
         O=[outer_sum.start],
         p=[outer_sum.step],
         P=[outer_sum.total],
-        z=[results],
+        z=[before(loads[7:9], results)],
     )
     perform(BACKWARD_PLAN, queues)
     gather.finish(False)
     reduce.finish()
     down.finish()
     outer_sum.finish()
+    for copy in out_copies:
+        copy.wait()
 
 
 def backward(
-    rg, out_rows, mixed, pk, lse, tables, orow, ocol, lengths, attn, res, keep, mp, dg, h, collective
+    rg, freq, orow, ocol, lengths, out_w, mixed, pk, lse, attn, res, mp, dg, h, collective
 ):
     rows, width = rg.shape
     group, w = mixed.shape
     valid = pk.shape[0]
     part = h.shape[1]
-    ff = h.shape[2] * 4
 
     def out(shape, dtype=jnp.float32):
         return jax.ShapeDtypeStruct(shape, dtype)
@@ -1750,53 +1885,67 @@
             out((1, 3 * w)),
             out((rows, width), jnp.bfloat16),
             out((8, 128)),
-            out((part, ff)),
-            out((part, ff)),
+            out(h.shape, jnp.bfloat16),
             out(dg.shape[1:]),
             out((part, width)),
         ),
-        in_specs=[VMEM_SPEC] * 10 + [SMEM_SPEC] + [VMEM_SPEC] * 6,
-        out_specs=(VMEM_SPEC,) * 8,
+        in_specs=[VMEM_SPEC] * 4 + [SMEM_SPEC] + [HBM_SPEC] * 9,
+        out_specs=(VMEM_SPEC,) * 4 + (ANY_SPEC,) * 2 + (VMEM_SPEC,),
         scratch_shapes=[
+            vm((4, part, width)),
+            vm(mixed.shape),
+            vm(pk.shape),
+            vm(lse.shape, jnp.float32),
+            vm(attn.shape, jnp.float32),
+            vm(res.shape, jnp.float32),
+            vm(mp.shape),
+            vm(dg.shape),
+            vm(h.shape),
+            vm(dg.shape[1:], jnp.float32),
             vm((rows, width)),
             vm((8, rows, width)),
             vm((group, w)),
             vm((4, part, width)),
             vm((rows, width), jnp.float32),
-            vm(h.shape),
             vm((valid, w)),
             vm((valid, w), jnp.float32),
             vm((valid, w), jnp.float32),
             vm((valid, w), jnp.float32),
             vm((valid, 3 * w)),
+            DMA((9,)),
+            DMA,
         ]
-        + SeqGather.scratch()
+        + SeqGather.scratch(2)
         + SeqReduce.scratch(rows, width)
         + RowExchange.scratch()
         + FsdpReduce.scratch(*dg.shape[1:])
         + FsdpReduce.scratch(part, width),
-        compiler_params=comm_params(collective, 60),
-    )(rg, out_rows, mixed, pk, lse, *tables, orow, ocol, lengths, attn, res, keep, mp, dg, h)
+        compiler_params=comm_params(collective),
+    )(rg, freq, orow, ocol, lengths, out_w, mixed, pk, lse, attn, res, mp, dg, h)
 
 
 def last_kernel(
     g_ref,
     b_ref,
+    n_ref,
+    vec_ref,
+    sum_ref,
+    qw_hbm,
+    a_hbm,
+    x_hbm,
+    rg_hbm,
+    ig_ref,
+    got,
+    total_ref,
     qw_ref,
     a_ref,
     x_ref,
     rg_ref,
-    n_ref,
-    vec_ref,
-    sum_ref,
-    ig_ref,
-    qg_ref,
-    total_ref,
+    load,
     part,
     first,
     grad,
     h,
-    got,
     msg,
     inbox,
     vec,
@@ -1809,8 +1958,9 @@
     rows, width = x_ref.shape
     w3 = g_ref.shape[1]
     w = w3 // 3
-    pr = qg_ref.shape[0]
+    loads = fetch([(qw_hbm, qw_ref), (a_hbm, a_ref), (x_hbm, x_ref), (rg_hbm, rg_ref)], load)
     greet_all(s, f)
+    loads[0].wait()
     reduce = SeqReduce(part, first, *scratch[:6])
     sums = ColSum(grad, h, *scratch[6:12])
     swap = RowExchange(h, got, *scratch[12:])
@@ -1827,6 +1977,8 @@
         block(2 * reduce.order(k) + y)
 
     def qkv_grad(k):
+        if k == 7:
+            loads[1].wait()
         i = peer(s, k)
         at = pl.ds(pl.multiple_of(i * 256, 256), 256)
         left = jnp.concatenate([a_ref[b, :, at] for b in range(8)], 0)
@@ -1848,6 +2000,8 @@
         vec[0:2] = jnp.zeros((2, width), jnp.float32)
         vec[2:4] = vec_ref[0:2]
         gain = n_ref[0:1]
+        loads[2].wait()
+        loads[3].wait()
 
         @tall(rows)
         def _(r):
@@ -1872,13 +2026,6 @@
         def _(k):
             message(k).start()
 
-    def spread():
-        swap.finish()
-        for i in range(8):
-            for n in range(3):
-                at = n * width + i * w
-                qg_ref[:, at : at + w] = got[i, :, n * w : n * w + w].astype(jnp.float32)
-
     p = functools.partial
     ks = [7, 6, 5, 4, 3, 2, 1, 0]
     queues = dict(
@@ -1889,7 +2036,7 @@
         e=[lambda k=k: sums.step(peer(s, k)) for k in ks],
         h=[p(hand_over, k) for k in ks],
         z=[norm_backward],
-        Z=[spread],
+        Z=[swap.finish],
     )
     perform(LAST_PLAN, queues)
     reduce.finish()
@@ -1919,14 +2066,18 @@
 
     return pl.pallas_call(
         last_kernel,
-        out_shape=(out((rows, width)), out((pr, 3 * width)), out((8, 128))),
-        in_specs=[VMEM_SPEC] * 9,
-        out_specs=(VMEM_SPEC,) * 3,
+        out_shape=(out((rows, width)), out((8, pr, w3), jnp.bfloat16), out((8, 128))),
+        in_specs=[VMEM_SPEC] * 5 + [HBM_SPEC] * 4,
+        out_specs=(VMEM_SPEC, ANY_SPEC, VMEM_SPEC),
         scratch_shapes=[
+            vm(qkv_w.shape),
+            vm(a.shape),
+            vm(x.shape),
+            vm(rg.shape, jnp.float32),
+            DMA((4,)),
             vm((8, rows, width)),
             vm((rows, width), jnp.float32),
             vm((width, w3)),
-            vm((8, pr, w3)),
             vm((8, pr, w3)),
             vm((16, 8, 128), jnp.float32),
             vm((32, 8, 128), jnp.float32),
@@ -1937,18 +2088,52 @@
         + SeqReduce.scratch(rows, width)
         + ColSum.scratch(pr, w3)
         + RowExchange.scratch(),
-        compiler_params=comm_params(collective, 56),
-    )(g, b, qkv_w, a, x, rg, norms, vec, sums)
-
-
-def rotary_tables(rel):
-    half = ROT // 2
-    d = jnp.arange(128, dtype=jnp.int32) % HEAD_DIM
-    freq = 10000.0 ** (-2.0 * (d % half).astype(jnp.float32) / ROT)
-    angle = rel[:, None] * freq[None, :]
-    c, s = jnp.cos(angle), jnp.sin(angle)
-    second = (d >= half) & (d < ROT)
-    return (jnp.where(d < ROT, c, 1.0), jnp.where(d < half, -s, 0.0), jnp.where(second, s, 0.0))
+        compiler_params=comm_params(collective),
+    )(g, b, norms, vec, sums, qkv_w, a, x, rg)
+
+
+def results_kernel(*refs):
+    same, pieces, outs = refs[:4], refs[4:6], refs[6:13]
+    bufs, wide, qkv, spread, load, store = refs[13:17], refs[17], refs[18], refs[19:22], refs[22], refs[23]
+    moves = list(zip(same, bufs)) + [(pieces[0], wide), (pieces[1], qkv)]
+    loads = fetch(moves, load)
+    stores = [pltpu.make_async_copy(bufs[i], outs[i], store.at[i]) for i in range(4)]
+    stores += [pltpu.make_async_copy(spread[i], outs[4 + i], store.at[4 + i]) for i in range(3)]
+    for i in range(4):
+        loads[i].wait()
+        stores[i].start()
+    loads[4].wait()
+    lf = wide.shape[2] // 2
+    for n in range(2):
+        for i in range(8):
+            value = wide[i, :, n * lf : n * lf + lf]
+            spread[n][:, i * lf : i * lf + lf] = value.astype(jnp.float32)
+        stores[4 + n].start()
+    loads[5].wait()
+    w = qkv.shape[2] // 3
+    for i in range(8):
+        for n in range(3):
+            at = (n * 8 + i) * w
+            spread[2][:, at : at + w] = qkv[i, :, n * w : n * w + w].astype(jnp.float32)
+    stores[6].start()
+    for copy in stores:
+        copy.wait()
+
+
+def results(same, wide, qkv):
+    part = wide.shape[1]
+    spread = [(part, 4 * wide.shape[2])] * 2 + [(part, 8 * qkv.shape[2])]
+    return pl.pallas_call(
+        results_kernel,
+        out_shape=[jax.ShapeDtypeStruct(v.shape, v.dtype) for v in same]
+        + [jax.ShapeDtypeStruct(v, jnp.float32) for v in spread],
+        in_specs=[HBM_SPEC] * 6,
+        out_specs=[ANY_SPEC] * 7,
+        scratch_shapes=[pltpu.VMEM(v.shape, v.dtype) for v in (*same, wide, qkv)]
+        + [pltpu.VMEM(v, jnp.float32) for v in spread]
+        + [DMA((6,)), DMA((7,))],
+        compiler_params=pltpu.CompilerParams(vmem_limit_bytes=63 << 20),
+    )(*same, wide, qkv)
 
 
 def line_body(
@@ -1977,42 +2162,31 @@
     lf = ff // nseq
     seq_at, fsdp_at = lax.axis_index("seq"), lax.axis_index("fsdp")
     order = deal_order[0]
-    lengths = seq_lengths[0]
     group_rows = order.shape[0]
     valid_rows = group_rows * 5 // 8
     orow, ocol = order[None, :], order[:, None]
-    local_pos = lax.dynamic_slice_in_dim(order, seq_at * rows, rows)
-    valid = (local_pos < valid_rows).astype(jnp.float32)[:, None]
-    dealt_seg, dealt_start = segment_of(order, lengths)
-    dealt_tables = rotary_tables((order - dealt_start).astype(jnp.float32))
-    packed_pos = jnp.arange(valid_rows, dtype=jnp.int32)
-    packed_seg, packed_start = segment_of(packed_pos, lengths)
-    packed_tables = rotary_tables((packed_pos - packed_start).astype(jnp.float32))
-
-    def column_parts(weights):
-        views = [w.reshape(part, nseq, -1) for w in weights]
-        return jnp.concatenate(views, 2).transpose(1, 0, 2)
-
+    lane = jnp.arange(128, dtype=jnp.int32) % HEAD_DIM % (ROT // 2)
+    freq = 10000.0 ** (-2.0 * lane.astype(jnp.float32) / ROT)
+    freq = freq[None, :]
     params = jnp.stack([ln1_gain, ln1_bias, ln2_gain, ln2_bias, *qkv_bias])
     params = jnp.pad(params.astype(jnp.float32), ((0, 1), (0, 64)))
     params = jnp.where(fsdp_at % 2 == 0, params, jnp.roll(params, part, 1))
-    qkv_parts = qkv_weight.reshape(part, 3, nseq, lw).transpose(2, 0, 1, 3).reshape(nseq, part, -1)
     first_in, qkv_w, norms, out_w, heads_out, packed, lse, mlp_grad, wide_w, down_w, mixed = forward(
         hidden_in[0],
         params,
-        qkv_parts,
+        qkv_weight,
         out_weight,
         out_grad[0],
-        column_parts([gate_weight, up_weight]),
+        gate_weight,
+        up_weight,
         down_weight,
-        dealt_tables,
+        freq,
         orow,
         ocol,
         seq_lengths,
         valid_rows,
         1,
     )
-    out_rows = lax.dynamic_slice_in_dim(out_w, seq_at * nfsdp, nfsdp).reshape(lw, width)
     attn, resid, resid_grad, norm2_grads, mlp_part, down_part, wide_sum = middle(
         heads_out,
         out_w.reshape(width, width),
@@ -2023,26 +2197,28 @@
         mlp_grad,
         3,
     )
-    qkv_act, bias_sums, result, sums, gate_grad, up_grad, down_grad, out_grad_w = backward(
+    qkv_act, bias_sums, result, sums, wide_pieces, down_grad, out_grad_w = backward(
         resid_grad,
-        out_rows,
+        freq,
+        orow,
+        ocol,
+        seq_lengths,
+        out_w,
         mixed.reshape(group_rows, lw),
         packed,
         lse,
-        packed_tables,
-        orow,
-        ocol,
-        seq_lengths,
         attn,
         resid,
-        valid,
         mlp_part,
         down_part.reshape(nfsdp, -1, width),
         wide_sum,
         4,
     )
-    input_grad, qkv_grad, total = last(
+    input_grad, qkv_pieces, total = last(
         qkv_act, bias_sums, qkv_w, first_in, hidden_in[0], resid_grad, norms, norm2_grads, sums, 5
+    )
+    result, input_grad, down_grad, out_grad_w, gate_grad, up_grad, qkv_grad = results(
+        (result, input_grad, down_grad, out_grad_w), wide_pieces, qkv_pieces
     )
     count = valid_rows * nfsdp * width
     rms = jnp.sqrt(total[4, :3] / count)

time: 528 us -> 484 us (0.917)
  local copies, waits for them, and re-layouts: 27.2 us -> 4.32 us
  Pallas kernels: 479 us -> 468 us
  other arithmetic: 10.7 us -> 2.39 us
    unnamed x48 -> x0, local copies, waits for them, and re-layouts: 14.4 us -> none
    pallas_call x1, Pallas kernels: 118 us -> 110 us  [middle(): pl.pallas_call(middle_kernel, out_shape=(out(wide, jnp.float32), out(wide...]
    reshape x6 -> x0, local copies, waits for them, and re-layouts: 6.76 us -> none  [the longest x2 3.96 us: line_body(): qkv_weight.reshape(part, 3, nseq, lw).transpose(2, 0, 1, 3)]
    pallas_call x1, Pallas kernels: 121 us -> 114 us  [backward(): pl.pallas_call(backward_kernel, out_shape=(out((group, 3 * w), jnp.bfloat...]
    pallas_call x1 -> x2, Pallas kernels: 73.3 us -> 76.2 us  [the longest x1 70.4 us: last(): pl.pallas_call(last_kernel, out_shape=(out((rows, width)), out((8, pr, w3...]
where the time goes in v6:
time: 484 us; the launch traced here: 476 us
  Pallas kernels  468 us (97%)
    pallas_call x1, Pallas kernels, forward(): pl.pallas_call(forward_kernel, out_shape=(out((8, rows, width)), out((wid...  168 us
    pallas_call x1, Pallas kernels, backward(): pl.pallas_call(backward_kernel, out_shape=(out((group, 3 * w), jnp.bfloat...  114 us
    pallas_call x1, Pallas kernels, middle(): pl.pallas_call(middle_kernel, out_shape=(out(wide, jnp.float32), out(wide...  110 us
    pallas_call x1, Pallas kernels, last(): pl.pallas_call(last_kernel, out_shape=(out((rows, width)), out((8, pr, w3...  70.4 us

profile of v6, /device:TPU:0, one launch (start us, length us, event | category | flops | bytes accessed | tf_op | source)
XLA Modules:
  0.0 475.8 jit_solution(8891979889954826947)
XLA Ops:
  0.7 0.5 fusion.2.freq_ref
  1.2 0.8 stack.20
  2.0 0.7 pad_select_fusion.p_ref
  2.6 1.7 copy.27.ocol_ref
  4.3 167.6 %shard_map.237 = (bf16[8,128,2048]{2,1,0:T(8,128)(2,1)}, bf16[2048,768]{1,0:T(8,128)(2,1)}, f32[8,2048]{1,0:T(8,128)}, bf16[32,64,2048]{2,1,0:T(8,128)(2,1)}, bf...) custom-call(bf16[128,2048]{1,0:T(8,128)(2,1)} %bitcast.25, ...), custom_call_target="tpu_custom_call" | custom-call | tf_op jit(solution)/shard_map/pallas_call | solution.py:1445
  172.0 110.1 %shard_map.238 = (f32[128,2048]{1,0:T(8,128)}, f32[128,2048]{1,0:T(8,128)}, f32[128,2048]{1,0:T(8,128)}, f32[8,2048]{1,0:T(8,128)}, bf16[8,128,2048]{2,1,0:T(8,1...) custom-call(bf16[8,128,256]{2,1,0:T(8,128)(2,1)} %get-tuple-element.48.ho_hbm, ...), custom_call_target="tpu_custom_call" | custom-call | tf_op jit(solution)/shard_map/pallas_call | solution.py:1650
  282.0 114.1 %shard_map.239 = (bf16[1024,768]{1,0:T(8,128)(2,1)}, f32[1,768]{1,0:T(1,128)}, bf16[128,2048]{1,0:T(8,128)(2,1)}, f32[8,128]{1,0:T(8,128)}, bf16[8,64,1408]{2,1,...) custom-call(f32[128,2048]{1,0:T(8,128)} %get-tuple-element.54.rg_ref.rg_hbm, f32[1,128]{1,0:T(1,128)} %fusion.2.freq_ref, ...), custom_call_target="tpu_custom_call" | custom-call | tf_op jit(solution)/shard_map/pallas_call | solution.py:1881
  396.1 70.4 %shard_map.240 = (f32[128,2048]{1,0:T(8,128)}, bf16[8,64,768]{2,1,0:T(8,128)(2,1)}, f32[8,128]{1,0:T(8,128)}) custom-call(bf16[1024,768]{1,0:T(8,128)(2,1)} %get-tuple-element.64.g_ref, f32[1,768]{1,0:T(1,128)} %get-tuple-element.65.b_ref, f32[8,2048]{1,0:T(8,128)} %get-tuple-element.50.n_ref, f32[8,2048]{1,0:T(8,128)} %get-tuple-element.66.vec_ref, ...), custom_call_target="tpu_custom_call" | custom-call | tf_op jit(solution)/shard_map/pallas_call | solution.py:2067
  466.5 1.2 sqrt_bitcast_fusion
  467.7 0.7 constant_dynamic-slice_fusion
  468.5 0.6 slice.33
  469.0 0.5 slice_bitcast_fusion
  469.6 5.7 %shard_map.241 = (bf16[128,2048]{1,0:T(8,128)(2,1)}, f32[128,2048]{1,0:T(8,128)}, f32[176,2048]{1,0:T(8,128)}, f32[64,2048]{1,0:T(8,128)}, f32[64,5632]{1,0:T(8,...) custom-call(bf16[128,2048]{1,0:T(8,128)(2,1)} %get-tuple-element.63.refs_0_, f32[128,2048]{1,0:T(8,128)} %get-tuple-element.70.refs_1_, ...), custom_call_target="tpu_custom_call" | custom-call | tf_op jit(solution)/shard_map/pallas_call | solution.py:2126
  (1 shorter events, 0.0 us)

commit v7 on v6

--- a/solution.py
+++ b/solution.py
@@ -379,6 +379,12 @@
     return s
 
 
+def peer_at(s, k):
+    for bit in (1, 2, 4):
+        s = s + ((k // bit) % 2) * bit * (1 - 2 * ((s // bit) % 2))
+    return s
+
+
 def dealer(i):
     return (i // 4, i % 4)
 
@@ -511,30 +517,17 @@
     def steps(self):
         return [functools.partial(self.arrive, i, c) for i in (1, 2, 3) for c in range(self.parts)]
 
-    def each(self, use, counts):
-        left = self.steps()
-
-        @pl.loop(0, 8)
-        def _(j):
-            i = (j + 1) // 2
-            column = (j == 0) | ((j % 2 == 1) & (j < 7))
-            for n, count in enumerate(counts):
-                now = [left.pop(0) for _ in range(count)]
-                if now:
-
-                    @pl.when(j == n)
-                    def _():
-                        for item in now:
-                            item()
-
-            other = jnp.where(j == 7, 3, j // 2 - 1)
-
-            @pl.when(jnp.logical_not(column))
-            def _():
-                self.cross(other)
-
-            zb = self.near(jnp.where(column, i, other))
-            use(2 * zb + jnp.where(column, self.y, 1 - self.y))
+    def turn(self, j):
+        i = (j + 1) // 2
+        column = (j == 0) | ((j % 2 == 1) & (j < 7))
+        other = jnp.where(j == 7, 3, j // 2 - 1)
+
+        @pl.when(jnp.logical_not(column))
+        def _():
+            self.cross(other)
+
+        zb = self.near(jnp.where(column, i, other))
+        return 2 * zb + jnp.where(column, self.y, 1 - self.y)
 
     def finish(self, own=True):
         if own:
@@ -566,9 +559,10 @@
         self.ch = p.shape[1] // CH
 
     def order(self, k):
-        a, b, c, d = [3, 2, 1, 0][k], [3, 0, 2, 1][k], [0, 3, 1, 2][k], [0, 1, 2, 3][k]
-        z = self.z
-        return jnp.where(z == 0, a, jnp.where(z == 1, b, jnp.where(z == 2, c, d)))
+        low = jnp.where(self.z < 2, self.z, 3 - self.z)
+        inner = jnp.where(k == 0, 3, jnp.where(k == 1, 0, jnp.where(k == 2, 2, 1)))
+        base = jnp.where(low == 0, 3 - k, inner)
+        return jnp.where(self.z < 2, base, 3 - base)
 
     def rows(self, c):
         return pl.ds(c * self.ch, self.ch)
@@ -1029,6 +1023,31 @@
     pass
 
 
+def looped(plan, name, work, queues):
+    count = plan.count(name)
+    groups = plan.split(name)
+    left = {k: list(v) for k, v in queues.items()}
+
+    def between(now, group):
+        items = [left[k].pop(0) for k in group]
+        if items:
+
+            @pl.when(now)
+            def _():
+                for item in items:
+                    item()
+
+    @pl.loop(0, count)
+    def _(i):
+        for n in range(count):
+            between(i == n, groups[n])
+        work(i)
+
+    for k in groups[count]:
+        left[k].pop(0)()
+    return left
+
+
 def fetch(refs, sems):
     copies = [pltpu.make_async_copy(a, b, sems.at[i]) for i, (a, b) in enumerate(refs)]
     for copy in copies:
@@ -1057,17 +1076,15 @@
     "nFngnWggssswwVnsnswwssvswsvsnsnssvsvwsnvDwwwcwcc",
     "wcfvccvwvdvdcwwcwwvcwcwcccvcccwdwvwwwcwwcXvvvww",
 )
-MIDDLE_ARRIVALS = (1, 2, 0, 1, 1, 1)
-MIDDLE_PLAN = ("ramaarteeraatelalmmetalteretlemmalltlehhthllhhhhtzhh",)
-BACKWARD_PLAN = ("bFggrgbbXgbgbgrbfbrtZtbcrotccoocotocootocqOcccptccccPttz",)
-LAST_PLAN = ("daddeawdahtaeeaaahatewwttheteetehhhwhttzhZ",)
-
-
-def merged(*lists):
-    keyed = []
-    for n, items in enumerate(lists):
-        keyed += [((i + 0.5) / len(items), n, item) for i, item in enumerate(items)]
-    return [item for _, _, item in sorted(keyed, key=lambda v: v[:2])]
+MIDDLE_PLAN = (
+    "gbggbbgbgbgbbb",
+    "raaaraeateaeearea",
+    "mertmeemm",
+    "Mlltllhtthhlltlthhl",
+    "LhhhHtz",
+)
+BACKWARD_PLAN = ("bFggrgbbXgbgbgrbfbrtZtb", "crotccoocotocootocqOcccptccccPttz")
+LAST_PLAN = ("ataaeeathtaheatttehehetaa", "eehthhzhZ")
 
 
 def dot(a, b, ca=1, cb=0):
@@ -1576,22 +1593,20 @@
         act[at] = jnp.concatenate([gate_act, up_act], 1)
         part[b] = dot(act[at], ww_ref[...], 1, 1).astype(jnp.bfloat16)
 
-    gather.each(block, MIDDLE_ARRIVALS)
-
     def wide_grad(i):
-        left = [c_ref[b, :, i * 256 : i * 256 + 256] for b in range(8)]
-        left = jnp.concatenate(left, 0)
-        big[i * 256 : i * 256 + 256, 0 : 2 * lf] = dot(left, act[...], 0, 0).astype(jnp.bfloat16)
+        at = row_at(i, 256)
+        left = jnp.concatenate([c_ref[b, :, at] for b in range(8)], 0)
+        big[at, 0 : 2 * lf] = dot(left, act[...], 0, 0).astype(jnp.bfloat16)
         sums.send(i)
 
     def mlp_part(i):
-        @pl.loop(2 * i, 2 * i + 2)
-        def _(b):
+        for k in range(2):
+            b = 2 * i + k
             at = pl.ds(pl.multiple_of(b * rows, rows), rows)
             mp_ref[b] = dot(hid[at], dw_ref[...]).astype(jnp.bfloat16)
 
     def down_grad(i):
-        cols = slice(i * 256, i * 256 + 256)
+        cols = row_at(i, 256)
         right = jnp.concatenate([dm_ref[b, :, cols] for b in range(8)], 0)
         dg_ref[:, cols] = dot(hid[...], right, 0, 0).astype(jnp.bfloat16)
 
@@ -1609,24 +1624,27 @@
 
     p = functools.partial
     each = range(8)
-    queues = dict(
-        r=[p(reduce.send, k) for k in range(4)],
-        t=reduce.steps(),
-        a=[p(wide_grad, i) for i in each],
-        e=[p(sums.step, i) for i in each],
-        h=[p(sums.total, i) for i in each],
-        m=[p(mlp_part, i) for i in range(4)],
-        l=[p(down_grad, i) for i in each],
-        z=[norm_backward],
-    )
     out_copies = [
         pltpu.make_async_copy(mp_ref, mp_hbm, store.at[2]),
         pltpu.make_async_copy(dg_ref, dg_hbm, store.at[3]),
         pltpu.make_async_copy(h_ref, h_hbm, store.at[4]),
     ]
-    for name, copy in zip("mlh", out_copies):
-        queues[name].append(copy.start)
-    perform(MIDDLE_PLAN, queues)
+    left = dict(
+        g=gather.steps(),
+        r=[p(reduce.send, k) for k in range(4)],
+        t=reduce.steps(),
+        e=[p(sums.step, i) for i in each],
+        h=[p(sums.total, i) for i in each],
+        z=[norm_backward],
+        M=[out_copies[0].start],
+        L=[out_copies[1].start],
+        H=[out_copies[2].start],
+    )
+    left = looped(MIDDLE_PLAN[0], "b", lambda j: block(gather.turn(j)), left)
+    left = looped(MIDDLE_PLAN[1], "a", wide_grad, left)
+    left = looped(MIDDLE_PLAN[2], "m", mlp_part, left)
+    left = looped(MIDDLE_PLAN[3], "l", down_grad, left)
+    perform(MIDDLE_PLAN[4], left)
     for copy in stores + out_copies:
         copy.wait()
     gather.finish(False)
@@ -1764,16 +1782,13 @@
         da[r] = rg_ref[r].astype(jnp.bfloat16)
 
     gather.start()
+    gather.own.wait()
+    loads[0].wait()
 
     def block(b):
         at = pl.ds(pl.multiple_of(b * rows, rows), rows)
         out_rows = jnp.concatenate([or_ref[k] for k in range(4)], 0)
         do_ref[at] = dot(full[b], out_rows, 1, 1).astype(jnp.bfloat16)
-
-    def own_block():
-        gather.own.wait()
-        loads[0].wait()
-        block(s)
 
     def before(copies, then):
         def run():
@@ -1788,12 +1803,6 @@
     def down_total():
         down.total()
         out_copies[0].start()
-
-    blocks = [own_block]
-    for i in range(4):
-        if i < 3:
-            blocks.append(lambda i=i: block(gather.column(i + 1)))
-        blocks.append(lambda i=i: block(gather.cross(i)))
 
     def out_grad(i):
         cols = slice(i * 256, i * 256 + 256)
@@ -1842,7 +1851,6 @@
         F=[before(loads[1:2], down.start)],
         f=[down.step],
         q=[down_total],
-        b=blocks,
         g=gather.steps(),
         r=[before(loads[2:3], sends[0])] + sends[1:],
         t=reduce.steps(),
@@ -1855,7 +1863,8 @@
         P=[outer_sum.total],
         z=[before(loads[7:9], results)],
     )
-    perform(BACKWARD_PLAN, queues)
+    left = looped(BACKWARD_PLAN[0], "b", lambda j: block(gather.turn(j)), queues)
+    perform(BACKWARD_PLAN[1], left)
     gather.finish(False)
     reduce.finish()
     down.finish()
@@ -1969,18 +1978,18 @@
         at = pl.ds(pl.multiple_of(b * rows, rows), rows)
         part[b] = dot(g_ref[at], qw_ref[...], 1, 1).astype(jnp.bfloat16)
 
-    def far_block(k):
-        block(2 * reduce.order(k) + 1 - y)
-        reduce.send(k)
-
-    def own_block(k):
-        block(2 * reduce.order(k) + y)
-
-    def qkv_grad(k):
-        if k == 7:
-            loads[1].wait()
-        i = peer(s, k)
-        at = pl.ds(pl.multiple_of(i * 256, 256), 256)
+    def block_at(j):
+        far = j < 4
+        zb = reduce.order(j % 4)
+        block(2 * zb + jnp.where(far, 1 - y, y))
+
+        @pl.when(far)
+        def _():
+            reduce.send(j)
+
+    def qkv_grad(n):
+        i = peer_at(s, 7 - n)
+        at = row_at(i, 256)
         left = jnp.concatenate([a_ref[b, :, at] for b in range(8)], 0)
         grad[at] = dot(left, g_ref[...], 0, 0).astype(jnp.bfloat16)
         sums.send(i)
@@ -2029,16 +2038,16 @@
     p = functools.partial
     ks = [7, 6, 5, 4, 3, 2, 1, 0]
     queues = dict(
-        d=[p(far_block, k) for k in range(4)],
-        w=[p(own_block, k) for k in range(4)],
         t=reduce.steps(),
-        a=[p(qkv_grad, k) for k in ks],
         e=[lambda k=k: sums.step(peer(s, k)) for k in ks],
         h=[p(hand_over, k) for k in ks],
         z=[norm_backward],
         Z=[swap.finish],
     )
-    perform(LAST_PLAN, queues)
+    pl.loop(0, 8)(block_at)
+    loads[1].wait()
+    left = looped(LAST_PLAN[0], "a", qkv_grad, queues)
+    perform(LAST_PLAN[1], left)
     reduce.finish()
     sums.finish()
     total_ref[...] = msg[me // 2]

time: 484 us -> 476 us (0.983); the launches traced: 476 us -> 475 us
  no operation moved by 1% of the time
where the time goes in v7:
time: 476 us; the launch traced here: 475 us
  Pallas kernels  468 us (98%)
    pallas_call x1, Pallas kernels, forward(): pl.pallas_call(forward_kernel, out_shape=(out((8, rows, width)), out((wid...  168 us
    pallas_call x1, Pallas kernels, backward(): pl.pallas_call(backward_kernel, out_shape=(out((group, 3 * w), jnp.bfloat...  114 us
    pallas_call x1, Pallas kernels, middle(): pl.pallas_call(middle_kernel, out_shape=(out(wide, jnp.float32), out(wide...  109 us
    pallas_call x1, Pallas kernels, last(): pl.pallas_call(last_kernel, out_shape=(out((rows, width)), out((8, pr, w3...  71.4 us

profile of v7, /device:TPU:0, one launch (start us, length us, event | category | flops | bytes accessed | tf_op | source)
XLA Modules:
  0.0 475.2 jit_solution(976690933610558498)
XLA Ops:
  0.7 0.5 fusion.2.freq_ref
  1.2 0.8 stack.20
  2.0 0.7 pad_select_fusion.p_ref
  2.6 1.7 copy.27.ocol_ref
  4.3 167.6 %shard_map.237 = (bf16[8,128,2048]{2,1,0:T(8,128)(2,1)}, bf16[2048,768]{1,0:T(8,128)(2,1)}, f32[8,2048]{1,0:T(8,128)}, bf16[32,64,2048]{2,1,0:T(8,128)(2,1)}, bf...) custom-call(bf16[128,2048]{1,0:T(8,128)(2,1)} %bitcast.25, ...), custom_call_target="tpu_custom_call" | custom-call | tf_op jit(solution)/shard_map/pallas_call | solution.py:1462
  172.0 108.8 %shard_map.238 = (f32[128,2048]{1,0:T(8,128)}, f32[128,2048]{1,0:T(8,128)}, f32[128,2048]{1,0:T(8,128)}, f32[8,2048]{1,0:T(8,128)}, bf16[8,128,2048]{2,1,0:T(8,1...) custom-call(bf16[8,128,256]{2,1,0:T(8,128)(2,1)} %get-tuple-element.48.ho_hbm, ...), custom_call_target="tpu_custom_call" | custom-call | tf_op jit(solution)/shard_map/pallas_call | solution.py:1668
  280.8 114.1 %shard_map.239 = (bf16[1024,768]{1,0:T(8,128)(2,1)}, f32[1,768]{1,0:T(1,128)}, bf16[128,2048]{1,0:T(8,128)(2,1)}, f32[8,128]{1,0:T(8,128)}, bf16[8,64,1408]{2,1,...) custom-call(f32[128,2048]{1,0:T(8,128)} %get-tuple-element.54.rg_ref.rg_hbm, f32[1,128]{1,0:T(1,128)} %fusion.2.freq_ref, ...), custom_call_target="tpu_custom_call" | custom-call | tf_op jit(solution)/shard_map/pallas_call | solution.py:1890
  394.8 71.4 %shard_map.240 = (f32[128,2048]{1,0:T(8,128)}, bf16[8,64,768]{2,1,0:T(8,128)(2,1)}, f32[8,128]{1,0:T(8,128)}) custom-call(bf16[1024,768]{1,0:T(8,128)(2,1)} %get-tuple-element.64.g_ref, f32[1,768]{1,0:T(1,128)} %get-tuple-element.65.b_ref, f32[8,2048]{1,0:T(8,128)} %get-tuple-element.50.n_ref, f32[8,2048]{1,0:T(8,128)} %get-tuple-element.66.vec_ref, ...), custom_call_target="tpu_custom_call" | custom-call | tf_op jit(solution)/shard_map/pallas_call | solution.py:2076
  466.2 1.2 sqrt_bitcast_fusion
  467.4 0.7 constant_dynamic-slice_fusion
  468.2 0.6 slice.33
  468.7 0.5 slice_bitcast_fusion
  469.3 5.7 %shard_map.241 = (bf16[128,2048]{1,0:T(8,128)(2,1)}, f32[128,2048]{1,0:T(8,128)}, f32[176,2048]{1,0:T(8,128)}, f32[64,2048]{1,0:T(8,128)}, f32[64,5632]{1,0:T(8,...) custom-call(bf16[128,2048]{1,0:T(8,128)(2,1)} %get-tuple-element.63.refs_0_, f32[128,2048]{1,0:T(8,128)} %get-tuple-element.70.refs_1_, ...), custom_call_target="tpu_custom_call" | custom-call | tf_op jit(solution)/shard_map/pallas_call | solution.py:2135
  (1 shorter events, 0.0 us)

commit v8 on v7

--- a/solution.py
+++ b/solution.py
@@ -841,10 +841,12 @@
         self.arrived(self.fx).wait_recv()
         self.pass_on(2, self.o.at[self.fx], self.fx, self.fc).start()
 
-    def finish(self):
+    def complete(self):
         self.mine.wait()
         self.arrived(self.fc).wait_recv()
         self.arrived(self.fd).wait_recv()
+
+    def finish(self):
         for n in range(3):
             self.pass_on(n, self.x, self.f, self.fc).wait_send()
 
@@ -969,12 +971,14 @@
                 out.append(p(self.side, sign, t, 1))
         return out
 
-    def finish(self):
+    def complete(self):
         self.mine.wait()
         for zb in range(4):
             for yy in range(2):
                 self.arrived(self.at(zb, yy, self.fc)).wait_recv()
                 self.arrived(self.at(zb, yy, self.fd)).wait_recv()
+
+    def finish(self):
         for zb in range(4):
             self.over_y(zb).wait_send()
 
@@ -1069,12 +1073,15 @@
     left = {name: list(items) for name, items in queues.items()}
     for name in "".join(plan):
         left[name].pop(0)()
-    assert not any(left.values())
+    return left
 
 
 FORWARD_PLAN = (
-    "nFngnWggssswwVnsnswwssvswsvsnsnssvsvwsnvDwwwcwcc",
-    "wcfvccvwvdvdcwwcwwvcwcwcccvcccwdwvwwwcwwcXvvvww",
+    "FnggsnWsgswwsDswwnnsssVswsswsws",
+    "nswwnsnnccwwccccvdvwcccwccwwcdv",
+    "vwwwfcccwwwccwwcvXwwwvvdvvvwvvY",
+    "PPvvvPP",
+    "Q",
 )
 MIDDLE_PLAN = (
     "gbggbbgbgbgbbb",
@@ -1290,16 +1297,25 @@
     orow_ref,
     ocol_ref,
     len_ref,
+    a_hbm,
+    qw_hbm,
+    n_ref,
+    or_hbm,
+    pk_hbm,
+    lse_hbm,
+    dmo_ref,
+    ww_ref,
+    dw_ref,
+    mix_hbm,
+    attn_ref,
+    res_ref,
+    second_ref,
     a_ref,
     qw_ref,
-    n_ref,
     ow_ref,
     ho_ref,
     pk_ref,
     lse_ref,
-    dmo_ref,
-    ww_ref,
-    dw_ref,
     mix_ref,
     x_ref,
     op_ref,
@@ -1314,6 +1330,7 @@
     qp_ref,
     wp_ref,
     load,
+    store,
     psend,
     precv,
     *sems,
@@ -1322,6 +1339,7 @@
     me = s * 4 + f
     w = rot.shape[1] // 3
     lf = wp_ref.shape[2] // 2
+    rows, width = x_ref.shape
 
     def piece_of(i):
         t, n = i // 3, i % 3
@@ -1409,6 +1427,39 @@
             wp_ref[i, :, 0:lf] = gate_ref[:, at]
             wp_ref[i, :, lf : 2 * lf] = up_ref[:, at]
         wide.start()
+
+    saved = [(a_ref, a_hbm), (qw_ref, qw_hbm), (pk_ref, pk_hbm), (lse_ref, lse_hbm)]
+    saved.append((mix_ref, mix_hbm))
+    stores = [pltpu.make_async_copy(u, v, store.at[i]) for i, (u, v) in enumerate(saved)]
+    here = pl.ds(pl.multiple_of(s * 4, 4), 4)
+    stores.append(pltpu.make_async_copy(ow_ref.at[here], or_hbm, store.at[5]))
+
+    def swap_start():
+        swap.start()
+        for copy in stores[:5]:
+            copy.start()
+
+    def mixed_ready():
+        swap.finish()
+        whole.complete()
+        stores[5].start()
+
+    def project_out(j):
+        cols = row_at(j, 512)
+        total = jnp.zeros((rows, 512), jnp.float32)
+        for k in range(8):
+            right = jnp.concatenate([ow_ref[4 * k + q, :, cols] for q in range(4)], 0)
+            total = total + dot(ho_ref[k], right)
+        attn_ref[:, cols] = total
+        res_ref[:, cols] = x_ref[:, cols].astype(jnp.float32) + total
+
+    def second_norm():
+        gain, shift = n_ref[2:3], n_ref[3:4]
+
+        @tall(rows)
+        def _(r):
+            normed, _ = normalize(res_ref[r])
+            second_ref[r] = (normed * gain + shift).astype(jnp.bfloat16)
 
     norms = [own]
     for i in range(4):
@@ -1429,17 +1480,24 @@
         V=[wide_start],
         W=[whole.start],
         F=[down.start],
-        X=[swap.start],
+        X=[swap_start],
+        Y=[mixed_ready],
+        Q=[second_norm],
     )
     work[0:2] = [lambda first=work[0], then=work[1]: (first(), then())]
-    perform(FORWARD_PLAN, queues)
+    left = perform(FORWARD_PLAN[:3], queues)
+    left = looped(FORWARD_PLAN[3], "P", project_out, left)
+    perform(FORWARD_PLAN[4:], left)
     for i in range(4):
         grads.cross(i)
-    swap.finish()
     wide.complete()
+    down.complete()
     for task in (slices, wide, whole, down, grads):
         task.finish()
     gather.finish(False)
+
+    for copy in stores:
+        copy.wait()
 
     @pl.loop(1, 32)
     def _(k):
@@ -1465,22 +1523,29 @@
             out((8, rows, width)),
             out((width, w3)),
             out((8, width), jnp.float32),
-            out((32,) + out_p.shape),
-            out((8, rows, w)),
+            out((4,) + out_p.shape),
             out((valid, w3)),
             out((heads, valid, 1), jnp.float32),
             out((8, rows, width)),
             out((width, wide)),
             out((4,) + down_p.shape),
             out((8, rows, w)),
+            out((rows, width), jnp.float32),
+            out((rows, width), jnp.float32),
+            out((rows, width)),
         ),
         in_specs=[HBM_SPEC, VMEM_SPEC] + [HBM_SPEC] * 6 + [VMEM_SPEC] * 3 + [SMEM_SPEC],
-        out_specs=(VMEM_SPEC,) * 3
-        + (ANY_SPEC,)
-        + (VMEM_SPEC,) * 3
-        + (ANY_SPEC,) * 3
-        + (VMEM_SPEC,),
-        scratch_shapes=[pltpu.VMEM(v.shape, v.dtype) for v in (x, out_p, dm, gate, up, down_p)]
+        out_specs=(ANY_SPEC,) * 2 + (VMEM_SPEC,) + (ANY_SPEC,) * 7 + (VMEM_SPEC,) * 3,
+        scratch_shapes=[
+            pltpu.VMEM((8, rows, width), jnp.bfloat16),
+            pltpu.VMEM((width, w3), jnp.bfloat16),
+            pltpu.VMEM((32,) + out_p.shape, jnp.bfloat16),
+            pltpu.VMEM((8, rows, w), jnp.bfloat16),
+            pltpu.VMEM((valid, w3), jnp.bfloat16),
+            pltpu.VMEM((heads, valid, 1), jnp.float32),
+            pltpu.VMEM((8, rows, w), jnp.bfloat16),
+        ]
+        + [pltpu.VMEM(v.shape, v.dtype) for v in (x, out_p, dm, gate, up, down_p)]
         + [
             pltpu.VMEM((8, rows, width), jnp.bfloat16),
             pltpu.VMEM((32, 8, 128), jnp.float32),
@@ -1489,6 +1554,7 @@
             pltpu.VMEM((8, part, w3), jnp.bfloat16),
             pltpu.VMEM((8, part, wide), jnp.bfloat16),
             DMA((30,)),
+            DMA((6,)),
             DMA((32,)),
             DMA((32,)),
         ]
@@ -1513,32 +1579,25 @@
 
 
 def middle_kernel(
-    ho_hbm,
-    ow_ref,
-    x_hbm,
+    cloc,
     n_ref,
     ww_hbm,
     dw_hbm,
     dm_hbm,
-    attn_hbm,
     res_hbm,
     rg_ref,
     vec_ref,
     mp_hbm,
     dg_hbm,
     h_hbm,
-    ho_ref,
-    x_ref,
     ww_ref,
     dw_ref,
     dm_ref,
-    attn_ref,
     res_ref,
     mp_ref,
     dg_ref,
     h_ref,
     big,
-    cloc,
     c_ref,
     hid,
     act,
@@ -1549,37 +1608,18 @@
     *scratch,
 ):
     s, f, z, y = where_am_i()
-    rows, width = x_ref.shape
+    rows, width = cloc.shape
     lf = dw_ref.shape[0]
-    lw = ho_ref.shape[2]
-    first = [(ho_hbm, ho_ref), (x_hbm, x_ref), (ow_ref, big)]
-    loads = fetch(first + [(ww_hbm, ww_ref), (dw_hbm, dw_ref), (dm_hbm, dm_ref)], load)
+    operands = [(ww_hbm, ww_ref), (dw_hbm, dw_ref), (dm_hbm, dm_ref), (res_hbm, res_ref)]
+    loads = fetch(operands, load)
     greet_columns(s, f)
     gather = SeqGather(cloc, c_ref, *scratch[:5])
     reduce = SeqReduce(part, second, *scratch[5:11])
     sums = ColSum(big, h_ref, *scratch[11:])
-    gain, shift = n_ref[2:3], n_ref[3:4]
-    for copy in loads[:3]:
-        copy.wait()
-
-    @pl.loop(0, width // 512)
-    def _(j):
-        cols = pl.ds(pl.multiple_of(j * 512, 512), 512)
-        total = dot(ho_ref[0], big[0:lw, cols])
-        for k in range(1, 8):
-            total = total + dot(ho_ref[k], big[k * lw : k * lw + lw, cols])
-        attn_ref[:, cols] = total
-        res_ref[:, cols] = x_ref[:, cols].astype(jnp.float32) + total
-
-    @tall(rows)
-    def _(r):
-        normed, _ = normalize(res_ref[r])
-        cloc[r] = (normed * gain + shift).astype(jnp.bfloat16)
-
+    gain = n_ref[2:3]
     gather.start()
-    stores = fetch([(attn_ref, attn_hbm), (res_ref, res_hbm)], store)
     gather.own.wait()
-    for copy in loads[3:]:
+    for copy in loads:
         copy.wait()
 
     def block(b):
@@ -1625,9 +1665,9 @@
     p = functools.partial
     each = range(8)
     out_copies = [
-        pltpu.make_async_copy(mp_ref, mp_hbm, store.at[2]),
-        pltpu.make_async_copy(dg_ref, dg_hbm, store.at[3]),
-        pltpu.make_async_copy(h_ref, h_hbm, store.at[4]),
+        pltpu.make_async_copy(mp_ref, mp_hbm, store.at[0]),
+        pltpu.make_async_copy(dg_ref, dg_hbm, store.at[1]),
+        pltpu.make_async_copy(h_ref, h_hbm, store.at[2]),
     ]
     left = dict(
         g=gather.steps(),
@@ -1645,15 +1685,15 @@
     left = looped(MIDDLE_PLAN[2], "m", mlp_part, left)
     left = looped(MIDDLE_PLAN[3], "l", down_grad, left)
     perform(MIDDLE_PLAN[4], left)
-    for copy in stores + out_copies:
+    for copy in out_copies:
         copy.wait()
     gather.finish(False)
     reduce.finish()
     sums.finish()
 
 
-def middle(heads_out, out_w, x, norms, wide_w, down_w, dm, collective):
-    rows, width = x.shape
+def middle(second, norms, wide_w, down_w, dm, res, collective):
+    rows, width = second.shape
     lf = down_w.shape[0]
     group = 8 * rows
     part = width // 32
@@ -1668,42 +1708,36 @@
     return pl.pallas_call(
         middle_kernel,
         out_shape=(
-            out(wide, jnp.float32),
-            out(wide, jnp.float32),
             out(wide, jnp.float32),
             out((8, width), jnp.float32),
             out((8,) + wide),
             out((lf, width)),
             out((8, part, 2 * lf)),
         ),
-        in_specs=[HBM_SPEC] * 3 + [VMEM_SPEC] + [HBM_SPEC] * 3,
-        out_specs=(ANY_SPEC,) * 2 + (VMEM_SPEC,) * 2 + (ANY_SPEC,) * 3,
+        in_specs=[VMEM_SPEC] * 2 + [HBM_SPEC] * 4,
+        out_specs=(VMEM_SPEC,) * 2 + (ANY_SPEC,) * 3,
         scratch_shapes=[
-            vm(heads_out.shape),
-            vm(wide),
             vm(wide_w.shape),
             vm(down_w.shape),
             vm(dm.shape),
             vm(wide, jnp.float32),
-            vm(wide, jnp.float32),
             vm((8,) + wide),
             vm((lf, width)),
             vm((8, part, 2 * lf)),
-            vm((width, width)),
-            vm(wide),
+            vm((width, 2 * lf)),
             vm((8,) + wide),
             vm((group, lf)),
             vm((group, 2 * lf)),
             vm((8,) + wide),
             vm(wide, jnp.float32),
-            DMA((6,)),
-            DMA((5,)),
+            DMA((4,)),
+            DMA((3,)),
         ]
         + SeqGather.scratch(2)
         + SeqReduce.scratch(rows, width)
         + ColSum.scratch(part, 2 * lf),
         compiler_params=comm_params(collective),
-    )(heads_out, out_w, x, norms, wide_w, down_w, dm)
+    )(second, norms, wide_w, down_w, dm, res)
 
 
 def backward_kernel(
@@ -1758,7 +1792,7 @@
     valid = pk_ref.shape[0]
     loads = fetch(
         [
-            (ow_hbm.at[pl.ds(pl.multiple_of(s * 4, 4), 4)], or_ref),
+            (ow_hbm, or_ref),
             (dg_hbm, dg_ref),
             (mp_hbm, mp_ref),
             (h_hbm, h_ref),
@@ -2180,7 +2214,21 @@
     params = jnp.stack([ln1_gain, ln1_bias, ln2_gain, ln2_bias, *qkv_bias])
     params = jnp.pad(params.astype(jnp.float32), ((0, 1), (0, 64)))
     params = jnp.where(fsdp_at % 2 == 0, params, jnp.roll(params, part, 1))
-    first_in, qkv_w, norms, out_w, heads_out, packed, lse, mlp_grad, wide_w, down_w, mixed = forward(
+    (
+        first_in,
+        qkv_w,
+        norms,
+        out_rows,
+        packed,
+        lse,
+        mlp_grad,
+        wide_w,
+        down_w,
+        mixed,
+        attn,
+        resid,
+        second,
+    ) = forward(
         hidden_in[0],
         params,
         qkv_weight,
@@ -2196,15 +2244,8 @@
         valid_rows,
         1,
     )
-    attn, resid, resid_grad, norm2_grads, mlp_part, down_part, wide_sum = middle(
-        heads_out,
-        out_w.reshape(width, width),
-        hidden_in[0],
-        norms,
-        wide_w,
-        down_w.reshape(lf, width),
-        mlp_grad,
-        3,
+    resid_grad, norm2_grads, mlp_part, down_part, wide_sum = middle(
+        second, norms, wide_w, down_w.reshape(lf, width), mlp_grad, resid, 3
     )
     qkv_act, bias_sums, result, sums, wide_pieces, down_grad, out_grad_w = backward(
         resid_grad,
@@ -2212,7 +2253,7 @@
         orow,
         ocol,
         seq_lengths,
-        out_w,
+        out_rows,
         mixed.reshape(group_rows, lw),
         packed,
         lse,

time: 476 us -> 468 us (0.983)
  Pallas kernels: 468 us -> 460 us
where the time goes in v8:
time: 468 us
  Pallas kernels  460 us (98%)
    pallas_call x1, Pallas kernels, forward(): pl.pallas_call(forward_kernel, out_shape=(out((8, rows, width)), out((wid...  166 us
    pallas_call x1, Pallas kernels, backward(): pl.pallas_call(backward_kernel, out_shape=(out((group, 3 * w), jnp.bfloat...  113 us
    pallas_call x1, Pallas kernels, middle(): pl.pallas_call(middle_kernel, out_shape=(out(wide, jnp.float32), out((8,...  104 us
    pallas_call x1, Pallas kernels, last(): pl.pallas_call(last_kernel, out_shape=(out((rows, width)), out((8, pr, w3...  70.3 us

profile of v8, /device:TPU:0, one launch (start us, length us, event | category | flops | bytes accessed | tf_op | source)
XLA Modules:
  0.0 467.6 jit_solution(8962603159751179900)
XLA Ops:
  0.7 0.5 fusion.2.freq_ref
  1.2 0.8 stack.20
  2.0 0.7 pad_select_fusion.p_ref
  2.6 1.7 copy.27.ocol_ref
  4.3 166.4 %shard_map.237 = (bf16[8,128,2048]{2,1,0:T(8,128)(2,1)}, bf16[2048,768]{1,0:T(8,128)(2,1)}, f32[8,2048]{1,0:T(8,128)}, bf16[4,64,2048]{2,1,0:T(8,128)(2,1)}, bf1...) custom-call(bf16[128,2048]{1,0:T(8,128)(2,1)} %bitcast.25, ...), custom_call_target="tpu_custom_call" | custom-call | tf_op jit(solution)/shard_map/pallas_call | solution.py:1520
  170.7 104.3 %shard_map.238 = (f32[128,2048]{1,0:T(8,128)}, f32[8,2048]{1,0:T(8,128)}, bf16[8,128,2048]{2,1,0:T(8,128)(2,1)}, bf16[704,2048]{1,0:T(8,128)(2,1)}, bf16[8,64,1408]{2,1,0:T(8,128)(2,1)}) custom-call(bf16[128,2048]{1,0:T(8,128)(2,1)} %get-tuple-element.48.cloc, f32[8,2048]{1,0:T(8,128)} %get-tuple-element.49.n_ref, ...), custom_call_target="tpu_custom_call" | custom-call | tf_op jit(solution)/shard_map/pallas_call | solution.py:1708
  275.1 113.2 %shard_map.239 = (bf16[1024,768]{1,0:T(8,128)(2,1)}, f32[1,768]{1,0:T(1,128)}, bf16[128,2048]{1,0:T(8,128)(2,1)}, f32[8,128]{1,0:T(8,128)}, bf16[8,64,1408]{2,1,...) custom-call(f32[128,2048]{1,0:T(8,128)} %get-tuple-element.54.rg_ref.rg_hbm, f32[1,128]{1,0:T(1,128)} %fusion.2.freq_ref, ...), custom_call_target="tpu_custom_call" | custom-call | tf_op jit(solution)/shard_map/pallas_call | solution.py:1924
  388.3 70.3 %shard_map.240 = (f32[128,2048]{1,0:T(8,128)}, bf16[8,64,768]{2,1,0:T(8,128)(2,1)}, f32[8,128]{1,0:T(8,128)}) custom-call(bf16[1024,768]{1,0:T(8,128)(2,1)} %get-tuple-element.64.g_ref, f32[1,768]{1,0:T(1,128)} %get-tuple-element.65.b_ref, f32[8,2048]{1,0:T(8,128)} %get-tuple-element.49.n_ref, f32[8,2048]{1,0:T(8,128)} %get-tuple-element.66.vec_ref, ...), custom_call_target="tpu_custom_call" | custom-call | tf_op jit(solution)/shard_map/pallas_call | solution.py:2110
  458.6 1.2 sqrt_bitcast_fusion
  459.8 0.7 constant_dynamic-slice_fusion
  460.5 0.6 slice.33
  461.1 0.5 slice_bitcast_fusion
  461.6 5.8 %shard_map.241 = (bf16[128,2048]{1,0:T(8,128)(2,1)}, f32[128,2048]{1,0:T(8,128)}, f32[176,2048]{1,0:T(8,128)}, f32[64,2048]{1,0:T(8,128)}, f32[64,5632]{1,0:T(8,...) custom-call(bf16[128,2048]{1,0:T(8,128)(2,1)} %get-tuple-element.63.refs_0_, f32[128,2048]{1,0:T(8,128)} %get-tuple-element.70.refs_1_, ...), custom_call_target="tpu_custom_call" | custom-call | tf_op jit(solution)/shard_map/pallas_call | solution.py:2169
  (1 shorter events, 0.0 us)

commit v9 on v8

--- a/solution.py
+++ b/solution.py
@@ -545,6 +545,101 @@
                     self.dsend(zb, c).wait_send()
 
 
+class EvenGather(SeqGather):
+    @staticmethod
+    def scratch():
+        return SeqGather.scratch(2) + [DMA((2,))]
+
+    def __init__(self, x, o, own, recv, sy, su, sd, side):
+        super().__init__(x, o, own, recv, sy, su, sd)
+        self.side_sems = side
+
+    def arrive(self, i, c=0):
+        zb = self.near(i)
+        self.arrived(self.at(zb), c).wait_recv()
+
+        @pl.when((zb < self.z) & (self.z < 3))
+        def _():
+            self.usend(zb, c).start()
+
+        @pl.when((zb > self.z) & (self.z > 0))
+        def _():
+            self.dsend(zb, c).start()
+
+        if c == 0:
+            self.ysend(zb, c).start()
+        else:
+
+            @pl.when((zb == 1) | (zb == 2))
+            def _():
+                self.ysend(zb, c).start()
+
+    def along(self, e):
+        b, r = 2 * e + 1 - self.y, self.rows(1)
+        v = self.o.at[b, r]
+        to = self.s + 2 if e == 0 else self.s - 2
+        return remote(v, v, self.side_sems.at[e // 3], self.recv.at[b, 1], (to, self.f))
+
+    def pass_along(self, e):
+        self.arrived(2 * e + 1 - self.y, 1).wait_recv()
+
+        @pl.when(self.z != 3 - e)
+        def _():
+            self.along(e).start()
+
+    def lead(self):
+        for e in (0, 3):
+
+            @pl.when(self.z == e)
+            def _():
+                self.pass_along(e)
+
+    def follow(self):
+        for first in (True, False):
+            for e in (0, 3):
+                closer = (self.z < 2) == (e == 0)
+
+                @pl.when((self.z != e) & (closer == first))
+                def _():
+                    self.pass_along(e)
+
+    def cross(self, i):
+        zb = self.near(i)
+        b = 2 * zb + 1 - self.y
+        self.arrived(b, 0).wait_recv()
+
+        @pl.when((zb == 1) | (zb == 2))
+        def _():
+            self.arrived(b, 1).wait_recv()
+
+        return b
+
+    def finish(self):
+        for c in range(2):
+            for zb in range(4):
+                if c == 0 or zb in (1, 2):
+                    self.ysend(zb, c).wait_send()
+                else:
+
+                    @pl.when(self.z == zb)
+                    def _():
+                        self.ysend(zb, c).wait_send()
+
+                @pl.when((self.z < 3) & (zb <= self.z))
+                def _():
+                    self.usend(zb, c).wait_send()
+
+                @pl.when((self.z > 0) & (zb >= self.z))
+                def _():
+                    self.dsend(zb, c).wait_send()
+
+        for e in (0, 3):
+
+            @pl.when(self.z != 3 - e)
+            def _():
+                self.along(e).wait_send()
+
+
 class SeqReduce:
     @staticmethod
     def scratch(rows, w):
@@ -1090,7 +1185,7 @@
     "Mlltllhtthhlltlthhl",
     "LhhhHtz",
 )
-BACKWARD_PLAN = ("bFggrgbbXgbgbgrbfbrtZtb", "crotccoocotocootocqOcccptccccPttz")
+BACKWARD_PLAN = ("bFggKrgbbXgbggSbrbfbrtZtb", "crotccoocotocootocqOcccptccccPttz")
 LAST_PLAN = ("ataaeeathtaheatttehehetaa", "eehthhzhZ")
 
 
@@ -1805,11 +1900,11 @@
         load,
     )
     greet_columns(s, f)
-    gather = SeqGather(da, full, *scratch[:5])
-    reduce = SeqReduce(mp_ref, mlp, *scratch[5:11])
-    swap = RowExchange(h_ref, got, *scratch[11:14])
-    down = FsdpReduce(dg_ref, down_ref, *scratch[14:18])
-    outer_sum = FsdpReduce(og, out_ref, *scratch[18:])
+    gather = EvenGather(da, full, *scratch[:6])
+    reduce = SeqReduce(mp_ref, mlp, *scratch[6:12])
+    swap = RowExchange(h_ref, got, *scratch[12:15])
+    down = FsdpReduce(dg_ref, down_ref, *scratch[15:19])
+    outer_sum = FsdpReduce(og, out_ref, *scratch[19:])
 
     @tall(rows)
     def _(r):
@@ -1886,6 +1981,8 @@
         f=[down.step],
         q=[down_total],
         g=gather.steps(),
+        K=[gather.lead],
+        S=[gather.follow],
         r=[before(loads[2:3], sends[0])] + sends[1:],
         t=reduce.steps(),
         X=[before(loads[3:4], swap.start)],
@@ -1899,7 +1996,7 @@
     )
     left = looped(BACKWARD_PLAN[0], "b", lambda j: block(gather.turn(j)), queues)
     perform(BACKWARD_PLAN[1], left)
-    gather.finish(False)
+    gather.finish()
     reduce.finish()
     down.finish()
     outer_sum.finish()
@@ -1958,7 +2055,7 @@
             DMA((9,)),
             DMA,
         ]
-        + SeqGather.scratch(2)
+        + EvenGather.scratch()
         + SeqReduce.scratch(rows, width)
         + RowExchange.scratch()
         + FsdpReduce.scratch(*dg.shape[1:])

time: 468 us -> 463 us (0.989)
  Pallas kernels: 460 us -> 455 us
    pallas_call x1, Pallas kernels: 113 us -> 108 us  [backward(): pl.pallas_call(backward_kernel, out_shape=(out((group, 3 * w), jnp.bfloat...]
where the time goes in v9:
time: 463 us
  Pallas kernels  455 us (98%)
    pallas_call x1, Pallas kernels, forward(): pl.pallas_call(forward_kernel, out_shape=(out((8, rows, width)), out((wid...  166 us
    pallas_call x1, Pallas kernels, backward(): pl.pallas_call(backward_kernel, out_shape=(out((group, 3 * w), jnp.bfloat...  108 us
    pallas_call x1, Pallas kernels, middle(): pl.pallas_call(middle_kernel, out_shape=(out(wide, jnp.float32), out((8,...  104 us
    pallas_call x1, Pallas kernels, last(): pl.pallas_call(last_kernel, out_shape=(out((rows, width)), out((8, pr, w3...  71.2 us

profile of v9, /device:TPU:0, one launch (start us, length us, event | category | flops | bytes accessed | tf_op | source)
XLA Modules:
  0.0 462.9 jit_solution(17892228642525510721)
XLA Ops:
  0.7 0.5 fusion.2.freq_ref
  1.2 0.8 stack.20
  2.0 0.7 pad_select_fusion.p_ref
  2.6 1.7 copy.27.ocol_ref
  4.3 166.4 %shard_map.237 = (bf16[8,128,2048]{2,1,0:T(8,128)(2,1)}, bf16[2048,768]{1,0:T(8,128)(2,1)}, f32[8,2048]{1,0:T(8,128)}, bf16[4,64,2048]{2,1,0:T(8,128)(2,1)}, bf1...) custom-call(bf16[128,2048]{1,0:T(8,128)(2,1)} %bitcast.25, ...), custom_call_target="tpu_custom_call" | custom-call | tf_op jit(solution)/shard_map/pallas_call | solution.py:1615
  170.7 104.3 %shard_map.238 = (f32[128,2048]{1,0:T(8,128)}, f32[8,2048]{1,0:T(8,128)}, bf16[8,128,2048]{2,1,0:T(8,128)(2,1)}, bf16[704,2048]{1,0:T(8,128)(2,1)}, bf16[8,64,1408]{2,1,0:T(8,128)(2,1)}) custom-call(bf16[128,2048]{1,0:T(8,128)(2,1)} %get-tuple-element.48.cloc, f32[8,2048]{1,0:T(8,128)} %get-tuple-element.49.n_ref, ...), custom_call_target="tpu_custom_call" | custom-call | tf_op jit(solution)/shard_map/pallas_call | solution.py:1803
  275.1 107.6 %shard_map.239 = (bf16[1024,768]{1,0:T(8,128)(2,1)}, f32[1,768]{1,0:T(1,128)}, bf16[128,2048]{1,0:T(8,128)(2,1)}, f32[8,128]{1,0:T(8,128)}, bf16[8,64,1408]{2,1,...) custom-call(f32[128,2048]{1,0:T(8,128)} %get-tuple-element.54.rg_ref.rg_hbm, f32[1,128]{1,0:T(1,128)} %fusion.2.freq_ref, ...), custom_call_target="tpu_custom_call" | custom-call | tf_op jit(solution)/shard_map/pallas_call | solution.py:2021
  382.7 71.2 %shard_map.240 = (f32[128,2048]{1,0:T(8,128)}, bf16[8,64,768]{2,1,0:T(8,128)(2,1)}, f32[8,128]{1,0:T(8,128)}) custom-call(bf16[1024,768]{1,0:T(8,128)(2,1)} %get-tuple-element.64.g_ref, f32[1,768]{1,0:T(1,128)} %get-tuple-element.65.b_ref, f32[8,2048]{1,0:T(8,128)} %get-tuple-element.49.n_ref, f32[8,2048]{1,0:T(8,128)} %get-tuple-element.66.vec_ref, ...), custom_call_target="tpu_custom_call" | custom-call | tf_op jit(solution)/shard_map/pallas_call | solution.py:2207
  453.9 1.2 sqrt_bitcast_fusion
  455.1 0.7 constant_dynamic-slice_fusion
  455.9 0.6 slice.33
  456.4 0.5 slice_bitcast_fusion
  457.0 5.8 %shard_map.241 = (bf16[128,2048]{1,0:T(8,128)(2,1)}, f32[128,2048]{1,0:T(8,128)}, f32[176,2048]{1,0:T(8,128)}, f32[64,2048]{1,0:T(8,128)}, f32[64,5632]{1,0:T(8,...) custom-call(bf16[128,2048]{1,0:T(8,128)(2,1)} %get-tuple-element.63.refs_0_, f32[128,2048]{1,0:T(8,128)} %get-tuple-element.70.refs_1_, ...), custom_call_target="tpu_custom_call" | custom-call | tf_op jit(solution)/shard_map/pallas_call | solution.py:2266
  (1 shorter events, 0.0 us)
